TPU v7x, 32 devices: a whole 2x2x4 slice. The times are simulated.
32 devices in a mesh: groups: 2 (over x), tgt: 16 (over z, y, core).
Axes of the slice: x: 2, y: 2, z: 4, core: 2. Of those that a mesh axis runs over, the one named last changes fastest.
Arguments:
- source_feats: bfloat16 [4096, 1024], P(('groups', 'tgt')), parts along dimension 0, may hold values from -18 to 18
- target_feats: bfloat16 [16384, 1024], P(('groups', 'tgt')), parts along dimension 0, may hold values from -18 to 18
- source_logits: float32 [4096], P('groups'), parts along dimension 0, may hold values from -1.2 to 1.2
- target_logits: float32 [16384], P(('groups', 'tgt')), parts along dimension 0, may hold values from -1 to 3.4
Outputs:
- grad_source: float32 [4096, 1024], P(('groups', 'tgt')), parts along dimension 0
- grad_target: float32 [16384, 1024], P(('groups', 'tgt')), parts along dimension 0
- potential_src: float32 [4096], P('groups'), parts along dimension 0
- potential_tgt: float32 [16384], P(('groups', 'tgt')), parts along dimension 0
There are 2 independent parts, one for each index of `groups`. A program takes and returns all parts, laid end to end along the dimension named above; each array names one. Nothing has to cross between parts.
All inputs are finite; a program needn't handle non-finite values.
Results may differ from a plain program's by a relative error of at most 0.0033.
Values may be sent and summed in bfloat16 or wider, within the bound.
No kernel may reach another device: no remote copies, remote signals or barrier semaphores. Data moves between devices by JAX's collectives and lax.ppermute only.
A program may use at most 64 MiB of HBM per device.

v0:
```python
import math

import jax
import jax.numpy as jnp
from jax import lax
from jax.sharding import PartitionSpec as P

ITERS = 3


def per_device(source_feats, target_feats, source_logits, target_logits):
    width = target_feats.shape[1]
    scale = 1.0 / math.sqrt(width)
    source_count = source_feats.shape[0] * lax.axis_size("tgt")
    target_count = target_feats.shape[0] * lax.axis_size("tgt")
    log_source = source_logits - jnp.log(jnp.sum(jnp.exp(source_logits)))
    target_total = lax.psum(jnp.sum(jnp.exp(target_logits)), "tgt")
    log_target = target_logits - jnp.log(target_total)
    target_sq = jnp.sum(jnp.square(target_feats.astype(jnp.float32)), axis=1)
    gathered = lax.all_gather(source_feats, "tgt", axis=0, tiled=True)
    cross = lax.dot_general(
        gathered, target_feats, (((1,), (1,)), ((), ())), preferred_element_type=jnp.float32
    )
    gathered_sq = jnp.sum(jnp.square(gathered.astype(jnp.float32)), axis=1)
    cost = (gathered_sq[:, None] + target_sq[None, :] - 2.0 * cross) * scale
    potential_tgt = jnp.zeros((target_feats.shape[0],), jnp.float32)
    potential_src = jnp.zeros((source_count,), jnp.float32)
    for step in range(ITERS):
        scores = (log_target + potential_tgt)[None, :] - cost
        top = lax.pmax(jnp.max(scores, axis=1), "tgt")
        total = lax.psum(jnp.sum(jnp.exp(scores - top[:, None]), axis=1), "tgt")
        potential_src = -(top + jnp.log(total))
        column = (log_source + potential_src)[:, None] - cost
        column_top = jnp.max(column, axis=0)
        potential_tgt = -(
            column_top + jnp.log(jnp.sum(jnp.exp(column - column_top[None, :]), axis=0))
        )
    plan = jnp.exp(
        math.log(source_count)
        + (log_source + potential_src)[:, None]
        + (log_target + potential_tgt)[None, :]
        - cost
    ).astype(jnp.bfloat16)
    row_mass = jnp.sum(plan.astype(jnp.float32), axis=1)
    row_part = jnp.dot(plan, target_feats, preferred_element_type=jnp.float32)
    share_part, share_mass = (
        lax.psum_scatter(row_part, "tgt", scatter_dimension=0, tiled=True),
        lax.psum_scatter(row_mass, "tgt", scatter_dimension=0, tiled=True),
    )
    grad_source = share_mass[:, None] * source_feats.astype(jnp.float32) - share_part
    col_part = lax.dot_general(
        plan, gathered, (((0,), (0,)), ((), ())), preferred_element_type=jnp.float32
    )
    col_mass = jnp.sum(plan.astype(jnp.float32), axis=0)
    grad_target = (
        target_count
        / source_count
        * (col_mass[:, None] * target_feats.astype(jnp.float32) - col_part)
    )
    return (grad_source, grad_target, potential_src, potential_tgt)


def solution(mesh):
    return jax.shard_map(
        per_device,
        mesh=mesh,
        in_specs=(
            P(("groups", "tgt"), None),
            P(("groups", "tgt"), None),
            P("groups"),
            P(("groups", "tgt")),
        ),
        out_specs=(
            P(("groups", "tgt"), None),
            P(("groups", "tgt"), None),
            P("groups"),
            P(("groups", "tgt")),
        ),
        check_vma=False,
    )
```

profile of v0, /device:TPU:0, one launch (start us, length us, event | category | flops | bytes accessed | tf_op | source)
XLA Modules:
  0.0 395.1 jit_solution(12551948818565337685)
XLA Ops:
  9.3 36.0 %psum.28 = f32[]{:T(128)} all-reduce(f32[]{:T(128)} %exponential_reduce_fusion.7), channel_id=1, replica_groups=mesh['groups'=2,'tgt'=16] {'tgt'}, use_global_device_ids=true, to_apply=%region_2.0 | all-reduce | flops 1 | bytes 8 | tf_op jit(solution)/shard_map/psum | solution.py:17
  45.9 1.3 exponential_reduce_fusion.6
  47.9 1.5 fusion
  50.2 13.4 %all-gather.2.cloned.1.call-done = bf16[2048,1024]{1,0:T(8,128)(2,1)} async-done(((bf16[128,1024]{1,0:T(8,128)(2,1)}), bf16[2048,1024]{1,0:T(8,128)(2,1)}) %all-gather.2.cloned.1.call-update) | async-done | bytes 4194320 | tf_op jit(solution)/shard_map/all_gather | solution.py:20
  63.6 3.2 multiply_reduce_fusion
  67.0 4.8 %subtract_reduce_fusion.5 = (f32[2048]{0:T(1024)S(1)}, f32[2048,512]{1,0:T(8,128)}) fusion(f32[512]{0:T(512)S(1)} %broadcast_subtract_fusion, bf16[2048,1024]{1,0:T(8,128)(2,1)S(1)} %copy-done.3, bf16[512,1024]{1,0:T(8,128)(2,1)S(1)} %copy-done.5, f32[512]{0:T(512)S(1)} %fusion, f32[2048]{0:T(1024)S(1)} %multiply_reduce_fusion), kind=kOutput, calls=%fused_computation.16 | convolution fusion | flops 2153773056 | bytes 9457664 | tf_op jit(solution)/shard_map/dot_general | solution.py:21
  71.8 31.6 %pmax.21 = f32[2048]{0:T(1024)S(1)} all-reduce(f32[2048]{0:T(1024)S(1)} %get-tuple-element.12), channel_id=1, replica_groups=mesh['groups'=2,'tgt'=16] {'tgt'}, use_global_device_ids=true, to_apply=%region_6.0 | all-reduce | flops 2048 | bytes 16384 | tf_op jit(solution)/shard_map/pmax | solution.py:30
  103.5 3.2 exponential_reduce_fusion.5
  106.7 30.0 %psum.29 = f32[2048]{0:T(1024)S(1)} all-reduce(f32[2048]{0:T(1024)S(1)} %exponential_reduce_fusion.5), channel_id=1, replica_groups=mesh['groups'=2,'tgt'=16] {'tgt'}, use_global_device_ids=true, to_apply=%region_8.0 | all-reduce | flops 2048 | bytes 16384 | tf_op jit(solution)/shard_map/psum | solution.py:31
  136.8 2.7 subtract_reduce_fusion.4
  141.3 30.0 %pmax.22 = f32[2048]{0:T(1024)S(1)} all-reduce(f32[2048]{0:T(1024)S(1)} %subtract_reduce_fusion.3), channel_id=1, replica_groups=mesh['groups'=2,'tgt'=16] {'tgt'}, use_global_device_ids=true, to_apply=%region_12.0 | all-reduce | flops 2048 | bytes 16384 | tf_op jit(solution)/shard_map/pmax | solution.py:30
  171.3 3.2 exponential_reduce_fusion.3
  174.5 30.0 %psum.30 = f32[2048]{0:T(1024)S(1)} all-reduce(f32[2048]{0:T(1024)S(1)} %exponential_reduce_fusion.3), channel_id=1, replica_groups=mesh['groups'=2,'tgt'=16] {'tgt'}, use_global_device_ids=true, to_apply=%region_14.0 | all-reduce | flops 2048 | bytes 16384 | tf_op jit(solution)/shard_map/psum | solution.py:31
  204.6 2.7 subtract_reduce_fusion.2
  209.1 30.0 %pmax.23 = f32[2048]{0:T(1024)S(1)} all-reduce(f32[2048]{0:T(1024)S(1)} %subtract_reduce_fusion.1), channel_id=1, replica_groups=mesh['groups'=2,'tgt'=16] {'tgt'}, use_global_device_ids=true, to_apply=%region_18.0 | all-reduce | flops 2048 | bytes 16384 | tf_op jit(solution)/shard_map/pmax | solution.py:30
  239.1 3.2 exponential_reduce_fusion.1
  242.3 30.2 %psum.31 = f32[2048]{0:T(1024)S(1)} all-reduce(f32[2048]{0:T(1024)S(1)} %exponential_reduce_fusion.1), channel_id=1, replica_groups=mesh['groups'=2,'tgt'=16] {'tgt'}, use_global_device_ids=true, to_apply=%region_20.0 | all-reduce | flops 2048 | bytes 16384 | tf_op jit(solution)/shard_map/psum | solution.py:31
  273.1 2.9 subtract_reduce_fusion
  277.4 1.3 convert_reduce_fusion
  278.7 5.6 %fusion.4 = f32[2048,1024]{1,0:T(8,128)} fusion(bf16[2048,512]{1,0:T(8,128)(2,1)S(1)} %get-tuple-element.6, bf16[512,1024]{1,0:T(8,128)(2,1)S(1)} %copy-done.5), kind=kOutput, calls=%fused_computation.35 | convolution fusion | flops 2147483648 | bytes 11534336 | tf_op jit(solution)/shard_map/dot_general | solution.py:45
  286.2 30.1 %all-reduce = f32[2048]{0:T(1024)S(1)} all-reduce(f32[2048]{0:T(1024)S(1)} %get-tuple-element.5), channel_id=2, replica_groups=mesh['groups'=2,'tgt'=16] {'tgt'}, use_global_device_ids=true, to_apply=%region_24.0.clone | all-reduce | flops 2048 | bytes 16384
  316.3 5.9 %fusion.2 = f32[512,1024]{1,0:T(8,128)} fusion(bf16[512,1024]{1,0:T(8,128)(2,1)S(1)} %copy-done.5, bf16[2048,512]{1,0:T(8,128)(2,1)S(1)} %get-tuple-element.6, bf16[2048,1024]{1,0:T(8,128)(2,1)} %all-gather.2.cloned.1.call-done, f32[512]{0:T(512)S(1)} %get-tuple-element.4), kind=kOutput, calls=%fused_computation.21 | convolution fusion | flops 2149580800 | bytes 9439232 | tf_op jit(solution)/shard_map/dot_general | solution.py:51
  322.2 64.0 %reduce-scatter.2.cloned.1.call-done = f32[128,1024]{1,0:T(8,128)} async-done(((f32[2048,1024]{1,0:T(8,128)}), f32[128,1024]{1,0:T(8,128)}) %reduce-scatter.2.cloned.1.call-update) | async-done | bytes 524304 | tf_op jit(solution)/shard_map/reduce_scatter | solution.py:47
  386.3 2.0 multiply_subtract_fusion
  (37 shorter events, 10.0 us)
Async XLA Ops:
  7.2 59.6 %copy-start.5 = (bf16[512,1024]{1,0:T(8,128)(2,1)S(1)}, bf16[512,1024]{1,0:T(8,128)(2,1)}, u32[]{:S(2)}) copy-start(bf16[512,1024]{1,0:T(8,128)(2,1)} %param.5) | copy-start | bytes 3145732
  7.2 56.4 %all-gather.2.cloned.1.call-start = ((), (), s32[]{:S(2)}) async-start(), calls=%async_computation.1 | async-start | bytes 4456448 | tf_op jit(solution)/shard_map/all_gather | solution.py:20
  7.9 378.4 %reduce-scatter.2.cloned.1.call-start = ((), (), s32[]{:S(2)}) async-start(), calls=%async_computation.2 | async-start | bytes 8912896 | tf_op jit(solution)/shard_map/reduce_scatter | solution.py:47
  63.6 3.4 copy-start.3
  71.8 64.9 %copy-start.6 = (f32[2048]{0:T(1024)S(1)}, f32[2048]{0:T(1024)}, u32[]{:S(2)}) copy-start(f32[2048]{0:T(1024)} %param.6) | copy-start | bytes 24580
  136.7 3.5 copy-start
  136.7 4.2 %copy-start.7 = (f32[512]{0:T(512)S(1)}, f32[512]{0:T(512)}, u32[]{:S(2)}) copy-start(f32[512]{0:T(512)} %param.7) | copy-start | bytes 6148
  204.5 3.5 copy-start.1
  272.5 3.5 copy-start.2
  284.3 0.7 copy-start.8
  316.3 69.9 %copy-start.4 = (bf16[128,1024]{1,0:T(8,128)(2,1)S(1)}, bf16[128,1024]{1,0:T(8,128)(2,1)}, u32[]{:S(2)}) copy-start(bf16[128,1024]{1,0:T(8,128)(2,1)} %param.4) | copy-start | bytes 786436
Sparse Core Ops, SparseCore 0:
  10.2 53.3 all-gather.1
  284.4 101.8 reduce-scatter.1
where the time goes:
time: 396 us; the launch traced here: 395 us
  blocking collectives  248 us (63%)
  waiting for transfers between devices  78.1 us (20%)
  other arithmetic  33.4 us (8%)
  matrix products  16.3 us (4%)
  between operations  16.3 us (4%)
    pmax x3, blocking collectives, per_device(): top = lax.pmax(jnp.max(scores, axis=1), 'tgt')  91.6 us
    psum x3, blocking collectives, per_device(): total = lax.psum(jnp.sum(jnp.exp(scores - top[:, None]), axis=1), 'tgt')  90.2 us
    reduce_scatter x1, waiting for transfers between devices, per_device(): lax.psum_scatter(row_part, 'tgt', scatter_dimension=0, tiled=True)  64 us
    psum x1, blocking collectives, per_device(): target_total = lax.psum(jnp.sum(jnp.exp(target_logits)), 'tgt')  36 us
    unnamed x1, blocking collectives  30.1 us
    all_gather x1, waiting for transfers between devices, per_device(): gathered = lax.all_gather(source_feats, 'tgt', axis=0, tiled=True)  13.4 us
    reduce_sum x3, other arithmetic, per_device(): total = lax.psum(jnp.sum(jnp.exp(scores - top[:, None]), axis=1), 'tgt')  9.62 us
    reduce_max x3, other arithmetic, per_device(): column_top = jnp.max(column, axis=0)  8.23 us
  transfers between devices with their start and end apart: 2, of which 2 were waited for; matrix products, arithmetic and copies ran while one was open for 3% of the time, Pallas kernels for 0%

commit v1 on v0

v1 whole, which is shorter than its diff:
```python
import functools
import math

import jax
import jax.numpy as jnp
from jax import lax
from jax.experimental import pallas as pl
from jax.experimental.pallas import tpu as pltpu
from jax.sharding import PartitionSpec as P

ITERS = 3
AXIS = "tgt"
VMEM = pl.BlockSpec(memory_space=pltpu.VMEM)
F32 = jnp.float32
BF16 = jnp.bfloat16


def params(mib):
    return pltpu.CompilerParams(vmem_limit_bytes=mib << 20)


def swap(value, mask):
    count = lax.axis_size(AXIS)
    return lax.ppermute(value, AXIS, [(i, i ^ mask) for i in range(count)])


def tree_levels(count):
    levels, step = [], 1
    while step < count:
        if step * 4 <= count:
            levels.append((step, 2 * step, 3 * step))
            step *= 4
        else:
            levels.append((step,))
            step *= 2
    return levels


def flip_blocks(value, mask, count):
    lead = value.shape[:-1]
    width = value.shape[-1] // count
    blocks = [value[..., (r ^ mask) * width : ((r ^ mask) + 1) * width] for r in range(count)]
    return jnp.concatenate(blocks, axis=-1)


def cost_kernel(scale, blocks, *refs):
    x_refs = refs[:blocks]
    y_ref, u_ref, s_ref, top_ref, sum_ref, x_out = refs[blocks:]
    rows = x_refs[0].shape[0]
    for q in range(blocks):
        x_out[q * rows : (q + 1) * rows, :] = x_refs[q][...]
    s = scale * lax.dot_general(
        y_ref[...], x_out[...], (((1,), (1,)), ((), ())), preferred_element_type=F32
    )
    s_ref[...] = s
    shifted = s + u_ref[...]
    top = jnp.max(shifted, axis=0, keepdims=True)
    top_ref[...] = top
    sum_ref[...] = jnp.sum(jnp.exp(shifted - top), axis=0, keepdims=True)


def first_column_kernel(chunks, *refs):
    s_refs = refs[:chunks]
    q_ref, w_ref, p_ref, row_ref, g_ref = refs[chunks:]
    width = s_refs[0].shape[1]
    q = q_ref[...]
    parts = [s_refs[k][...] + q[:, k * width : (k + 1) * width] for k in range(chunks)]
    top = functools.reduce(
        jnp.maximum, [jnp.max(part, axis=1, keepdims=True) for part in parts]
    )
    parts = [jnp.exp(part - top) for part in parts]
    total = functools.reduce(
        jnp.add, [jnp.sum(part, axis=1, keepdims=True) for part in parts]
    )
    g_ref[...] = -(top + jnp.log(total))
    inverse = 1.0 / total

    @pl.when(pl.program_id(0) == 0)
    def _():
        row_ref[...] = jnp.zeros_like(row_ref)

    for k in range(chunks):
        p = parts[k] * inverse
        p_ref[:, k * width : (k + 1) * width] = p
        row_ref[:, k * width : (k + 1) * width] += jnp.sum(
            p * w_ref[...], axis=0, keepdims=True
        )


def step_kernel(p_ref, a_ref, w_ref, row_ref):
    p = p_ref[...]
    c = jnp.sum(p * a_ref[...], axis=1, keepdims=True)

    @pl.when(pl.program_id(0) == 0)
    def _():
        row_ref[...] = jnp.zeros_like(row_ref)

    row_ref[...] += jnp.sum(p * (w_ref[...] / c), axis=0, keepdims=True)


def plan_kernel(chunks, p_ref, a_ref, w_ref, *refs):
    plan_refs = refs[:chunks]
    logb_ref, col_ref, row_ref = refs[chunks:]
    p = p_ref[...] * a_ref[...]
    c = jnp.sum(p, axis=1, keepdims=True)
    logb_ref[...] = -jnp.log(c)
    plan = (p * (w_ref[...] / c)).astype(BF16)
    width = plan_refs[0].shape[1]
    for k in range(chunks):
        plan_refs[k][...] = plan[:, k * width : (k + 1) * width]
    wide = plan.astype(F32)
    col_ref[...] = jnp.sum(wide, axis=1, keepdims=True)

    @pl.when(pl.program_id(0) == 0)
    def _():
        row_ref[...] = jnp.zeros_like(row_ref)

    row_ref[...] += jnp.sum(wide, axis=0, keepdims=True)


def all_sum(vector, count):
    for level in tree_levels(count):
        vector = vector + sum(
            flip_blocks(swap(vector, mask), mask, count) for mask in level
        )
    return vector


def all_lse(top, total, extra, count):
    for level in tree_levels(count):
        packed = jnp.concatenate([top, total, extra], axis=1)
        width = top.shape[1]
        tops, totals, extras = [top], [total], [extra]
        for mask in level:
            other = swap(packed, mask)
            tops.append(flip_blocks(other[:, :width], mask, count))
            totals.append(flip_blocks(other[:, width : 2 * width], mask, count))
            extras.append(other[:, 2 * width :])
        top = functools.reduce(jnp.maximum, tops)
        total = sum(t * jnp.exp(m - top) for m, t in zip(tops, totals))
        extra = sum(extras)
    return top, total, extra


def per_device(source_feats, target_feats, source_logits, target_logits):
    count = lax.axis_size(AXIS)
    me = lax.axis_index(AXIS)
    rows, width = source_feats.shape
    cols = target_feats.shape[0]
    source_count = rows * count
    target_count = cols * count
    scale = 1.0 / math.sqrt(width)
    direct = count == 16
    chunks = 4
    chunk = source_count // chunks
    order = jnp.bitwise_xor(me, jnp.arange(count))

    by_chunk = []
    if direct:
        for k in range(chunks):
            block = source_feats if k == 0 else swap(source_feats, 4 * k)
            pair = [block, swap(block, 2)]
            by_chunk.append([pair[0], swap(pair[0], 1), pair[1], swap(pair[1], 1)])
    else:
        gathered = lax.all_gather(source_feats, AXIS, axis=0)[order]
        gathered = gathered.reshape(chunks, chunk, width)
        by_chunk = [[gathered[k]] for k in range(chunks)]

    target_weight = jnp.exp(target_logits)[:, None]
    target_sq = scale * jnp.sum(jnp.square(target_feats.astype(F32)), axis=1, keepdims=True)
    lift = target_logits[:, None] - target_sq

    cost_call = pl.pallas_call(
        functools.partial(cost_kernel, 2.0 * scale, len(by_chunk[0])),
        name="cost",
        out_shape=(
            jax.ShapeDtypeStruct((cols, chunk), F32),
            jax.ShapeDtypeStruct((1, chunk), F32),
            jax.ShapeDtypeStruct((1, chunk), F32),
            jax.ShapeDtypeStruct((chunk, width), BF16),
        ),
        in_specs=[VMEM] * (len(by_chunk[0]) + 2),
        out_specs=(VMEM,) * 4,
        compiler_params=params(24),
        cost_estimate=pl.CostEstimate(
            flops=2 * cols * chunk * width, bytes_accessed=5 << 20, transcendentals=cols * chunk
        ),
    )
    scores, tops, sums, feats = zip(
        *[cost_call(*blocks, target_feats, lift) for blocks in by_chunk]
    )

    source_rel = source_logits.reshape(count, rows)[order].reshape(1, source_count)
    source_log = source_rel - jnp.log(jnp.sum(jnp.exp(source_logits)))
    source_mass = jnp.exp(source_log)

    local_total = jnp.broadcast_to(jnp.sum(target_weight), (1, 128))
    top, total, target_total = all_lse(
        jnp.concatenate(tops, axis=1), jnp.concatenate(sums, axis=1), local_total, count
    )
    target_total = target_total[:, :1]
    f1 = jnp.log(target_total) - (top + jnp.log(total))

    tile = 64
    grid = (cols // tile,)
    tall = pl.BlockSpec((tile, source_count), lambda j: (j, 0))
    thin = pl.BlockSpec((tile, 1), lambda j: (j, 0))
    flat = pl.BlockSpec((1, source_count), lambda j: (0, 0))
    part = pl.BlockSpec((tile, chunk), lambda j: (j, 0))
    thin_shape = jax.ShapeDtypeStruct((cols, 1), F32)
    flat_shape = jax.ShapeDtypeStruct((1, source_count), F32)

    p1, row, g1 = pl.pallas_call(
        functools.partial(first_column_kernel, chunks),
        name="first_column",
        grid=grid,
        out_shape=(jax.ShapeDtypeStruct((cols, source_count), F32), flat_shape, thin_shape),
        in_specs=[part] * chunks + [flat, thin],
        out_specs=(tall, flat, thin),
        compiler_params=params(24),
    )(*scores, source_log + f1, target_weight)

    scaled_mass = source_mass * target_total
    for _ in range(ITERS - 2):
        ratio = scaled_mass / all_sum(row, count)
        row = pl.pallas_call(
            step_kernel,
            name="step",
            grid=grid,
            out_shape=flat_shape,
            in_specs=[tall, flat, thin],
            out_specs=flat,
            compiler_params=params(24),
        )(p1, ratio, target_weight)
    ratio = scaled_mass / all_sum(row, count)

    *plans, logb, col_mass, row_mass = pl.pallas_call(
        functools.partial(plan_kernel, chunks),
        name="plan",
        grid=grid,
        out_shape=[jax.ShapeDtypeStruct((cols, chunk), BF16)] * chunks
        + [thin_shape, thin_shape, flat_shape],
        in_specs=[tall, flat, thin],
        out_specs=[part] * chunks + [thin, thin, flat],
        compiler_params=params(24),
    )(p1, ratio, target_weight * (source_count / target_total))

    row_part = None
    if not direct:
        full = lax.dot_general(
            jnp.concatenate(plans, axis=1),
            target_feats,
            (((0,), (0,)), ((), ())),
            preferred_element_type=F32,
        ).reshape(count, rows, width)[order]
        row_part = lax.psum_scatter(full, AXIS, scatter_dimension=0)
    for k in [3, 2, 1, 0] if direct else []:
        full = lax.dot_general(
            plans[k], target_feats, (((0,), (0,)), ((), ())), preferred_element_type=F32
        ).reshape(2, 2, rows, width)
        chip = full[:, 0] + swap(full[:, 1], 1)
        line = chip[0] + swap(chip[1].astype(BF16), 2).astype(F32)
        if k:
            line = swap(line.astype(BF16), 4 * k).astype(F32)
        row_part = line if row_part is None else row_part + line

    mass = all_sum(row_mass, count)[0, :rows]
    grad_source = mass[:, None] * source_feats.astype(F32) - row_part

    col_part = sum(
        lax.dot_general(plans[k], feats[k], (((1,), (0,)), ((), ())), preferred_element_type=F32)
        for k in range(chunks)
    )
    grad_target = (target_count / source_count) * (
        col_mass * target_feats.astype(F32) - col_part
    )

    source_sq = scale * jnp.concatenate(
        [jnp.sum(jnp.square(x.astype(F32)), axis=1) for x in feats]
    )
    potential_src = (f1 + jnp.log(ratio)).reshape(source_count) + source_sq
    potential_src = potential_src.reshape(count, rows)[order].reshape(source_count)
    potential_tgt = (g1 + logb + target_sq).reshape(cols)
    return (grad_source, grad_target, potential_src, potential_tgt)


def solution(mesh):
    return jax.shard_map(
        per_device,
        mesh=mesh,
        in_specs=(
            P(("groups", "tgt"), None),
            P(("groups", "tgt"), None),
            P("groups"),
            P(("groups", "tgt")),
        ),
        out_specs=(
            P(("groups", "tgt"), None),
            P(("groups", "tgt"), None),
            P("groups"),
            P(("groups", "tgt")),
        ),
        check_vma=False,
    )
```

time: 396 us -> 185 us (0.47)
  blocking collectives: 248 us -> 0 us
  starting transfers between devices: 0.08 us -> 45.9 us
  local copies, waits for them, and re-layouts: 2.98 us -> 28.9 us
  other arithmetic: 33.4 us -> 13 us
  Pallas kernels: 0 us -> 16.1 us
  waiting for transfers between devices: 78.1 us -> 63.4 us
  between operations: 16.3 us -> 2.65 us
    psum x4 -> x0, blocking collectives: 126 us -> none  [the longest x3 90.2 us: per_device(): total = lax.psum(jnp.sum(jnp.exp(scores - top[:, None]), axis=1), 'tgt')]
    pmax x3 -> x0, blocking collectives: 91.6 us -> none  [per_device(): top = lax.pmax(jnp.max(scores, axis=1), 'tgt')]
    reduce_scatter x1 -> x0, waiting for transfers between devices: 64 us -> none  [per_device(): lax.psum_scatter(row_part, 'tgt', scatter_dimension=0, tiled=True)]
    ppermute x0 -> x50, waiting for transfers between devices: none -> 63.4 us  [swap(): return lax.ppermute(value, AXIS, [(i, i ^ mask) for i in range(count)])]
    ppermute x0 -> x50, starting transfers between devices: none -> 45.9 us  [swap(): return lax.ppermute(value, AXIS, [(i, i ^ mask) for i in range(count)])]
    unnamed x1 -> x0, blocking collectives: 30.1 us -> none
    unnamed x20 -> x241, local copies, waits for them, and re-layouts: 2.98 us -> 19.9 us
    reduce_sum x11 -> x6, other arithmetic: 20.6 us -> 3.93 us  [the longest x1 1.5 us: per_device(): jnp.sum(jnp.square(target_feats.astype(F32)), axis=1, keepdims=True)]
  transfers between devices with their start and end apart: 2 -> 50, of which waited for: 2 -> 21; matrix products, arithmetic and copies ran while one was open for 3% -> 19% of each run, Pallas kernels for 0% -> 3%
where the time goes in v1:
time: 185 us; the launch traced here: 184 us
  waiting for transfers between devices  63.4 us (34%)
  starting transfers between devices  45.9 us (25%)
  local copies, waits for them, and re-layouts  28.9 us (16%)
  Pallas kernels  16.1 us (9%)
  matrix products  14.1 us (8%)
  other arithmetic  13 us (7%)
  between operations  2.65 us (1%)
    ppermute x50, waiting for transfers between devices, swap(): return lax.ppermute(value, AXIS, [(i, i ^ mask) for i in range(count)])  63.4 us
    ppermute x50, starting transfers between devices, swap(): return lax.ppermute(value, AXIS, [(i, i ^ mask) for i in range(count)])  45.9 us
    unnamed x241, local copies, waits for them, and re-layouts  19.9 us
    dot_general x4, matrix products, per_device(): lax.dot_general(plans[k], feats[k], (((1,), (0,)), ((), ())), preferred_e...  11.2 us
    pallas_call x4, Pallas kernels, per_device(): cost_call(*blocks, target_feats, lift)  7.48 us
    add x4, other arithmetic, per_device(): chip = full[:, 0] + swap(full[:, 1], 1)  4.58 us
    squeeze x4, local copies, waits for them, and re-layouts, per_device(): chip = full[:, 0] + swap(full[:, 1], 1)  4.41 us
  transfers between devices with their start and end apart: 50, of which 21 were waited for; matrix products, arithmetic and copies ran while one was open for 19% of the time, Pallas kernels for 3%

profile of v1, /device:TPU:0, one launch (start us, length us, event | category | flops | bytes accessed | tf_op | source)
XLA Modules:
  0.0 184.0 jit_solution(4189343730260608285)
XLA Ops:
  1.2 2.6 %collective-permute-start.1 = (bf16[128,1024]{1,0:T(8,128)(2,1)}, bf16[128,1024]{1,0:T(8,128)(2,1)S(1)}, u32[]{:S(2)}, u32[]{:S(2)}) collective-permute-start(bf16[128,1024]{1,0:T(8,128)(2,1)} %refs_0_.1), channel_id=1, source_target_pairs={{0,2},{1,3},{2,0},{3,1},{4,6},{5,7},{6,4},{7,5},{8,10},{9,11},{10,... | collective-permute-start | bytes 786440 | tf_op jit(solution)/shard_map/ppermute | solution.py:24
  5.3 2.6 %collective-permute-start.7 = (bf16[128,1024]{1,0:T(8,128)(2,1)}, bf16[128,1024]{1,0:T(8,128)(2,1)}, u32[]{:S(2)}, u32[]{:S(2)}) collective-permute-start(bf16[128,1024]{1,0:T(8,128)(2,1)} %refs_0_.1), channel_id=1, source_target_pairs={{0,8},{1,9},{2,10},{3,11},{4,12},{5,13},{6,14},{7,15},{8,0},{9,1},... | collective-permute-start | bytes 786440 | tf_op jit(solution)/shard_map/ppermute | solution.py:24
  11.0 6.3 %collective-permute-done.3.refs_0_ = bf16[128,1024]{1,0:T(8,128)(2,1)S(1)} collective-permute-done((bf16[128,1024]{1,0:T(8,128)(2,1)}, bf16[128,1024]{1,0:T(8,128)(2,1)S(1)}, u32[]{:S(2)}, u32[]{:S(2)}) %collective-permute-start.3) | collective-permute-done | bytes 262176 | tf_op jit(solution)/shard_map/ppermute | solution.py:24
  17.8 9.2 %collective-permute-done.7.refs_0_ = bf16[128,1024]{1,0:T(8,128)(2,1)} collective-permute-done((bf16[128,1024]{1,0:T(8,128)(2,1)}, bf16[128,1024]{1,0:T(8,128)(2,1)}, u32[]{:S(2)}, u32[]{:S(2)}) %collective-permute-start.7) | collective-permute-done | bytes 262176 | tf_op jit(solution)/shard_map/ppermute | solution.py:24
  31.5 2.7 %collective-permute-done.9.refs_2_ = bf16[128,1024]{1,0:T(8,128)(2,1)} collective-permute-done((bf16[128,1024]{1,0:T(8,128)(2,1)}, bf16[128,1024]{1,0:T(8,128)(2,1)}, u32[]{:S(2)}, u32[]{:S(2)}) %collective-permute-start.9) | collective-permute-done | bytes 262176 | tf_op jit(solution)/shard_map/ppermute | solution.py:24
  47.0 2.2 %cost.6 = (f32[512,512]{1,0:T(8,128)S(1)}, f32[1,512]{1,0:T(1,128)S(1)}, f32[1,512]{1,0:T(1,128)S(1)}, bf16[512,1024]{1,0:T(8,128)(2,1)S(1)}) custom-call(bf16[128,1024]{1,0:T(8,128)(2,1)} %collective-permute-done.7.refs_0_, bf16[128,1024]{1,0:T(8,128)(2,1)} %collective-permute-done.8.refs_1_, bf16[128,1024]{1,0:T(8,128)(2,1)} %collective-permute-done.9.refs_2_, ...), custom_call_target="tpu_custom_call" | custom-call | flops 536870912 | bytes 5242880 | tf_op jit(solution)/shard_map/cost/pallas_call | solution.py:190
  50.2 2.4 %cost.7 = (f32[512,512]{1,0:T(8,128)S(1)}, f32[1,512]{1,0:T(1,128)S(1)}, f32[1,512]{1,0:T(1,128)S(1)}, bf16[512,1024]{1,0:T(8,128)(2,1)S(1)}) custom-call(bf16[128,1024]{1,0:T(8,128)(2,1)} %collective-permute-done.11.refs_0_, bf16[128,1024]{1,0:T(8,128)(2,1)S(1)} %collective-permute-done.12.refs_1_, bf16[128,1024]{1,0:T(8,128)(2,1)} %collective-permute-done.13.refs_2_, ...), custom_call_target="tpu_custom_call" | custom-call | flops 536870912 | bytes 5242880 | tf_op jit(solution)/shard_map/cost/pallas_call | solution.py:190
  61.7 2.5 %collective-permute-start.20 = (f32[1,4224]{1,0:T(1,128)S(1)}, f32[1,4224]{1,0:T(1,128)S(1)}, u32[]{:S(2)}, u32[]{:S(2)}) collective-permute-start(f32[1,4224]{1,0:T(1,128)S(1)} %pad_maximum_fusion), channel_id=1, source_target_pairs={{0,12},{1,13},{2,14},{3,15},{4,8},{5,9},{6,10},{7,11},{8,4},{9,5},... | collective-permute-start | bytes 50696 | tf_op jit(solution)/shard_map/ppermute | solution.py:24
  72.8 3.3 %first_column.1 = (f32[512,2048]{1,0:T(8,128)S(1)}, f32[1,2048]{1,0:T(1,128)S(1)}, f32[512,1]{1,0:T(8,128)S(1)}) custom-call(f32[512,512]{1,0:T(8,128)S(1)} %copy-done.13, f32[512,512]{1,0:T(8,128)S(1)} %copy-done.15, f32[512,512]{1,0:T(8,128)S(1)} %copy-done.17, f32[512,512]{1,0:T(8,128)S(1)} %copy-done.19, f32[1,2048]{1,0:T(1,128)S(1)} %get-tuple-element.58.refs_4_, ...), custom_call_target="tpu_custom_call" | custom-call | tf_op jit(solution)/shard_map/first_column/pallas_call | solution.py:213
  80.3 2.3 %collective-permute-done.22 = f32[1,2048]{1,0:T(1,128)S(1)} collective-permute-done((f32[1,2048]{1,0:T(1,128)S(1)}, f32[1,2048]{1,0:T(1,128)S(1)}, u32[]{:S(2)}, u32[]{:S(2)}) %collective-permute-start.22) | collective-permute-done | bytes 8224 | tf_op jit(solution)/shard_map/ppermute | solution.py:24
  82.7 2.1 %collective-permute-start.25 = (f32[1,2048]{1,0:T(1,128)S(1)}, f32[1,2048]{1,0:T(1,128)S(1)}, u32[]{:S(2)}, u32[]{:S(2)}) collective-permute-start(f32[1,2048]{1,0:T(1,128)S(1)} %add_add_fusion.2), channel_id=1, source_target_pairs={{0,8},{1,9},{2,10},{3,11},{4,12},{5,13},{6,14},{7,15},{8,0},{9,1},... | collective-permute-start | bytes 24584 | tf_op jit(solution)/shard_map/ppermute | solution.py:24
  87.3 3.3 %collective-permute-done.26 = f32[1,2048]{1,0:T(1,128)S(1)} collective-permute-done((f32[1,2048]{1,0:T(1,128)S(1)}, f32[1,2048]{1,0:T(1,128)S(1)}, u32[]{:S(2)}, u32[]{:S(2)}) %collective-permute-start.26) | collective-permute-done | bytes 8224 | tf_op jit(solution)/shard_map/ppermute | solution.py:24
  90.7 2.1 %step.1 = f32[1,2048]{1,0:T(1,128)S(1)} custom-call(f32[512,2048]{1,0:T(8,128)S(1)} %get-tuple-element.42.p_ref, f32[1,2048]{1,0:T(1,128)S(1)} %fusion.31.a_ref, f32[512,1]{1,0:T(8,128)S(1)} %copy.20.refs_5_.w_ref), custom_call_target="tpu_custom_call" | custom-call | tf_op jit(solution)/shard_map/step/pallas_call | solution.py:226
  104.0 2.2 %copy-done.3 = f32[512,2048]{1,0:T(8,128)S(1)} copy-done((f32[512,2048]{1,0:T(8,128)S(1)}, f32[512,2048]{1,0:T(8,128)}, u32[]{:S(2)}) %copy-start.3) | copy-done | bytes 4194328
  106.2 3.2 %plan.1 = (bf16[512,512]{1,0:T(8,128)(2,1)S(1)}, bf16[512,512]{1,0:T(8,128)(2,1)S(1)}, bf16[512,512]{1,0:T(8,128)(2,1)S(1)}, bf16[512,512]{1,0:T(8,128)(2,1)S(1)...) custom-call(f32[512,2048]{1,0:T(8,128)S(1)} %copy-done.3, ...), custom_call_target="tpu_custom_call" | custom-call | tf_op jit(solution)/shard_map/plan/pallas_call | solution.py:237
  127.2 5.1 %fusion.2 = f32[512,1024]{1,0:T(8,128)} fusion(bf16[512,1024]{1,0:T(8,128)(2,1)S(1)} %copy-done.1, f32[512,1024]{1,0:T(8,128)} %fusion.57, f32[512,1024]{1,0:T(8,128)} %fusion.55, f32[512,1024]{1,0:T(8,128)} %fusion.56, f32[512]{0:T(512)S(1)} %reduce.1, bf16[512,512]{1,0:T(8,128)(2,1)S(1)} %copy-done.11, bf16[512,1024]{1,0:T(8,128)(2,1)S(1)} %copy-done.9), kind=kOutput, calls=%fused_computation.6 | convolution fusion | flops 540540928 | bytes 11012096 | tf_op jit(solution)/shard_map/dot_general | solution.py:271
  133.4 2.1 %collective-permute-start.38 = (f32[1,2048]{1,0:T(1,128)S(1)}, f32[1,2048]{1,0:T(1,128)S(1)}, u32[]{:S(2)}, u32[]{:S(2)}) collective-permute-start(f32[1,2048]{1,0:T(1,128)S(1)} %add_add_fusion), channel_id=1, source_target_pairs={{0,12},{1,13},{2,14},{3,15},{4,8},{5,9},{6,10},{7,11},{8,4},{9,5},... | collective-permute-start | bytes 24584 | tf_op jit(solution)/shard_map/ppermute | solution.py:24
  139.0 4.5 %collective-permute-done.37 = f32[1,2048]{1,0:T(1,128)S(1)} collective-permute-done((f32[1,2048]{1,0:T(1,128)S(1)}, f32[1,2048]{1,0:T(1,128)S(1)}, u32[]{:S(2)}, u32[]{:S(2)}) %collective-permute-start.37) | collective-permute-done | bytes 8224 | tf_op jit(solution)/shard_map/ppermute | solution.py:24
  152.8 7.2 %collective-permute-done.46 = bf16[128,1024]{1,0:T(8,128)(2,1)S(1)} collective-permute-done((bf16[128,1024]{1,0:T(8,128)(2,1)S(1)}, bf16[128,1024]{1,0:T(8,128)(2,1)S(1)}, u32[]{:S(2)}, u32[]{:S(2)}) %collective-permute-start.46) | collective-permute-done | bytes 262176 | tf_op jit(solution)/shard_map/ppermute | solution.py:24
  160.1 2.1 %collective-permute-start.47 = (bf16[128,1024]{1,0:T(8,128)(2,1)S(1)}, bf16[128,1024]{1,0:T(8,128)(2,1)S(1)}, u32[]{:S(2)}, u32[]{:S(2)}) collective-permute-start(bf16[128,1024]{1,0:T(8,128)(2,1)S(1)} %fusion.11), channel_id=1, source_target_pairs={{0,4},{1,5},{2,6},{3,7},{4,0},{5,1},{6,2},{7,3},{8,12},{9,13},{10,... | collective-permute-start | bytes 786440 | tf_op jit(solution)/shard_map/ppermute | solution.py:24
  162.2 3.2 %collective-permute-done.43 = bf16[128,1024]{1,0:T(8,128)(2,1)S(1)} collective-permute-done((bf16[128,1024]{1,0:T(8,128)(2,1)S(1)}, bf16[128,1024]{1,0:T(8,128)(2,1)S(1)}, u32[]{:S(2)}, u32[]{:S(2)}) %collective-permute-start.43) | collective-permute-done | bytes 262176 | tf_op jit(solution)/shard_map/ppermute | solution.py:24
  165.4 2.4 %collective-permute-start.44 = (bf16[128,1024]{1,0:T(8,128)(2,1)S(1)}, bf16[128,1024]{1,0:T(8,128)(2,1)S(1)}, u32[]{:S(2)}, u32[]{:S(2)}) collective-permute-start(bf16[128,1024]{1,0:T(8,128)(2,1)S(1)} %fusion.13), channel_id=1, source_target_pairs={{0,8},{1,9},{2,10},{3,11},{4,12},{5,13},{6,14},{7,15},{8,0},{9,1},... | collective-permute-start | bytes 786440 | tf_op jit(solution)/shard_map/ppermute | solution.py:24
  168.3 2.1 %collective-permute-start.41 = (bf16[128,1024]{1,0:T(8,128)(2,1)S(1)}, bf16[128,1024]{1,0:T(8,128)(2,1)S(1)}, u32[]{:S(2)}, u32[]{:S(2)}) collective-permute-start(bf16[128,1024]{1,0:T(8,128)(2,1)S(1)} %fusion.15), channel_id=1, source_target_pairs={{0,12},{1,13},{2,14},{3,15},{4,8},{5,9},{6,10},{7,11},{8,4},{9,5},... | collective-permute-start | bytes 786440 | tf_op jit(solution)/shard_map/ppermute | solution.py:24
  170.4 12.5 %collective-permute-done.44 = bf16[128,1024]{1,0:T(8,128)(2,1)S(1)} collective-permute-done((bf16[128,1024]{1,0:T(8,128)(2,1)S(1)}, bf16[128,1024]{1,0:T(8,128)(2,1)S(1)}, u32[]{:S(2)}, u32[]{:S(2)}) %collective-permute-start.44) | collective-permute-done | bytes 262176 | tf_op jit(solution)/shard_map/ppermute | solution.py:24
  (403 shorter events, 91.1 us)
Async XLA Ops:
  0.6 28.1 %collective-permute-start = (bf16[128,1024]{1,0:T(8,128)(2,1)}, bf16[128,1024]{1,0:T(8,128)(2,1)S(1)}, u32[]{:S(2)}, u32[]{:S(2)}) collective-permute-start(bf16[128,1024]{1,0:T(8,128)(2,1)} %refs_0_.1), channel_id=1, source_target_pairs={{0,1},{1,0},{2,3},{3,2},{4,5},{5,4},{6,7},{7,6},{8,9},{9,8},{10,11... | collective-permute-start | bytes 786440 | tf_op jit(solution)/shard_map/ppermute | solution.py:24
  3.8 13.6 %collective-permute-start.3 = (bf16[128,1024]{1,0:T(8,128)(2,1)}, bf16[128,1024]{1,0:T(8,128)(2,1)S(1)}, u32[]{:S(2)}, u32[]{:S(2)}) collective-permute-start(bf16[128,1024]{1,0:T(8,128)(2,1)} %refs_0_.1), channel_id=1, source_target_pairs={{0,4},{1,5},{2,6},{3,7},{4,0},{5,1},{6,2},{7,3},{8,12},{9,13},{10,... | collective-permute-start | bytes 786440 | tf_op jit(solution)/shard_map/ppermute | solution.py:24
  5.3 21.6 %collective-permute-start.7 = (bf16[128,1024]{1,0:T(8,128)(2,1)}, bf16[128,1024]{1,0:T(8,128)(2,1)}, u32[]{:S(2)}, u32[]{:S(2)}) collective-permute-start(bf16[128,1024]{1,0:T(8,128)(2,1)} %refs_0_.1), channel_id=1, source_target_pairs={{0,8},{1,9},{2,10},{3,11},{4,12},{5,13},{6,14},{7,15},{8,0},{9,1},... | collective-permute-start | bytes 786440 | tf_op jit(solution)/shard_map/ppermute | solution.py:24
  7.9 20.9 %collective-permute-start.11 = (bf16[128,1024]{1,0:T(8,128)(2,1)}, bf16[128,1024]{1,0:T(8,128)(2,1)}, u32[]{:S(2)}, u32[]{:S(2)}) collective-permute-start(bf16[128,1024]{1,0:T(8,128)(2,1)} %refs_0_.1), channel_id=1, source_target_pairs={{0,12},{1,13},{2,14},{3,15},{4,8},{5,9},{6,10},{7,11},{8,4},{9,5},... | collective-permute-start | bytes 786440 | tf_op jit(solution)/shard_map/ppermute | solution.py:24
  11.0 18.3 %collective-permute-start.2 = (bf16[128,1024]{1,0:T(8,128)(2,1)S(1)}, bf16[128,1024]{1,0:T(8,128)(2,1)S(1)}, u32[]{:S(2)}, u32[]{:S(2)}) collective-permute-start(bf16[128,1024]{1,0:T(8,128)(2,1)S(1)} %collective-permute-done.1.refs_2_), channel_id=1, source_target_pairs={{0,1},{1,0},{2,3},{3,2},{4,5},{5,4},{6,7},{7,6},{8,9},{9,8},{10,11... | collective-permute-start | bytes 786440 | tf_op jit(solution)/shard_map/ppermute | solution.py:24
  17.4 14.1 %collective-permute-start.5 = (bf16[128,1024]{1,0:T(8,128)(2,1)S(1)}, bf16[128,1024]{1,0:T(8,128)(2,1)S(1)}, u32[]{:S(2)}, u32[]{:S(2)}) collective-permute-start(bf16[128,1024]{1,0:T(8,128)(2,1)S(1)} %collective-permute-done.3.refs_0_), channel_id=1, source_target_pairs={{0,2},{1,3},{2,0},{3,1},{4,6},{5,7},{6,4},{7,5},{8,10},{9,11},{10,... | collective-permute-start | bytes 786440 | tf_op jit(solution)/shard_map/ppermute | solution.py:24
  28.8 12.7 %collective-permute-start.4 = (bf16[128,1024]{1,0:T(8,128)(2,1)S(1)}, bf16[128,1024]{1,0:T(8,128)(2,1)}, u32[]{:S(2)}, u32[]{:S(2)}) collective-permute-start(bf16[128,1024]{1,0:T(8,128)(2,1)S(1)} %collective-permute-done.3.refs_0_), channel_id=1, source_target_pairs={{0,1},{1,0},{2,3},{3,2},{4,5},{5,4},{6,7},{7,6},{8,9},{9,8},{10,11... | collective-permute-start | bytes 786440 | tf_op jit(solution)/shard_map/ppermute | solution.py:24
  28.8 18.2 %collective-permute-start.8 = (bf16[128,1024]{1,0:T(8,128)(2,1)}, bf16[128,1024]{1,0:T(8,128)(2,1)}, u32[]{:S(2)}, u32[]{:S(2)}) collective-permute-start(bf16[128,1024]{1,0:T(8,128)(2,1)} %collective-permute-done.7.refs_0_), channel_id=1, source_target_pairs={{0,1},{1,0},{2,3},{3,2},{4,5},{5,4},{6,7},{7,6},{8,9},{9,8},{10,11... | collective-permute-start | bytes 786440 | tf_op jit(solution)/shard_map/ppermute | solution.py:24
  30.0 12.0 %collective-permute-start.13 = (bf16[128,1024]{1,0:T(8,128)(2,1)}, bf16[128,1024]{1,0:T(8,128)(2,1)}, u32[]{:S(2)}, u32[]{:S(2)}) collective-permute-start(bf16[128,1024]{1,0:T(8,128)(2,1)} %collective-permute-done.11.refs_0_), channel_id=1, source_target_pairs={{0,2},{1,3},{2,0},{3,1},{4,6},{5,7},{6,4},{7,5},{8,10},{9,11},{10,... | collective-permute-start | bytes 786440 | tf_op jit(solution)/shard_map/ppermute | solution.py:24
  34.3 12.7 %collective-permute-start.10 = (bf16[128,1024]{1,0:T(8,128)(2,1)}, bf16[128,1024]{1,0:T(8,128)(2,1)}, u32[]{:S(2)}, u32[]{:S(2)}) collective-permute-start(bf16[128,1024]{1,0:T(8,128)(2,1)} %collective-permute-done.9.refs_2_), channel_id=1, source_target_pairs={{0,1},{1,0},{2,3},{3,2},{4,5},{5,4},{6,7},{7,6},{8,9},{9,8},{10,11... | collective-permute-start | bytes 786440 | tf_op jit(solution)/shard_map/ppermute | solution.py:24
  109.4 22.9 %collective-permute-start.35 = (f32[1,2048]{1,0:T(1,128)S(1)}, f32[1,2048]{1,0:T(1,128)S(1)}, u32[]{:S(2)}, u32[]{:S(2)}) collective-permute-start(f32[1,2048]{1,0:T(1,128)S(1)} %get-tuple-element.44), channel_id=1, source_target_pairs={{0,3},{1,2},{2,1},{3,0},{4,7},{5,6},{6,5},{7,4},{8,11},{9,10},{10,... | collective-permute-start | bytes 24584 | tf_op jit(solution)/shard_map/ppermute | solution.py:24
  109.5 23.1 %collective-permute-start.33 = (f32[1,2048]{1,0:T(1,128)S(1)}, f32[1,2048]{1,0:T(1,128)S(1)}, u32[]{:S(2)}, u32[]{:S(2)}) collective-permute-start(f32[1,2048]{1,0:T(1,128)S(1)} %get-tuple-element.44), channel_id=1, source_target_pairs={{0,1},{1,0},{2,3},{3,2},{4,5},{5,4},{6,7},{7,6},{8,9},{9,8},{10,11... | collective-permute-start | bytes 24584 | tf_op jit(solution)/shard_map/ppermute | solution.py:24
  111.3 22.0 %collective-permute-start.34 = (f32[1,2048]{1,0:T(1,128)S(1)}, f32[1,2048]{1,0:T(1,128)S(1)}, u32[]{:S(2)}, u32[]{:S(2)}) collective-permute-start(f32[1,2048]{1,0:T(1,128)S(1)} %get-tuple-element.44), channel_id=1, source_target_pairs={{0,2},{1,3},{2,0},{3,1},{4,6},{5,7},{6,4},{7,5},{8,10},{9,11},{10,... | collective-permute-start | bytes 24584 | tf_op jit(solution)/shard_map/ppermute | solution.py:24
  121.1 22.5 %collective-permute-start.48 = (f32[2,128,1024]{2,1,0:T(8,128)}, f32[2,128,1024]{2,1,0:T(8,128)}, u32[]{:S(2)}, u32[]{:S(2)}) collective-permute-start(f32[2,128,1024]{2,1,0:T(8,128)} %slice_bitcast_fusion), channel_id=1, source_target_pairs={{0,1},{1,0},{2,3},{3,2},{4,5},{5,4},{6,7},{7,6},{8,9},{9,8},{10,11... | collective-permute-start | bytes 3145736 | tf_op jit(solution)/shard_map/ppermute | solution.py:24
  122.2 24.8 %collective-permute-start.45 = (f32[2,128,1024]{2,1,0:T(8,128)}, f32[2,128,1024]{2,1,0:T(8,128)}, u32[]{:S(2)}, u32[]{:S(2)}) collective-permute-start(f32[2,128,1024]{2,1,0:T(8,128)} %slice_bitcast_fusion.2), channel_id=1, source_target_pairs={{0,1},{1,0},{2,3},{3,2},{4,5},{5,4},{6,7},{7,6},{8,9},{9,8},{10,11... | collective-permute-start | bytes 3145736 | tf_op jit(solution)/shard_map/ppermute | solution.py:24
  132.3 16.7 %collective-permute-start.42 = (f32[2,128,1024]{2,1,0:T(8,128)}, f32[2,128,1024]{2,1,0:T(8,128)S(1)}, u32[]{:S(2)}, u32[]{:S(2)}) collective-permute-start(f32[2,128,1024]{2,1,0:T(8,128)} %slice_bitcast_fusion.4), channel_id=1, source_target_pairs={{0,1},{1,0},{2,3},{3,2},{4,5},{5,4},{6,7},{7,6},{8,9},{9,8},{10,11... | collective-permute-start | bytes 3145736 | tf_op jit(solution)/shard_map/ppermute | solution.py:24
  132.6 18.2 %collective-permute-start.39 = (f32[2,128,1024]{2,1,0:T(8,128)}, f32[2,128,1024]{2,1,0:T(8,128)}, u32[]{:S(2)}, u32[]{:S(2)}) collective-permute-start(f32[2,128,1024]{2,1,0:T(8,128)} %slice_bitcast_fusion.6), channel_id=1, source_target_pairs={{0,1},{1,0},{2,3},{3,2},{4,5},{5,4},{6,7},{7,6},{8,9},{9,8},{10,11... | collective-permute-start | bytes 3145736 | tf_op jit(solution)/shard_map/ppermute | solution.py:24
  143.5 26.8 %collective-permute-start.36 = (f32[1,2048]{1,0:T(1,128)S(1)}, f32[1,2048]{1,0:T(1,128)S(1)}, u32[]{:S(2)}, u32[]{:S(2)}) collective-permute-start(f32[1,2048]{1,0:T(1,128)S(1)} %add_add_fusion), channel_id=1, source_target_pairs={{0,4},{1,5},{2,6},{3,7},{4,0},{5,1},{6,2},{7,3},{8,12},{9,13},{10,... | collective-permute-start | bytes 24584 | tf_op jit(solution)/shard_map/ppermute | solution.py:24
  145.3 25.1 %collective-permute-start.49 = (bf16[128,1024]{1,0:T(8,128)(2,1)S(1)}, bf16[128,1024]{1,0:T(8,128)(2,1)S(1)}, u32[]{:S(2)}, u32[]{:S(2)}) collective-permute-start(bf16[128,1024]{1,0:T(8,128)(2,1)S(1)} %fusion.19), channel_id=1, source_target_pairs={{0,2},{1,3},{2,0},{3,1},{4,6},{5,7},{6,4},{7,5},{8,10},{9,11},{10,... | collective-permute-start | bytes 786440 | tf_op jit(solution)/shard_map/ppermute | solution.py:24
  148.4 11.6 %collective-permute-start.46 = (bf16[128,1024]{1,0:T(8,128)(2,1)S(1)}, bf16[128,1024]{1,0:T(8,128)(2,1)S(1)}, u32[]{:S(2)}, u32[]{:S(2)}) collective-permute-start(bf16[128,1024]{1,0:T(8,128)(2,1)S(1)} %fusion.18), channel_id=1, source_target_pairs={{0,2},{1,3},{2,0},{3,1},{4,6},{5,7},{6,4},{7,5},{8,10},{9,11},{10,... | collective-permute-start | bytes 786440 | tf_op jit(solution)/shard_map/ppermute | solution.py:24
  149.2 16.2 %collective-permute-start.43 = (bf16[128,1024]{1,0:T(8,128)(2,1)S(1)}, bf16[128,1024]{1,0:T(8,128)(2,1)S(1)}, u32[]{:S(2)}, u32[]{:S(2)}) collective-permute-start(bf16[128,1024]{1,0:T(8,128)(2,1)S(1)} %fusion.17), channel_id=1, source_target_pairs={{0,2},{1,3},{2,0},{3,1},{4,6},{5,7},{6,4},{7,5},{8,10},{9,11},{10,... | collective-permute-start | bytes 786440 | tf_op jit(solution)/shard_map/ppermute | solution.py:24
  152.2 16.0 %collective-permute-start.40 = (bf16[128,1024]{1,0:T(8,128)(2,1)S(1)}, bf16[128,1024]{1,0:T(8,128)(2,1)S(1)}, u32[]{:S(2)}, u32[]{:S(2)}) collective-permute-start(bf16[128,1024]{1,0:T(8,128)(2,1)S(1)} %fusion.16), channel_id=1, source_target_pairs={{0,2},{1,3},{2,0},{3,1},{4,6},{5,7},{6,4},{7,5},{8,10},{9,11},{10,... | collective-permute-start | bytes 786440 | tf_op jit(solution)/shard_map/ppermute | solution.py:24
  165.4 17.5 %collective-permute-start.44 = (bf16[128,1024]{1,0:T(8,128)(2,1)S(1)}, bf16[128,1024]{1,0:T(8,128)(2,1)S(1)}, u32[]{:S(2)}, u32[]{:S(2)}) collective-permute-start(bf16[128,1024]{1,0:T(8,128)(2,1)S(1)} %fusion.13), channel_id=1, source_target_pairs={{0,8},{1,9},{2,10},{3,11},{4,12},{5,13},{6,14},{7,15},{8,0},{9,1},... | collective-permute-start | bytes 786440 | tf_op jit(solution)/shard_map/ppermute | solution.py:24
  168.3 14.7 %collective-permute-start.41 = (bf16[128,1024]{1,0:T(8,128)(2,1)S(1)}, bf16[128,1024]{1,0:T(8,128)(2,1)S(1)}, u32[]{:S(2)}, u32[]{:S(2)}) collective-permute-start(bf16[128,1024]{1,0:T(8,128)(2,1)S(1)} %fusion.15), channel_id=1, source_target_pairs={{0,12},{1,13},{2,14},{3,15},{4,8},{5,9},{6,10},{7,11},{8,4},{9,5},... | collective-permute-start | bytes 786440 | tf_op jit(solution)/shard_map/ppermute | solution.py:24
  (69 other events, 416.2 us)

commit v2 on v0

v2 whole, which is shorter than its diff:
```python
import functools
import math

import jax
import jax.numpy as jnp
from jax import lax
from jax.experimental import pallas as pl
from jax.experimental.pallas import tpu as pltpu
from jax.sharding import PartitionSpec as P

ITERS = 3
AXIS = "tgt"
F32 = jnp.float32
BF16 = jnp.bfloat16
TAIL = 8


def call(body, name, ins, outs, grid=(), in_specs=None, out_specs=None, flops=0, **kw):
    def whole(a):
        return pl.BlockSpec(a.shape, lambda *_: (0,) * len(a.shape))

    size = sum(math.prod(a.shape) * jnp.dtype(a.dtype).itemsize for a in [*ins, *outs])
    return pl.pallas_call(
        body,
        name=name,
        grid=grid,
        out_shape=outs,
        in_specs=in_specs or [whole(a) for a in ins],
        out_specs=out_specs or [whole(a) for a in outs],
        compiler_params=pltpu.CompilerParams(vmem_limit_bytes=56 << 20),
        cost_estimate=pl.CostEstimate(flops=flops, bytes_accessed=size, transcendentals=0),
        **kw,
    )(*ins)


def shape(dims, dtype=F32):
    return jax.ShapeDtypeStruct(dims, dtype)


def swap(value, mask):
    count = lax.axis_size(AXIS)
    return lax.ppermute(value, AXIS, [(i, i ^ mask) for i in range(count)])


def tree_levels(count):
    levels, step = [], 1
    while step < count:
        if step * 4 <= count:
            levels.append((step, 2 * step, 3 * step))
            step *= 4
        else:
            levels.append((step,))
            step *= 2
    return levels


def flip(value, mask, count):
    width = value.shape[-1] // count
    blocks = [value[..., (r ^ mask) * width : ((r ^ mask) + 1) * width] for r in range(count)]
    return jnp.concatenate(blocks, axis=-1)


def cost_kernel(scale, blocks, chunk_index, *refs):
    x_refs = refs[:blocks]
    y_ref, u_ref, w_ref, pack_ref, s_ref, x_out, pack_out = refs[blocks:]
    rows = x_refs[0].shape[0]
    chunk = rows * blocks
    for q in range(blocks):
        x_out[q * rows : (q + 1) * rows, :] = x_refs[q][...]
    s = scale * lax.dot_general(
        y_ref[...], x_out[...], (((1,), (1,)), ((), ())), preferred_element_type=F32
    )
    s_ref[...] = s
    shifted = s + u_ref[...]
    top = jnp.max(shifted, axis=0, keepdims=True)
    half = (pack_ref.shape[1] - 128) // 2
    pack_out[...] = pack_ref[...]
    start = chunk_index * chunk
    pack_out[:, start : start + chunk] = top
    pack_out[:, half + start : half + start + chunk] = jnp.sum(
        jnp.exp(shifted - top), axis=0, keepdims=True
    )
    total = jnp.sum(w_ref[...], axis=0, keepdims=True)
    pack_out[:, 2 * half :] = jnp.broadcast_to(total, (1, 128))


def merge(packs, masks, count):
    half = (packs[0].shape[1] - 128) // 2
    tops = [flip(p[:, :half], m, count) for p, m in zip(packs, masks)]
    sums = [flip(p[:, half : 2 * half], m, count) for p, m in zip(packs, masks)]
    top = functools.reduce(jnp.maximum, tops)
    total = sum(s * jnp.exp(t - top) for t, s in zip(tops, sums))
    return top, total, sum(p[:, 2 * half :] for p in packs)


def merge_kernel(masks, count, *refs):
    top, total, mass = merge([r[...] for r in refs[:-1]], masks, count)
    half = top.shape[1]
    refs[-1][:, :half] = top
    refs[-1][:, half : 2 * half] = total
    refs[-1][:, 2 * half :] = mass


def first_kernel(chunks, masks, count, source_count, *refs):
    s_refs, refs = refs[:chunks], refs[chunks:]
    pack_refs, refs = refs[: len(masks)], refs[len(masks) :]
    logit_ref, w_ref, q_ref, h_ref, row_ref, g_ref, share_ref = refs
    width = s_refs[0].shape[1]

    @pl.when(pl.program_id(0) == 0)
    def _():
        top, total, mass = merge([r[...] for r in pack_refs], masks, count)
        logit = logit_ref[...]
        h = logit - jnp.log(jnp.sum(jnp.exp(logit))) + jnp.log(mass[:, :1])
        h_ref[...] = h
        q_ref[...] = h - top - jnp.log(total)
        row_ref[...] = jnp.zeros_like(row_ref)

    mass = sum(r[:, r.shape[1] - 1 :] for r in pack_refs)
    w = w_ref[...]
    share_ref[...] = w * (source_count / mass)
    q = q_ref[...]
    parts = [s_refs[k][...] + q[:, k * width : (k + 1) * width] for k in range(chunks)]
    top = functools.reduce(jnp.maximum, [jnp.max(p, axis=1, keepdims=True) for p in parts])
    parts = [jnp.exp(p - top) for p in parts]
    total = sum(jnp.sum(p, axis=1, keepdims=True) for p in parts)
    g_ref[...] = -(top + jnp.log(total))
    w = w / total
    for k in range(chunks):
        row_ref[:, k * width : (k + 1) * width] += jnp.sum(parts[k] * w, axis=0, keepdims=True)


def advance(sum_refs, masks, count, q_ref, h_ref, q_out):
    total = sum(flip(r[...], m, count) for r, m in zip(sum_refs, masks))
    q_out[...] = q_ref[...] + h_ref[...] - jnp.log(total)


def step_kernel(chunks, masks, count, *refs):
    s_refs, refs = refs[:chunks], refs[chunks:]
    sum_refs, refs = refs[: len(masks)], refs[len(masks) :]
    q_ref, h_ref, w_ref, g_ref, q_out, row_ref = refs
    width = s_refs[0].shape[1]

    @pl.when(pl.program_id(0) == 0)
    def _():
        advance(sum_refs, masks, count, q_ref, h_ref, q_out)
        row_ref[...] = jnp.zeros_like(row_ref)

    q, g = q_out[...], g_ref[...]
    parts = [
        jnp.exp(s_refs[k][...] + q[:, k * width : (k + 1) * width] + g) for k in range(chunks)
    ]
    w = w_ref[...] / sum(jnp.sum(p, axis=1, keepdims=True) for p in parts)
    for k in range(chunks):
        row_ref[:, k * width : (k + 1) * width] += jnp.sum(parts[k] * w, axis=0, keepdims=True)


def plan_kernel(chunks, masks, count, *refs):
    s_refs, refs = refs[:chunks], refs[chunks:]
    sum_refs, refs = refs[: len(masks)], refs[len(masks) :]
    q_ref, h_ref, w_ref, g_ref = refs[:4]
    plan_refs = refs[4 : 4 + chunks]
    q_out, logb_ref, col_ref, row_ref = refs[4 + chunks :]
    width = s_refs[0].shape[1]

    @pl.when(pl.program_id(0) == 0)
    def _():
        advance(sum_refs, masks, count, q_ref, h_ref, q_out)
        row_ref[...] = jnp.zeros_like(row_ref)

    q, g = q_out[...], g_ref[...]
    parts = [
        jnp.exp(s_refs[k][...] + q[:, k * width : (k + 1) * width] + g) for k in range(chunks)
    ]
    total = sum(jnp.sum(p, axis=1, keepdims=True) for p in parts)
    logb_ref[...] = -jnp.log(total)
    w = w_ref[...] / total
    col = jnp.zeros_like(total)
    for k in range(chunks):
        plan = (parts[k] * w).astype(BF16)
        plan_refs[k][...] = plan
        wide = plan.astype(F32)
        col = col + jnp.sum(wide, axis=1, keepdims=True)
        row_ref[:, k * width : (k + 1) * width] += jnp.sum(wide, axis=0, keepdims=True)
    col_ref[...] = col


def row_part_kernel(plan_ref, y_ref, mass_ref, keep_ref, send_ref):
    rows = keep_ref.shape[1] - TAIL
    part = lax.dot_general(
        plan_ref[...], y_ref[...], (((0,), (0,)), ((), ())), preferred_element_type=F32
    )
    for block in range(4):
        ref = send_ref if block % 2 else keep_ref
        half = block // 2
        ref[half, :rows, :] = part[block * rows : (block + 1) * rows, :]
        ref[half, rows:, :] = jnp.zeros((TAIL, ref.shape[2]), F32)
        ref[half, rows : rows + 1, :rows] = mass_ref[:, block * rows : (block + 1) * rows]


def split_mass(mass):
    high = mass.astype(BF16).astype(F32)
    rest = mass - high
    middle = rest.astype(BF16).astype(F32)
    row = lax.broadcasted_iota(jnp.int32, (TAIL, mass.shape[1]), 0)
    out = jnp.where(row == 0, high, jnp.where(row == 1, middle, rest - middle))
    return jnp.where(row < 3, out, 0.0).astype(BF16)


def chip_kernel(keep_ref, other_ref, own_ref, send_ref):
    rows = own_ref.shape[0] - TAIL
    own_ref[...] = keep_ref[0] + other_ref[0]
    send_ref[:rows, :] = (keep_ref[1, :rows, :] + other_ref[1, :rows, :]).astype(BF16)
    send_ref[rows:, :] = split_mass(
        keep_ref[1, rows : rows + 1, :] + other_ref[1, rows : rows + 1, :]
    )


def gathered_sum(own_ref, other_refs):
    rows = own_ref.shape[0] - TAIL
    part = own_ref[:rows, :]
    mass = own_ref[rows : rows + 1, :]
    for ref in other_refs:
        part = part + ref[:rows, :].astype(F32)
        mass = mass + jnp.sum(ref[rows:, :].astype(F32), axis=0, keepdims=True)
    return part, mass


def line_kernel(own_ref, *refs):
    part, mass = gathered_sum(own_ref, refs[:-1])
    rows = part.shape[0]
    refs[-1][:rows, :] = part.astype(BF16)
    refs[-1][rows:, :] = split_mass(mass)


def last_kernel(own_ref, *refs):
    *others, x_ref, out_ref = refs
    part, mass = gathered_sum(own_ref, others)
    rows = part.shape[0]
    wide = jnp.broadcast_to(mass[:, :rows], (rows, rows))
    same = lax.broadcasted_iota(jnp.int32, (rows, rows), 0) == lax.broadcasted_iota(
        jnp.int32, (rows, rows), 1
    )
    column = jnp.sum(jnp.where(same, wide, 0.0), axis=1, keepdims=True)
    out_ref[...] = column * x_ref[...].astype(F32) - part


def column_kernel(chunks, factor, *refs):
    plan_refs, x_refs = refs[:chunks], refs[chunks : 2 * chunks]
    y_ref, mass_ref, out_ref = refs[2 * chunks :]
    part = sum(
        jnp.dot(plan_refs[k][...], x_refs[k][...], preferred_element_type=F32)
        for k in range(chunks)
    )
    out_ref[...] = factor * (mass_ref[...] * y_ref[...].astype(F32) - part)


def per_device(source_feats, target_feats, source_logits, target_logits):
    count = lax.axis_size(AXIS)
    me = lax.axis_index(AXIS)
    rows, width = source_feats.shape
    cols = target_feats.shape[0]
    source_count = rows * count
    target_count = cols * count
    scale = 1.0 / math.sqrt(width)
    direct = count == 16
    chunks = 4
    chunk = source_count // chunks
    order = jnp.bitwise_xor(me, jnp.arange(count))

    if direct:
        far = swap(source_feats, 8)
        line = [source_feats, swap(source_feats, 4), far, swap(far, 4)]
        by_chunk = []
        for block in line:
            other = swap(block, 2)
            by_chunk.append([block, swap(block, 1), other, swap(other, 1)])
    else:
        gathered = lax.all_gather(source_feats, AXIS, axis=0)[order]
        gathered = gathered.reshape(chunks, chunk, width)
        by_chunk = [[gathered[k]] for k in range(chunks)]

    weight = jnp.exp(target_logits)[:, None]
    target_sq = scale * jnp.sum(jnp.square(target_feats.astype(F32)), axis=1, keepdims=True)
    lift = target_logits[:, None] - target_sq
    logits = source_logits.reshape(count, rows)[order].reshape(1, source_count)
    weight, lift, logits = lax.optimization_barrier((weight, lift, logits))

    pack = jnp.zeros((1, 2 * source_count + 128), F32)
    scores, feats = [None] * chunks, [None] * chunks
    for k in (0, 1, 2, 3):
        scores[k], feats[k], pack = call(
            functools.partial(cost_kernel, 2.0 * scale, len(by_chunk[k]), k),
            "cost",
            [*by_chunk[k], target_feats, lift, weight, pack],
            [shape((cols, chunk)), shape((chunk, width), BF16), shape(pack.shape)],
            flops=2 * cols * chunk * width,
        )

    *levels, last = tree_levels(count)
    masks = (0, *last)
    for level in levels:
        packs = [pack] + [swap(pack, m) for m in level]
        (pack,) = call(
            functools.partial(merge_kernel, (0, *level), count),
            "merge",
            packs,
            [shape(pack.shape)],
        )
    packs = [pack] + [swap(pack, m) for m in last]

    tile = 128
    grid = (cols // tile,)
    thin = pl.BlockSpec((tile, 1), lambda j: (j, 0))
    flat = pl.BlockSpec((1, source_count), lambda j: (0, 0))
    part = pl.BlockSpec((tile, chunk), lambda j: (j, 0))
    packed = pl.BlockSpec(pack.shape, lambda j: (0, 0))
    thin_shape, flat_shape = shape((cols, 1)), shape((1, source_count))

    q, h, row, g, share = call(
        functools.partial(first_kernel, chunks, masks, count, source_count),
        "first",
        [*scores, *packs, logits, weight],
        [flat_shape, flat_shape, flat_shape, thin_shape, thin_shape],
        grid=grid,
        in_specs=[part] * chunks + [packed] * len(masks) + [flat, thin],
        out_specs=[flat, flat, flat, thin, thin],
    )

    def row_sums(row):
        for level in levels:
            row = row + sum(flip(swap(row, m), m, count) for m in level)
        return [row] + [swap(row, m) for m in last]

    for _ in range(ITERS - 2):
        q, row = call(
            functools.partial(step_kernel, chunks, masks, count),
            "step",
            [*scores, *row_sums(row), q, h, weight, g],
            [flat_shape, flat_shape],
            grid=grid,
            in_specs=[part] * chunks + [flat] * (len(masks) + 2) + [thin, thin],
            out_specs=[flat, flat],
        )

    *plans, q, logb, col_mass, row_mass = call(
        functools.partial(plan_kernel, chunks, masks, count),
        "plan",
        [*scores, *row_sums(row), q, h, share, g],
        [shape((cols, chunk), BF16)] * chunks + [flat_shape, thin_shape, thin_shape, flat_shape],
        grid=grid,
        in_specs=[part] * chunks + [flat] * (len(masks) + 2) + [thin, thin],
        out_specs=[part] * chunks + [flat, thin, thin, flat],
    )

    block = shape((rows + TAIL, width))
    block_out = shape((rows + TAIL, width), BF16)

    def line_sum(own, *others):
        return call(line_kernel, "line", [own, *others], [block_out])[0]

    gate = row_mass
    if direct:
        own, crossed = {}, {}
        for k in (3, 2, 1, 0):
            plan, _ = lax.optimization_barrier((plans[k], gate))
            pair = shape((2, rows + TAIL, width))
            keep, send = call(
                row_part_kernel,
                "row_part",
                [plan, target_feats, row_mass[:, k * chunk : (k + 1) * chunk]],
                [pair, pair],
                flops=2 * cols * chunk * width,
            )
            gate = send
            own[k], out = call(
                chip_kernel, "chip", [keep, swap(send, 1)], [block, block_out]
            )
            crossed[k] = swap(out, 2)
        near = swap(line_sum(own[3], crossed[3]), 4)
        far = swap(line_sum(own[2], crossed[2], near), 8)
        near = swap(line_sum(own[1], crossed[1]), 4)
        grad_source = call(
            last_kernel,
            "last",
            [own[0], crossed[0], near, far, source_feats],
            [shape((rows, width))],
        )[0]
        gate = out
    else:
        full = lax.dot_general(
            jnp.concatenate(plans, axis=1),
            target_feats,
            (((0,), (0,)), ((), ())),
            preferred_element_type=F32,
        ).reshape(count, rows, width)[order]
        mass = row_mass.reshape(count, rows)[order]
        grad_source = lax.psum_scatter(mass, AXIS, scatter_dimension=0)[:, None] * (
            source_feats.astype(F32)
        ) - lax.psum_scatter(full, AXIS, scatter_dimension=0)

    *plans, _ = lax.optimization_barrier((*plans, gate))
    (grad_target,) = call(
        functools.partial(column_kernel, chunks, target_count / source_count),
        "column",
        [*plans, *feats, target_feats, col_mass],
        [shape((cols, width))],
        flops=2 * cols * source_count * width,
    )

    source_sq = scale * jnp.concatenate(
        [jnp.sum(jnp.square(x.astype(F32)), axis=1) for x in feats]
    )
    log_total = jnp.log(jnp.sum(jnp.exp(source_logits)))
    potential_src = (q - logits + log_total).reshape(source_count) + source_sq
    potential_src = potential_src.reshape(count, rows)[order].reshape(source_count)
    potential_tgt = (g + logb + target_sq).reshape(cols)
    return (grad_source, grad_target, potential_src, potential_tgt)


def solution(mesh):
    return jax.shard_map(
        per_device,
        mesh=mesh,
        in_specs=(
            P(("groups", "tgt"), None),
            P(("groups", "tgt"), None),
            P("groups"),
            P(("groups", "tgt")),
        ),
        out_specs=(
            P(("groups", "tgt"), None),
            P(("groups", "tgt"), None),
            P("groups"),
            P(("groups", "tgt")),
        ),
        check_vma=False,
    )
```

time: 396 us -> 179 us (0.45)
  blocking collectives: 248 us -> 0 us
  Pallas kernels: 0 us -> 69.6 us
  starting transfers between devices: 0.08 us -> 40.2 us
  waiting for transfers between devices: 78.1 us -> 45.3 us
  other arithmetic: 33.4 us -> 6.11 us
  matrix products: 16.3 us -> 0 us
  between operations: 16.3 us -> 1.94 us
  local copies, waits for them, and re-layouts: 2.98 us -> 15.1 us
    psum x4 -> x0, blocking collectives: 126 us -> none  [the longest x3 90.2 us: per_device(): total = lax.psum(jnp.sum(jnp.exp(scores - top[:, None]), axis=1), 'tgt')]
    pmax x3 -> x0, blocking collectives: 91.6 us -> none  [per_device(): top = lax.pmax(jnp.max(scores, axis=1), 'tgt')]
    pallas_call x0 -> x21, Pallas kernels: none -> 69.6 us  [call(): pl.pallas_call(body, name=name, grid=grid, out_shape=outs, in_specs=in_sp...]
    reduce_scatter x1 -> x0, waiting for transfers between devices: 64 us -> none  [per_device(): lax.psum_scatter(row_part, 'tgt', scatter_dimension=0, tiled=True)]
    ppermute x0 -> x44, waiting for transfers between devices: none -> 45.3 us  [swap(): return lax.ppermute(value, AXIS, [(i, i ^ mask) for i in range(count)])]
    ppermute x0 -> x44, starting transfers between devices: none -> 40.2 us  [swap(): return lax.ppermute(value, AXIS, [(i, i ^ mask) for i in range(count)])]
    unnamed x1 -> x0, blocking collectives: 30.1 us -> none
    reduce_sum x11 -> x6, other arithmetic: 20.6 us -> 3.22 us  [the longest x1 1.5 us: per_device(): jnp.sum(jnp.square(target_feats.astype(F32)), axis=1, keepdims=True)]
  transfers between devices with their start and end apart: 2 -> 44, of which waited for: 2 -> 21; matrix products, arithmetic and copies ran while one was open for 3% -> 6% of each run, Pallas kernels for 0% -> 25%
where the time goes in v2:
time: 179 us; the launch traced here: 178 us
  Pallas kernels  69.6 us (39%)
  waiting for transfers between devices  45.3 us (25%)
  starting transfers between devices  40.2 us (22%)
  local copies, waits for them, and re-layouts  15.1 us (8%)
  other arithmetic  6.11 us (3%)
  between operations  1.94 us (1%)
    pallas_call x21, Pallas kernels, call(): pl.pallas_call(body, name=name, grid=grid, out_shape=outs, in_specs=in_sp...  69.6 us
    ppermute x44, waiting for transfers between devices, swap(): return lax.ppermute(value, AXIS, [(i, i ^ mask) for i in range(count)])  45.3 us
    ppermute x44, starting transfers between devices, swap(): return lax.ppermute(value, AXIS, [(i, i ^ mask) for i in range(count)])  40.2 us
    unnamed x162, local copies, waits for them, and re-layouts  9.01 us
  transfers between devices with their start and end apart: 44, of which 21 were waited for; matrix products, arithmetic and copies ran while one was open for 6% of the time, Pallas kernels for 25%

profile of v2, /device:TPU:0, one launch (start us, length us, event | category | flops | bytes accessed | tf_op | source)
XLA Modules:
  0.0 178.3 jit_solution(7066247598560671374)
XLA Ops:
  0.6 4.1 %collective-permute-start.7 = (bf16[128,1024]{1,0:T(8,128)(2,1)}, bf16[128,1024]{1,0:T(8,128)(2,1)S(1)}, u32[]{:S(2)}, u32[]{:S(2)}) collective-permute-start(bf16[128,1024]{1,0:T(8,128)(2,1)} %refs_3_.1), channel_id=1, source_target_pairs={{0,8},{1,9},{2,10},{3,11},{4,12},{5,13},{6,14},{7,15},{8,0},{9,1},... | collective-permute-start | bytes 786440 | tf_op jit(solution)/shard_map/ppermute | solution.py:42
  7.8 9.1 %collective-permute-done.7.refs_0_ = bf16[128,1024]{1,0:T(8,128)(2,1)S(1)} collective-permute-done((bf16[128,1024]{1,0:T(8,128)(2,1)}, bf16[128,1024]{1,0:T(8,128)(2,1)S(1)}, u32[]{:S(2)}, u32[]{:S(2)}) %collective-permute-start.7) | collective-permute-done | bytes 262176 | tf_op jit(solution)/shard_map/ppermute | solution.py:42
  21.6 2.9 %collective-permute-done.11.refs_0_ = bf16[128,1024]{1,0:T(8,128)(2,1)S(1)} collective-permute-done((bf16[128,1024]{1,0:T(8,128)(2,1)S(1)}, bf16[128,1024]{1,0:T(8,128)(2,1)S(1)}, u32[]{:S(2)}, u32[]{:S(2)}) %collective-permute-start.11) | collective-permute-done | bytes 262176 | tf_op jit(solution)/shard_map/ppermute | solution.py:42
  27.4 5.1 %collective-permute-done.9.refs_2_ = bf16[128,1024]{1,0:T(8,128)(2,1)S(1)} collective-permute-done((bf16[128,1024]{1,0:T(8,128)(2,1)S(1)}, bf16[128,1024]{1,0:T(8,128)(2,1)S(1)}, u32[]{:S(2)}, u32[]{:S(2)}) %collective-permute-start.9) | collective-permute-done | bytes 262176 | tf_op jit(solution)/shard_map/ppermute | solution.py:42
  33.1 3.8 %collective-permute-done.13.refs_2_ = bf16[128,1024]{1,0:T(8,128)(2,1)S(1)} collective-permute-done((bf16[128,1024]{1,0:T(8,128)(2,1)S(1)}, bf16[128,1024]{1,0:T(8,128)(2,1)S(1)}, u32[]{:S(2)}, u32[]{:S(2)}) %collective-permute-start.13) | collective-permute-done | bytes 262176 | tf_op jit(solution)/shard_map/ppermute | solution.py:42
  40.4 3.5 %cost.4 = (f32[512,512]{1,0:T(8,128)}, bf16[512,1024]{1,0:T(8,128)(2,1)}, f32[1,4224]{1,0:T(1,128)}) custom-call(bf16[128,1024]{1,0:T(8,128)(2,1)} %refs_3_.1, bf16[128,1024]{1,0:T(8,128)(2,1)} %copy-done.20, bf16[128,1024]{1,0:T(8,128)(2,1)} %copy-done.18, bf16[128,1024]{1,0:T(8,128)(2,1)} %copy-done.25, bf16[512,1024]{1,0:T(8,128)(2,1)} %refs_8_.1, ...), custom_call_target="tpu_custom_call" | custom-call | flops 536870912 | bytes 4232192 | tf_op jit(solution)/shard_map/cost/pallas_call | solution.py:23
  44.0 3.5 %cost.5 = (f32[512,512]{1,0:T(8,128)}, bf16[512,1024]{1,0:T(8,128)(2,1)}, f32[1,4224]{1,0:T(1,128)}) custom-call(bf16[128,1024]{1,0:T(8,128)(2,1)} %copy-done.17, bf16[128,1024]{1,0:T(8,128)(2,1)} %copy-done.23, bf16[128,1024]{1,0:T(8,128)(2,1)} %copy-done.21, bf16[128,1024]{1,0:T(8,128)(2,1)} %collective-permute-done.6.refs_3_, bf16[512,1024]{1,0:T(8,128)(2,1)} %refs_8_.1, ...), custom_call_target="tpu_custom_call" | custom-call | flops 536870912 | bytes 4232192 | tf_op jit(solution)/shard_map/cost/pallas_call | solution.py:23
  48.2 3.5 %cost.6 = (f32[512,512]{1,0:T(8,128)}, bf16[512,1024]{1,0:T(8,128)(2,1)}, f32[1,4224]{1,0:T(1,128)}) custom-call(bf16[128,1024]{1,0:T(8,128)(2,1)} %copy-done.15, bf16[128,1024]{1,0:T(8,128)(2,1)} %copy-done.24, bf16[128,1024]{1,0:T(8,128)(2,1)} %copy-done.19, bf16[128,1024]{1,0:T(8,128)(2,1)} %copy-done.27, bf16[512,1024]{1,0:T(8,128)(2,1)} %refs_8_.1, ...), custom_call_target="tpu_custom_call" | custom-call | flops 536870912 | bytes 4232192 | tf_op jit(solution)/shard_map/cost/pallas_call | solution.py:23
  52.4 3.5 %cost.7 = (f32[512,512]{1,0:T(8,128)}, bf16[512,1024]{1,0:T(8,128)(2,1)}, f32[1,4224]{1,0:T(1,128)}) custom-call(bf16[128,1024]{1,0:T(8,128)(2,1)} %copy-done.16, bf16[128,1024]{1,0:T(8,128)(2,1)} %copy-done.26, bf16[128,1024]{1,0:T(8,128)(2,1)} %copy-done.22, bf16[128,1024]{1,0:T(8,128)(2,1)} %collective-permute-done.14.refs_3_, bf16[512,1024]{1,0:T(8,128)(2,1)} %refs_8_.1, ...), custom_call_target="tpu_custom_call" | custom-call | flops 536870912 | bytes 4232192 | tf_op jit(solution)/shard_map/cost/pallas_call | solution.py:23
  64.1 3.1 %collective-permute-start.20 = (f32[1,4224]{1,0:T(1,128)}, f32[1,4224]{1,0:T(1,128)S(1)}, u32[]{:S(2)}, u32[]{:S(2)}) collective-permute-start(f32[1,4224]{1,0:T(1,128)} %merge.1.refs_4_), channel_id=1, source_target_pairs={{0,12},{1,13},{2,14},{3,15},{4,8},{5,9},{6,10},{7,11},{8,4},{9,5},... | collective-permute-start | bytes 50696 | tf_op jit(solution)/shard_map/ppermute | solution.py:42
  72.7 5.1 %first.1 = (f32[1,2048]{1,0:T(1,128)}, f32[1,2048]{1,0:T(1,128)}, f32[1,2048]{1,0:T(1,128)}, f32[512,1]{1,0:T(8,128)}, f32[512,1]{1,0:T(8,128)}) custom-call(f32[512,512]{1,0:T(8,128)} %get-tuple-element.60.refs_0_, f32[512,512]{1,0:T(8,128)} %get-tuple-element.62.refs_1_, f32[512,512]{1,0:T(8,128)} %get-tuple-element.64.refs_2_, ...), custom_call_target="tpu_custom_call" | custom-call | bytes 4300800 | tf_op jit(solution)/shard_map/first/pallas_call | solution.py:23
  90.2 4.5 %step.1 = (f32[1,2048]{1,0:T(1,128)}, f32[1,2048]{1,0:T(1,128)}) custom-call(f32[512,512]{1,0:T(8,128)} %get-tuple-element.60.refs_0_, f32[512,512]{1,0:T(8,128)} %get-tuple-element.62.refs_1_, f32[512,512]{1,0:T(8,128)} %get-tuple-element.64.refs_2_, f32[512,512]{1,0:T(8,128)} %get-tuple-element.66.refs_3_, f32[1,2048]{1,0:T(1,128)} %copy-done.30, ...), custom_call_target="tpu_custom_call" | custom-call | bytes 4263936 | tf_op jit(solution)/shard_map/step/pallas_call | solution.py:23
  106.7 5.2 %plan.1 = (bf16[512,512]{1,0:T(8,128)(2,1)}, bf16[512,512]{1,0:T(8,128)(2,1)}, bf16[512,512]{1,0:T(8,128)(2,1)}, bf16[512,512]{1,0:T(8,128)(2,1)}, f32[1,2048]{1...) custom-call(f32[512,512]{1,0:T(8,128)} %get-tuple-element.60.refs_0_, ...), custom_call_target="tpu_custom_call" | custom-call | bytes 6365184 | tf_op jit(solution)/shard_map/plan/pallas_call | solution.py:23
  113.2 3.4 %row_part.4 = (f32[2,136,1024]{2,1,0:T(8,128)}, f32[2,136,1024]{2,1,0:T(8,128)}) custom-call(bf16[512,512]{1,0:T(8,128)(2,1)} %get-tuple-element.104.plan_ref.refs_3_, bf16[512,1024]{1,0:T(8,128)(2,1)} %refs_8_.1, f32[1,512]{1,0:T(1,128)} %get-tuple-element.115.mass_ref), custom_call_target="tpu_custom_call" | custom-call | flops 536870912 | bytes 3803136 | tf_op jit(solution)/shard_map/row_part/pallas_call | solution.py:23
  116.6 3.5 %row_part.5 = (f32[2,136,1024]{2,1,0:T(8,128)}, f32[2,136,1024]{2,1,0:T(8,128)}) custom-call(bf16[512,512]{1,0:T(8,128)(2,1)} %get-tuple-element.103.plan_ref.refs_2_, bf16[512,1024]{1,0:T(8,128)(2,1)} %refs_8_.1, f32[1,512]{1,0:T(1,128)} %get-tuple-element.114.mass_ref), custom_call_target="tpu_custom_call" | custom-call | flops 536870912 | bytes 3803136 | tf_op jit(solution)/shard_map/row_part/pallas_call | solution.py:23
  120.6 3.6 %row_part.6 = (f32[2,136,1024]{2,1,0:T(8,128)}, f32[2,136,1024]{2,1,0:T(8,128)}) custom-call(bf16[512,512]{1,0:T(8,128)(2,1)} %get-tuple-element.102.plan_ref.refs_1_, bf16[512,1024]{1,0:T(8,128)(2,1)} %refs_8_.1, f32[1,512]{1,0:T(1,128)} %get-tuple-element.113.mass_ref), custom_call_target="tpu_custom_call" | custom-call | flops 536870912 | bytes 3803136 | tf_op jit(solution)/shard_map/row_part/pallas_call | solution.py:23
  125.9 3.5 %row_part.7 = (f32[2,136,1024]{2,1,0:T(8,128)}, f32[2,136,1024]{2,1,0:T(8,128)}) custom-call(bf16[512,512]{1,0:T(8,128)(2,1)} %get-tuple-element.101.plan_ref.refs_0_, bf16[512,1024]{1,0:T(8,128)(2,1)} %refs_8_.1, f32[1,512]{1,0:T(1,128)} %get-tuple-element.112.mass_ref), custom_call_target="tpu_custom_call" | custom-call | flops 536870912 | bytes 3803136 | tf_op jit(solution)/shard_map/row_part/pallas_call | solution.py:23
  130.3 2.7 %chip.7 = (f32[136,1024]{1,0:T(8,128)}, bf16[136,1024]{1,0:T(8,128)(2,1)}) custom-call(f32[2,136,1024]{2,1,0:T(8,128)} %get-tuple-element.98.keep_ref, f32[2,136,1024]{2,1,0:T(8,128)} %collective-permute-done.40.other_ref), custom_call_target="tpu_custom_call" | custom-call | bytes 3063808 | tf_op jit(solution)/shard_map/chip/pallas_call | solution.py:23
  134.1 2.6 %chip.6 = (f32[136,1024]{1,0:T(8,128)}, bf16[136,1024]{1,0:T(8,128)(2,1)}) custom-call(f32[2,136,1024]{2,1,0:T(8,128)} %get-tuple-element.95.keep_ref, f32[2,136,1024]{2,1,0:T(8,128)} %collective-permute-done.38.other_ref), custom_call_target="tpu_custom_call" | custom-call | bytes 3063808 | tf_op jit(solution)/shard_map/chip/pallas_call | solution.py:23
  138.2 2.6 %chip.5 = (f32[136,1024]{1,0:T(8,128)}, bf16[136,1024]{1,0:T(8,128)(2,1)}) custom-call(f32[2,136,1024]{2,1,0:T(8,128)} %get-tuple-element.92.keep_ref, f32[2,136,1024]{2,1,0:T(8,128)} %collective-permute-done.35.other_ref), custom_call_target="tpu_custom_call" | custom-call | bytes 3063808 | tf_op jit(solution)/shard_map/chip/pallas_call | solution.py:23
  149.2 2.6 %chip.4 = (f32[136,1024]{1,0:T(8,128)}, bf16[136,1024]{1,0:T(8,128)(2,1)}) custom-call(f32[2,136,1024]{2,1,0:T(8,128)} %get-tuple-element.88.keep_ref, f32[2,136,1024]{2,1,0:T(8,128)} %copy-done.5), custom_call_target="tpu_custom_call" | custom-call | bytes 3063808 | tf_op jit(solution)/shard_map/chip/pallas_call | solution.py:23
  163.6 6.8 %column.1 = f32[512,1024]{1,0:T(8,128)} custom-call(bf16[512,512]{1,0:T(8,128)(2,1)} %get-tuple-element.101.plan_ref.refs_0_, bf16[512,512]{1,0:T(8,128)(2,1)} %get-tuple-element.102.plan_ref.refs_1_, bf16[512,512]{1,0:T(8,128)(2,1)} %get-tuple-element.103.plan_ref.refs_2_, bf16[512,512]{1,0:T(8,128)(2,1)} %get-tuple-element.104.plan_ref.refs_3_, ...), custom_call_target="tpu_custom_call" | custom-call | flops 2147483648 | bytes 9439232 | tf_op jit(solution)/shard_map/column/pallas_call | solution.py:23
  170.4 4.8 %collective-permute-done.43.refs_2_ = bf16[136,1024]{1,0:T(8,128)(2,1)S(1)} collective-permute-done((bf16[136,1024]{1,0:T(8,128)(2,1)}, bf16[136,1024]{1,0:T(8,128)(2,1)S(1)}, u32[]{:S(2)}, u32[]{:S(2)}) %collective-permute-start.43) | collective-permute-done | bytes 278560 | tf_op jit(solution)/shard_map/ppermute | solution.py:42
  175.9 2.4 %last.1 = f32[128,1024]{1,0:T(8,128)} custom-call(f32[136,1024]{1,0:T(8,128)} %get-tuple-element.90.own_ref, bf16[136,1024]{1,0:T(8,128)(2,1)} %copy-done.7, bf16[136,1024]{1,0:T(8,128)(2,1)} %copy-done.8, bf16[136,1024]{1,0:T(8,128)(2,1)} %copy-done.9, bf16[128,1024]{1,0:T(8,128)(2,1)} %refs_3_.1), custom_call_target="tpu_custom_call" | custom-call | bytes 2179072 | tf_op jit(solution)/shard_map/last/pallas_call | solution.py:23
  (274 shorter events, 81.3 us)
Async XLA Ops:
  0.6 16.3 %collective-permute-start.7 = (bf16[128,1024]{1,0:T(8,128)(2,1)}, bf16[128,1024]{1,0:T(8,128)(2,1)S(1)}, u32[]{:S(2)}, u32[]{:S(2)}) collective-permute-start(bf16[128,1024]{1,0:T(8,128)(2,1)} %refs_3_.1), channel_id=1, source_target_pairs={{0,8},{1,9},{2,10},{3,11},{4,12},{5,13},{6,14},{7,15},{8,0},{9,1},... | collective-permute-start | bytes 786440 | tf_op jit(solution)/shard_map/ppermute | solution.py:42
  4.7 13.0 %collective-permute-start.3 = (bf16[128,1024]{1,0:T(8,128)(2,1)}, bf16[128,1024]{1,0:T(8,128)(2,1)S(1)}, u32[]{:S(2)}, u32[]{:S(2)}) collective-permute-start(bf16[128,1024]{1,0:T(8,128)(2,1)} %refs_3_.1), channel_id=1, source_target_pairs={{0,4},{1,5},{2,6},{3,7},{4,0},{5,1},{6,2},{7,3},{8,12},{9,13},{10,... | collective-permute-start | bytes 786440 | tf_op jit(solution)/shard_map/ppermute | solution.py:42
  6.3 12.9 %collective-permute-start.1 = (bf16[128,1024]{1,0:T(8,128)(2,1)}, bf16[128,1024]{1,0:T(8,128)(2,1)S(1)}, u32[]{:S(2)}, u32[]{:S(2)}) collective-permute-start(bf16[128,1024]{1,0:T(8,128)(2,1)} %refs_3_.1), channel_id=1, source_target_pairs={{0,2},{1,3},{2,0},{3,1},{4,6},{5,7},{6,4},{7,5},{8,10},{9,11},{10,... | collective-permute-start | bytes 786440 | tf_op jit(solution)/shard_map/ppermute | solution.py:42
  7.8 13.5 %collective-permute-start = (bf16[128,1024]{1,0:T(8,128)(2,1)}, bf16[128,1024]{1,0:T(8,128)(2,1)S(1)}, u32[]{:S(2)}, u32[]{:S(2)}) collective-permute-start(bf16[128,1024]{1,0:T(8,128)(2,1)} %refs_3_.1), channel_id=1, source_target_pairs={{0,1},{1,0},{2,3},{3,2},{4,5},{5,4},{6,7},{7,6},{8,9},{9,8},{10,11... | collective-permute-start | bytes 786440 | tf_op jit(solution)/shard_map/ppermute | solution.py:42
  17.7 9.2 %collective-permute-start.5 = (bf16[128,1024]{1,0:T(8,128)(2,1)S(1)}, bf16[128,1024]{1,0:T(8,128)(2,1)S(1)}, u32[]{:S(2)}, u32[]{:S(2)}) collective-permute-start(bf16[128,1024]{1,0:T(8,128)(2,1)S(1)} %collective-permute-done.3.refs_0_), channel_id=1, source_target_pairs={{0,2},{1,3},{2,0},{3,1},{4,6},{5,7},{6,4},{7,5},{8,10},{9,11},{10,... | collective-permute-start | bytes 786440 | tf_op jit(solution)/shard_map/ppermute | solution.py:42
  19.2 13.3 %collective-permute-start.9 = (bf16[128,1024]{1,0:T(8,128)(2,1)S(1)}, bf16[128,1024]{1,0:T(8,128)(2,1)S(1)}, u32[]{:S(2)}, u32[]{:S(2)}) collective-permute-start(bf16[128,1024]{1,0:T(8,128)(2,1)S(1)} %collective-permute-done.7.refs_0_), channel_id=1, source_target_pairs={{0,2},{1,3},{2,0},{3,1},{4,6},{5,7},{6,4},{7,5},{8,10},{9,11},{10,... | collective-permute-start | bytes 786440 | tf_op jit(solution)/shard_map/ppermute | solution.py:42
  21.3 11.2 %collective-permute-start.2 = (bf16[128,1024]{1,0:T(8,128)(2,1)S(1)}, bf16[128,1024]{1,0:T(8,128)(2,1)S(1)}, u32[]{:S(2)}, u32[]{:S(2)}) collective-permute-start(bf16[128,1024]{1,0:T(8,128)(2,1)S(1)} %collective-permute-done.1.refs_2_), channel_id=1, source_target_pairs={{0,1},{1,0},{2,3},{3,2},{4,5},{5,4},{6,7},{7,6},{8,9},{9,8},{10,11... | collective-permute-start | bytes 786440 | tf_op jit(solution)/shard_map/ppermute | solution.py:42
  24.4 12.5 %collective-permute-start.13 = (bf16[128,1024]{1,0:T(8,128)(2,1)S(1)}, bf16[128,1024]{1,0:T(8,128)(2,1)S(1)}, u32[]{:S(2)}, u32[]{:S(2)}) collective-permute-start(bf16[128,1024]{1,0:T(8,128)(2,1)S(1)} %collective-permute-done.11.refs_0_), channel_id=1, source_target_pairs={{0,2},{1,3},{2,0},{3,1},{4,6},{5,7},{6,4},{7,5},{8,10},{9,11},{10,... | collective-permute-start | bytes 786440 | tf_op jit(solution)/shard_map/ppermute | solution.py:42
  26.9 20.5 %collective-permute-start.8 = (bf16[128,1024]{1,0:T(8,128)(2,1)S(1)}, bf16[128,1024]{1,0:T(8,128)(2,1)S(1)}, u32[]{:S(2)}, u32[]{:S(2)}) collective-permute-start(bf16[128,1024]{1,0:T(8,128)(2,1)S(1)} %collective-permute-done.7.refs_0_), channel_id=1, source_target_pairs={{0,1},{1,0},{2,3},{3,2},{4,5},{5,4},{6,7},{7,6},{8,9},{9,8},{10,11... | collective-permute-start | bytes 786440 | tf_op jit(solution)/shard_map/ppermute | solution.py:42
  26.9 17.0 %collective-permute-start.6 = (bf16[128,1024]{1,0:T(8,128)(2,1)S(1)}, bf16[128,1024]{1,0:T(8,128)(2,1)}, u32[]{:S(2)}, u32[]{:S(2)}) collective-permute-start(bf16[128,1024]{1,0:T(8,128)(2,1)S(1)} %collective-permute-done.5.refs_2_), channel_id=1, source_target_pairs={{0,1},{1,0},{2,3},{3,2},{4,5},{5,4},{6,7},{7,6},{8,9},{9,8},{10,11... | collective-permute-start | bytes 786440 | tf_op jit(solution)/shard_map/ppermute | solution.py:42
  32.5 14.9 %collective-permute-start.10 = (bf16[128,1024]{1,0:T(8,128)(2,1)S(1)}, bf16[128,1024]{1,0:T(8,128)(2,1)S(1)}, u32[]{:S(2)}, u32[]{:S(2)}) collective-permute-start(bf16[128,1024]{1,0:T(8,128)(2,1)S(1)} %collective-permute-done.9.refs_2_), channel_id=1, source_target_pairs={{0,1},{1,0},{2,3},{3,2},{4,5},{5,4},{6,7},{7,6},{8,9},{9,8},{10,11... | collective-permute-start | bytes 786440 | tf_op jit(solution)/shard_map/ppermute | solution.py:42
  32.6 19.1 %collective-permute-start.12 = (bf16[128,1024]{1,0:T(8,128)(2,1)S(1)}, bf16[128,1024]{1,0:T(8,128)(2,1)S(1)}, u32[]{:S(2)}, u32[]{:S(2)}) collective-permute-start(bf16[128,1024]{1,0:T(8,128)(2,1)S(1)} %collective-permute-done.11.refs_0_), channel_id=1, source_target_pairs={{0,1},{1,0},{2,3},{3,2},{4,5},{5,4},{6,7},{7,6},{8,9},{9,8},{10,11... | collective-permute-start | bytes 786440 | tf_op jit(solution)/shard_map/ppermute | solution.py:42
  36.9 14.8 %collective-permute-start.14 = (bf16[128,1024]{1,0:T(8,128)(2,1)S(1)}, bf16[128,1024]{1,0:T(8,128)(2,1)}, u32[]{:S(2)}, u32[]{:S(2)}) collective-permute-start(bf16[128,1024]{1,0:T(8,128)(2,1)S(1)} %collective-permute-done.13.refs_2_), channel_id=1, source_target_pairs={{0,1},{1,0},{2,3},{3,2},{4,5},{5,4},{6,7},{7,6},{8,9},{9,8},{10,11... | collective-permute-start | bytes 786440 | tf_op jit(solution)/shard_map/ppermute | solution.py:42
  116.6 13.6 %collective-permute-start.40 = (f32[2,136,1024]{2,1,0:T(8,128)}, f32[2,136,1024]{2,1,0:T(8,128)}, u32[]{:S(2)}, u32[]{:S(2)}) collective-permute-start(f32[2,136,1024]{2,1,0:T(8,128)} %get-tuple-element.82), channel_id=1, source_target_pairs={{0,1},{1,0},{2,3},{3,2},{4,5},{5,4},{6,7},{7,6},{8,9},{9,8},{10,11... | collective-permute-start | bytes 3342344 | tf_op jit(solution)/shard_map/ppermute | solution.py:42
  120.1 13.9 %collective-permute-start.38 = (f32[2,136,1024]{2,1,0:T(8,128)}, f32[2,136,1024]{2,1,0:T(8,128)}, u32[]{:S(2)}, u32[]{:S(2)}) collective-permute-start(f32[2,136,1024]{2,1,0:T(8,128)} %get-tuple-element.84), channel_id=1, source_target_pairs={{0,1},{1,0},{2,3},{3,2},{4,5},{5,4},{6,7},{7,6},{8,9},{9,8},{10,11... | collective-permute-start | bytes 3342344 | tf_op jit(solution)/shard_map/ppermute | solution.py:42
  124.2 14.0 %collective-permute-start.35 = (f32[2,136,1024]{2,1,0:T(8,128)}, f32[2,136,1024]{2,1,0:T(8,128)}, u32[]{:S(2)}, u32[]{:S(2)}) collective-permute-start(f32[2,136,1024]{2,1,0:T(8,128)} %get-tuple-element.86), channel_id=1, source_target_pairs={{0,1},{1,0},{2,3},{3,2},{4,5},{5,4},{6,7},{7,6},{8,9},{9,8},{10,11... | collective-permute-start | bytes 3342344 | tf_op jit(solution)/shard_map/ppermute | solution.py:42
  129.5 18.7 %collective-permute-start.33 = (f32[2,136,1024]{2,1,0:T(8,128)}, f32[2,136,1024]{2,1,0:T(8,128)S(1)}, u32[]{:S(2)}, u32[]{:S(2)}) collective-permute-start(f32[2,136,1024]{2,1,0:T(8,128)} %get-tuple-element.89), channel_id=1, source_target_pairs={{0,1},{1,0},{2,3},{3,2},{4,5},{5,4},{6,7},{7,6},{8,9},{9,8},{10,11... | collective-permute-start | bytes 3342344 | tf_op jit(solution)/shard_map/ppermute | solution.py:42
  133.0 9.7 %collective-permute-start.41 = (bf16[136,1024]{1,0:T(8,128)(2,1)}, bf16[136,1024]{1,0:T(8,128)(2,1)S(1)}, u32[]{:S(2)}, u32[]{:S(2)}) collective-permute-start(bf16[136,1024]{1,0:T(8,128)(2,1)} %get-tuple-element.100), channel_id=1, source_target_pairs={{0,2},{1,3},{2,0},{3,1},{4,6},{5,7},{6,4},{7,5},{8,10},{9,11},{10,... | collective-permute-start | bytes 835592 | tf_op jit(solution)/shard_map/ppermute | solution.py:42
  136.6 22.3 %collective-permute-start.39 = (bf16[136,1024]{1,0:T(8,128)(2,1)}, bf16[136,1024]{1,0:T(8,128)(2,1)S(1)}, u32[]{:S(2)}, u32[]{:S(2)}) collective-permute-start(bf16[136,1024]{1,0:T(8,128)(2,1)} %get-tuple-element.97), channel_id=1, source_target_pairs={{0,2},{1,3},{2,0},{3,1},{4,6},{5,7},{6,4},{7,5},{8,10},{9,11},{10,... | collective-permute-start | bytes 835592 | tf_op jit(solution)/shard_map/ppermute | solution.py:42
  140.7 13.9 %collective-permute-start.36 = (bf16[136,1024]{1,0:T(8,128)(2,1)}, bf16[136,1024]{1,0:T(8,128)(2,1)S(1)}, u32[]{:S(2)}, u32[]{:S(2)}) collective-permute-start(bf16[136,1024]{1,0:T(8,128)(2,1)} %get-tuple-element.94), channel_id=1, source_target_pairs={{0,2},{1,3},{2,0},{3,1},{4,6},{5,7},{6,4},{7,5},{8,10},{9,11},{10,... | collective-permute-start | bytes 835592 | tf_op jit(solution)/shard_map/ppermute | solution.py:42
  145.4 13.6 %collective-permute-start.42 = (bf16[136,1024]{1,0:T(8,128)(2,1)}, bf16[136,1024]{1,0:T(8,128)(2,1)S(1)}, u32[]{:S(2)}, u32[]{:S(2)}) collective-permute-start(bf16[136,1024]{1,0:T(8,128)(2,1)} %line.4), channel_id=1, source_target_pairs={{0,4},{1,5},{2,6},{3,7},{4,0},{5,1},{6,2},{7,3},{8,12},{9,13},{10,... | collective-permute-start | bytes 835592 | tf_op jit(solution)/shard_map/ppermute | solution.py:42
  151.7 18.7 %collective-permute-start.34 = (bf16[136,1024]{1,0:T(8,128)(2,1)}, bf16[136,1024]{1,0:T(8,128)(2,1)S(1)}, u32[]{:S(2)}, u32[]{:S(2)}) collective-permute-start(bf16[136,1024]{1,0:T(8,128)(2,1)} %get-tuple-element.91), channel_id=1, source_target_pairs={{0,2},{1,3},{2,0},{3,1},{4,6},{5,7},{6,4},{7,5},{8,10},{9,11},{10,... | collective-permute-start | bytes 835592 | tf_op jit(solution)/shard_map/ppermute | solution.py:42
  157.3 13.1 %collective-permute-start.37 = (bf16[136,1024]{1,0:T(8,128)(2,1)}, bf16[136,1024]{1,0:T(8,128)(2,1)S(1)}, u32[]{:S(2)}, u32[]{:S(2)}) collective-permute-start(bf16[136,1024]{1,0:T(8,128)(2,1)} %line.3), channel_id=1, source_target_pairs={{0,4},{1,5},{2,6},{3,7},{4,0},{5,1},{6,2},{7,3},{8,12},{9,13},{10,... | collective-permute-start | bytes 835592 | tf_op jit(solution)/shard_map/ppermute | solution.py:42
  161.8 13.5 %collective-permute-start.43 = (bf16[136,1024]{1,0:T(8,128)(2,1)}, bf16[136,1024]{1,0:T(8,128)(2,1)S(1)}, u32[]{:S(2)}, u32[]{:S(2)}) collective-permute-start(bf16[136,1024]{1,0:T(8,128)(2,1)} %line.5), channel_id=1, source_target_pairs={{0,8},{1,9},{2,10},{3,11},{4,12},{5,13},{6,14},{7,15},{8,0},{9,1},... | collective-permute-start | bytes 835592 | tf_op jit(solution)/shard_map/ppermute | solution.py:42
  (64 other events, 385.0 us)

commit v3 on v0

v3 whole, which is shorter than its diff:
```python
import functools
import math

import jax
import jax.numpy as jnp
from jax import lax
from jax.experimental import pallas as pl
from jax.experimental.pallas import tpu as pltpu
from jax.sharding import PartitionSpec as P

ITERS = 3
AXIS = "tgt"
F32 = jnp.float32
BF16 = jnp.bfloat16
TAIL = 8
LOW = -1e30
ANY = pl.BlockSpec(memory_space=pl.ANY)


def whole(a):
    return pl.BlockSpec(a.shape, lambda *_: (0,) * len(a.shape))


def call(body, name, ins, outs, grid=(1,), in_specs=None, out_specs=None, flops=0, **kw):
    size = sum(math.prod(a.shape) * jnp.dtype(a.dtype).itemsize for a in [*ins, *outs])
    return pl.pallas_call(
        body,
        name=name,
        grid=grid,
        out_shape=outs,
        in_specs=in_specs or [whole(a) for a in ins],
        out_specs=out_specs or [whole(a) for a in outs],
        compiler_params=pltpu.CompilerParams(vmem_limit_bytes=60 << 20),
        cost_estimate=pl.CostEstimate(flops=flops, bytes_accessed=size, transcendentals=0),
        **kw,
    )(*ins)


def shape(dims, dtype=F32):
    return jax.ShapeDtypeStruct(dims, dtype)


def swap(value, mask):
    count = lax.axis_size(AXIS)
    return lax.ppermute(value, AXIS, [(i, i ^ mask) for i in range(count)])


def row_levels(count):
    levels, step = [(1,)], 4
    while step < count:
        if step * 4 <= count:
            levels.append((step, 2 * step, 3 * step))
            step *= 4
        else:
            levels.append((step,))
            step *= 2
    return levels


def flip(value, mask, blocks):
    move = (mask & 1) * (blocks // 2) + (mask >> 2)
    if not move:
        return value
    width = value.shape[-1] // blocks
    parts = [value[..., (r ^ move) * width : ((r ^ move) + 1) * width] for r in range(blocks)]
    return jnp.concatenate(parts, axis=-1)


def diagonal():
    return lax.broadcasted_iota(jnp.int32, (128, 128), 0) == lax.broadcasted_iota(
        jnp.int32, (128, 128), 1
    )


def to_column(row):
    same = diagonal()
    parts = [
        jnp.sum(
            jnp.where(same, jnp.broadcast_to(row[:, i : i + 128], (128, 128)), 0.0),
            axis=1,
            keepdims=True,
        )
        for i in range(0, row.shape[1], 128)
    ]
    return jnp.concatenate(parts, axis=0)


def to_row(column):
    same = diagonal()
    parts = [
        jnp.sum(
            jnp.where(same, jnp.broadcast_to(column[i : i + 128, :], (128, 128)), 0.0),
            axis=0,
            keepdims=True,
        )
        for i in range(0, column.shape[0], 128)
    ]
    return jnp.concatenate(parts, axis=1)


def cost_kernel(scale, copy, add_mass, offsets, *refs):
    x_refs, y_ref, logit_ref, pack_ref = refs[:2], refs[2], refs[3], refs[4]
    outs = refs[-5:] if copy else refs[-3:]
    s_outs, pack_out = outs[:2], outs[-1]
    y = y_ref[...]
    wide = y.astype(F32)
    logit = logit_ref[...]
    lift = to_column(logit) - scale * jnp.sum(wide * wide, axis=1, keepdims=True)
    pack_out[...] = pack_ref[...]
    if add_mass:
        pack_out[2:3, :] = pack_ref[2:3, :] + jnp.sum(jnp.exp(logit), axis=1, keepdims=True)
    for c in range(2):
        x = x_refs[c][...]
        if copy:
            outs[2 + c][...] = x
        s = (2.0 * scale) * lax.dot_general(
            y, x, (((1,), (1,)), ((), ())), preferred_element_type=F32
        )
        s_outs[c][...] = s
        s = s + lift
        lanes = slice(offsets[c], offsets[c] + s.shape[1])
        old = pack_ref[0:1, lanes]
        top = jnp.maximum(old, jnp.max(s, axis=0, keepdims=True))
        pack_out[0:1, lanes] = top
        pack_out[1:2, lanes] = pack_ref[1:2, lanes] * jnp.exp(old - top) + jnp.sum(
            jnp.exp(s - top), axis=0, keepdims=True
        )


def merge(packs, masks, blocks):
    packs = [flip(p, m, blocks) for p, m in zip(packs, masks)]
    top = functools.reduce(jnp.maximum, [p[0:1] for p in packs])
    total = sum(p[1:2] * jnp.exp(p[0:1] - top) for p in packs)
    return top, total, sum(p[2:3] for p in packs)


def merge_kernel(masks, blocks, *refs):
    top, total, mass = merge([r[...] for r in refs[:-1]], masks, blocks)
    refs[-1][0:1, :] = top
    refs[-1][1:2, :] = total
    refs[-1][2:3, :] = mass


def first_kernel(masks, blocks, *refs):
    pack_refs, refs = refs[: len(masks)], refs[len(masks) :]
    s_refs, refs = refs[:2], refs[2:]
    logit_ref, total_ref, e_ref, col_ref, q_ref, h_ref = refs

    @pl.when(pl.program_id(0) == 0)
    def _():
        top, total, mass = merge([r[...] for r in pack_refs], masks, blocks)
        h = logit_ref[...] - total_ref[...] + jnp.log(mass)
        h_ref[0:1, :] = h
        h_ref[1:2, :] = mass
        q_ref[...] = h - top - jnp.log(total)

    half = s_refs[0].shape[1]
    parts = [s_refs[c][...] + q_ref[:, c * half : (c + 1) * half] for c in range(2)]
    top = jnp.maximum(*[jnp.max(p, axis=1, keepdims=True) for p in parts])
    total = jnp.zeros_like(top)
    for c in range(2):
        e = jnp.exp(parts[c] - top)
        e_ref[:, c * half : (c + 1) * half] = e
        total = total + jnp.sum(e, axis=1, keepdims=True)
    col_ref[0:1, :] = to_row(top)
    col_ref[1:2, :] = to_row(total)


def weighted_rows(e_ref, weight, row_ref):
    @pl.when(pl.program_id(0) == 0)
    def _():
        row_ref[...] = jnp.zeros_like(row_ref)

    row_ref[...] += jnp.sum(e_ref[...] * to_column(weight), axis=0, keepdims=True)


def first_row_kernel(e_ref, own_ref, other_ref, logit_ref, row_ref, phi_ref, g_ref):
    tops = own_ref[0:1, :], other_ref[0:1, :]
    top = jnp.maximum(*tops)
    total = own_ref[1:2, :] * jnp.exp(tops[0] - top) + other_ref[1:2, :] * jnp.exp(tops[1] - top)
    g_ref[...] = -(top + jnp.log(total))
    phi = jnp.exp(tops[0] - top) / total
    phi_ref[...] = phi
    weighted_rows(e_ref, jnp.exp(logit_ref[...]) * phi, row_ref)


def row_kernel(e_ref, own_ref, other_ref, logit_ref, phi_ref, row_ref):
    weight = jnp.exp(logit_ref[...]) * phi_ref[...] / (own_ref[...] + other_ref[...])
    weighted_rows(e_ref, weight, row_ref)


def column_kernel(masks, blocks, *refs):
    sum_refs, refs = refs[: len(masks)], refs[len(masks) :]
    e_ref, h_ref, phi_ref, col_ref, a_ref = refs

    @pl.when(pl.program_id(0) == 0)
    def _():
        total = sum(flip(r[...], m, blocks) for r, m in zip(sum_refs, masks))
        a_ref[...] = jnp.exp(h_ref[0:1, :]) / total

    total = jnp.sum(e_ref[...] * a_ref[...], axis=1, keepdims=True)
    col_ref[...] = to_row(total) * phi_ref[...]


def plan_kernel(source_count, *refs):
    e_ref, a_ref, h_ref, own_ref, other_ref, logit_ref, phi_ref = refs[:7]
    keep_ref, send_ref, mass_ref, logb_ref = refs[7:]
    c = own_ref[...] + other_ref[...]
    logb_ref[...] = -jnp.log(c)
    mass = h_ref[1:2, : c.shape[1]]
    share = to_column(jnp.exp(logit_ref[...]) * phi_ref[...] * (source_count / mass) / c)
    plan = ((e_ref[...] * a_ref[...]) * share).astype(BF16)
    half = keep_ref.shape[1]
    keep_ref[...] = plan[:, :half]
    send_ref[...] = plan[:, half:]
    mass_ref[...] = to_row(jnp.sum(plan.astype(F32), axis=1, keepdims=True))


def split_mass(mass, width):
    mass = jnp.concatenate([mass, jnp.zeros((1, width - mass.shape[1]), F32)], axis=1)
    high = mass.astype(BF16).astype(F32)
    rest = mass - high
    middle = rest.astype(BF16).astype(F32)
    row = lax.broadcasted_iota(jnp.int32, (TAIL, width), 0)
    out = jnp.where(row == 0, high, jnp.where(row == 1, middle, rest - middle))
    return jnp.where(row < 3, out, 0.0).astype(BF16)


def joined_mass(ref, width):
    return jnp.sum(ref[ref.shape[0] - TAIL :, :width].astype(F32), axis=0, keepdims=True)


def row_part_kernel(keep_ref, other_ref, *refs):
    y_refs, (own_ref, out_ref) = refs[:-2], refs[-2:]
    group = len(y_refs) // 2
    part = mass = 0.0
    for plan_ref, ys in ((keep_ref, y_refs[:group]), (other_ref, y_refs[group:])):
        start = 0
        for y in ys:
            block = plan_ref[start : start + y.shape[0], :]
            start += y.shape[0]
            part = part + lax.dot_general(
                block, y[...], (((0,), (0,)), ((), ())), preferred_element_type=F32
            )
            mass = mass + jnp.sum(block.astype(F32), axis=0, keepdims=True)
    rows = own_ref.shape[0] - TAIL
    width = own_ref.shape[1]
    own_ref[:rows, :] = part[:rows, :]
    own_ref[rows:, :] = jnp.concatenate(
        [jnp.broadcast_to(mass[:, :rows], (TAIL, rows)), jnp.zeros((TAIL, width - rows), F32)],
        axis=1,
    )
    out_ref[:rows, :] = part[rows:, :].astype(BF16)
    out_ref[rows:, :] = split_mass(mass[:, rows:], width)


def line_kernel(own_ref, other_ref, out_ref):
    rows, width = out_ref.shape[0] - TAIL, out_ref.shape[1]
    out_ref[:rows, :] = (own_ref[:rows, :] + other_ref[:rows, :].astype(F32)).astype(BF16)
    mass = own_ref[rows : rows + 1, :rows] + joined_mass(other_ref, rows)
    out_ref[rows:, :] = split_mass(mass, width)


def source_kernel(own_ref, near_ref, far_ref, x_ref, out_ref):
    rows = out_ref.shape[0]
    part = own_ref[:rows, :] + near_ref[:rows, :].astype(F32) + far_ref[:rows, :].astype(F32)
    mass = own_ref[rows : rows + 1, :rows] + joined_mass(near_ref, rows)
    mass = mass + joined_mass(far_ref, rows)
    out_ref[...] = to_column(mass) * x_ref[...].astype(F32) - part


def col_part(keep_ref, send_ref, x_refs):
    return jnp.dot(keep_ref[...], x_refs[0][...], preferred_element_type=F32) + jnp.dot(
        send_ref[...], x_refs[1][...], preferred_element_type=F32
    )


def col_send_kernel(keep_ref, send_ref, x0_ref, x1_ref, mass_ref, *out_refs):
    part = col_part(keep_ref, send_ref, (x0_ref, x1_ref))
    width = part.shape[1]
    cols = part.shape[0] // len(out_refs)
    for p, ref in enumerate(out_refs):
        ref[:cols, :] = part[p * cols : (p + 1) * cols, :].astype(BF16)
        ref[cols:, :] = split_mass(mass_ref[:, p * cols : (p + 1) * cols], width)


def col_keep_kernel(keep_ref, send_ref, x0_ref, x1_ref, out_ref):
    out_ref[...] = col_part(keep_ref, send_ref, (x0_ref, x1_ref))


def target_kernel(factor, own_ref, other_ref, mass_ref, y_ref, *refs):
    cols = own_ref.shape[0]
    part = own_ref[...] + other_ref[:cols, :].astype(F32)
    mass = to_column(mass_ref[...] + joined_mass(other_ref, cols))
    refs[-1][...] = factor * (mass * y_ref[...].astype(F32) - part)


def per_device(source_feats, target_feats, source_logits, target_logits):
    count = lax.axis_size(AXIS)
    me = lax.axis_index(AXIS)
    rows, width = source_feats.shape
    cols = target_feats.shape[0]
    source_count = rows * count
    target_count = cols * count
    scale = 1.0 / math.sqrt(width)
    direct = count == 16
    blocks = count // 2
    lines = blocks // 2
    mine = source_count // 2
    half = mine // 2
    part = cols // 2
    masks = [4 * k + c for c in range(2) for k in range(lines)]
    order = jnp.bitwise_xor(me, jnp.array(masks))

    y_pieces = [target_feats[:part], target_feats[part:]]
    if direct:
        far = swap(source_feats, 8)
        line = [source_feats, swap(source_feats, 4), far]
    crossed = [swap(y, 2) for y in y_pieces]
    logits_here = target_logits.reshape(1, cols)
    logits_there = swap(logits_here, 2)
    logits = jnp.concatenate([logits_here, logits_there], axis=1)
    source_rel = source_logits.reshape(count, rows)[order].reshape(1, mine)
    source_total = jnp.log(jnp.sum(jnp.exp(source_logits))).reshape(1, 1)
    logits_here, source_rel, source_total = lax.optimization_barrier(
        (logits_here, source_rel, source_total)
    )
    pack = jnp.concatenate([jnp.full((1, mine), LOW, F32), jnp.zeros((2, mine), F32)])

    s_shape, x_shape = shape((2 * cols, half)), shape((half, width), BF16)
    store = None
    if direct:
        gate = None
        for k in range(lines):
            x = source_feats if k == 0 else line[k]
            if k:
                x, _ = lax.optimization_barrier((x, gate))
            pair = [x, swap(x, 1)]
            ins = [*pair, target_feats, logits_here, pack]
            column = pl.BlockSpec((cols, rows), lambda _, k=k: (0, k))
            block = pl.BlockSpec((rows, width), lambda _, k=k: (k, 0))
            *store, pack = call(
                functools.partial(
                    cost_kernel, scale, True, k == 0, (k * rows, half + k * rows)
                ),
                "cost",
                ins + (store or []),
                [s_shape, s_shape, x_shape, x_shape, shape(pack.shape)],
                in_specs=[whole(a) for a in ins] + [ANY] * len(store or []),
                out_specs=[column, column, block, block, whole(pack)],
                flops=4 * cols * rows * width,
                input_output_aliases={5 + i: i for i in range(4)} if store else {},
            )
            gate = pack
            if k == 0:
                far_gated, _ = lax.optimization_barrier((far, gate))
                line.append(swap(far_gated, 4))
        s0, s1, x0, x1 = store
    else:
        gathered = lax.all_gather(source_feats, AXIS, axis=0)[order].reshape(2, half, width)
        x0, x1 = gathered[0], gathered[1]

    def cost_piece(y, logit, index, height, store, pack):
        ins = [x0, x1, y, logit, pack]
        block = pl.BlockSpec((height, half), lambda _: (index, 0))
        return call(
            functools.partial(cost_kernel, scale, False, True, (0, half)),
            "cost",
            ins + store,
            [s_shape, s_shape, shape(pack.shape)],
            in_specs=[whole(a) for a in ins] + [ANY] * len(store),
            out_specs=[block, block, whole(pack)],
            flops=2 * height * mine * width,
            input_output_aliases={5 + i: i for i in range(len(store))},
        )

    if not direct:
        s0, s1, pack = cost_piece(target_feats, logits_here, 0, cols, [], pack)
    for p in range(2):
        s0, s1, pack = cost_piece(
            crossed[p], logits_there[:, p * part : (p + 1) * part], 2 + p, part, [s0, s1], pack
        )

    *levels, last = row_levels(count)
    last_masks = (0, *last)
    for level in levels:
        packs = [pack] + [swap(pack, m) for m in level]
        (pack,) = call(
            functools.partial(merge_kernel, (0, *level), blocks),
            "merge",
            packs,
            [shape(pack.shape)],
        )
    packs = [pack] + [swap(pack, m) for m in last]

    tile = part
    tiles = 2 * cols // tile
    grid = (tiles,)
    turn = tiles // 2
    tall = pl.BlockSpec((tile, mine), lambda j: (j, 0))
    tall_half = pl.BlockSpec((tile, half), lambda j: (j, 0))
    flat = pl.BlockSpec((1, mine), lambda j: (0, 0))
    flat2 = pl.BlockSpec((2, mine), lambda j: (0, 0))
    lane = pl.BlockSpec((1, tile), lambda j: (0, j))
    lane2 = pl.BlockSpec((2, tile), lambda j: (0, j))
    lane_other = pl.BlockSpec((1, tile), lambda j: (0, (j + turn) % tiles))
    lane2_other = pl.BlockSpec((2, tile), lambda j: (0, (j + turn) % tiles))
    flat_shape, lane_shape = shape((1, mine)), shape((1, 2 * cols))
    e_shape = shape((2 * cols, mine))

    e, col, q, h = call(
        functools.partial(first_kernel, last_masks, blocks),
        "first",
        [*packs, s0, s1, source_rel, source_total],
        [e_shape, shape((2, 2 * cols)), flat_shape, shape((2, mine))],
        grid=grid,
        in_specs=[pl.BlockSpec(pack.shape, lambda j: (0, 0))] * len(packs)
        + [tall_half, tall_half, flat, pl.BlockSpec((1, 1), lambda j: (0, 0))],
        out_specs=[tall, lane2, flat, flat2],
    )
    row, phi, g = call(
        first_row_kernel,
        "first_row",
        [e, col, swap(col, 2), logits],
        [flat_shape, lane_shape, lane_shape],
        grid=grid,
        in_specs=[tall, lane2, lane2_other, lane],
        out_specs=[flat, lane, lane],
    )

    def columns(row):
        for level in levels:
            row = row + sum(flip(swap(row, m), m, blocks) for m in level)
        sums = [row] + [swap(row, m) for m in last]
        return call(
            functools.partial(column_kernel, last_masks, blocks),
            "column",
            [*sums, e, h, phi],
            [lane_shape, flat_shape],
            grid=grid,
            in_specs=[flat] * len(sums) + [tall, flat2, lane],
            out_specs=[lane, flat],
        )

    for _ in range(ITERS - 2):
        col, a = columns(row)
        (row,) = call(
            row_kernel,
            "row",
            [e, col, swap(col, 2), logits, phi],
            [flat_shape],
            grid=grid,
            in_specs=[tall, lane, lane_other, lane, lane],
            out_specs=[flat],
        )
    col, a = columns(row)
    keep, send, mass, logb = call(
        functools.partial(plan_kernel, source_count),
        "plan",
        [e, a, h, col, swap(col, 2), logits, phi],
        [shape((2 * cols, half), BF16)] * 2 + [lane_shape, lane_shape],
        grid=grid,
        in_specs=[tall, flat, flat2, lane, lane_other, lane, lane],
        out_specs=[tall_half, tall_half, lane, lane],
    )

    upper = pl.BlockSpec((cols, half), lambda _: (0, 0))
    lower = pl.BlockSpec((cols, half), lambda _: (1, 0))
    feats = pl.BlockSpec((half, width), lambda _: (0, 0))
    outs = call(
        col_send_kernel,
        "col_send",
        [keep, send, x0, x1, mass],
        [shape((part + TAIL, width), BF16)] * 2,
        in_specs=[lower, lower, feats, feats, pl.BlockSpec((1, cols), lambda _: (0, 1))],
        flops=2 * cols * mine * width,
    )
    back = [swap(o, 2) for o in outs]
    gate = outs[1]
    if direct:
        other_plan = swap(send, 1)
        ys = [target_feats, *crossed]
        ys = ys + [swap(y, 1) for y in ys]
        block, block_out = shape((rows + TAIL, width)), shape((rows + TAIL, width), BF16)

        def row_parts(pair, gate):
            plan, other, _ = lax.optimization_barrier((keep, other_plan, gate))
            lanes = pl.BlockSpec((2 * cols, 2 * rows), lambda _: (0, pair))
            return call(
                row_part_kernel,
                "row_part",
                [plan, other, *ys],
                [block, block_out],
                in_specs=[lanes, lanes] + [whole(y) for y in ys],
                flops=8 * cols * 2 * rows * width,
            )

        own2, out3 = row_parts(1, gate)
        own0, out1 = row_parts(0, out3)
        near3 = swap(out3, 4)
        near1 = swap(out1, 4)
        (out2,) = call(line_kernel, "line", [own2, near3], [block_out])
        far2 = swap(out2, 8)
        (grad_source,) = call(
            source_kernel,
            "source",
            [own0, near1, far2, source_feats],
            [shape((rows, width))],
        )
        gate = out1
    else:
        plan = jnp.concatenate([keep, send], axis=1)
        both = jnp.concatenate([target_feats, *crossed], axis=0)
        full = lax.dot_general(
            plan, both, (((0,), (0,)), ((), ())), preferred_element_type=F32
        ).reshape(blocks, rows, width)
        row_mass = jnp.sum(plan.astype(F32), axis=0).reshape(blocks, rows)
        full = jnp.zeros((count, rows, width), F32).at[order].set(full)
        row_mass = jnp.zeros((count, rows), F32).at[order].set(row_mass)
        grad_source = lax.psum_scatter(row_mass, AXIS, scatter_dimension=0)[:, None] * (
            source_feats.astype(F32)
        ) - lax.psum_scatter(full, AXIS, scatter_dimension=0)

    keep_later, _ = lax.optimization_barrier((keep, gate))
    (own_col,) = call(
        col_keep_kernel,
        "col_keep",
        [keep_later, send, x0, x1],
        [shape((cols, width))],
        in_specs=[upper, upper, feats, feats],
        flops=2 * cols * mine * width,
    )
    grad_target = None
    for p in range(2):
        piece = pl.BlockSpec((part, width), lambda _, p=p: (p, 0))
        done = [] if grad_target is None else [grad_target]
        (grad_target,) = call(
            functools.partial(target_kernel, target_count / source_count),
            "target",
            [own_col, back[p], mass, target_feats, *done],
            [shape((cols, width))],
            in_specs=[
                piece,
                whole(back[p]),
                pl.BlockSpec((1, part), lambda _, p=p: (0, p)),
                piece,
            ]
            + [ANY] * len(done),
            out_specs=[piece],
            input_output_aliases={4: 0} if done else {},
        )

    source_sq = scale * jnp.concatenate(
        [jnp.sum(jnp.square(x.astype(F32)), axis=1) for x in (x0, x1)]
    )
    potential = (q + jnp.log(a) - source_rel + source_total).reshape(mine) + source_sq
    potential = potential.reshape(1, mine)
    pair = [v.reshape(2, lines, rows) for v in (potential, swap(potential, 2))]
    potential_src = jnp.stack(pair).transpose(2, 0, 1, 3).reshape(count, rows)
    everyone = jnp.bitwise_xor(me, jnp.arange(count))
    potential_src = potential_src[everyone].reshape(source_count)
    target_sq = scale * jnp.sum(jnp.square(target_feats.astype(F32)), axis=1)
    potential_tgt = (g + logb)[0, :cols] + target_sq
    return (grad_source, grad_target, potential_src, potential_tgt)


def solution(mesh):
    return jax.shard_map(
        per_device,
        mesh=mesh,
        in_specs=(
            P(("groups", "tgt"), None),
            P(("groups", "tgt"), None),
            P("groups"),
            P(("groups", "tgt")),
        ),
        out_specs=(
            P(("groups", "tgt"), None),
            P(("groups", "tgt"), None),
            P("groups"),
            P(("groups", "tgt")),
        ),
        check_vma=False,
    )
```

time: 396 us -> 179 us (0.45)
  blocking collectives: 248 us -> 0 us
  Pallas kernels: 0 us -> 74.3 us
  starting transfers between devices: 0.08 us -> 34.8 us
  waiting for transfers between devices: 78.1 us -> 47.6 us
  other arithmetic: 33.4 us -> 5.36 us
  matrix products: 16.3 us -> 0 us
  between operations: 16.3 us -> 1.6 us
  local copies, waits for them, and re-layouts: 2.98 us -> 14.6 us
    psum x4 -> x0, blocking collectives: 126 us -> none  [the longest x3 90.2 us: per_device(): total = lax.psum(jnp.sum(jnp.exp(scores - top[:, None]), axis=1), 'tgt')]
    pmax x3 -> x0, blocking collectives: 91.6 us -> none  [per_device(): top = lax.pmax(jnp.max(scores, axis=1), 'tgt')]
    pallas_call x0 -> x21, Pallas kernels: none -> 74.3 us  [call(): pl.pallas_call(body, name=name, grid=grid, out_shape=outs, in_specs=in_sp...]
    reduce_scatter x1 -> x0, waiting for transfers between devices: 64 us -> none  [per_device(): lax.psum_scatter(row_part, 'tgt', scatter_dimension=0, tiled=True)]
    ppermute x0 -> x35, waiting for transfers between devices: none -> 47.6 us  [swap(): return lax.ppermute(value, AXIS, [(i, i ^ mask) for i in range(count)])]
    ppermute x0 -> x35, starting transfers between devices: none -> 34.8 us  [swap(): return lax.ppermute(value, AXIS, [(i, i ^ mask) for i in range(count)])]
    unnamed x1 -> x0, blocking collectives: 30.1 us -> none
    reduce_sum x11 -> x3, other arithmetic: 20.6 us -> 2.07 us  [the longest x1 1.31 us: per_device(): source_total = jnp.log(jnp.sum(jnp.exp(source_logits))).reshape(1, 1)]
  transfers between devices with their start and end apart: 2 -> 35, of which waited for: 2 -> 17; matrix products, arithmetic and copies ran while one was open for 3% -> 5% of each run, Pallas kernels for 0% -> 28%
where the time goes in v3:
time: 179 us; the launch traced here: 178 us
  Pallas kernels  74.3 us (42%)
  waiting for transfers between devices  47.6 us (27%)
  starting transfers between devices  34.8 us (19%)
  local copies, waits for them, and re-layouts  14.6 us (8%)
  other arithmetic  5.36 us (3%)
    pallas_call x21, Pallas kernels, call(): pl.pallas_call(body, name=name, grid=grid, out_shape=outs, in_specs=in_sp...  74.3 us
    ppermute x35, waiting for transfers between devices, swap(): return lax.ppermute(value, AXIS, [(i, i ^ mask) for i in range(count)])  47.6 us
    ppermute x35, starting transfers between devices, swap(): return lax.ppermute(value, AXIS, [(i, i ^ mask) for i in range(count)])  34.8 us
    unnamed x78, local copies, waits for them, and re-layouts  10.9 us
  transfers between devices with their start and end apart: 35, of which 17 were waited for; matrix products, arithmetic and copies ran while one was open for 5% of the time, Pallas kernels for 28%

profile of v3, /device:TPU:0, one launch (start us, length us, event | category | flops | bytes accessed | tf_op | source)
XLA Modules:
  0.0 178.1 jit_solution(12834239301489613284)
XLA Ops:
  1.1 2.7 %collective-permute-start.3 = (bf16[128,1024]{1,0:T(8,128)(2,1)}, bf16[128,1024]{1,0:T(8,128)(2,1)S(1)}, u32[]{:S(2)}, u32[]{:S(2)}) collective-permute-start(bf16[128,1024]{1,0:T(8,128)(2,1)} %x_ref.1), channel_id=1, source_target_pairs={{0,4},{1,5},{2,6},{3,7},{4,0},{5,1},{6,2},{7,3},{8,12},{9,13},{10,... | collective-permute-start | bytes 786440 | tf_op jit(solution)/shard_map/ppermute | solution.py:45
  3.8 2.6 %collective-permute-start = (bf16[128,1024]{1,0:T(8,128)(2,1)}, bf16[128,1024]{1,0:T(8,128)(2,1)S(1)}, u32[]{:S(2)}, u32[]{:S(2)}) collective-permute-start(bf16[128,1024]{1,0:T(8,128)(2,1)} %x_ref.1), channel_id=1, source_target_pairs={{0,8},{1,9},{2,10},{3,11},{4,12},{5,13},{6,14},{7,15},{8,0},{9,1},... | collective-permute-start | bytes 786440 | tf_op jit(solution)/shard_map/ppermute | solution.py:45
  11.6 3.0 %cost.6 = (f32[1024,512]{1,0:T(8,128)}, f32[1024,512]{1,0:T(8,128)}, bf16[512,1024]{1,0:T(8,128)(2,1)}, bf16[512,1024]{1,0:T(8,128)(2,1)}, f32[3,1024]{1,0:T(4,128)}) custom-call(bf16[128,1024]{1,0:T(8,128)(2,1)} %x_ref.1, bf16[128,1024]{1,0:T(8,128)(2,1)} %copy-done.13, bf16[512,1024]{1,0:T(8,128)(2,1)} %y_ref.3, f32[1,512]{1,0:T(1,128)} %bitcast.20, ...), custom_call_target="tpu_custom_call" | custom-call | flops 268435456 | bytes 7890944 | tf_op jit(solution)/shard_map/cost/pallas_call | solution.py:26
  20.1 3.1 %cost.7 = (f32[1024,512]{1,0:T(8,128)}, f32[1024,512]{1,0:T(8,128)}, bf16[512,1024]{1,0:T(8,128)(2,1)}, bf16[512,1024]{1,0:T(8,128)(2,1)}, f32[3,1024]{1,0:T(4,128)}) custom-call(bf16[128,1024]{1,0:T(8,128)(2,1)} %copy-done.12, bf16[128,1024]{1,0:T(8,128)(2,1)} %copy-done.16, ...), custom_call_target="tpu_custom_call", output_to_operand_aliasing={{0}: (5, {}), {1}: (6, {}), {2}: (7, {}), {3}: (8, {})} | custom-call | flops 268435456 | bytes 14182400 | tf_op jit(solution)/shard_map/cost/pallas_call | solution.py:26
  26.1 3.1 %cost.8 = (f32[1024,512]{1,0:T(8,128)}, f32[1024,512]{1,0:T(8,128)}, bf16[512,1024]{1,0:T(8,128)(2,1)}, bf16[512,1024]{1,0:T(8,128)(2,1)}, f32[3,1024]{1,0:T(4,128)}) custom-call(bf16[128,1024]{1,0:T(8,128)(2,1)} %copy-done.10, bf16[128,1024]{1,0:T(8,128)(2,1)} %copy-done.14, ...), custom_call_target="tpu_custom_call", output_to_operand_aliasing={{0}: (5, {}), {1}: (6, {}), {2}: (7, {}), {3}: (8, {})} | custom-call | flops 268435456 | bytes 14182400 | tf_op jit(solution)/shard_map/cost/pallas_call | solution.py:26
  30.9 18.2 %collective-permute-done.8 = f32[1,512]{1,0:T(1,128)S(1)} collective-permute-done((f32[1,512]{1,0:T(1,128)S(1)}, f32[1,512]{1,0:T(1,128)S(1)}, u32[]{:S(2)}, u32[]{:S(2)}) %collective-permute-start.8) | collective-permute-done | bytes 2080 | tf_op jit(solution)/shard_map/ppermute | solution.py:45
  50.4 3.1 %cost.9 = (f32[1024,512]{1,0:T(8,128)}, f32[1024,512]{1,0:T(8,128)}, bf16[512,1024]{1,0:T(8,128)(2,1)}, bf16[512,1024]{1,0:T(8,128)(2,1)}, f32[3,1024]{1,0:T(4,128)}) custom-call(bf16[128,1024]{1,0:T(8,128)(2,1)} %copy-done.11, bf16[128,1024]{1,0:T(8,128)(2,1)} %copy-done.15, ...), custom_call_target="tpu_custom_call", output_to_operand_aliasing={{0}: (5, {}), {1}: (6, {}), {2}: (7, {}), {3}: (8, {})} | custom-call | flops 268435456 | bytes 14182400 | tf_op jit(solution)/shard_map/cost/pallas_call | solution.py:26
  53.4 3.4 %cost.10 = (f32[1024,512]{1,0:T(8,128)}, f32[1024,512]{1,0:T(8,128)}, f32[3,1024]{1,0:T(4,128)}) custom-call(bf16[512,1024]{1,0:T(8,128)(2,1)} %get-tuple-element.82.refs_0_.x0_ref, bf16[512,1024]{1,0:T(8,128)(2,1)} %get-tuple-element.83.refs_1_.x1_ref, ...), custom_call_target="tpu_custom_call", output_to_operand_aliasing={{0}: (5, {}), {1}: (6, {})} | custom-call | flops 536870912 | bytes 11035648 | tf_op jit(solution)/shard_map/cost/pallas_call | solution.py:26
  56.8 3.4 %cost.11 = (f32[1024,512]{1,0:T(8,128)}, f32[1024,512]{1,0:T(8,128)}, f32[3,1024]{1,0:T(4,128)}) custom-call(bf16[512,1024]{1,0:T(8,128)(2,1)} %get-tuple-element.82.refs_0_.x0_ref, bf16[512,1024]{1,0:T(8,128)(2,1)} %get-tuple-element.83.refs_1_.x1_ref, ...), custom_call_target="tpu_custom_call", output_to_operand_aliasing={{0}: (5, {}), {1}: (6, {})} | custom-call | flops 536870912 | bytes 11035648 | tf_op jit(solution)/shard_map/cost/pallas_call | solution.py:26
  72.6 5.3 %first.1 = (f32[1024,1024]{1,0:T(8,128)}, f32[2,1024]{1,0:T(2,128)}, f32[1,1024]{1,0:T(1,128)}, f32[2,1024]{1,0:T(2,128)}) custom-call(f32[3,1024]{1,0:T(4,128)} %merge.1.refs_0_, f32[3,1024]{1,0:T(4,128)} %copy-done.24, f32[3,1024]{1,0:T(4,128)} %copy-done.25, f32[3,1024]{1,0:T(4,128)} %copy-done.26, f32[1024,512]{1,0:T(8,128)} %get-tuple-element.91.refs_4_, ...), custom_call_target="tpu_custom_call" | custom-call | bytes 8462340 | tf_op jit(solution)/shard_map/first/pallas_call | solution.py:26
  82.4 4.1 %first_row.1 = (f32[1,1024]{1,0:T(1,128)}, f32[1,1024]{1,0:T(1,128)}, f32[1,1024]{1,0:T(1,128)}) custom-call(f32[1024,1024]{1,0:T(8,128)} %get-tuple-element.95.e_ref.refs_4_.refs_0_, f32[2,1024]{1,0:T(2,128)} %get-tuple-element.96.own_ref, f32[2,1024]{1,0:T(2,128)} %copy-done.27, f32[1,1024]{1,0:T(1,128)} %pad_maximum_fusion.logit_ref.refs_5_), custom_call_target="tpu_custom_call" | custom-call | bytes 4227072 | tf_op jit(solution)/shard_map/first_row/pallas_call | solution.py:26
  93.3 3.0 %collective-permute-done.18.refs_3_ = f32[1,1024]{1,0:T(1,128)S(1)} collective-permute-done((f32[1,1024]{1,0:T(1,128)S(1)}, f32[1,1024]{1,0:T(1,128)S(1)}, u32[]{:S(2)}, u32[]{:S(2)}) %collective-permute-start.18) | collective-permute-done | bytes 4128 | tf_op jit(solution)/shard_map/ppermute | solution.py:45
  96.9 4.0 %column.2 = (f32[1,1024]{1,0:T(1,128)}, f32[1,1024]{1,0:T(1,128)}) custom-call(f32[1,1024]{1,0:T(1,128)} %copy-done.22, f32[1,1024]{1,0:T(1,128)} %copy-done.29, f32[1,1024]{1,0:T(1,128)} %copy-done.31, f32[1,1024]{1,0:T(1,128)} %copy-done.34, f32[1024,1024]{1,0:T(8,128)} %get-tuple-element.95.e_ref.refs_4_.refs_0_, ...), custom_call_target="tpu_custom_call" | custom-call | bytes 4231168 | tf_op jit(solution)/shard_map/column/pallas_call | solution.py:26
  105.4 4.0 %row.1 = f32[1,1024]{1,0:T(1,128)} custom-call(f32[1024,1024]{1,0:T(8,128)} %get-tuple-element.95.e_ref.refs_4_.refs_0_, f32[1,1024]{1,0:T(1,128)} %get-tuple-element.100.own_ref, f32[1,1024]{1,0:T(1,128)} %copy-done.35, f32[1,1024]{1,0:T(1,128)} %pad_maximum_fusion.logit_ref.refs_5_, f32[1,1024]{1,0:T(1,128)} %get-tuple-element.99.refs_6_.phi_ref), custom_call_target="tpu_custom_call" | custom-call | bytes 4214784 | tf_op jit(solution)/shard_map/row/pallas_call | solution.py:26
  111.5 2.6 %collective-permute-start.22 = (f32[1,1024]{1,0:T(1,128)S(1)}, f32[1,1024]{1,0:T(1,128)S(1)}, u32[]{:S(2)}, u32[]{:S(2)}) collective-permute-start(f32[1,1024]{1,0:T(1,128)S(1)} %maximum_add_fusion.1.refs_0_), channel_id=1, source_target_pairs={{0,8},{1,9},{2,10},{3,11},{4,12},{5,13},{6,14},{7,15},{8,0},{9,1},... | collective-permute-start | bytes 12296 | tf_op jit(solution)/shard_map/ppermute | solution.py:45
  116.1 3.5 %collective-permute-done.23.refs_3_ = f32[1,1024]{1,0:T(1,128)S(1)} collective-permute-done((f32[1,1024]{1,0:T(1,128)S(1)}, f32[1,1024]{1,0:T(1,128)S(1)}, u32[]{:S(2)}, u32[]{:S(2)}) %collective-permute-start.23) | collective-permute-done | bytes 4128 | tf_op jit(solution)/shard_map/ppermute | solution.py:45
  120.2 4.0 %column.3 = (f32[1,1024]{1,0:T(1,128)}, f32[1,1024]{1,0:T(1,128)}) custom-call(f32[1,1024]{1,0:T(1,128)} %copy-done.21, f32[1,1024]{1,0:T(1,128)} %copy-done.28, f32[1,1024]{1,0:T(1,128)} %copy-done.30, f32[1,1024]{1,0:T(1,128)} %copy-done.32, f32[1024,1024]{1,0:T(8,128)} %get-tuple-element.95.e_ref.refs_4_.refs_0_, ...), custom_call_target="tpu_custom_call" | custom-call | bytes 4231168 | tf_op jit(solution)/shard_map/column/pallas_call | solution.py:26
  128.6 4.9 %plan.1 = (bf16[1024,512]{1,0:T(8,128)(2,1)}, bf16[1024,512]{1,0:T(8,128)(2,1)}, f32[1,1024]{1,0:T(1,128)}, f32[1,1024]{1,0:T(1,128)}) custom-call(f32[1024,1024]{1,0:T(8,128)} %get-tuple-element.95.e_ref.refs_4_.refs_0_, f32[1,1024]{1,0:T(1,128)} %get-tuple-element.101.refs_1_, f32[2,1024]{1,0:T(2,128)} %get-tuple-element.98.refs_5_.refs_2_, ...), custom_call_target="tpu_custom_call" | custom-call | bytes 6328320 | tf_op jit(solution)/shard_map/plan/pallas_call | solution.py:26
  138.7 4.0 %col_send.1 = (bf16[264,1024]{1,0:T(8,128)(2,1)}, bf16[264,1024]{1,0:T(8,128)(2,1)}) custom-call(bf16[1024,512]{1,0:T(8,128)(2,1)} %get-tuple-element.115.keep_ref, bf16[1024,512]{1,0:T(8,128)(2,1)} %get-tuple-element.104.send_ref, bf16[512,1024]{1,0:T(8,128)(2,1)} %get-tuple-element.82.refs_0_.x0_ref, bf16[512,1024]{1,0:T(8,128)(2,1)} %get-tuple-element.83.refs_1_.x1_ref, ...), custom_call_target="tpu_custom_call" | custom-call | flops 1073741824 | bytes 5279744 | tf_op jit(solution)/shard_map/col_send/pallas_call | solution.py:26
  146.8 4.6 %row_part.2 = (f32[136,1024]{1,0:T(8,128)}, bf16[136,1024]{1,0:T(8,128)(2,1)}) custom-call(bf16[1024,512]{1,0:T(8,128)(2,1)} %get-tuple-element.115.keep_ref, bf16[1024,512]{1,0:T(8,128)(2,1)} %collective-permute-done.25.other_ref, bf16[512,1024]{1,0:T(8,128)(2,1)} %y_ref.3, bf16[256,1024]{1,0:T(8,128)(2,1)} %collective-permute-done.9.refs_2_.refs_1_, ...), custom_call_target="tpu_custom_call" | custom-call | flops 1073741824 | bytes 7127040 | tf_op jit(solution)/shard_map/row_part/pallas_call | solution.py:26
  151.5 4.6 %row_part.3 = (f32[136,1024]{1,0:T(8,128)}, bf16[136,1024]{1,0:T(8,128)(2,1)}) custom-call(bf16[1024,512]{1,0:T(8,128)(2,1)} %get-tuple-element.115.keep_ref, bf16[1024,512]{1,0:T(8,128)(2,1)} %collective-permute-done.25.other_ref, bf16[512,1024]{1,0:T(8,128)(2,1)} %y_ref.3, bf16[256,1024]{1,0:T(8,128)(2,1)} %collective-permute-done.9.refs_2_.refs_1_, ...), custom_call_target="tpu_custom_call" | custom-call | flops 1073741824 | bytes 7127040 | tf_op jit(solution)/shard_map/row_part/pallas_call | solution.py:26
  163.4 4.4 %col_keep.1.own_ref = f32[512,1024]{1,0:T(8,128)} custom-call(bf16[1024,512]{1,0:T(8,128)(2,1)} %get-tuple-element.115.keep_ref, bf16[1024,512]{1,0:T(8,128)(2,1)} %get-tuple-element.104.send_ref, bf16[512,1024]{1,0:T(8,128)(2,1)} %get-tuple-element.82.refs_0_.x0_ref, bf16[512,1024]{1,0:T(8,128)(2,1)} %get-tuple-element.83.refs_1_.x1_ref), custom_call_target="tpu_custom_call" | custom-call | flops 1073741824 | bytes 6291456 | tf_op jit(solution)/shard_map/col_keep/pallas_call | solution.py:26
  168.6 2.8 %target.2.refs_0_ = f32[512,1024]{1,0:T(8,128)} custom-call(f32[512,1024]{1,0:T(8,128)} %col_keep.1.own_ref, bf16[264,1024]{1,0:T(8,128)(2,1)} %copy-done.5, f32[1,1024]{1,0:T(1,128)} %get-tuple-element.105.mass_ref, bf16[512,1024]{1,0:T(8,128)(2,1)} %y_ref.3), custom_call_target="tpu_custom_call" | custom-call | bytes 5787648 | tf_op jit(solution)/shard_map/target/pallas_call | solution.py:26
  172.2 2.8 %target.3 = f32[512,1024]{1,0:T(8,128)} custom-call(f32[512,1024]{1,0:T(8,128)} %col_keep.1.own_ref, bf16[264,1024]{1,0:T(8,128)(2,1)} %copy-done.6, f32[1,1024]{1,0:T(1,128)} %get-tuple-element.105.mass_ref, bf16[512,1024]{1,0:T(8,128)(2,1)} %y_ref.3, f32[512,1024]{1,0:T(8,128)} %target.2.refs_0_), custom_call_target="tpu_custom_call", output_to_operand_aliasing={{}: (4, {})} | custom-call | bytes 7884800 | tf_op jit(solution)/shard_map/target/pallas_call | solution.py:26
  (167 shorter events, 75.2 us)
Async XLA Ops:
  0.6 10.3 %collective-permute-start.1 = (bf16[128,1024]{1,0:T(8,128)(2,1)}, bf16[128,1024]{1,0:T(8,128)(2,1)S(1)}, u32[]{:S(2)}, u32[]{:S(2)}) collective-permute-start(bf16[128,1024]{1,0:T(8,128)(2,1)} %x_ref.1), channel_id=1, source_target_pairs={{0,1},{1,0},{2,3},{3,2},{4,5},{5,4},{6,7},{7,6},{8,9},{9,8},{10,11... | collective-permute-start | bytes 786440 | tf_op jit(solution)/shard_map/ppermute | solution.py:45
  1.1 15.2 %collective-permute-start.3 = (bf16[128,1024]{1,0:T(8,128)(2,1)}, bf16[128,1024]{1,0:T(8,128)(2,1)S(1)}, u32[]{:S(2)}, u32[]{:S(2)}) collective-permute-start(bf16[128,1024]{1,0:T(8,128)(2,1)} %x_ref.1), channel_id=1, source_target_pairs={{0,4},{1,5},{2,6},{3,7},{4,0},{5,1},{6,2},{7,3},{8,12},{9,13},{10,... | collective-permute-start | bytes 786440 | tf_op jit(solution)/shard_map/ppermute | solution.py:45
  3.8 15.2 %collective-permute-start = (bf16[128,1024]{1,0:T(8,128)(2,1)}, bf16[128,1024]{1,0:T(8,128)(2,1)S(1)}, u32[]{:S(2)}, u32[]{:S(2)}) collective-permute-start(bf16[128,1024]{1,0:T(8,128)(2,1)} %x_ref.1), channel_id=1, source_target_pairs={{0,8},{1,9},{2,10},{3,11},{4,12},{5,13},{6,14},{7,15},{8,0},{9,1},... | collective-permute-start | bytes 786440 | tf_op jit(solution)/shard_map/ppermute | solution.py:45
  19.0 10.3 %collective-permute-start.2 = (bf16[128,1024]{1,0:T(8,128)(2,1)S(1)}, bf16[128,1024]{1,0:T(8,128)(2,1)S(1)}, u32[]{:S(2)}, u32[]{:S(2)}) collective-permute-start(bf16[128,1024]{1,0:T(8,128)(2,1)S(1)} %collective-permute-done.refs_0_), channel_id=1, source_target_pairs={{0,4},{1,5},{2,6},{3,7},{4,0},{5,1},{6,2},{7,3},{8,12},{9,13},{10,... | collective-permute-start | bytes 786440 | tf_op jit(solution)/shard_map/ppermute | solution.py:45
  23.3 30.1 %collective-permute-start.9 = (bf16[256,1024]{1,0:T(8,128)(2,1)S(1)}, bf16[256,1024]{1,0:T(8,128)(2,1)}, u32[]{:S(2)}, u32[]{:S(2)}) collective-permute-start(bf16[256,1024]{1,0:T(8,128)(2,1)S(1)} %get-tuple-element.122), channel_id=1, source_target_pairs={{0,2},{1,3},{2,0},{3,1},{4,6},{5,7},{6,4},{7,5},{8,10},{9,11},{10,... | collective-permute-start | bytes 1572872 | tf_op jit(solution)/shard_map/ppermute | solution.py:45
  24.9 31.9 %collective-permute-start.7 = (bf16[256,1024]{1,0:T(8,128)(2,1)S(1)}, bf16[256,1024]{1,0:T(8,128)(2,1)}, u32[]{:S(2)}, u32[]{:S(2)}) collective-permute-start(bf16[256,1024]{1,0:T(8,128)(2,1)S(1)} %get-tuple-element.123), channel_id=1, source_target_pairs={{0,2},{1,3},{2,0},{3,1},{4,6},{5,7},{6,4},{7,5},{8,10},{9,11},{10,... | collective-permute-start | bytes 1572872 | tf_op jit(solution)/shard_map/ppermute | solution.py:45
  29.3 20.4 %collective-permute-start.6 = (bf16[128,1024]{1,0:T(8,128)(2,1)S(1)}, bf16[128,1024]{1,0:T(8,128)(2,1)S(1)}, u32[]{:S(2)}, u32[]{:S(2)}) collective-permute-start(bf16[128,1024]{1,0:T(8,128)(2,1)S(1)} %collective-permute-done.2.refs_0_), channel_id=1, source_target_pairs={{0,1},{1,0},{2,3},{3,2},{4,5},{5,4},{6,7},{7,6},{8,9},{9,8},{10,11... | collective-permute-start | bytes 786440 | tf_op jit(solution)/shard_map/ppermute | solution.py:45
  29.3 19.7 %collective-permute-start.8 = (f32[1,512]{1,0:T(1,128)S(1)}, f32[1,512]{1,0:T(1,128)S(1)}, u32[]{:S(2)}, u32[]{:S(2)}) collective-permute-start(f32[1,512]{1,0:T(1,128)S(1)} %bitcast.24), channel_id=1, source_target_pairs={{0,2},{1,3},{2,0},{3,1},{4,6},{5,7},{6,4},{7,5},{8,10},{9,11},{10,... | collective-permute-start | bytes 6152 | tf_op jit(solution)/shard_map/ppermute | solution.py:45
  65.2 4.9 %collective-permute-start.12 = (f32[3,1024]{1,0:T(4,128)}, f32[3,1024]{1,0:T(4,128)S(1)}, u32[]{:S(2)}, u32[]{:S(2)}) collective-permute-start(f32[3,1024]{1,0:T(4,128)} %merge.1.refs_0_), channel_id=1, source_target_pairs={{0,8},{1,9},{2,10},{3,11},{4,12},{5,13},{6,14},{7,15},{8,0},{9,1},... | collective-permute-start | bytes 36872 | tf_op jit(solution)/shard_map/ppermute | solution.py:45
  66.2 5.7 %collective-permute-start.13 = (f32[3,1024]{1,0:T(4,128)}, f32[3,1024]{1,0:T(4,128)S(1)}, u32[]{:S(2)}, u32[]{:S(2)}) collective-permute-start(f32[3,1024]{1,0:T(4,128)} %merge.1.refs_0_), channel_id=1, source_target_pairs={{0,12},{1,13},{2,14},{3,15},{4,8},{5,9},{6,10},{7,11},{8,4},{9,5},... | collective-permute-start | bytes 36872 | tf_op jit(solution)/shard_map/ppermute | solution.py:45
  88.8 4.5 %collective-permute-start.17 = (f32[1,1024]{1,0:T(1,128)S(1)}, f32[1,1024]{1,0:T(1,128)S(1)}, u32[]{:S(2)}, u32[]{:S(2)}) collective-permute-start(f32[1,1024]{1,0:T(1,128)S(1)} %maximum_add_fusion.refs_0_), channel_id=1, source_target_pairs={{0,8},{1,9},{2,10},{3,11},{4,12},{5,13},{6,14},{7,15},{8,0},{9,1},... | collective-permute-start | bytes 12296 | tf_op jit(solution)/shard_map/ppermute | solution.py:45
  90.9 5.4 %collective-permute-start.18 = (f32[1,1024]{1,0:T(1,128)S(1)}, f32[1,1024]{1,0:T(1,128)S(1)}, u32[]{:S(2)}, u32[]{:S(2)}) collective-permute-start(f32[1,1024]{1,0:T(1,128)S(1)} %maximum_add_fusion.refs_0_), channel_id=1, source_target_pairs={{0,12},{1,13},{2,14},{3,15},{4,8},{5,9},{6,10},{7,11},{8,4},{9,5},... | collective-permute-start | bytes 12296 | tf_op jit(solution)/shard_map/ppermute | solution.py:45
  109.4 36.7 %collective-permute-start.26 = (bf16[512,1024]{1,0:T(8,128)(2,1)S(1)}, bf16[512,1024]{1,0:T(8,128)(2,1)}, u32[]{:S(2)}, u32[]{:S(2)}) collective-permute-start(bf16[512,1024]{1,0:T(8,128)(2,1)S(1)} %copy-done.1), channel_id=1, source_target_pairs={{0,1},{1,0},{2,3},{3,2},{4,5},{5,4},{6,7},{7,6},{8,9},{9,8},{10,11... | collective-permute-start | bytes 3145736 | tf_op jit(solution)/shard_map/ppermute | solution.py:45
  111.4 4.5 %collective-permute-start.21 = (f32[1,1024]{1,0:T(1,128)S(1)}, f32[1,1024]{1,0:T(1,128)S(1)}, u32[]{:S(2)}, u32[]{:S(2)}) collective-permute-start(f32[1,1024]{1,0:T(1,128)S(1)} %maximum_add_fusion.1.refs_0_), channel_id=1, source_target_pairs={{0,4},{1,5},{2,6},{3,7},{4,0},{5,1},{6,2},{7,3},{8,12},{9,13},{10,... | collective-permute-start | bytes 12296 | tf_op jit(solution)/shard_map/ppermute | solution.py:45
  111.5 4.6 %collective-permute-start.22 = (f32[1,1024]{1,0:T(1,128)S(1)}, f32[1,1024]{1,0:T(1,128)S(1)}, u32[]{:S(2)}, u32[]{:S(2)}) collective-permute-start(f32[1,1024]{1,0:T(1,128)S(1)} %maximum_add_fusion.1.refs_0_), channel_id=1, source_target_pairs={{0,8},{1,9},{2,10},{3,11},{4,12},{5,13},{6,14},{7,15},{8,0},{9,1},... | collective-permute-start | bytes 12296 | tf_op jit(solution)/shard_map/ppermute | solution.py:45
  114.1 5.4 %collective-permute-start.23 = (f32[1,1024]{1,0:T(1,128)S(1)}, f32[1,1024]{1,0:T(1,128)S(1)}, u32[]{:S(2)}, u32[]{:S(2)}) collective-permute-start(f32[1,1024]{1,0:T(1,128)S(1)} %maximum_add_fusion.1.refs_0_), channel_id=1, source_target_pairs={{0,12},{1,13},{2,14},{3,15},{4,8},{5,9},{6,10},{7,11},{8,4},{9,5},... | collective-permute-start | bytes 12296 | tf_op jit(solution)/shard_map/ppermute | solution.py:45
  133.5 11.9 %collective-permute-start.25 = (bf16[1024,512]{1,0:T(8,128)(2,1)}, bf16[1024,512]{1,0:T(8,128)(2,1)}, u32[]{:S(2)}, u32[]{:S(2)}) collective-permute-start(bf16[1024,512]{1,0:T(8,128)(2,1)} %get-tuple-element.104.send_ref), channel_id=1, source_target_pairs={{0,1},{1,0},{2,3},{3,2},{4,5},{5,4},{6,7},{7,6},{8,9},{9,8},{10,11... | collective-permute-start | bytes 3145736 | tf_op jit(solution)/shard_map/ppermute | solution.py:45
  133.9 12.2 %collective-permute-start.27 = (bf16[256,1024]{1,0:T(8,128)(2,1)}, bf16[256,1024]{1,0:T(8,128)(2,1)S(1)}, u32[]{:S(2)}, u32[]{:S(2)}) collective-permute-start(bf16[256,1024]{1,0:T(8,128)(2,1)} %collective-permute-done.9.refs_2_.refs_1_), channel_id=1, source_target_pairs={{0,1},{1,0},{2,3},{3,2},{4,5},{5,4},{6,7},{7,6},{8,9},{9,8},{10,11... | collective-permute-start | bytes 1572872 | tf_op jit(solution)/shard_map/ppermute | solution.py:45
  134.4 11.6 %collective-permute-start.28 = (bf16[256,1024]{1,0:T(8,128)(2,1)}, bf16[256,1024]{1,0:T(8,128)(2,1)}, u32[]{:S(2)}, u32[]{:S(2)}) collective-permute-start(bf16[256,1024]{1,0:T(8,128)(2,1)} %collective-permute-done.7.refs_2_), channel_id=1, source_target_pairs={{0,1},{1,0},{2,3},{3,2},{4,5},{5,4},{6,7},{7,6},{8,9},{9,8},{10,11... | collective-permute-start | bytes 1572872 | tf_op jit(solution)/shard_map/ppermute | solution.py:45
  142.8 25.0 %collective-permute-start.33 = (bf16[264,1024]{1,0:T(8,128)(2,1)}, bf16[264,1024]{1,0:T(8,128)(2,1)S(1)}, u32[]{:S(2)}, u32[]{:S(2)}) collective-permute-start(bf16[264,1024]{1,0:T(8,128)(2,1)} %get-tuple-element.116), channel_id=1, source_target_pairs={{0,2},{1,3},{2,0},{3,1},{4,6},{5,7},{6,4},{7,5},{8,10},{9,11},{10,... | collective-permute-start | bytes 1622024 | tf_op jit(solution)/shard_map/ppermute | solution.py:45
  145.5 26.0 %collective-permute-start.32 = (bf16[264,1024]{1,0:T(8,128)(2,1)}, bf16[264,1024]{1,0:T(8,128)(2,1)S(1)}, u32[]{:S(2)}, u32[]{:S(2)}) collective-permute-start(bf16[264,1024]{1,0:T(8,128)(2,1)} %get-tuple-element.106), channel_id=1, source_target_pairs={{0,2},{1,3},{2,0},{3,1},{4,6},{5,7},{6,4},{7,5},{8,10},{9,11},{10,... | collective-permute-start | bytes 1622024 | tf_op jit(solution)/shard_map/ppermute | solution.py:45
  151.4 8.8 %collective-permute-start.30 = (bf16[136,1024]{1,0:T(8,128)(2,1)}, bf16[136,1024]{1,0:T(8,128)(2,1)S(1)}, u32[]{:S(2)}, u32[]{:S(2)}) collective-permute-start(bf16[136,1024]{1,0:T(8,128)(2,1)} %get-tuple-element.109), channel_id=1, source_target_pairs={{0,4},{1,5},{2,6},{3,7},{4,0},{5,1},{6,2},{7,3},{8,12},{9,13},{10,... | collective-permute-start | bytes 835592 | tf_op jit(solution)/shard_map/ppermute | solution.py:45
  156.1 18.9 %collective-permute-start.29 = (bf16[136,1024]{1,0:T(8,128)(2,1)}, bf16[136,1024]{1,0:T(8,128)(2,1)S(1)}, u32[]{:S(2)}, u32[]{:S(2)}) collective-permute-start(bf16[136,1024]{1,0:T(8,128)(2,1)} %get-tuple-element.113), channel_id=1, source_target_pairs={{0,4},{1,5},{2,6},{3,7},{4,0},{5,1},{6,2},{7,3},{8,12},{9,13},{10,... | collective-permute-start | bytes 835592 | tf_op jit(solution)/shard_map/ppermute | solution.py:45
  162.8 12.3 %collective-permute-start.31 = (bf16[136,1024]{1,0:T(8,128)(2,1)}, bf16[136,1024]{1,0:T(8,128)(2,1)S(1)}, u32[]{:S(2)}, u32[]{:S(2)}) collective-permute-start(bf16[136,1024]{1,0:T(8,128)(2,1)} %line.1), channel_id=1, source_target_pairs={{0,8},{1,9},{2,10},{3,11},{4,12},{5,13},{6,14},{7,15},{8,0},{9,1},... | collective-permute-start | bytes 835592 | tf_op jit(solution)/shard_map/ppermute | solution.py:45
  (50 other events, 158.1 us)

commit v4 on v3

--- a/solution.py
+++ b/solution.py
@@ -21,8 +21,7 @@
     return pl.BlockSpec(a.shape, lambda *_: (0,) * len(a.shape))
 
 
-def call(body, name, ins, outs, grid=(1,), in_specs=None, out_specs=None, flops=0, **kw):
-    size = sum(math.prod(a.shape) * jnp.dtype(a.dtype).itemsize for a in [*ins, *outs])
+def call(body, name, ins, outs, grid=(1,), in_specs=None, out_specs=None, size=1, **kw):
     return pl.pallas_call(
         body,
         name=name,
@@ -30,8 +29,8 @@
         out_shape=outs,
         in_specs=in_specs or [whole(a) for a in ins],
         out_specs=out_specs or [whole(a) for a in outs],
-        compiler_params=pltpu.CompilerParams(vmem_limit_bytes=60 << 20),
-        cost_estimate=pl.CostEstimate(flops=flops, bytes_accessed=size, transcendentals=0),
+        compiler_params=pltpu.CompilerParams(vmem_limit_bytes=16 << 20),
+        cost_estimate=pl.CostEstimate(flops=1, bytes_accessed=size, transcendentals=0),
         **kw,
     )(*ins)
 
@@ -312,11 +311,12 @@
     masks = [4 * k + c for c in range(2) for k in range(lines)]
     order = jnp.bitwise_xor(me, jnp.array(masks))
 
-    y_pieces = [target_feats[:part], target_feats[part:]]
     if direct:
         far = swap(source_feats, 8)
         line = [source_feats, swap(source_feats, 4), far]
-    crossed = [swap(y, 2) for y in y_pieces]
+    crossed = [swap(target_feats, 2)]
+    if direct:
+        ys = [target_feats, swap(target_feats, 1)]
     logits_here = target_logits.reshape(1, cols)
     logits_there = swap(logits_here, 2)
     logits = jnp.concatenate([logits_here, logits_there], axis=1)
@@ -330,11 +330,10 @@
     s_shape, x_shape = shape((2 * cols, half)), shape((half, width), BF16)
     store = None
     if direct:
-        gate = None
         for k in range(lines):
-            x = source_feats if k == 0 else line[k]
-            if k:
-                x, _ = lax.optimization_barrier((x, gate))
+            x = line[k]
+            if k == 3:
+                x, _ = lax.optimization_barrier((x, pack))
             pair = [x, swap(x, 1)]
             ins = [*pair, target_feats, logits_here, pack]
             column = pl.BlockSpec((cols, rows), lambda _, k=k: (0, k))
@@ -348,13 +347,11 @@
                 [s_shape, s_shape, x_shape, x_shape, shape(pack.shape)],
                 in_specs=[whole(a) for a in ins] + [ANY] * len(store or []),
                 out_specs=[column, column, block, block, whole(pack)],
-                flops=4 * cols * rows * width,
                 input_output_aliases={5 + i: i for i in range(4)} if store else {},
             )
-            gate = pack
             if k == 0:
-                far_gated, _ = lax.optimization_barrier((far, gate))
-                line.append(swap(far_gated, 4))
+                line[1:], _ = lax.optimization_barrier((line[1:], pack))
+                line.append(swap(line[2], 4))
         s0, s1, x0, x1 = store
     else:
         gathered = lax.all_gather(source_feats, AXIS, axis=0)[order].reshape(2, half, width)
@@ -370,16 +367,12 @@
             [s_shape, s_shape, shape(pack.shape)],
             in_specs=[whole(a) for a in ins] + [ANY] * len(store),
             out_specs=[block, block, whole(pack)],
-            flops=2 * height * mine * width,
             input_output_aliases={5 + i: i for i in range(len(store))},
         )
 
     if not direct:
         s0, s1, pack = cost_piece(target_feats, logits_here, 0, cols, [], pack)
-    for p in range(2):
-        s0, s1, pack = cost_piece(
-            crossed[p], logits_there[:, p * part : (p + 1) * part], 2 + p, part, [s0, s1], pack
-        )
+    s0, s1, pack = cost_piece(crossed[0], logits_there, 1, cols, [s0, s1], pack)
 
     *levels, last = row_levels(count)
     last_masks = (0, *last)
@@ -418,10 +411,15 @@
         + [tall_half, tall_half, flat, pl.BlockSpec((1, 1), lambda j: (0, 0))],
         out_specs=[tall, lane2, flat, flat2],
     )
+    col_other = swap(col, 2)
+    if direct:
+        crossed, _ = lax.optimization_barrier((crossed, pack))
+        ys = [ys[0], crossed[0], ys[1], swap(crossed[0], 1)]
+        col_other, *ys = lax.optimization_barrier((col_other, *ys))
     row, phi, g = call(
         first_row_kernel,
         "first_row",
-        [e, col, swap(col, 2), logits],
+        [e, col, col_other, logits],
         [flat_shape, lane_shape, lane_shape],
         grid=grid,
         in_specs=[tall, lane2, lane2_other, lane],
@@ -464,23 +462,23 @@
         out_specs=[tall_half, tall_half, lane, lane],
     )
 
-    upper = pl.BlockSpec((cols, half), lambda _: (0, 0))
-    lower = pl.BlockSpec((cols, half), lambda _: (1, 0))
     feats = pl.BlockSpec((half, width), lambda _: (0, 0))
-    outs = call(
-        col_send_kernel,
-        "col_send",
-        [keep, send, x0, x1, mass],
-        [shape((part + TAIL, width), BF16)] * 2,
-        in_specs=[lower, lower, feats, feats, pl.BlockSpec((1, cols), lambda _: (0, 1))],
-        flops=2 * cols * mine * width,
-    )
-    back = [swap(o, 2) for o in outs]
-    gate = outs[1]
+
+    def col_send(p, keep):
+        piece = pl.BlockSpec((part, half), lambda _: (2 + p, 0))
+        (out,) = call(
+            col_send_kernel,
+            "col_send",
+            [keep, send, x0, x1, mass],
+            [shape((part + TAIL, width), BF16)],
+            in_specs=[piece, piece, feats, feats, pl.BlockSpec((1, part), lambda _: (0, 2 + p))],
+        )
+        return out
+
+    out = col_send(0, keep)
+    back = [swap(out, 2)]
     if direct:
         other_plan = swap(send, 1)
-        ys = [target_feats, *crossed]
-        ys = ys + [swap(y, 1) for y in ys]
         block, block_out = shape((rows + TAIL, width)), shape((rows + TAIL, width), BF16)
 
         def row_parts(pair, gate):
@@ -492,12 +490,14 @@
                 [plan, other, *ys],
                 [block, block_out],
                 in_specs=[lanes, lanes] + [whole(y) for y in ys],
-                flops=8 * cols * 2 * rows * width,
             )
 
-        own2, out3 = row_parts(1, gate)
-        own0, out1 = row_parts(0, out3)
+        own2, out3 = row_parts(1, out)
         near3 = swap(out3, 4)
+        keep_gated, _ = lax.optimization_barrier((keep, out3))
+        out = col_send(1, keep_gated)
+        back.append(swap(out, 2))
+        own0, out1 = row_parts(0, out)
         near1 = swap(out1, 4)
         (out2,) = call(line_kernel, "line", [own2, near3], [block_out])
         far2 = swap(out2, 8)
@@ -509,6 +509,9 @@
         )
         gate = out1
     else:
+        out = col_send(1, keep)
+        back.append(swap(out, 2))
+        gate = out
         plan = jnp.concatenate([keep, send], axis=1)
         both = jnp.concatenate([target_feats, *crossed], axis=0)
         full = lax.dot_general(
@@ -521,14 +524,14 @@
             source_feats.astype(F32)
         ) - lax.psum_scatter(full, AXIS, scatter_dimension=0)
 
-    keep_later, _ = lax.optimization_barrier((keep, gate))
+    upper = pl.BlockSpec((cols, half), lambda _: (0, 0))
+    keep_later, x0, x1, a, q, _ = lax.optimization_barrier((keep, x0, x1, a, q, gate))
     (own_col,) = call(
         col_keep_kernel,
         "col_keep",
         [keep_later, send, x0, x1],
         [shape((cols, width))],
         in_specs=[upper, upper, feats, feats],
-        flops=2 * cols * mine * width,
     )
     grad_target = None
     for p in range(2):
@@ -547,6 +550,7 @@
             ]
             + [ANY] * len(done),
             out_specs=[piece],
+            size=7 * part * width,
             input_output_aliases={4: 0} if done else {},
         )
 

time: 179 us -> 115 us (0.64)
  Pallas kernels: 74.3 us -> 25.2 us
  local copies, waits for them, and re-layouts: 14.6 us -> 5.99 us
  starting transfers between devices: 34.8 us -> 29.3 us
  other arithmetic: 5.36 us -> 3.4 us
    pallas_call x21, Pallas kernels: 74.3 us -> 25.2 us  [call(): pl.pallas_call(body, name=name, grid=grid, out_shape=outs, in_specs=in_sp...]
    unnamed x78 -> x16, local copies, waits for them, and re-layouts: 10.9 us -> 3.58 us
    ppermute x35 -> x33, starting transfers between devices: 34.8 us -> 29.3 us  [swap(): return lax.ppermute(value, AXIS, [(i, i ^ mask) for i in range(count)])]
    ppermute x35 -> x33, waiting for transfers between devices: 47.6 us -> 48.9 us  [swap(): return lax.ppermute(value, AXIS, [(i, i ^ mask) for i in range(count)])]
  transfers between devices with their start and end apart: 35 -> 33, of which waited for: 17 -> 22; matrix products, arithmetic and copies ran while one was open for 5% -> 5% of each run, Pallas kernels for 28% -> 14%
where the time goes in v4:
time: 115 us; the launch traced here: 114 us
  waiting for transfers between devices  48.9 us (43%)
  starting transfers between devices  29.3 us (25%)
  Pallas kernels  25.2 us (22%)
  local copies, waits for them, and re-layouts  5.99 us (5%)
  other arithmetic  3.4 us (3%)
  between operations  1.57 us (1%)
    ppermute x33, waiting for transfers between devices, swap(): return lax.ppermute(value, AXIS, [(i, i ^ mask) for i in range(count)])  48.9 us
    ppermute x33, starting transfers between devices, swap(): return lax.ppermute(value, AXIS, [(i, i ^ mask) for i in range(count)])  29.3 us
    pallas_call x21, Pallas kernels, call(): pl.pallas_call(body, name=name, grid=grid, out_shape=outs, in_specs=in_sp...  25.2 us
    unnamed x16, local copies, waits for them, and re-layouts  3.58 us
  transfers between devices with their start and end apart: 33, of which 22 were waited for; matrix products, arithmetic and copies ran while one was open for 5% of the time, Pallas kernels for 14%

profile of v4, /device:TPU:0, one launch (start us, length us, event | category | flops | bytes accessed | tf_op | source)
XLA Modules:
  0.0 114.4 jit_solution(11552127785602534664)
XLA Ops:
  0.6 3.0 %collective-permute-start.7 = (bf16[512,1024]{1,0:T(8,128)(2,1)}, bf16[512,1024]{1,0:T(8,128)(2,1)S(1)}, u32[]{:S(2)}, u32[]{:S(2)}) collective-permute-start(bf16[512,1024]{1,0:T(8,128)(2,1)} %y_ref.3), channel_id=1, source_target_pairs={{0,2},{1,3},{2,0},{3,1},{4,6},{5,7},{6,4},{7,5},{8,10},{9,11},{10,... | collective-permute-start | bytes 3145736 | tf_op jit(solution)/shard_map/ppermute | solution.py:44
  3.7 1.6 %collective-permute-start = (bf16[128,1024]{1,0:T(8,128)(2,1)}, bf16[128,1024]{1,0:T(8,128)(2,1)S(1)}, u32[]{:S(2)}, u32[]{:S(2)}) collective-permute-start(bf16[128,1024]{1,0:T(8,128)(2,1)} %x_ref.1), channel_id=1, source_target_pairs={{0,4},{1,5},{2,6},{3,7},{4,0},{5,1},{6,2},{7,3},{8,12},{9,13},{10,... | collective-permute-start | bytes 786440 | tf_op jit(solution)/shard_map/ppermute | solution.py:44
  5.2 2.6 %collective-permute-start.1 = (bf16[128,1024]{1,0:T(8,128)(2,1)}, bf16[128,1024]{1,0:T(8,128)(2,1)S(1)}, u32[]{:S(2)}, u32[]{:S(2)}) collective-permute-start(bf16[128,1024]{1,0:T(8,128)(2,1)} %x_ref.1), channel_id=1, source_target_pairs={{0,8},{1,9},{2,10},{3,11},{4,12},{5,13},{6,14},{7,15},{8,0},{9,1},... | collective-permute-start | bytes 786440 | tf_op jit(solution)/shard_map/ppermute | solution.py:44
  16.2 1.8 %collective-permute-done.refs_0_ = bf16[128,1024]{1,0:T(8,128)(2,1)S(1)} collective-permute-done((bf16[128,1024]{1,0:T(8,128)(2,1)}, bf16[128,1024]{1,0:T(8,128)(2,1)S(1)}, u32[]{:S(2)}, u32[]{:S(2)}) %collective-permute-start) | collective-permute-done | bytes 262176 | tf_op jit(solution)/shard_map/ppermute | solution.py:44
  18.1 2.4 %collective-permute-done.1.refs_0_ = bf16[128,1024]{1,0:T(8,128)(2,1)S(1)} collective-permute-done((bf16[128,1024]{1,0:T(8,128)(2,1)}, bf16[128,1024]{1,0:T(8,128)(2,1)S(1)}, u32[]{:S(2)}, u32[]{:S(2)}) %collective-permute-start.1) | collective-permute-done | bytes 262176 | tf_op jit(solution)/shard_map/ppermute | solution.py:44
  23.8 5.4 %collective-permute-done.3.refs_0_ = bf16[128,1024]{1,0:T(8,128)(2,1)S(1)} collective-permute-done((bf16[128,1024]{1,0:T(8,128)(2,1)S(1)}, bf16[128,1024]{1,0:T(8,128)(2,1)S(1)}, u32[]{:S(2)}, u32[]{:S(2)}) %collective-permute-start.3) | collective-permute-done | bytes 262176 | tf_op jit(solution)/shard_map/ppermute | solution.py:44
  32.8 1.9 %cost.9 = (f32[1024,512]{1,0:T(8,128)S(1)}, f32[1024,512]{1,0:T(8,128)S(1)}, f32[3,1024]{1,0:T(4,128)S(1)}) custom-call(bf16[512,1024]{1,0:T(8,128)(2,1)S(1)} %get-tuple-element.124.refs_0_.x0_ref, bf16[512,1024]{1,0:T(8,128)(2,1)S(1)} %get-tuple-element.125.refs_1_.x1_ref, ...), custom_call_target="tpu_custom_call", output_to_operand_aliasing={{0}: (5, {}), {1}: (6, {})} | custom-call | flops 1 | bytes 1 | tf_op jit(solution)/shard_map/cost/pallas_call | solution.py:25
  36.6 2.6 %collective-permute-start.11 = (f32[3,1024]{1,0:T(4,128)S(1)}, f32[3,1024]{1,0:T(4,128)S(1)}, u32[]{:S(2)}, u32[]{:S(2)}) collective-permute-start(f32[3,1024]{1,0:T(4,128)S(1)} %merge.1.refs_0_), channel_id=1, source_target_pairs={{0,8},{1,9},{2,10},{3,11},{4,12},{5,13},{6,14},{7,15},{8,0},{9,1},... | collective-permute-start | bytes 36872 | tf_op jit(solution)/shard_map/ppermute | solution.py:44
  41.2 3.5 %collective-permute-done.12.refs_3_ = f32[3,1024]{1,0:T(4,128)S(1)} collective-permute-done((f32[3,1024]{1,0:T(4,128)S(1)}, f32[3,1024]{1,0:T(4,128)S(1)}, u32[]{:S(2)}, u32[]{:S(2)}) %collective-permute-start.12) | collective-permute-done | bytes 12320 | tf_op jit(solution)/shard_map/ppermute | solution.py:44
  46.8 3.1 %collective-permute-done.13.other_ref = f32[2,1024]{1,0:T(2,128)S(1)} collective-permute-done((f32[2,1024]{1,0:T(2,128)S(1)}, f32[2,1024]{1,0:T(2,128)S(1)}, u32[]{:S(2)}, u32[]{:S(2)}) %collective-permute-start.13) | collective-permute-done | bytes 8224 | tf_op jit(solution)/shard_map/ppermute | solution.py:44
  52.3 1.9 %collective-permute-start.18 = (f32[1,1024]{1,0:T(1,128)S(1)}, f32[1,1024]{1,0:T(1,128)S(1)}, u32[]{:S(2)}, u32[]{:S(2)}) collective-permute-start(f32[1,1024]{1,0:T(1,128)S(1)} %maximum_add_fusion.refs_0_), channel_id=1, source_target_pairs={{0,8},{1,9},{2,10},{3,11},{4,12},{5,13},{6,14},{7,15},{8,0},{9,1},... | collective-permute-start | bytes 12296 | tf_op jit(solution)/shard_map/ppermute | solution.py:44
  54.3 2.5 %collective-permute-start.19 = (f32[1,1024]{1,0:T(1,128)S(1)}, f32[1,1024]{1,0:T(1,128)S(1)}, u32[]{:S(2)}, u32[]{:S(2)}) collective-permute-start(f32[1,1024]{1,0:T(1,128)S(1)} %maximum_add_fusion.refs_0_), channel_id=1, source_target_pairs={{0,12},{1,13},{2,14},{3,15},{4,8},{5,9},{6,10},{7,11},{8,4},{9,5},... | collective-permute-start | bytes 12296 | tf_op jit(solution)/shard_map/ppermute | solution.py:44
  56.9 2.8 %collective-permute-done.19.refs_3_ = f32[1,1024]{1,0:T(1,128)S(1)} collective-permute-done((f32[1,1024]{1,0:T(1,128)S(1)}, f32[1,1024]{1,0:T(1,128)S(1)}, u32[]{:S(2)}, u32[]{:S(2)}) %collective-permute-start.19) | collective-permute-done | bytes 4128 | tf_op jit(solution)/shard_map/ppermute | solution.py:44
  61.3 3.1 %collective-permute-done.20.other_ref = f32[1,1024]{1,0:T(1,128)S(1)} collective-permute-done((f32[1,1024]{1,0:T(1,128)S(1)}, f32[1,1024]{1,0:T(1,128)S(1)}, u32[]{:S(2)}, u32[]{:S(2)}) %collective-permute-start.20) | collective-permute-done | bytes 4128 | tf_op jit(solution)/shard_map/ppermute | solution.py:44
  66.8 3.0 %collective-permute-start.23 = (f32[1,1024]{1,0:T(1,128)S(1)}, f32[1,1024]{1,0:T(1,128)S(1)}, u32[]{:S(2)}, u32[]{:S(2)}) collective-permute-start(f32[1,1024]{1,0:T(1,128)S(1)} %maximum_add_fusion.1.refs_0_), channel_id=1, source_target_pairs={{0,8},{1,9},{2,10},{3,11},{4,12},{5,13},{6,14},{7,15},{8,0},{9,1},... | collective-permute-start | bytes 12296 | tf_op jit(solution)/shard_map/ppermute | solution.py:44
  71.4 3.8 %collective-permute-done.24.refs_3_ = f32[1,1024]{1,0:T(1,128)S(1)} collective-permute-done((f32[1,1024]{1,0:T(1,128)S(1)}, f32[1,1024]{1,0:T(1,128)S(1)}, u32[]{:S(2)}, u32[]{:S(2)}) %collective-permute-start.24) | collective-permute-done | bytes 4128 | tf_op jit(solution)/shard_map/ppermute | solution.py:44
  76.5 3.1 %collective-permute-done.25.refs_4_ = f32[1,1024]{1,0:T(1,128)S(1)} collective-permute-done((f32[1,1024]{1,0:T(1,128)S(1)}, f32[1,1024]{1,0:T(1,128)S(1)}, u32[]{:S(2)}, u32[]{:S(2)}) %collective-permute-start.25) | collective-permute-done | bytes 4128 | tf_op jit(solution)/shard_map/ppermute | solution.py:44
  79.6 1.6 %plan.1 = (bf16[1024,512]{1,0:T(8,128)(2,1)S(1)}, bf16[1024,512]{1,0:T(8,128)(2,1)S(1)}, f32[1,1024]{1,0:T(1,128)S(1)}, f32[1,1024]{1,0:T(1,128)S(1)}) custom-call(f32[1024,1024]{1,0:T(8,128)S(1)} %get-tuple-element.96.e_ref.refs_4_.refs_0_, f32[1,1024]{1,0:T(1,128)S(1)} %get-tuple-element.127.refs_1_, f32[2,1024]{1,0:T(2,128)S(1)} %get-tuple-element.101.refs_5_.refs_2_, ...), custom_call_target="tpu_custom_call" | custom-call | flops 1 | bytes 1 | tf_op jit(solution)/shard_map/plan/pallas_call | solution.py:25
  85.3 1.6 %col_send.3 = bf16[264,1024]{1,0:T(8,128)(2,1)} custom-call(bf16[1024,512]{1,0:T(8,128)(2,1)S(1)} %get-tuple-element.123.keep_ref, bf16[1024,512]{1,0:T(8,128)(2,1)S(1)} %get-tuple-element.107.send_ref, bf16[512,1024]{1,0:T(8,128)(2,1)S(1)} %get-tuple-element.124.refs_0_.x0_ref, bf16[512,1024]{1,0:T(8,128)(2,1)S(1)} %get-tuple-element.125.refs_1_.x1_ref, ...), custom_call_target="tpu_custom_call" | custom-call | flops 1 | bytes 1 | tf_op jit(solution)/shard_map/col_send/pallas_call | solution.py:25
  88.0 2.0 %row_part.3 = (f32[136,1024]{1,0:T(8,128)S(1)}, bf16[136,1024]{1,0:T(8,128)(2,1)}) custom-call(bf16[1024,512]{1,0:T(8,128)(2,1)S(1)} %get-tuple-element.123.keep_ref, bf16[1024,512]{1,0:T(8,128)(2,1)S(1)} %collective-permute-done.26.other_ref, bf16[512,1024]{1,0:T(8,128)(2,1)S(1)} %copy-done.1, bf16[512,1024]{1,0:T(8,128)(2,1)S(1)} %collective-permute-done.7.refs_2_.refs_1_, ...), custom_call_target="tpu_custom_call" | custom-call | flops 1 | bytes 1 | tf_op jit(solution)/shard_map/row_part/pallas_call | solution.py:25
  89.9 2.0 %collective-permute-start.27 = (bf16[136,1024]{1,0:T(8,128)(2,1)}, bf16[136,1024]{1,0:T(8,128)(2,1)}, u32[]{:S(2)}, u32[]{:S(2)}) collective-permute-start(bf16[136,1024]{1,0:T(8,128)(2,1)} %get-tuple-element.120), channel_id=1, source_target_pairs={{0,4},{1,5},{2,6},{3,7},{4,0},{5,1},{6,2},{7,3},{8,12},{9,13},{10,... | collective-permute-start | bytes 835592 | tf_op jit(solution)/shard_map/ppermute | solution.py:44
  98.8 10.0 %collective-permute-done.32 = f32[1,1024]{1,0:T(1,128)S(1)} collective-permute-done((f32[1,1024]{1,0:T(1,128)S(1)}, f32[1,1024]{1,0:T(1,128)S(1)}, u32[]{:S(2)}, u32[]{:S(2)}) %collective-permute-start.32) | collective-permute-done | bytes 4128 | tf_op jit(solution)/shard_map/ppermute | solution.py:44
  110.0 2.4 %target.3 = f32[512,1024]{1,0:T(8,128)} custom-call(f32[512,1024]{1,0:T(8,128)S(1)} %col_keep.1.own_ref, bf16[264,1024]{1,0:T(8,128)(2,1)} %collective-permute-done.30.other_ref, f32[1,1024]{1,0:T(1,128)S(1)} %get-tuple-element.108.mass_ref, bf16[512,1024]{1,0:T(8,128)(2,1)S(1)} %copy-done.1, f32[512,1024]{1,0:T(8,128)} %target.2.refs_0_), custom_call_target="tpu_custom_call", output_to_operand_aliasing={{}: (4, {})} | custom-call | flops 1 | bytes 1835008 | tf_op jit(solution)/shard_map/target/pallas_call | solution.py:25
  112.4 2.0 %source.1 = f32[128,1024]{1,0:T(8,128)} custom-call(f32[136,1024]{1,0:T(8,128)S(1)} %copy-done.5, bf16[136,1024]{1,0:T(8,128)(2,1)} %collective-permute-done.27.near_ref, bf16[136,1024]{1,0:T(8,128)(2,1)} %collective-permute-done.29.far_ref, bf16[128,1024]{1,0:T(8,128)(2,1)S(1)} %copy-done.3), custom_call_target="tpu_custom_call" | custom-call | flops 1 | bytes 1 | tf_op jit(solution)/shard_map/source/pallas_call | solution.py:25
  (99 shorter events, 43.1 us)
Async XLA Ops:
  0.6 32.2 %collective-permute-start.7 = (bf16[512,1024]{1,0:T(8,128)(2,1)}, bf16[512,1024]{1,0:T(8,128)(2,1)S(1)}, u32[]{:S(2)}, u32[]{:S(2)}) collective-permute-start(bf16[512,1024]{1,0:T(8,128)(2,1)} %y_ref.3), channel_id=1, source_target_pairs={{0,2},{1,3},{2,0},{3,1},{4,6},{5,7},{6,4},{7,5},{8,10},{9,11},{10,... | collective-permute-start | bytes 3145736 | tf_op jit(solution)/shard_map/ppermute | solution.py:44
  3.7 8.1 %collective-permute-start.2 = (bf16[128,1024]{1,0:T(8,128)(2,1)}, bf16[128,1024]{1,0:T(8,128)(2,1)S(1)}, u32[]{:S(2)}, u32[]{:S(2)}) collective-permute-start(bf16[128,1024]{1,0:T(8,128)(2,1)} %x_ref.1), channel_id=1, source_target_pairs={{0,1},{1,0},{2,3},{3,2},{4,5},{5,4},{6,7},{7,6},{8,9},{9,8},{10,11... | collective-permute-start | bytes 786440 | tf_op jit(solution)/shard_map/ppermute | solution.py:44
  3.7 14.4 %collective-permute-start = (bf16[128,1024]{1,0:T(8,128)(2,1)}, bf16[128,1024]{1,0:T(8,128)(2,1)S(1)}, u32[]{:S(2)}, u32[]{:S(2)}) collective-permute-start(bf16[128,1024]{1,0:T(8,128)(2,1)} %x_ref.1), channel_id=1, source_target_pairs={{0,4},{1,5},{2,6},{3,7},{4,0},{5,1},{6,2},{7,3},{8,12},{9,13},{10,... | collective-permute-start | bytes 786440 | tf_op jit(solution)/shard_map/ppermute | solution.py:44
  5.2 15.2 %collective-permute-start.1 = (bf16[128,1024]{1,0:T(8,128)(2,1)}, bf16[128,1024]{1,0:T(8,128)(2,1)S(1)}, u32[]{:S(2)}, u32[]{:S(2)}) collective-permute-start(bf16[128,1024]{1,0:T(8,128)(2,1)} %x_ref.1), channel_id=1, source_target_pairs={{0,8},{1,9},{2,10},{3,11},{4,12},{5,13},{6,14},{7,15},{8,0},{9,1},... | collective-permute-start | bytes 786440 | tf_op jit(solution)/shard_map/ppermute | solution.py:44
  21.0 8.2 %collective-permute-start.3 = (bf16[128,1024]{1,0:T(8,128)(2,1)S(1)}, bf16[128,1024]{1,0:T(8,128)(2,1)S(1)}, u32[]{:S(2)}, u32[]{:S(2)}) collective-permute-start(bf16[128,1024]{1,0:T(8,128)(2,1)S(1)} %collective-permute-done.1.refs_0_), channel_id=1, source_target_pairs={{0,4},{1,5},{2,6},{3,7},{4,0},{5,1},{6,2},{7,3},{8,12},{9,13},{10,... | collective-permute-start | bytes 786440 | tf_op jit(solution)/shard_map/ppermute | solution.py:44
  34.7 12.0 %collective-permute-start.14 = (bf16[512,1024]{1,0:T(8,128)(2,1)S(1)}, bf16[512,1024]{1,0:T(8,128)(2,1)S(1)}, u32[]{:S(2)}, u32[]{:S(2)}) collective-permute-start(bf16[512,1024]{1,0:T(8,128)(2,1)S(1)} %copy-done.1), channel_id=1, source_target_pairs={{0,1},{1,0},{2,3},{3,2},{4,5},{5,4},{6,7},{7,6},{8,9},{9,8},{10,11... | collective-permute-start | bytes 3145736 | tf_op jit(solution)/shard_map/ppermute | solution.py:44
  35.9 14.0 %collective-permute-start.15 = (bf16[512,1024]{1,0:T(8,128)(2,1)S(1)}, bf16[512,1024]{1,0:T(8,128)(2,1)S(1)}, u32[]{:S(2)}, u32[]{:S(2)}) collective-permute-start(bf16[512,1024]{1,0:T(8,128)(2,1)S(1)} %collective-permute-done.7.refs_2_.refs_1_), channel_id=1, source_target_pairs={{0,1},{1,0},{2,3},{3,2},{4,5},{5,4},{6,7},{7,6},{8,9},{9,8},{10,11... | collective-permute-start | bytes 3145736 | tf_op jit(solution)/shard_map/ppermute | solution.py:44
  36.2 4.4 %collective-permute-start.10 = (f32[3,1024]{1,0:T(4,128)S(1)}, f32[3,1024]{1,0:T(4,128)S(1)}, u32[]{:S(2)}, u32[]{:S(2)}) collective-permute-start(f32[3,1024]{1,0:T(4,128)S(1)} %merge.1.refs_0_), channel_id=1, source_target_pairs={{0,4},{1,5},{2,6},{3,7},{4,0},{5,1},{6,2},{7,3},{8,12},{9,13},{10,... | collective-permute-start | bytes 36872 | tf_op jit(solution)/shard_map/ppermute | solution.py:44
  36.6 4.6 %collective-permute-start.11 = (f32[3,1024]{1,0:T(4,128)S(1)}, f32[3,1024]{1,0:T(4,128)S(1)}, u32[]{:S(2)}, u32[]{:S(2)}) collective-permute-start(f32[3,1024]{1,0:T(4,128)S(1)} %merge.1.refs_0_), channel_id=1, source_target_pairs={{0,8},{1,9},{2,10},{3,11},{4,12},{5,13},{6,14},{7,15},{8,0},{9,1},... | collective-permute-start | bytes 36872 | tf_op jit(solution)/shard_map/ppermute | solution.py:44
  39.2 5.5 %collective-permute-start.12 = (f32[3,1024]{1,0:T(4,128)S(1)}, f32[3,1024]{1,0:T(4,128)S(1)}, u32[]{:S(2)}, u32[]{:S(2)}) collective-permute-start(f32[3,1024]{1,0:T(4,128)S(1)} %merge.1.refs_0_), channel_id=1, source_target_pairs={{0,12},{1,13},{2,14},{3,15},{4,8},{5,9},{6,10},{7,11},{8,4},{9,5},... | collective-permute-start | bytes 36872 | tf_op jit(solution)/shard_map/ppermute | solution.py:44
  46.2 3.7 %collective-permute-start.13 = (f32[2,1024]{1,0:T(2,128)S(1)}, f32[2,1024]{1,0:T(2,128)S(1)}, u32[]{:S(2)}, u32[]{:S(2)}) collective-permute-start(f32[2,1024]{1,0:T(2,128)S(1)} %get-tuple-element.97.own_ref), channel_id=1, source_target_pairs={{0,2},{1,3},{2,0},{3,1},{4,6},{5,7},{6,4},{7,5},{8,10},{9,11},{10,... | collective-permute-start | bytes 24584 | tf_op jit(solution)/shard_map/ppermute | solution.py:44
  52.3 4.5 %collective-permute-start.17 = (f32[1,1024]{1,0:T(1,128)S(1)}, f32[1,1024]{1,0:T(1,128)S(1)}, u32[]{:S(2)}, u32[]{:S(2)}) collective-permute-start(f32[1,1024]{1,0:T(1,128)S(1)} %maximum_add_fusion.refs_0_), channel_id=1, source_target_pairs={{0,4},{1,5},{2,6},{3,7},{4,0},{5,1},{6,2},{7,3},{8,12},{9,13},{10,... | collective-permute-start | bytes 12296 | tf_op jit(solution)/shard_map/ppermute | solution.py:44
  52.3 4.6 %collective-permute-start.18 = (f32[1,1024]{1,0:T(1,128)S(1)}, f32[1,1024]{1,0:T(1,128)S(1)}, u32[]{:S(2)}, u32[]{:S(2)}) collective-permute-start(f32[1,1024]{1,0:T(1,128)S(1)} %maximum_add_fusion.refs_0_), channel_id=1, source_target_pairs={{0,8},{1,9},{2,10},{3,11},{4,12},{5,13},{6,14},{7,15},{8,0},{9,1},... | collective-permute-start | bytes 12296 | tf_op jit(solution)/shard_map/ppermute | solution.py:44
  54.3 5.4 %collective-permute-start.19 = (f32[1,1024]{1,0:T(1,128)S(1)}, f32[1,1024]{1,0:T(1,128)S(1)}, u32[]{:S(2)}, u32[]{:S(2)}) collective-permute-start(f32[1,1024]{1,0:T(1,128)S(1)} %maximum_add_fusion.refs_0_), channel_id=1, source_target_pairs={{0,12},{1,13},{2,14},{3,15},{4,8},{5,9},{6,10},{7,11},{8,4},{9,5},... | collective-permute-start | bytes 12296 | tf_op jit(solution)/shard_map/ppermute | solution.py:44
  66.7 4.5 %collective-permute-start.22 = (f32[1,1024]{1,0:T(1,128)S(1)}, f32[1,1024]{1,0:T(1,128)S(1)}, u32[]{:S(2)}, u32[]{:S(2)}) collective-permute-start(f32[1,1024]{1,0:T(1,128)S(1)} %maximum_add_fusion.1.refs_0_), channel_id=1, source_target_pairs={{0,4},{1,5},{2,6},{3,7},{4,0},{5,1},{6,2},{7,3},{8,12},{9,13},{10,... | collective-permute-start | bytes 12296 | tf_op jit(solution)/shard_map/ppermute | solution.py:44
  66.8 4.6 %collective-permute-start.23 = (f32[1,1024]{1,0:T(1,128)S(1)}, f32[1,1024]{1,0:T(1,128)S(1)}, u32[]{:S(2)}, u32[]{:S(2)}) collective-permute-start(f32[1,1024]{1,0:T(1,128)S(1)} %maximum_add_fusion.1.refs_0_), channel_id=1, source_target_pairs={{0,8},{1,9},{2,10},{3,11},{4,12},{5,13},{6,14},{7,15},{8,0},{9,1},... | collective-permute-start | bytes 12296 | tf_op jit(solution)/shard_map/ppermute | solution.py:44
  69.8 5.4 %collective-permute-start.24 = (f32[1,1024]{1,0:T(1,128)S(1)}, f32[1,1024]{1,0:T(1,128)S(1)}, u32[]{:S(2)}, u32[]{:S(2)}) collective-permute-start(f32[1,1024]{1,0:T(1,128)S(1)} %maximum_add_fusion.1.refs_0_), channel_id=1, source_target_pairs={{0,12},{1,13},{2,14},{3,15},{4,8},{5,9},{6,10},{7,11},{8,4},{9,5},... | collective-permute-start | bytes 12296 | tf_op jit(solution)/shard_map/ppermute | solution.py:44
  75.9 3.7 %collective-permute-start.25 = (f32[1,1024]{1,0:T(1,128)S(1)}, f32[1,1024]{1,0:T(1,128)S(1)}, u32[]{:S(2)}, u32[]{:S(2)}) collective-permute-start(f32[1,1024]{1,0:T(1,128)S(1)} %get-tuple-element.105.refs_3_), channel_id=1, source_target_pairs={{0,2},{1,3},{2,0},{3,1},{4,6},{5,7},{6,4},{7,5},{8,10},{9,11},{10,... | collective-permute-start | bytes 12296 | tf_op jit(solution)/shard_map/ppermute | solution.py:44
  82.3 15.1 %collective-permute-start.31 = (bf16[264,1024]{1,0:T(8,128)(2,1)S(1)}, bf16[264,1024]{1,0:T(8,128)(2,1)S(1)}, u32[]{:S(2)}, u32[]{:S(2)}) collective-permute-start(bf16[264,1024]{1,0:T(8,128)(2,1)S(1)} %col_send.2), channel_id=1, source_target_pairs={{0,2},{1,3},{2,0},{3,1},{4,6},{5,7},{6,4},{7,5},{8,10},{9,11},{10,... | collective-permute-start | bytes 1622024 | tf_op jit(solution)/shard_map/ppermute | solution.py:44
  85.2 9.6 %collective-permute-start.28 = (bf16[136,1024]{1,0:T(8,128)(2,1)S(1)}, bf16[136,1024]{1,0:T(8,128)(2,1)S(1)}, u32[]{:S(2)}, u32[]{:S(2)}) collective-permute-start(bf16[136,1024]{1,0:T(8,128)(2,1)S(1)} %get-tuple-element.115), channel_id=1, source_target_pairs={{0,4},{1,5},{2,6},{3,7},{4,0},{5,1},{6,2},{7,3},{8,12},{9,13},{10,... | collective-permute-start | bytes 835592 | tf_op jit(solution)/shard_map/ppermute | solution.py:44
  86.9 23.1 %collective-permute-start.30 = (bf16[264,1024]{1,0:T(8,128)(2,1)}, bf16[264,1024]{1,0:T(8,128)(2,1)}, u32[]{:S(2)}, u32[]{:S(2)}) collective-permute-start(bf16[264,1024]{1,0:T(8,128)(2,1)} %col_send.3), channel_id=1, source_target_pairs={{0,2},{1,3},{2,0},{3,1},{4,6},{5,7},{6,4},{7,5},{8,10},{9,11},{10,... | collective-permute-start | bytes 1622024 | tf_op jit(solution)/shard_map/ppermute | solution.py:44
  89.9 22.4 %collective-permute-start.27 = (bf16[136,1024]{1,0:T(8,128)(2,1)}, bf16[136,1024]{1,0:T(8,128)(2,1)}, u32[]{:S(2)}, u32[]{:S(2)}) collective-permute-start(bf16[136,1024]{1,0:T(8,128)(2,1)} %get-tuple-element.120), channel_id=1, source_target_pairs={{0,4},{1,5},{2,6},{3,7},{4,0},{5,1},{6,2},{7,3},{8,12},{9,13},{10,... | collective-permute-start | bytes 835592 | tf_op jit(solution)/shard_map/ppermute | solution.py:44
  92.5 16.3 %collective-permute-start.32 = (f32[1,1024]{1,0:T(1,128)S(1)}, f32[1,1024]{1,0:T(1,128)S(1)}, u32[]{:S(2)}, u32[]{:S(2)}) collective-permute-start(f32[1,1024]{1,0:T(1,128)S(1)} %get-tuple-element.130), channel_id=1, source_target_pairs={{0,2},{1,3},{2,0},{3,1},{4,6},{5,7},{6,4},{7,5},{8,10},{9,11},{10,... | collective-permute-start | bytes 12296 | tf_op jit(solution)/shard_map/ppermute | solution.py:44
  94.9 17.5 %collective-permute-start.29 = (bf16[136,1024]{1,0:T(8,128)(2,1)S(1)}, bf16[136,1024]{1,0:T(8,128)(2,1)}, u32[]{:S(2)}, u32[]{:S(2)}) collective-permute-start(bf16[136,1024]{1,0:T(8,128)(2,1)S(1)} %line.1), channel_id=1, source_target_pairs={{0,8},{1,9},{2,10},{3,11},{4,12},{5,13},{6,14},{7,15},{8,0},{9,1},... | collective-permute-start | bytes 835592 | tf_op jit(solution)/shard_map/ppermute | solution.py:44
  (17 other events, 40.5 us)

commit v5 on v4

v5 whole, which is shorter than its diff:
```python
import functools
import math

import jax
import jax.numpy as jnp
from jax import lax
from jax.experimental import pallas as pl
from jax.experimental.pallas import tpu as pltpu
from jax.sharding import PartitionSpec as P

ITERS = 3
AXIS = "tgt"
F32 = jnp.float32
BF16 = jnp.bfloat16
TAIL = 8
LOW = -1e30


def call(body, name, ins, outs, size=1, in_hbm=(), out_hbm=False, scalar=False, **kw):
    held, away = pl.BlockSpec(memory_space=pltpu.VMEM), pl.BlockSpec(memory_space=pl.ANY)
    specs = [away if i in in_hbm else held for i in range(len(ins))]
    if scalar:
        specs[0] = pl.BlockSpec(memory_space=pltpu.SMEM)
    return pl.pallas_call(
        body,
        name=name,
        out_shape=outs,
        in_specs=specs,
        out_specs=[away if out_hbm else held] * len(outs),
        compiler_params=pltpu.CompilerParams(vmem_limit_bytes=12 << 20),
        cost_estimate=pl.CostEstimate(flops=1, bytes_accessed=size, transcendentals=0),
        **kw,
    )(*ins)


def tiles(count):
    step = min(count, 256)
    return [slice(i, i + step) for i in range(0, count, step)]


def shape(dims, dtype=F32):
    return jax.ShapeDtypeStruct(dims, dtype)


def swap(value, mask):
    count = lax.axis_size(AXIS)
    return lax.ppermute(value, AXIS, [(i, i ^ mask) for i in range(count)])


def row_levels(count):
    levels, step = [(1,)], 4
    while step < count:
        if step * 4 <= count:
            levels.append((3 * step, 2 * step, step))
            step *= 4
        else:
            levels.append((step,))
            step *= 2
    return levels


def flip(value, mask, blocks):
    move = (mask & 1) * (blocks // 2) + (mask >> 2)
    if not move:
        return value
    width = value.shape[-1] // blocks
    parts = [value[..., (r ^ move) * width : ((r ^ move) + 1) * width] for r in range(blocks)]
    return jnp.concatenate(parts, axis=-1)


def by_index(value, me, blocks):
    width = value.shape[1] // blocks
    bit = 1
    while bit < blocks:
        parts = [value[:, (r ^ bit) * width : ((r ^ bit) + 1) * width] for r in range(blocks)]
        value = jnp.where((me & bit) != 0, jnp.concatenate(parts, axis=1), value)
        bit *= 2
    return value


def prep_kernel(count, me_ref, logit_ref, rel_ref, total_ref):
    logit = logit_ref[...]
    total_ref[...] = jnp.log(jnp.sum(jnp.exp(logit), axis=1, keepdims=True))
    value = by_index(logit, me_ref[0, 0], count)
    rows = logit.shape[1] // count
    lines = count // 4
    for c in range(2):
        for k in range(lines):
            here, there = (c * lines + k) * rows, (4 * k + c) * rows
            rel_ref[:, here : here + rows] = value[:, there : there + rows]


def potential_kernel(
    count, scale, me_ref, own_ref, other_ref, g_ref, logb_ref, y_ref, source_ref, target_ref
):
    rows = source_ref.shape[1] // count
    lines = count // 4
    parts = []
    for r in range(count):
        start = ((r & 1) * lines + (r >> 2)) * rows
        ref = other_ref if r & 2 else own_ref
        parts.append(ref[1:2, start : start + rows])
    source_ref[...] = by_index(jnp.concatenate(parts, axis=1), me_ref[0, 0], count)
    cols = target_ref.shape[1]
    wide = y_ref[...].astype(F32)
    square = to_row(jnp.sum(wide * wide, axis=1, keepdims=True))
    target_ref[...] = g_ref[:, :cols] + logb_ref[:, :cols] + scale * square


def diagonal():
    return lax.broadcasted_iota(jnp.int32, (128, 128), 0) == lax.broadcasted_iota(
        jnp.int32, (128, 128), 1
    )


def to_column(row):
    same = diagonal()
    parts = [
        jnp.sum(
            jnp.where(same, jnp.broadcast_to(row[:, i : i + 128], (128, 128)), 0.0),
            axis=1,
            keepdims=True,
        )
        for i in range(0, row.shape[1], 128)
    ]
    return jnp.concatenate(parts, axis=0)


def to_row(column):
    same = diagonal()
    parts = [
        jnp.sum(
            jnp.where(same, jnp.broadcast_to(column[i : i + 128, :], (128, 128)), 0.0),
            axis=0,
            keepdims=True,
        )
        for i in range(0, column.shape[0], 128)
    ]
    return jnp.concatenate(parts, axis=1)


def cost_kernel(scale, copy, add_mass, cols, line, *refs):
    x_refs, y_ref, logit_ref, pack_ref = refs[:2], refs[2], refs[3], refs[4]
    outs = refs[-5:] if copy else refs[-3:]
    s_outs, pack_out = outs[:2], outs[-1]
    half = s_outs[0].shape[1]
    y = y_ref[...]
    wide = y.astype(F32)
    logit = logit_ref[...]
    lift = to_column(logit) - scale * jnp.sum(wide * wide, axis=1, keepdims=True)
    pack_out[...] = pack_ref[...]
    if add_mass:
        pack_out[2:3, :] = pack_ref[2:3, :] + jnp.sum(jnp.exp(logit), axis=1, keepdims=True)
    for c in range(2):
        x = x_refs[c][...] if copy else x_refs[c][line, :]
        if copy:
            outs[2 + c][line, :] = x
        s = (2.0 * scale) * lax.dot_general(
            y, x, (((1,), (1,)), ((), ())), preferred_element_type=F32
        )
        s_outs[c][cols, line] = s
        s = s + lift
        lanes = slice(c * half + line.start, c * half + line.stop)
        old = pack_ref[0:1, lanes]
        top = jnp.maximum(old, jnp.max(s, axis=0, keepdims=True))
        pack_out[0:1, lanes] = top
        pack_out[1:2, lanes] = pack_ref[1:2, lanes] * jnp.exp(old - top) + jnp.sum(
            jnp.exp(s - top), axis=0, keepdims=True
        )


def merge(packs, masks, blocks):
    packs = [flip(p, m, blocks) for p, m in zip(packs, masks)]
    top = functools.reduce(jnp.maximum, [p[0:1] for p in packs])
    total = sum(p[1:2] * jnp.exp(p[0:1] - top) for p in packs)
    return top, total, sum(p[2:3] for p in packs)


def merge_kernel(masks, blocks, *refs):
    top, total, mass = merge([r[...] for r in refs[:-1]], masks, blocks)
    refs[-1][0:1, :] = top
    refs[-1][1:2, :] = total
    refs[-1][2:3, :] = mass


def first_kernel(masks, blocks, *refs):
    pack_refs, refs = refs[: len(masks)], refs[len(masks) :]
    s_refs, refs = refs[:2], refs[2:]
    logit_ref, total_ref, e_ref, col_ref, q_ref, h_ref = refs
    top, total, mass = merge([r[...] for r in pack_refs], masks, blocks)
    h = logit_ref[...] - total_ref[...] + jnp.log(mass)
    h_ref[0:1, :] = h
    h_ref[1:2, :] = mass
    q = h - top - jnp.log(total)
    q_ref[...] = q
    half = s_refs[0].shape[1]
    for t in tiles(e_ref.shape[0]):
        parts = [s_refs[c][t, :] + q[:, c * half : (c + 1) * half] for c in range(2)]
        top = jnp.maximum(*[jnp.max(p, axis=1, keepdims=True) for p in parts])
        total = jnp.zeros_like(top)
        for c in range(2):
            e = jnp.exp(parts[c] - top)
            e_ref[t, c * half : (c + 1) * half] = e
            total = total + jnp.sum(e, axis=1, keepdims=True)
        col_ref[0:1, t] = to_row(top)
        col_ref[1:2, t] = to_row(total)


def turn(value):
    half = value.shape[1] // 2
    return jnp.concatenate([value[:, half:], value[:, :half]], axis=1)


def weighted_rows(e_ref, weight):
    return sum(
        jnp.sum(e_ref[t, :] * to_column(weight[:, t]), axis=0, keepdims=True)
        for t in tiles(e_ref.shape[0])
    )


def first_row_kernel(e_ref, own_ref, other_ref, logit_ref, row_ref, phi_ref, g_ref):
    own, other = own_ref[...], turn(other_ref[...])
    top = jnp.maximum(own[0:1, :], other[0:1, :])
    total = own[1:2, :] * jnp.exp(own[0:1, :] - top) + other[1:2, :] * jnp.exp(other[0:1, :] - top)
    g_ref[...] = -(top + jnp.log(total))
    phi = jnp.exp(own[0:1, :] - top) / total
    phi_ref[...] = phi
    row_ref[...] = weighted_rows(e_ref, jnp.exp(logit_ref[...]) * phi)


def row_kernel(e_ref, own_ref, other_ref, logit_ref, phi_ref, row_ref):
    c = own_ref[...] + turn(other_ref[...])
    row_ref[...] = weighted_rows(e_ref, jnp.exp(logit_ref[...]) * phi_ref[...] / c)


def column_kernel(masks, blocks, *refs):
    sum_refs, refs = refs[: len(masks)], refs[len(masks) :]
    e_ref, h_ref, phi_ref, *base_ref, col_ref, a_ref = refs
    total = sum(flip(r[...], m, blocks) for r, m in zip(sum_refs, masks))
    a = jnp.exp(h_ref[0:1, :]) / total
    a_ref[...] = a
    for t in tiles(e_ref.shape[0]):
        total = jnp.sum(e_ref[t, :] * a, axis=1, keepdims=True)
        col_ref[0:1, t] = to_row(total) * phi_ref[:, t]
    if base_ref:
        col_ref[1:2, :] = base_ref[0][...] + jnp.log(a)


def plan_kernel(source_count, *refs):
    e_ref, a_ref, h_ref, own_ref, other_ref, logit_ref, phi_ref = refs[:7]
    keep_ref, near_ref, far_ref, mass_ref, logb_ref = refs[7:]
    c = own_ref[0:1, :] + turn(other_ref[0:1, :])
    logb_ref[...] = -jnp.log(c)
    share = jnp.exp(logit_ref[...]) * phi_ref[...] * (source_count / h_ref[1:2, :1]) / c
    half = keep_ref.shape[1]
    a = a_ref[...]
    for t in tiles(e_ref.shape[0]):
        plan = ((e_ref[t, :] * a) * to_column(share[:, t])).astype(BF16)
        keep_ref[t, :] = plan[:, :half]
        near_ref[t, :] = plan[:, half : half + half // 2]
        far_ref[t, :] = plan[:, half + half // 2 :]
        mass_ref[:, t] = to_row(jnp.sum(plan.astype(F32), axis=1, keepdims=True))


def split_mass(mass, width):
    mass = jnp.concatenate([mass, jnp.zeros((1, width - mass.shape[1]), F32)], axis=1)
    high = mass.astype(BF16).astype(F32)
    rest = mass - high
    middle = rest.astype(BF16).astype(F32)
    row = lax.broadcasted_iota(jnp.int32, (TAIL, width), 0)
    out = jnp.where(row == 0, high, jnp.where(row == 1, middle, rest - middle))
    return jnp.where(row < 3, out, 0.0).astype(BF16)


def joined_mass(ref, width):
    return jnp.sum(ref[ref.shape[0] - TAIL :, :width].astype(F32), axis=0, keepdims=True)


def row_part_kernel(lanes, keep_ref, other_ref, *refs):
    y_refs, (own_ref, out_ref) = refs[:-2], refs[-2:]
    group = len(y_refs) // 2
    part = mass = 0.0
    for plan_ref, part_lanes, ys in (
        (keep_ref, lanes, y_refs[:group]),
        (other_ref, slice(None), y_refs[group:]),
    ):
        start = 0
        for y in ys:
            block = plan_ref[start : start + y.shape[0], part_lanes]
            start += y.shape[0]
            part = part + lax.dot_general(
                block, y[...], (((0,), (0,)), ((), ())), preferred_element_type=F32
            )
            mass = mass + jnp.sum(block.astype(F32), axis=0, keepdims=True)
    rows = own_ref.shape[0] - TAIL
    width = own_ref.shape[1]
    own_ref[:rows, :] = part[:rows, :]
    own_ref[rows:, :] = jnp.concatenate(
        [jnp.broadcast_to(mass[:, :rows], (TAIL, rows)), jnp.zeros((TAIL, width - rows), F32)],
        axis=1,
    )
    out_ref[:rows, :] = part[rows:, :].astype(BF16)
    out_ref[rows:, :] = split_mass(mass[:, rows:], width)


def line_kernel(own_ref, other_ref, out_ref):
    rows, width = out_ref.shape[0] - TAIL, out_ref.shape[1]
    out_ref[:rows, :] = (own_ref[:rows, :] + other_ref[:rows, :].astype(F32)).astype(BF16)
    mass = own_ref[rows : rows + 1, :rows] + joined_mass(other_ref, rows)
    out_ref[rows:, :] = split_mass(mass, width)


def source_kernel(own_ref, near_ref, far_ref, x_ref, out_ref):
    rows = out_ref.shape[0]
    part = own_ref[:rows, :] + near_ref[:rows, :].astype(F32) + far_ref[:rows, :].astype(F32)
    mass = own_ref[rows : rows + 1, :rows] + joined_mass(near_ref, rows)
    mass = mass + joined_mass(far_ref, rows)
    out_ref[...] = to_column(mass) * x_ref[:rows, :].astype(F32) - part


def col_part(keep_ref, near_ref, far_ref, x0_ref, x1_ref, cols):
    half = near_ref.shape[1]
    part = jnp.dot(keep_ref[cols, :], x0_ref[...], preferred_element_type=F32)
    part = part + jnp.dot(near_ref[cols, :], x1_ref[:half, :], preferred_element_type=F32)
    return part + jnp.dot(far_ref[cols, :], x1_ref[half:, :], preferred_element_type=F32)


def col_send_kernel(cols, *refs):
    *refs, mass_ref, out_ref = refs
    part = col_part(*refs, cols)
    out_ref[: part.shape[0], :] = part.astype(BF16)
    out_ref[part.shape[0] :, :] = split_mass(mass_ref[:, cols], part.shape[1])


def col_keep_kernel(*refs):
    *refs, out_ref = refs
    out_ref[...] = col_part(*refs, slice(0, out_ref.shape[0]))


def target_rows(factor, cols, own_ref, other_ref, mass_ref, y_ref, out_ref, held_ref, sem_ref):
    count = cols.stop - cols.start
    mass = mass_ref[:, cols] + joined_mass(other_ref, count)
    copies = []
    for n, t in enumerate(slice(i, i + 128) for i in range(0, count, 128)):
        here = slice(cols.start + t.start, cols.start + t.stop)
        part = own_ref[here, :] + other_ref[t, :].astype(F32)
        held_ref[t, :] = factor * (to_column(mass[:, t]) * y_ref[here, :].astype(F32) - part)
        copies.append(pltpu.make_async_copy(held_ref.at[t], out_ref.at[here], sem_ref.at[n]))
        copies[-1].start()
    return copies


def target_kernel(factor, cols, *refs):
    for copy in target_rows(factor, cols, *refs):
        copy.wait()


def last_kernel(factor, cols, *refs):
    target_ins, (_, own_ref, near_ref, far_ref, x_ref), refs = refs[:4], refs[4:9], refs[9:]
    target_out, source_out, held_target, sem_target, held_source, sem_source = refs
    source_kernel(own_ref, near_ref, far_ref, x_ref, held_source)
    first = pltpu.make_async_copy(held_source, source_out, sem_source)
    first.start()
    copies = target_rows(factor, cols, *target_ins, target_out, held_target, sem_target)
    for copy in [first, *copies]:
        copy.wait()


def per_device(source_feats, target_feats, source_logits, target_logits):
    count = lax.axis_size(AXIS)
    me = lax.axis_index(AXIS)
    rows, width = source_feats.shape
    cols = target_feats.shape[0]
    source_count = rows * count
    target_count = cols * count
    scale = 1.0 / math.sqrt(width)
    direct = count == 16
    blocks = count // 2
    lines = blocks // 2
    mine = source_count // 2
    half = mine // 2
    parts = [slice(0, cols * 3 // 4), slice(cols * 3 // 4, cols)]
    masks = [4 * k + c for c in range(2) for k in range(lines)]
    order = jnp.bitwise_xor(me, jnp.array(masks))

    if direct:
        far = swap(source_feats, 8)
        line = [source_feats, swap(source_feats, 4), far]
    crossed = [swap(target_feats, 2)]
    logits_here = target_logits.reshape(1, cols)
    logits_there = swap(logits_here, 2)
    logits = jnp.concatenate([logits_here, logits_there], axis=1)
    here = me.astype(jnp.int32).reshape(1, 1)
    source_rel, source_total = call(
        functools.partial(prep_kernel, count),
        "prep",
        [here, source_logits.reshape(1, source_count)],
        [shape((1, mine)), shape((1, 1))],
        scalar=True,
    )
    logits_here, source_rel, source_total = lax.optimization_barrier(
        (logits_here, source_rel, source_total)
    )
    pack = jnp.concatenate([jnp.full((1, mine), LOW, F32), jnp.zeros((2, mine), F32)])

    s_shape, x_shape = shape((2 * cols, half)), shape((half, width), BF16)
    store = None

    def cost_piece(y, logit, start, line, xs, store, pack, first=True):
        return call(
            functools.partial(cost_kernel, scale, False, first, slice(start, start + cols), line),
            "cost",
            [*xs, y, logit, pack, *store],
            [s_shape, s_shape, shape(pack.shape)],
            input_output_aliases={5 + i: i for i in range(len(store))},
        )

    if direct:
        for k in range(lines):
            x = line[k]
            if k == 3:
                x, *_ = lax.optimization_barrier((x, logits_there, pack))
                s0, s1, pack = cost_piece(
                    crossed[0], logits_there, cols, slice(0, k * rows), store[2:], store[:2], pack
                )
                store = [s0, s1, *store[2:]]
            pair = [x, swap(x, 1)]
            ins = [*pair, target_feats, logits_here, pack]
            *store, pack = call(
                functools.partial(
                    cost_kernel,
                    scale,
                    True,
                    k == 0,
                    slice(0, cols),
                    slice(k * rows, (k + 1) * rows),
                ),
                "cost",
                ins + (store or []),
                [s_shape, s_shape, x_shape, x_shape, shape(pack.shape)],
                input_output_aliases={5 + i: i for i in range(4)} if store else {},
            )
            if k == 0:
                *line[1:], y, _ = lax.optimization_barrier((*line[1:], target_feats, pack))
                line.append(swap(line[2], 4))
                ys = [target_feats, swap(y, 1)]
        s0, s1, x0, x1 = store
        s0, s1, pack = cost_piece(
            crossed[0],
            logits_there,
            cols,
            slice(3 * rows, half),
            [x0, x1],
            [s0, s1],
            pack,
            first=False,
        )
    else:
        gathered = lax.all_gather(source_feats, AXIS, axis=0)[order].reshape(2, half, width)
        x0, x1 = gathered[0], gathered[1]
        full = slice(0, half)
        s0, s1, pack = cost_piece(target_feats, logits_here, 0, full, [x0, x1], [], pack)
        s0, s1, pack = cost_piece(crossed[0], logits_there, cols, full, [x0, x1], [s0, s1], pack)

    *levels, last = row_levels(count)
    last_masks = (0, *last)
    for level in levels:
        packs = [pack] + [swap(pack, m) for m in level]
        (pack,) = call(
            functools.partial(merge_kernel, (0, *level), blocks),
            "merge",
            packs,
            [shape(pack.shape)],
        )
    packs = [pack] + [swap(pack, m) for m in last]

    flat_shape, lane_shape = shape((1, mine)), shape((1, 2 * cols))
    e_shape = shape((2 * cols, mine))

    e, col, q, h = call(
        functools.partial(first_kernel, last_masks, blocks),
        "first",
        [*packs, s0, s1, source_rel, source_total],
        [e_shape, shape((2, 2 * cols)), flat_shape, shape((2, mine))],
    )
    col_other = swap(col, 2)
    if direct:
        crossed, _ = lax.optimization_barrier((crossed, pack))
        ys = [ys[0], crossed[0], ys[1], swap(crossed[0], 1)]
        col_other, *ys = lax.optimization_barrier((col_other, *ys))
    row, phi, g = call(
        first_row_kernel,
        "first_row",
        [e, col, col_other, logits],
        [flat_shape, lane_shape, lane_shape],
    )

    def columns(row, *base):
        for level in levels:
            row = row + sum(flip(swap(row, m), m, blocks) for m in level)
        sums = [row] + [swap(row, m) for m in last]
        return call(
            functools.partial(column_kernel, last_masks, blocks),
            "column",
            [*sums, e, h, phi, *base],
            [shape((1 + len(base), 2 * cols)), flat_shape],
        )

    for _ in range(ITERS - 2):
        col, a = columns(row)
        (row,) = call(
            row_kernel,
            "row",
            [e, col, swap(col, 2), logits, phi],
            [flat_shape],
        )
    assert mine == 2 * cols
    source_sq = scale * jnp.concatenate(
        [jnp.sum(jnp.square(x.astype(F32)), axis=1) for x in (x0, x1)]
    )
    base = q - source_rel + source_total + source_sq.reshape(1, mine)
    col, a = columns(row, base)
    col_other = swap(col, 2)
    keep, *sends, mass, logb = call(
        functools.partial(plan_kernel, source_count),
        "plan",
        [e, a, h, col, col_other, logits, phi],
        [shape((2 * cols, half), BF16)]
        + [shape((2 * cols, half // 2), BF16)] * 2
        + [lane_shape, lane_shape],
    )

    def col_send(p, keep):
        piece = slice(cols + parts[p].start, cols + parts[p].stop)
        (out,) = call(
            functools.partial(col_send_kernel, piece),
            "col_send",
            [keep, *sends, x0, x1, mass],
            [shape((parts[p].stop - parts[p].start + TAIL, width), BF16)],
        )
        return out

    out = col_send(0, keep)
    back = [swap(out, 2)]
    if direct:
        others = [None, swap(sends[1], 1)]
        others[0] = swap(sends[0], 1)
        block, block_out = shape((rows + TAIL, width)), shape((rows + TAIL, width), BF16)

        def row_parts(pair, gate):
            plan, other, _ = lax.optimization_barrier((keep, others[pair], gate))
            lanes = slice(2 * pair * rows, 2 * (pair + 1) * rows)
            return call(
                functools.partial(row_part_kernel, lanes),
                "row_part",
                [plan, other, *ys],
                [block, block_out],
            )

        own2, out3 = row_parts(1, out)
        near3 = swap(out3, 4)
        keep_gated, _ = lax.optimization_barrier((keep, out3))
        out = col_send(1, keep_gated)
        back.append(swap(out, 2))
        own0, out1 = row_parts(0, out)
        near1 = swap(out1, 4)
        (out2,) = call(line_kernel, "line", [own2, near3], [block_out])
        far2 = swap(out2, 8)
        ends = [own0, near1, far2, x0]
        gate = out1
    else:
        out = col_send(1, keep)
        back.append(swap(out, 2))
        gate = out
        plan = jnp.concatenate([keep, *sends], axis=1)
        both = jnp.concatenate([target_feats, *crossed], axis=0)
        full = lax.dot_general(
            plan, both, (((0,), (0,)), ((), ())), preferred_element_type=F32
        ).reshape(blocks, rows, width)
        row_mass = jnp.sum(plan.astype(F32), axis=0).reshape(blocks, rows)
        full = jnp.zeros((count, rows, width), F32).at[order].set(full)
        row_mass = jnp.zeros((count, rows), F32).at[order].set(row_mass)
        grad_source = lax.psum_scatter(row_mass, AXIS, scatter_dimension=0)[:, None] * (
            source_feats.astype(F32)
        ) - lax.psum_scatter(full, AXIS, scatter_dimension=0)

    logb, _ = lax.optimization_barrier((logb, gate))
    potential_src, potential_tgt = call(
        functools.partial(potential_kernel, count, scale),
        "potential",
        [here, col, col_other, g, logb, target_feats],
        [shape((1, source_count)), shape((1, cols))],
        scalar=True,
    )
    keep_later, _ = lax.optimization_barrier((keep, potential_tgt))
    (own_col,) = call(
        col_keep_kernel,
        "col_keep",
        [keep_later, *sends, x0, x1],
        [shape((cols, width))],
    )
    factor = target_count / source_count

    def held(p):
        size = parts[p].stop - parts[p].start
        return [pltpu.VMEM((size, width), F32), pltpu.SemaphoreType.DMA((size // 128,))]

    ins = [own_col, back[0], mass, target_feats]
    (grad_target,) = call(
        functools.partial(target_kernel, factor, parts[0]),
        "target",
        ins,
        [shape((cols, width))],
        size=4 * cols * width,
        out_hbm=True,
        scratch_shapes=held(0),
    )
    ins = [own_col, back[1], mass, target_feats, grad_target]
    kw = dict(size=cols * width, in_hbm=(4,), out_hbm=True, input_output_aliases={4: 0})
    if direct:
        grad_target, grad_source = call(
            functools.partial(last_kernel, factor, parts[1]),
            "last",
            ins + ends,
            [shape((cols, width)), shape((rows, width))],
            scratch_shapes=held(1) + [pltpu.VMEM((rows, width), F32), pltpu.SemaphoreType.DMA],
            **kw,
        )
    else:
        (grad_target,) = call(
            lambda *refs: target_kernel(factor, parts[1], *refs[:4], *refs[5:]),
            "target",
            ins,
            [shape((cols, width))],
            scratch_shapes=held(1),
            **kw,
        )

    potential_src = potential_src.reshape(source_count)
    potential_tgt = potential_tgt.reshape(cols)
    return (grad_source, grad_target, potential_src, potential_tgt)


def solution(mesh):
    return jax.shard_map(
        per_device,
        mesh=mesh,
        in_specs=(
            P(("groups", "tgt"), None),
            P(("groups", "tgt"), None),
            P("groups"),
            P(("groups", "tgt")),
        ),
        out_specs=(
            P(("groups", "tgt"), None),
            P(("groups", "tgt"), None),
            P("groups"),
            P(("groups", "tgt")),
        ),
        check_vma=False,
    )
```

time: 115 us -> 103 us (0.90)
  waiting for transfers between devices: 48.9 us -> 42.9 us
  Pallas kernels: 25.2 us -> 20.8 us
  starting transfers between devices: 29.3 us -> 32.4 us
  other arithmetic: 3.4 us -> 1.16 us
  local copies, waits for them, and re-layouts: 5.99 us -> 4.28 us
    ppermute x33, waiting for transfers between devices: 48.9 us -> 42.9 us  [swap(): return lax.ppermute(value, AXIS, [(i, i ^ mask) for i in range(count)])]
    pallas_call x21 -> x23, Pallas kernels: 25.2 us -> 20.8 us  [call(): pl.pallas_call(body, name=name, out_shape=outs, in_specs=specs, out_specs...]
    ppermute x33, starting transfers between devices: 29.3 us -> 32.4 us  [swap(): return lax.ppermute(value, AXIS, [(i, i ^ mask) for i in range(count)])]
    gather x2 -> x0, local copies, waits for them, and re-layouts: 2.4 us -> none  [the longest x1 1.25 us: per_device(): source_rel = source_logits.reshape(count, rows)[order].reshape(1, mine)]
    reduce_sum x2 -> x0, other arithmetic: 1.59 us -> none  [the longest x1 1.31 us: per_device(): source_total = jnp.log(jnp.sum(jnp.exp(source_logits))).reshape(1, 1)]
    unnamed x16 -> x12, local copies, waits for them, and re-layouts: 3.58 us -> 4.27 us
  transfers between devices with their start and end apart: 33 -> 33, of which waited for: 22 -> 21; matrix products, arithmetic and copies ran while one was open for 5% -> 1% of each run, Pallas kernels for 14% -> 14%
where the time goes in v5:
time: 103 us
  waiting for transfers between devices  42.9 us (42%)
  starting transfers between devices  32.4 us (31%)
  Pallas kernels  20.8 us (20%)
  local copies, waits for them, and re-layouts  4.28 us (4%)
  other arithmetic  1.16 us (1%)
    ppermute x33, waiting for transfers between devices, swap(): return lax.ppermute(value, AXIS, [(i, i ^ mask) for i in range(count)])  42.9 us
    ppermute x33, starting transfers between devices, swap(): return lax.ppermute(value, AXIS, [(i, i ^ mask) for i in range(count)])  32.4 us
    pallas_call x23, Pallas kernels, call(): pl.pallas_call(body, name=name, out_shape=outs, in_specs=specs, out_specs...  20.8 us
    unnamed x12, local copies, waits for them, and re-layouts  4.27 us
  transfers between devices with their start and end apart: 33, of which 21 were waited for; matrix products, arithmetic and copies ran while one was open for 1% of the time, Pallas kernels for 14%

profile of v5, /device:TPU:0, one launch (start us, length us, event | category | flops | bytes accessed | tf_op | source)
XLA Modules:
  0.0 102.6 jit_solution(17816188103304404791)
XLA Ops:
  0.6 3.0 %collective-permute-start.8 = (bf16[512,1024]{1,0:T(8,128)(2,1)}, bf16[512,1024]{1,0:T(8,128)(2,1)S(1)}, u32[]{:S(2)}, u32[]{:S(2)}) collective-permute-start(bf16[512,1024]{1,0:T(8,128)(2,1)} %refs_3_.3), channel_id=1, source_target_pairs={{0,2},{1,3},{2,0},{3,1},{4,6},{5,7},{6,4},{7,5},{8,10},{9,11},{10,... | collective-permute-start | bytes 3145736 | tf_op jit(solution)/shard_map/ppermute | solution.py:47
  3.7 1.6 %collective-permute-start = (bf16[128,1024]{1,0:T(8,128)(2,1)}, bf16[128,1024]{1,0:T(8,128)(2,1)S(1)}, u32[]{:S(2)}, u32[]{:S(2)}) collective-permute-start(bf16[128,1024]{1,0:T(8,128)(2,1)} %refs_0_.1), channel_id=1, source_target_pairs={{0,4},{1,5},{2,6},{3,7},{4,0},{5,1},{6,2},{7,3},{8,12},{9,13},{10,... | collective-permute-start | bytes 786440 | tf_op jit(solution)/shard_map/ppermute | solution.py:47
  5.2 2.6 %collective-permute-start.1 = (bf16[128,1024]{1,0:T(8,128)(2,1)}, bf16[128,1024]{1,0:T(8,128)(2,1)S(1)}, u32[]{:S(2)}, u32[]{:S(2)}) collective-permute-start(bf16[128,1024]{1,0:T(8,128)(2,1)} %refs_0_.1), channel_id=1, source_target_pairs={{0,8},{1,9},{2,10},{3,11},{4,12},{5,13},{6,14},{7,15},{8,0},{9,1},... | collective-permute-start | bytes 786440 | tf_op jit(solution)/shard_map/ppermute | solution.py:47
  13.6 4.5 %collective-permute-done.refs_0_ = bf16[128,1024]{1,0:T(8,128)(2,1)S(1)} collective-permute-done((bf16[128,1024]{1,0:T(8,128)(2,1)}, bf16[128,1024]{1,0:T(8,128)(2,1)S(1)}, u32[]{:S(2)}, u32[]{:S(2)}) %collective-permute-start) | collective-permute-done | bytes 262176 | tf_op jit(solution)/shard_map/ppermute | solution.py:47
  18.1 2.4 %collective-permute-done.1.refs_0_ = bf16[128,1024]{1,0:T(8,128)(2,1)S(1)} collective-permute-done((bf16[128,1024]{1,0:T(8,128)(2,1)}, bf16[128,1024]{1,0:T(8,128)(2,1)S(1)}, u32[]{:S(2)}, u32[]{:S(2)}) %collective-permute-start.1) | collective-permute-done | bytes 262176 | tf_op jit(solution)/shard_map/ppermute | solution.py:47
  23.8 3.3 %collective-permute-done.4.refs_3_ = f32[1,512]{1,0:T(1,128)S(1)} collective-permute-done((f32[1,512]{1,0:T(1,128)S(1)}, f32[1,512]{1,0:T(1,128)S(1)}, u32[]{:S(2)}, u32[]{:S(2)}) %collective-permute-start.4) | collective-permute-done | bytes 2080 | tf_op jit(solution)/shard_map/ppermute | solution.py:47
  27.1 2.1 %collective-permute-done.3.refs_0_ = bf16[128,1024]{1,0:T(8,128)(2,1)S(1)} collective-permute-done((bf16[128,1024]{1,0:T(8,128)(2,1)S(1)}, bf16[128,1024]{1,0:T(8,128)(2,1)S(1)}, u32[]{:S(2)}, u32[]{:S(2)}) %collective-permute-start.3) | collective-permute-done | bytes 262176 | tf_op jit(solution)/shard_map/ppermute | solution.py:47
  29.2 1.6 %cost.9 = (f32[1024,512]{1,0:T(8,128)S(1)}, f32[1024,512]{1,0:T(8,128)S(1)}, f32[3,1024]{1,0:T(4,128)S(1)}) custom-call(bf16[512,1024]{1,0:T(8,128)(2,1)S(1)} %get-tuple-element.92.refs_0_.refs_7_, bf16[512,1024]{1,0:T(8,128)(2,1)S(1)} %get-tuple-element.93.refs_1_.refs_8_, ...), custom_call_target="tpu_custom_call", output_to_operand_aliasing={{0}: (5, {}), {1}: (6, {})} | custom-call | flops 1 | bytes 1 | tf_op jit(solution)/shard_map/cost/pallas_call | solution.py:24
  34.5 2.4 %collective-permute-start.10 = (f32[3,1024]{1,0:T(4,128)S(1)}, f32[3,1024]{1,0:T(4,128)S(1)}, u32[]{:S(2)}, u32[]{:S(2)}) collective-permute-start(f32[3,1024]{1,0:T(4,128)S(1)} %merge.1.refs_0_), channel_id=1, source_target_pairs={{0,12},{1,13},{2,14},{3,15},{4,8},{5,9},{6,10},{7,11},{8,4},{9,5},... | collective-permute-start | bytes 36872 | tf_op jit(solution)/shard_map/ppermute | solution.py:47
  37.0 1.9 %collective-permute-start.12 = (f32[3,1024]{1,0:T(4,128)S(1)}, f32[3,1024]{1,0:T(4,128)S(1)}, u32[]{:S(2)}, u32[]{:S(2)}) collective-permute-start(f32[3,1024]{1,0:T(4,128)S(1)} %merge.1.refs_0_), channel_id=1, source_target_pairs={{0,4},{1,5},{2,6},{3,7},{4,0},{5,1},{6,2},{7,3},{8,12},{9,13},{10,... | collective-permute-start | bytes 36872 | tf_op jit(solution)/shard_map/ppermute | solution.py:47
  40.1 1.5 %collective-permute-done.11.refs_2_ = f32[3,1024]{1,0:T(4,128)S(1)} collective-permute-done((f32[3,1024]{1,0:T(4,128)S(1)}, f32[3,1024]{1,0:T(4,128)S(1)}, u32[]{:S(2)}, u32[]{:S(2)}) %collective-permute-start.11) | collective-permute-done | bytes 12320 | tf_op jit(solution)/shard_map/ppermute | solution.py:47
  41.6 1.8 %first.1 = (f32[1024,1024]{1,0:T(8,128)S(1)}, f32[2,1024]{1,0:T(2,128)S(1)}, f32[1,1024]{1,0:T(1,128)S(1)}, f32[2,1024]{1,0:T(2,128)S(1)}) custom-call(f32[3,1024]{1,0:T(4,128)S(1)} %merge.1.refs_0_, f32[3,1024]{1,0:T(4,128)S(1)} %collective-permute-done.10.refs_1_, f32[3,1024]{1,0:T(4,128)S(1)} %collective-permute-done.11.refs_2_, ...), custom_call_target="tpu_custom_call" | custom-call | flops 1 | bytes 1 | tf_op jit(solution)/shard_map/first/pallas_call | solution.py:24
  44.3 2.9 %collective-permute-done.13.other_ref = f32[2,1024]{1,0:T(2,128)S(1)} collective-permute-done((f32[2,1024]{1,0:T(2,128)S(1)}, f32[2,1024]{1,0:T(2,128)S(1)}, u32[]{:S(2)}, u32[]{:S(2)}) %collective-permute-start.13) | collective-permute-done | bytes 8224 | tf_op jit(solution)/shard_map/ppermute | solution.py:47
  49.0 1.6 %collective-permute-start.17 = (f32[1,1024]{1,0:T(1,128)S(1)}, f32[1,1024]{1,0:T(1,128)S(1)}, u32[]{:S(2)}, u32[]{:S(2)}) collective-permute-start(f32[1,1024]{1,0:T(1,128)S(1)} %maximum_add_fusion.refs_0_), channel_id=1, source_target_pairs={{0,12},{1,13},{2,14},{3,15},{4,8},{5,9},{6,10},{7,11},{8,4},{9,5},... | collective-permute-start | bytes 12296 | tf_op jit(solution)/shard_map/ppermute | solution.py:47
  51.6 1.9 %collective-permute-start.19 = (f32[1,1024]{1,0:T(1,128)S(1)}, f32[1,1024]{1,0:T(1,128)S(1)}, u32[]{:S(2)}, u32[]{:S(2)}) collective-permute-start(f32[1,1024]{1,0:T(1,128)S(1)} %maximum_add_fusion.refs_0_), channel_id=1, source_target_pairs={{0,4},{1,5},{2,6},{3,7},{4,0},{5,1},{6,2},{7,3},{8,12},{9,13},{10,... | collective-permute-start | bytes 12296 | tf_op jit(solution)/shard_map/ppermute | solution.py:47
  56.6 2.9 %collective-permute-done.20.other_ref = f32[1,1024]{1,0:T(1,128)S(1)} collective-permute-done((f32[1,1024]{1,0:T(1,128)S(1)}, f32[1,1024]{1,0:T(1,128)S(1)}, u32[]{:S(2)}, u32[]{:S(2)}) %collective-permute-start.20) | collective-permute-done | bytes 4128 | tf_op jit(solution)/shard_map/ppermute | solution.py:47
  61.4 2.5 %collective-permute-start.22 = (f32[1,1024]{1,0:T(1,128)S(1)}, f32[1,1024]{1,0:T(1,128)S(1)}, u32[]{:S(2)}, u32[]{:S(2)}) collective-permute-start(f32[1,1024]{1,0:T(1,128)S(1)} %maximum_add_fusion.1.refs_0_), channel_id=1, source_target_pairs={{0,12},{1,13},{2,14},{3,15},{4,8},{5,9},{6,10},{7,11},{8,4},{9,5},... | collective-permute-start | bytes 12296 | tf_op jit(solution)/shard_map/ppermute | solution.py:47
  66.9 1.5 %collective-permute-done.23.refs_2_ = f32[1,1024]{1,0:T(1,128)S(1)} collective-permute-done((f32[1,1024]{1,0:T(1,128)S(1)}, f32[1,1024]{1,0:T(1,128)S(1)}, u32[]{:S(2)}, u32[]{:S(2)}) %collective-permute-start.23) | collective-permute-done | bytes 4128 | tf_op jit(solution)/shard_map/ppermute | solution.py:47
  69.7 2.9 %collective-permute-done.25.refs_4_.other_ref = f32[2,1024]{1,0:T(2,128)S(1)} collective-permute-done((f32[2,1024]{1,0:T(2,128)S(1)}, f32[2,1024]{1,0:T(2,128)S(1)}, u32[]{:S(2)}, u32[]{:S(2)}) %collective-permute-start.25) | collective-permute-done | bytes 8224 | tf_op jit(solution)/shard_map/ppermute | solution.py:47
  78.9 1.4 %collective-permute-start.28 = (bf16[136,1024]{1,0:T(8,128)(2,1)S(1)}, bf16[136,1024]{1,0:T(8,128)(2,1)S(1)}, u32[]{:S(2)}, u32[]{:S(2)}) collective-permute-start(bf16[136,1024]{1,0:T(8,128)(2,1)S(1)} %col_send.3), channel_id=1, source_target_pairs={{0,2},{1,3},{2,0},{3,1},{4,6},{5,7},{6,4},{7,5},{8,10},{9,11},{10,... | collective-permute-start | bytes 835592 | tf_op jit(solution)/shard_map/ppermute | solution.py:47
  82.7 4.4 %collective-permute-done.31.other_ref = bf16[136,1024]{1,0:T(8,128)(2,1)S(1)} collective-permute-done((bf16[136,1024]{1,0:T(8,128)(2,1)S(1)}, bf16[136,1024]{1,0:T(8,128)(2,1)S(1)}, u32[]{:S(2)}, u32[]{:S(2)}) %collective-permute-start.31) | collective-permute-done | bytes 278560 | tf_op jit(solution)/shard_map/ppermute | solution.py:47
  87.2 2.0 %collective-permute-start.32 = (bf16[136,1024]{1,0:T(8,128)(2,1)S(1)}, bf16[136,1024]{1,0:T(8,128)(2,1)S(1)}, u32[]{:S(2)}, u32[]{:S(2)}) collective-permute-start(bf16[136,1024]{1,0:T(8,128)(2,1)S(1)} %line.1), channel_id=1, source_target_pairs={{0,8},{1,9},{2,10},{3,11},{4,12},{5,13},{6,14},{7,15},{8,0},{9,1},... | collective-permute-start | bytes 835592 | tf_op jit(solution)/shard_map/ppermute | solution.py:47
  91.3 4.8 %collective-permute-done.29.refs_1_ = bf16[392,1024]{1,0:T(8,128)(2,1)S(1)} collective-permute-done((bf16[392,1024]{1,0:T(8,128)(2,1)S(1)}, bf16[392,1024]{1,0:T(8,128)(2,1)S(1)}, u32[]{:S(2)}, u32[]{:S(2)}) %collective-permute-start.29) | collective-permute-done | bytes 802848 | tf_op jit(solution)/shard_map/ppermute | solution.py:47
  97.5 3.7 %collective-permute-done.28.refs_1_ = bf16[136,1024]{1,0:T(8,128)(2,1)S(1)} collective-permute-done((bf16[136,1024]{1,0:T(8,128)(2,1)S(1)}, bf16[136,1024]{1,0:T(8,128)(2,1)S(1)}, u32[]{:S(2)}, u32[]{:S(2)}) %collective-permute-start.28) | collective-permute-done | bytes 278560 | tf_op jit(solution)/shard_map/ppermute | solution.py:47
  (84 shorter events, 40.2 us)
Async XLA Ops:
  0.6 28.6 %collective-permute-start.8 = (bf16[512,1024]{1,0:T(8,128)(2,1)}, bf16[512,1024]{1,0:T(8,128)(2,1)S(1)}, u32[]{:S(2)}, u32[]{:S(2)}) collective-permute-start(bf16[512,1024]{1,0:T(8,128)(2,1)} %refs_3_.3), channel_id=1, source_target_pairs={{0,2},{1,3},{2,0},{3,1},{4,6},{5,7},{6,4},{7,5},{8,10},{9,11},{10,... | collective-permute-start | bytes 3145736 | tf_op jit(solution)/shard_map/ppermute | solution.py:47
  3.7 5.5 %collective-permute-start.2 = (bf16[128,1024]{1,0:T(8,128)(2,1)}, bf16[128,1024]{1,0:T(8,128)(2,1)S(1)}, u32[]{:S(2)}, u32[]{:S(2)}) collective-permute-start(bf16[128,1024]{1,0:T(8,128)(2,1)} %refs_0_.1), channel_id=1, source_target_pairs={{0,1},{1,0},{2,3},{3,2},{4,5},{5,4},{6,7},{7,6},{8,9},{9,8},{10,11... | collective-permute-start | bytes 786440 | tf_op jit(solution)/shard_map/ppermute | solution.py:47
  3.7 14.4 %collective-permute-start = (bf16[128,1024]{1,0:T(8,128)(2,1)}, bf16[128,1024]{1,0:T(8,128)(2,1)S(1)}, u32[]{:S(2)}, u32[]{:S(2)}) collective-permute-start(bf16[128,1024]{1,0:T(8,128)(2,1)} %refs_0_.1), channel_id=1, source_target_pairs={{0,4},{1,5},{2,6},{3,7},{4,0},{5,1},{6,2},{7,3},{8,12},{9,13},{10,... | collective-permute-start | bytes 786440 | tf_op jit(solution)/shard_map/ppermute | solution.py:47
  5.2 15.2 %collective-permute-start.1 = (bf16[128,1024]{1,0:T(8,128)(2,1)}, bf16[128,1024]{1,0:T(8,128)(2,1)S(1)}, u32[]{:S(2)}, u32[]{:S(2)}) collective-permute-start(bf16[128,1024]{1,0:T(8,128)(2,1)} %refs_0_.1), channel_id=1, source_target_pairs={{0,8},{1,9},{2,10},{3,11},{4,12},{5,13},{6,14},{7,15},{8,0},{9,1},... | collective-permute-start | bytes 786440 | tf_op jit(solution)/shard_map/ppermute | solution.py:47
  21.0 8.2 %collective-permute-start.3 = (bf16[128,1024]{1,0:T(8,128)(2,1)S(1)}, bf16[128,1024]{1,0:T(8,128)(2,1)S(1)}, u32[]{:S(2)}, u32[]{:S(2)}) collective-permute-start(bf16[128,1024]{1,0:T(8,128)(2,1)S(1)} %collective-permute-done.1.refs_0_), channel_id=1, source_target_pairs={{0,4},{1,5},{2,6},{3,7},{4,0},{5,1},{6,2},{7,3},{8,12},{9,13},{10,... | collective-permute-start | bytes 786440 | tf_op jit(solution)/shard_map/ppermute | solution.py:47
  21.4 5.7 %collective-permute-start.4 = (f32[1,512]{1,0:T(1,128)S(1)}, f32[1,512]{1,0:T(1,128)S(1)}, u32[]{:S(2)}, u32[]{:S(2)}) collective-permute-start(f32[1,512]{1,0:T(1,128)S(1)} %bitcast.9), channel_id=1, source_target_pairs={{0,2},{1,3},{2,0},{3,1},{4,6},{5,7},{6,4},{7,5},{8,10},{9,11},{10,... | collective-permute-start | bytes 6152 | tf_op jit(solution)/shard_map/ppermute | solution.py:47
  33.2 13.9 %collective-permute-start.14 = (bf16[512,1024]{1,0:T(8,128)(2,1)S(1)}, bf16[512,1024]{1,0:T(8,128)(2,1)S(1)}, u32[]{:S(2)}, u32[]{:S(2)}) collective-permute-start(bf16[512,1024]{1,0:T(8,128)(2,1)S(1)} %copy-done.1), channel_id=1, source_target_pairs={{0,1},{1,0},{2,3},{3,2},{4,5},{5,4},{6,7},{7,6},{8,9},{9,8},{10,11... | collective-permute-start | bytes 3145736 | tf_op jit(solution)/shard_map/ppermute | solution.py:47
  34.1 13.0 %collective-permute-start.15 = (bf16[512,1024]{1,0:T(8,128)(2,1)S(1)}, bf16[512,1024]{1,0:T(8,128)(2,1)S(1)}, u32[]{:S(2)}, u32[]{:S(2)}) collective-permute-start(bf16[512,1024]{1,0:T(8,128)(2,1)S(1)} %collective-permute-done.8.refs_2_.refs_1_), channel_id=1, source_target_pairs={{0,1},{1,0},{2,3},{3,2},{4,5},{5,4},{6,7},{7,6},{8,9},{9,8},{10,11... | collective-permute-start | bytes 3145736 | tf_op jit(solution)/shard_map/ppermute | solution.py:47
  34.5 5.5 %collective-permute-start.10 = (f32[3,1024]{1,0:T(4,128)S(1)}, f32[3,1024]{1,0:T(4,128)S(1)}, u32[]{:S(2)}, u32[]{:S(2)}) collective-permute-start(f32[3,1024]{1,0:T(4,128)S(1)} %merge.1.refs_0_), channel_id=1, source_target_pairs={{0,12},{1,13},{2,14},{3,15},{4,8},{5,9},{6,10},{7,11},{8,4},{9,5},... | collective-permute-start | bytes 36872 | tf_op jit(solution)/shard_map/ppermute | solution.py:47
  37.0 4.6 %collective-permute-start.11 = (f32[3,1024]{1,0:T(4,128)S(1)}, f32[3,1024]{1,0:T(4,128)S(1)}, u32[]{:S(2)}, u32[]{:S(2)}) collective-permute-start(f32[3,1024]{1,0:T(4,128)S(1)} %merge.1.refs_0_), channel_id=1, source_target_pairs={{0,8},{1,9},{2,10},{3,11},{4,12},{5,13},{6,14},{7,15},{8,0},{9,1},... | collective-permute-start | bytes 36872 | tf_op jit(solution)/shard_map/ppermute | solution.py:47
  37.0 4.6 %collective-permute-start.12 = (f32[3,1024]{1,0:T(4,128)S(1)}, f32[3,1024]{1,0:T(4,128)S(1)}, u32[]{:S(2)}, u32[]{:S(2)}) collective-permute-start(f32[3,1024]{1,0:T(4,128)S(1)} %merge.1.refs_0_), channel_id=1, source_target_pairs={{0,4},{1,5},{2,6},{3,7},{4,0},{5,1},{6,2},{7,3},{8,12},{9,13},{10,... | collective-permute-start | bytes 36872 | tf_op jit(solution)/shard_map/ppermute | solution.py:47
  43.4 3.7 %collective-permute-start.13 = (f32[2,1024]{1,0:T(2,128)S(1)}, f32[2,1024]{1,0:T(2,128)S(1)}, u32[]{:S(2)}, u32[]{:S(2)}) collective-permute-start(f32[2,1024]{1,0:T(2,128)S(1)} %get-tuple-element.110.own_ref), channel_id=1, source_target_pairs={{0,2},{1,3},{2,0},{3,1},{4,6},{5,7},{6,4},{7,5},{8,10},{9,11},{10,... | collective-permute-start | bytes 24584 | tf_op jit(solution)/shard_map/ppermute | solution.py:47
  49.0 5.5 %collective-permute-start.17 = (f32[1,1024]{1,0:T(1,128)S(1)}, f32[1,1024]{1,0:T(1,128)S(1)}, u32[]{:S(2)}, u32[]{:S(2)}) collective-permute-start(f32[1,1024]{1,0:T(1,128)S(1)} %maximum_add_fusion.refs_0_), channel_id=1, source_target_pairs={{0,12},{1,13},{2,14},{3,15},{4,8},{5,9},{6,10},{7,11},{8,4},{9,5},... | collective-permute-start | bytes 12296 | tf_op jit(solution)/shard_map/ppermute | solution.py:47
  50.7 4.5 %collective-permute-start.18 = (f32[1,1024]{1,0:T(1,128)S(1)}, f32[1,1024]{1,0:T(1,128)S(1)}, u32[]{:S(2)}, u32[]{:S(2)}) collective-permute-start(f32[1,1024]{1,0:T(1,128)S(1)} %maximum_add_fusion.refs_0_), channel_id=1, source_target_pairs={{0,8},{1,9},{2,10},{3,11},{4,12},{5,13},{6,14},{7,15},{8,0},{9,1},... | collective-permute-start | bytes 12296 | tf_op jit(solution)/shard_map/ppermute | solution.py:47
  61.4 5.5 %collective-permute-start.22 = (f32[1,1024]{1,0:T(1,128)S(1)}, f32[1,1024]{1,0:T(1,128)S(1)}, u32[]{:S(2)}, u32[]{:S(2)}) collective-permute-start(f32[1,1024]{1,0:T(1,128)S(1)} %maximum_add_fusion.1.refs_0_), channel_id=1, source_target_pairs={{0,12},{1,13},{2,14},{3,15},{4,8},{5,9},{6,10},{7,11},{8,4},{9,5},... | collective-permute-start | bytes 12296 | tf_op jit(solution)/shard_map/ppermute | solution.py:47
  63.9 4.5 %collective-permute-start.23 = (f32[1,1024]{1,0:T(1,128)S(1)}, f32[1,1024]{1,0:T(1,128)S(1)}, u32[]{:S(2)}, u32[]{:S(2)}) collective-permute-start(f32[1,1024]{1,0:T(1,128)S(1)} %maximum_add_fusion.1.refs_0_), channel_id=1, source_target_pairs={{0,8},{1,9},{2,10},{3,11},{4,12},{5,13},{6,14},{7,15},{8,0},{9,1},... | collective-permute-start | bytes 12296 | tf_op jit(solution)/shard_map/ppermute | solution.py:47
  64.8 3.6 %collective-permute-start.24 = (f32[1,1024]{1,0:T(1,128)S(1)}, f32[1,1024]{1,0:T(1,128)S(1)}, u32[]{:S(2)}, u32[]{:S(2)}) collective-permute-start(f32[1,1024]{1,0:T(1,128)S(1)} %maximum_add_fusion.1.refs_0_), channel_id=1, source_target_pairs={{0,4},{1,5},{2,6},{3,7},{4,0},{5,1},{6,2},{7,3},{8,12},{9,13},{10,... | collective-permute-start | bytes 12296 | tf_op jit(solution)/shard_map/ppermute | solution.py:47
  68.8 3.7 %collective-permute-start.25 = (f32[2,1024]{1,0:T(2,128)S(1)}, f32[2,1024]{1,0:T(2,128)S(1)}, u32[]{:S(2)}, u32[]{:S(2)}) collective-permute-start(f32[2,1024]{1,0:T(2,128)S(1)} %get-tuple-element.120.refs_3_.own_ref), channel_id=1, source_target_pairs={{0,2},{1,3},{2,0},{3,1},{4,6},{5,7},{6,4},{7,5},{8,10},{9,11},{10,... | collective-permute-start | bytes 24584 | tf_op jit(solution)/shard_map/ppermute | solution.py:47
  73.9 6.5 %collective-permute-start.26 = (bf16[1024,256]{1,0:T(8,128)(2,1)S(1)}, bf16[1024,256]{1,0:T(8,128)(2,1)S(1)}, u32[]{:S(2)}, u32[]{:S(2)}) collective-permute-start(bf16[1024,256]{1,0:T(8,128)(2,1)S(1)} %get-tuple-element.124.refs_1_), channel_id=1, source_target_pairs={{0,1},{1,0},{2,3},{3,2},{4,5},{5,4},{6,7},{7,6},{8,9},{9,8},{10,11... | collective-permute-start | bytes 1572872 | tf_op jit(solution)/shard_map/ppermute | solution.py:47
  75.4 20.8 %collective-permute-start.29 = (bf16[392,1024]{1,0:T(8,128)(2,1)S(1)}, bf16[392,1024]{1,0:T(8,128)(2,1)S(1)}, u32[]{:S(2)}, u32[]{:S(2)}) collective-permute-start(bf16[392,1024]{1,0:T(8,128)(2,1)S(1)} %col_send.2), channel_id=1, source_target_pairs={{0,2},{1,3},{2,0},{3,1},{4,6},{5,7},{6,4},{7,5},{8,10},{9,11},{10,... | collective-permute-start | bytes 2408456 | tf_op jit(solution)/shard_map/ppermute | solution.py:47
  77.5 9.6 %collective-permute-start.31 = (bf16[136,1024]{1,0:T(8,128)(2,1)S(1)}, bf16[136,1024]{1,0:T(8,128)(2,1)S(1)}, u32[]{:S(2)}, u32[]{:S(2)}) collective-permute-start(bf16[136,1024]{1,0:T(8,128)(2,1)S(1)} %get-tuple-element.133), channel_id=1, source_target_pairs={{0,4},{1,5},{2,6},{3,7},{4,0},{5,1},{6,2},{7,3},{8,12},{9,13},{10,... | collective-permute-start | bytes 835592 | tf_op jit(solution)/shard_map/ppermute | solution.py:47
  78.9 22.4 %collective-permute-start.28 = (bf16[136,1024]{1,0:T(8,128)(2,1)S(1)}, bf16[136,1024]{1,0:T(8,128)(2,1)S(1)}, u32[]{:S(2)}, u32[]{:S(2)}) collective-permute-start(bf16[136,1024]{1,0:T(8,128)(2,1)S(1)} %col_send.3), channel_id=1, source_target_pairs={{0,2},{1,3},{2,0},{3,1},{4,6},{5,7},{6,4},{7,5},{8,10},{9,11},{10,... | collective-permute-start | bytes 835592 | tf_op jit(solution)/shard_map/ppermute | solution.py:47
  81.6 15.9 %collective-permute-start.30 = (bf16[136,1024]{1,0:T(8,128)(2,1)S(1)}, bf16[136,1024]{1,0:T(8,128)(2,1)S(1)}, u32[]{:S(2)}, u32[]{:S(2)}) collective-permute-start(bf16[136,1024]{1,0:T(8,128)(2,1)S(1)} %get-tuple-element.137), channel_id=1, source_target_pairs={{0,4},{1,5},{2,6},{3,7},{4,0},{5,1},{6,2},{7,3},{8,12},{9,13},{10,... | collective-permute-start | bytes 835592 | tf_op jit(solution)/shard_map/ppermute | solution.py:47
  87.2 14.1 %collective-permute-start.32 = (bf16[136,1024]{1,0:T(8,128)(2,1)S(1)}, bf16[136,1024]{1,0:T(8,128)(2,1)S(1)}, u32[]{:S(2)}, u32[]{:S(2)}) collective-permute-start(bf16[136,1024]{1,0:T(8,128)(2,1)S(1)} %line.1), channel_id=1, source_target_pairs={{0,8},{1,9},{2,10},{3,11},{4,12},{5,13},{6,14},{7,15},{8,0},{9,1},... | collective-permute-start | bytes 835592 | tf_op jit(solution)/shard_map/ppermute | solution.py:47
  (15 other events, 32.7 us)

commit v6 on v5

--- a/solution.py
+++ b/solution.py
@@ -34,7 +34,7 @@
 
 
 def tiles(count):
-    step = min(count, 256)
+    step = min(count, 128)
     return [slice(i, i + step) for i in range(0, count, step)]
 
 
@@ -78,9 +78,9 @@
     return value
 
 
-def prep_kernel(count, me_ref, logit_ref, rel_ref, total_ref):
+def prep_kernel(count, me_ref, logit_ref, rel_ref):
     logit = logit_ref[...]
-    total_ref[...] = jnp.log(jnp.sum(jnp.exp(logit), axis=1, keepdims=True))
+    logit = logit - jnp.log(jnp.sum(jnp.exp(logit), axis=1, keepdims=True))
     value = by_index(logit, me_ref[0, 0], count)
     rows = logit.shape[1] // count
     lines = count // 4
@@ -139,34 +139,39 @@
     return jnp.concatenate(parts, axis=1)
 
 
-def cost_kernel(scale, copy, add_mass, cols, line, *refs):
-    x_refs, y_ref, logit_ref, pack_ref = refs[:2], refs[2], refs[3], refs[4]
-    outs = refs[-5:] if copy else refs[-3:]
-    s_outs, pack_out = outs[:2], outs[-1]
+def cost_kernel(scale, copy, fresh, add_mass, cols, line, *refs):
+    count = len(cols)
+    x_refs, y_refs, side_refs = refs[:2], refs[2 : 2 + count], refs[2 + count : 2 + 2 * count]
+    pack_ref = refs[2 + 2 * count]
+    outs = refs[-(3 + 2 * copy + fresh) :]
+    s_outs, pack_out = outs[:2], outs[2 + 2 * copy]
     half = s_outs[0].shape[1]
-    y = y_ref[...]
-    wide = y.astype(F32)
-    logit = logit_ref[...]
-    lift = to_column(logit) - scale * jnp.sum(wide * wide, axis=1, keepdims=True)
     pack_out[...] = pack_ref[...]
-    if add_mass:
-        pack_out[2:3, :] = pack_ref[2:3, :] + jnp.sum(jnp.exp(logit), axis=1, keepdims=True)
+    lifts = [side[...] for side in side_refs]
+    if fresh:
+        logit = lifts[0]
+        wide = y_refs[0][...].astype(F32)
+        lifts = [to_column(logit) - scale * jnp.sum(wide * wide, axis=1, keepdims=True)]
+        outs[-1][...] = lifts[0]
+        if add_mass:
+            mass = jnp.sum(jnp.exp(logit), axis=1, keepdims=True)
+            pack_out[2:3, :] = pack_ref[2:3, :] + mass
     for c in range(2):
         x = x_refs[c][...] if copy else x_refs[c][line, :]
         if copy:
             outs[2 + c][line, :] = x
-        s = (2.0 * scale) * lax.dot_general(
-            y, x, (((1,), (1,)), ((), ())), preferred_element_type=F32
-        )
-        s_outs[c][cols, line] = s
-        s = s + lift
         lanes = slice(c * half + line.start, c * half + line.stop)
-        old = pack_ref[0:1, lanes]
-        top = jnp.maximum(old, jnp.max(s, axis=0, keepdims=True))
+        top, total = pack_ref[0:1, lanes], pack_ref[1:2, lanes]
+        for y_ref, lift, here in zip(y_refs, lifts, cols):
+            s = (2.0 * scale) * lax.dot_general(
+                y_ref[...], x, (((1,), (1,)), ((), ())), preferred_element_type=F32
+            )
+            s_outs[c][here, line] = s
+            s = s + lift
+            old, top = top, jnp.maximum(top, jnp.max(s, axis=0, keepdims=True))
+            total = total * jnp.exp(old - top) + jnp.sum(jnp.exp(s - top), axis=0, keepdims=True)
         pack_out[0:1, lanes] = top
-        pack_out[1:2, lanes] = pack_ref[1:2, lanes] * jnp.exp(old - top) + jnp.sum(
-            jnp.exp(s - top), axis=0, keepdims=True
-        )
+        pack_out[1:2, lanes] = total
 
 
 def merge(packs, masks, blocks):
@@ -186,9 +191,9 @@
 def first_kernel(masks, blocks, *refs):
     pack_refs, refs = refs[: len(masks)], refs[len(masks) :]
     s_refs, refs = refs[:2], refs[2:]
-    logit_ref, total_ref, e_ref, col_ref, q_ref, h_ref = refs
+    log_ref, e_ref, col_ref, q_ref, h_ref = refs
     top, total, mass = merge([r[...] for r in pack_refs], masks, blocks)
-    h = logit_ref[...] - total_ref[...] + jnp.log(mass)
+    h = log_ref[...] + jnp.log(mass)
     h_ref[0:1, :] = h
     h_ref[1:2, :] = mass
     q = h - top - jnp.log(total)
@@ -235,15 +240,16 @@
 
 def column_kernel(masks, blocks, *refs):
     sum_refs, refs = refs[: len(masks)], refs[len(masks) :]
-    e_ref, h_ref, phi_ref, *base_ref, col_ref, a_ref = refs
+    (e_ref, h_ref, phi_ref), rest = refs[:3], refs[3:]
+    col_ref = rest[-2] if len(rest) > 1 else rest[0]
     total = sum(flip(r[...], m, blocks) for r, m in zip(sum_refs, masks))
     a = jnp.exp(h_ref[0:1, :]) / total
-    a_ref[...] = a
     for t in tiles(e_ref.shape[0]):
         total = jnp.sum(e_ref[t, :] * a, axis=1, keepdims=True)
         col_ref[0:1, t] = to_row(total) * phi_ref[:, t]
-    if base_ref:
-        col_ref[1:2, :] = base_ref[0][...] + jnp.log(a)
+    if len(rest) > 1:
+        rest[-1][...] = a
+        col_ref[1:2, :] = rest[0][...] + jnp.log(a)
 
 
 def plan_kernel(source_count, *refs):
@@ -391,76 +397,80 @@
     logits_there = swap(logits_here, 2)
     logits = jnp.concatenate([logits_here, logits_there], axis=1)
     here = me.astype(jnp.int32).reshape(1, 1)
-    source_rel, source_total = call(
+    (source_log,) = call(
         functools.partial(prep_kernel, count),
         "prep",
         [here, source_logits.reshape(1, source_count)],
-        [shape((1, mine)), shape((1, 1))],
+        [shape((1, mine))],
         scalar=True,
     )
-    logits_here, source_rel, source_total = lax.optimization_barrier(
-        (logits_here, source_rel, source_total)
-    )
+    logits_here, source_log = lax.optimization_barrier((logits_here, source_log))
     pack = jnp.concatenate([jnp.full((1, mine), LOW, F32), jnp.zeros((2, mine), F32)])
 
     s_shape, x_shape = shape((2 * cols, half)), shape((half, width), BF16)
-    store = None
-
-    def cost_piece(y, logit, start, line, xs, store, pack, first=True):
+    here_cols, there_cols = slice(0, cols), slice(cols, 2 * cols)
+    lift_shape = shape((cols, 1))
+
+    def cost(xs, ys, sides, where, line, store, pack, copy=False, fresh=False):
+        ins = [*xs, *ys, *sides, pack]
         return call(
-            functools.partial(cost_kernel, scale, False, first, slice(start, start + cols), line),
+            functools.partial(cost_kernel, scale, copy, fresh, fresh, where, line),
             "cost",
-            [*xs, y, logit, pack, *store],
-            [s_shape, s_shape, shape(pack.shape)],
-            input_output_aliases={5 + i: i for i in range(len(store))},
+            ins + store,
+            [s_shape] * 2 + [x_shape] * 2 * copy + [shape(pack.shape)] + [lift_shape] * fresh,
+            input_output_aliases={len(ins) + i: i for i in range(len(store))},
         )
 
     if direct:
-        for k in range(lines):
-            x = line[k]
+        store = []
+        for k in (0, 2, 1, 3):
+            x, ours, sides, where = line[k], [target_feats], [], [here_cols]
+            if k == 0:
+                sides = [logits_here]
             if k == 3:
                 x, *_ = lax.optimization_barrier((x, logits_there, pack))
-                s0, s1, pack = cost_piece(
-                    crossed[0], logits_there, cols, slice(0, k * rows), store[2:], store[:2], pack
+                s0, s1, pack, lift_there = cost(
+                    store[2:],
+                    crossed,
+                    [logits_there],
+                    [there_cols],
+                    slice(0, k * rows),
+                    store[:2],
+                    pack,
+                    fresh=True,
                 )
                 store = [s0, s1, *store[2:]]
-            pair = [x, swap(x, 1)]
-            ins = [*pair, target_feats, logits_here, pack]
-            *store, pack = call(
-                functools.partial(
-                    cost_kernel,
-                    scale,
-                    True,
-                    k == 0,
-                    slice(0, cols),
-                    slice(k * rows, (k + 1) * rows),
-                ),
-                "cost",
-                ins + (store or []),
-                [s_shape, s_shape, x_shape, x_shape, shape(pack.shape)],
-                input_output_aliases={5 + i: i for i in range(4)} if store else {},
+                ours, where = [target_feats, *crossed], [here_cols, there_cols]
+                sides = [lift, lift_there]
+            *store, pack = cost(
+                [x, swap(x, 1)],
+                ours,
+                sides or [lift],
+                where,
+                slice(k * rows, (k + 1) * rows),
+                store,
+                pack,
+                copy=True,
+                fresh=k == 0,
             )
             if k == 0:
-                *line[1:], y, _ = lax.optimization_barrier((*line[1:], target_feats, pack))
+                *store, pack, lift = [*store, pack]
+                line[2], y, _ = lax.optimization_barrier((line[2], target_feats, pack))
                 line.append(swap(line[2], 4))
                 ys = [target_feats, swap(y, 1)]
         s0, s1, x0, x1 = store
-        s0, s1, pack = cost_piece(
-            crossed[0],
-            logits_there,
-            cols,
-            slice(3 * rows, half),
-            [x0, x1],
-            [s0, s1],
-            pack,
-            first=False,
-        )
     else:
         gathered = lax.all_gather(source_feats, AXIS, axis=0)[order].reshape(2, half, width)
         x0, x1 = gathered[0], gathered[1]
-        full = slice(0, half)
-        s0, s1, pack = cost_piece(target_feats, logits_here, 0, full, [x0, x1], [], pack)
-        s0, s1, pack = cost_piece(crossed[0], logits_there, cols, full, [x0, x1], [s0, s1], pack)
+        store = []
+        for y, logit, where in (
+            (target_feats, logits_here, here_cols),
+            (crossed[0], logits_there, there_cols),
+        ):
+            *store, pack, _ = cost(
+                [x0, x1], [y], [logit], [where], slice(0, half), store, pack, fresh=True
+            )
+        s0, s1 = store
 
     *levels, last = row_levels(count)
     last_masks = (0, *last)
@@ -480,7 +490,7 @@
     e, col, q, h = call(
         functools.partial(first_kernel, last_masks, blocks),
         "first",
-        [*packs, s0, s1, source_rel, source_total],
+        [*packs, s0, s1, source_log],
         [e_shape, shape((2, 2 * cols)), flat_shape, shape((2, mine))],
     )
     col_other = swap(col, 2)
@@ -503,11 +513,11 @@
             functools.partial(column_kernel, last_masks, blocks),
             "column",
             [*sums, e, h, phi, *base],
-            [shape((1 + len(base), 2 * cols)), flat_shape],
+            [shape((1 + len(base), 2 * cols))] + [flat_shape] * len(base),
         )
 
     for _ in range(ITERS - 2):
-        col, a = columns(row)
+        (col,) = columns(row)
         (row,) = call(
             row_kernel,
             "row",
@@ -518,7 +528,7 @@
     source_sq = scale * jnp.concatenate(
         [jnp.sum(jnp.square(x.astype(F32)), axis=1) for x in (x0, x1)]
     )
-    base = q - source_rel + source_total + source_sq.reshape(1, mine)
+    base = q - source_log + source_sq.reshape(1, mine)
     col, a = columns(row, base)
     col_other = swap(col, 2)
     keep, *sends, mass, logb = call(

time: 103 us -> 101 us (0.981)
  Pallas kernels: 20.8 us -> 18.7 us
  starting transfers between devices: 32.4 us -> 33.8 us
    pallas_call x23 -> x22, Pallas kernels: 20.8 us -> 18.7 us  [call(): pl.pallas_call(body, name=name, out_shape=outs, in_specs=specs, out_specs...]
    ppermute x33, starting transfers between devices: 32.4 us -> 33.8 us  [swap(): return lax.ppermute(value, AXIS, [(i, i ^ mask) for i in range(count)])]
  transfers between devices with their start and end apart: 33 -> 33, of which waited for: 21 -> 19; matrix products, arithmetic and copies ran while one was open for 1% -> 0% of each run, Pallas kernels for 14% -> 13%
where the time goes in v6:
time: 101 us
  waiting for transfers between devices  42.4 us (42%)
  starting transfers between devices  33.8 us (33%)
  Pallas kernels  18.7 us (19%)
  local copies, waits for them, and re-layouts  4.27 us (4%)
    ppermute x33, waiting for transfers between devices, swap(): return lax.ppermute(value, AXIS, [(i, i ^ mask) for i in range(count)])  42.4 us
    ppermute x33, starting transfers between devices, swap(): return lax.ppermute(value, AXIS, [(i, i ^ mask) for i in range(count)])  33.8 us
    pallas_call x22, Pallas kernels, call(): pl.pallas_call(body, name=name, out_shape=outs, in_specs=specs, out_specs...  18.7 us
    unnamed x12, local copies, waits for them, and re-layouts  4.27 us
  transfers between devices with their start and end apart: 33, of which 19 were waited for; matrix products, arithmetic and copies ran while one was open for 0% of the time, Pallas kernels for 13%

profile of v6, /device:TPU:0, one launch (start us, length us, event | category | flops | bytes accessed | tf_op | source)
XLA Modules:
  0.0 100.6 jit_solution(5840806405023683931)
XLA Ops:
  0.6 3.0 %collective-permute-start.8 = (bf16[512,1024]{1,0:T(8,128)(2,1)}, bf16[512,1024]{1,0:T(8,128)(2,1)S(1)}, u32[]{:S(2)}, u32[]{:S(2)}) collective-permute-start(bf16[512,1024]{1,0:T(8,128)(2,1)} %refs_3_.3), channel_id=1, source_target_pairs={{0,2},{1,3},{2,0},{3,1},{4,6},{5,7},{6,4},{7,5},{8,10},{9,11},{10,... | collective-permute-start | bytes 3145736 | tf_op jit(solution)/shard_map/ppermute | solution.py:47
  3.7 2.6 %collective-permute-start = (bf16[128,1024]{1,0:T(8,128)(2,1)}, bf16[128,1024]{1,0:T(8,128)(2,1)S(1)}, u32[]{:S(2)}, u32[]{:S(2)}) collective-permute-start(bf16[128,1024]{1,0:T(8,128)(2,1)} %refs_0_.1), channel_id=1, source_target_pairs={{0,8},{1,9},{2,10},{3,11},{4,12},{5,13},{6,14},{7,15},{8,0},{9,1},... | collective-permute-start | bytes 786440 | tf_op jit(solution)/shard_map/ppermute | solution.py:47
  6.3 1.6 %collective-permute-start.4 = (bf16[128,1024]{1,0:T(8,128)(2,1)}, bf16[128,1024]{1,0:T(8,128)(2,1)S(1)}, u32[]{:S(2)}, u32[]{:S(2)}) collective-permute-start(bf16[128,1024]{1,0:T(8,128)(2,1)} %refs_0_.1), channel_id=1, source_target_pairs={{0,4},{1,5},{2,6},{3,7},{4,0},{5,1},{6,2},{7,3},{8,12},{9,13},{10,... | collective-permute-start | bytes 786440 | tf_op jit(solution)/shard_map/ppermute | solution.py:47
  13.2 6.1 %collective-permute-done.refs_0_ = bf16[128,1024]{1,0:T(8,128)(2,1)S(1)} collective-permute-done((bf16[128,1024]{1,0:T(8,128)(2,1)}, bf16[128,1024]{1,0:T(8,128)(2,1)S(1)}, u32[]{:S(2)}, u32[]{:S(2)}) %collective-permute-start) | collective-permute-done | bytes 262176 | tf_op jit(solution)/shard_map/ppermute | solution.py:47
  23.0 4.0 %collective-permute-done.3.refs_3_ = f32[1,512]{1,0:T(1,128)S(1)} collective-permute-done((f32[1,512]{1,0:T(1,128)S(1)}, f32[1,512]{1,0:T(1,128)S(1)}, u32[]{:S(2)}, u32[]{:S(2)}) %collective-permute-start.3) | collective-permute-done | bytes 2080 | tf_op jit(solution)/shard_map/ppermute | solution.py:47
  28.1 1.7 %cost.8 = (f32[1024,512]{1,0:T(8,128)S(1)}, f32[1024,512]{1,0:T(8,128)S(1)}, f32[3,1024]{1,0:T(4,128)S(1)}, f32[512,1]{1,0:T(8,128)S(1)}) custom-call(bf16[512,1024]{1,0:T(8,128)(2,1)S(1)} %get-tuple-element.84.refs_0_.refs_9_, bf16[512,1024]{1,0:T(8,128)(2,1)S(1)} %get-tuple-element.85.refs_1_.refs_10_, ...), custom_call_target="tpu_custom_call", output_to_operand_aliasing={{0}: (5, {}), {1}: (6, {})} | custom-call | flops 1 | bytes 1 | tf_op jit(solution)/shard_map/cost/pallas_call | solution.py:24
  29.8 1.4 %cost.9 = (f32[1024,512]{1,0:T(8,128)S(1)}, f32[1024,512]{1,0:T(8,128)S(1)}, bf16[512,1024]{1,0:T(8,128)(2,1)S(1)}, bf16[512,1024]{1,0:T(8,128)(2,1)S(1)}, f32[3,1024]{1,0:T(4,128)S(1)}) custom-call(bf16[128,1024]{1,0:T(8,128)(2,1)S(1)} %collective-permute-done.2.refs_0_, ...), custom_call_target="tpu_custom_call", output_to_operand_aliasing={{0}: (7, {}), {1}: (8, {}), {2}: (9, {}), {3}: (10, {})} | custom-call | flops 1 | bytes 1 | tf_op jit(solution)/shard_map/cost/pallas_call | solution.py:24
  33.1 3.3 %collective-permute-start.10 = (f32[3,1024]{1,0:T(4,128)S(1)}, f32[3,1024]{1,0:T(4,128)S(1)}, u32[]{:S(2)}, u32[]{:S(2)}) collective-permute-start(f32[3,1024]{1,0:T(4,128)S(1)} %merge.1.refs_0_), channel_id=1, source_target_pairs={{0,12},{1,13},{2,14},{3,15},{4,8},{5,9},{6,10},{7,11},{8,4},{9,5},... | collective-permute-start | bytes 36872 | tf_op jit(solution)/shard_map/ppermute | solution.py:47
  38.7 2.3 %collective-permute-done.11.refs_2_ = f32[3,1024]{1,0:T(4,128)S(1)} collective-permute-done((f32[3,1024]{1,0:T(4,128)S(1)}, f32[3,1024]{1,0:T(4,128)S(1)}, u32[]{:S(2)}, u32[]{:S(2)}) %collective-permute-start.11) | collective-permute-done | bytes 12320 | tf_op jit(solution)/shard_map/ppermute | solution.py:47
  41.0 1.3 %first.1 = (f32[1024,1024]{1,0:T(8,128)S(1)}, f32[2,1024]{1,0:T(2,128)S(1)}, f32[1,1024]{1,0:T(1,128)S(1)}, f32[2,1024]{1,0:T(2,128)S(1)}) custom-call(f32[3,1024]{1,0:T(4,128)S(1)} %merge.1.refs_0_, f32[3,1024]{1,0:T(4,128)S(1)} %collective-permute-done.10.refs_1_, f32[3,1024]{1,0:T(4,128)S(1)} %collective-permute-done.11.refs_2_, ...), custom_call_target="tpu_custom_call" | custom-call | flops 1 | bytes 1 | tf_op jit(solution)/shard_map/first/pallas_call | solution.py:24
  43.5 2.6 %collective-permute-done.13.other_ref = f32[2,1024]{1,0:T(2,128)S(1)} collective-permute-done((f32[2,1024]{1,0:T(2,128)S(1)}, f32[2,1024]{1,0:T(2,128)S(1)}, u32[]{:S(2)}, u32[]{:S(2)}) %collective-permute-start.13) | collective-permute-done | bytes 8224 | tf_op jit(solution)/shard_map/ppermute | solution.py:47
  47.8 1.5 %collective-permute-start.17 = (f32[1,1024]{1,0:T(1,128)S(1)}, f32[1,1024]{1,0:T(1,128)S(1)}, u32[]{:S(2)}, u32[]{:S(2)}) collective-permute-start(f32[1,1024]{1,0:T(1,128)S(1)} %maximum_add_fusion.refs_0_), channel_id=1, source_target_pairs={{0,12},{1,13},{2,14},{3,15},{4,8},{5,9},{6,10},{7,11},{8,4},{9,5},... | collective-permute-start | bytes 12296 | tf_op jit(solution)/shard_map/ppermute | solution.py:47
  50.0 2.3 %collective-permute-start.19 = (f32[1,1024]{1,0:T(1,128)S(1)}, f32[1,1024]{1,0:T(1,128)S(1)}, u32[]{:S(2)}, u32[]{:S(2)}) collective-permute-start(f32[1,1024]{1,0:T(1,128)S(1)} %maximum_add_fusion.refs_0_), channel_id=1, source_target_pairs={{0,4},{1,5},{2,6},{3,7},{4,0},{5,1},{6,2},{7,3},{8,12},{9,13},{10,... | collective-permute-start | bytes 12296 | tf_op jit(solution)/shard_map/ppermute | solution.py:47
  55.4 2.6 %collective-permute-done.20.other_ref = f32[1,1024]{1,0:T(1,128)S(1)} collective-permute-done((f32[1,1024]{1,0:T(1,128)S(1)}, f32[1,1024]{1,0:T(1,128)S(1)}, u32[]{:S(2)}, u32[]{:S(2)}) %collective-permute-start.20) | collective-permute-done | bytes 4128 | tf_op jit(solution)/shard_map/ppermute | solution.py:47
  59.6 2.6 %collective-permute-start.22 = (f32[1,1024]{1,0:T(1,128)S(1)}, f32[1,1024]{1,0:T(1,128)S(1)}, u32[]{:S(2)}, u32[]{:S(2)}) collective-permute-start(f32[1,1024]{1,0:T(1,128)S(1)} %maximum_add_fusion.1.refs_0_), channel_id=1, source_target_pairs={{0,12},{1,13},{2,14},{3,15},{4,8},{5,9},{6,10},{7,11},{8,4},{9,5},... | collective-permute-start | bytes 12296 | tf_op jit(solution)/shard_map/ppermute | solution.py:47
  65.1 1.6 %collective-permute-done.23.refs_2_ = f32[1,1024]{1,0:T(1,128)S(1)} collective-permute-done((f32[1,1024]{1,0:T(1,128)S(1)}, f32[1,1024]{1,0:T(1,128)S(1)}, u32[]{:S(2)}, u32[]{:S(2)}) %collective-permute-start.23) | collective-permute-done | bytes 4128 | tf_op jit(solution)/shard_map/ppermute | solution.py:47
  68.3 2.6 %collective-permute-done.25.refs_4_.other_ref = f32[2,1024]{1,0:T(2,128)S(1)} collective-permute-done((f32[2,1024]{1,0:T(2,128)S(1)}, f32[2,1024]{1,0:T(2,128)S(1)}, u32[]{:S(2)}, u32[]{:S(2)}) %collective-permute-start.25) | collective-permute-done | bytes 8224 | tf_op jit(solution)/shard_map/ppermute | solution.py:47
  74.5 1.5 %row_part.2 = (f32[136,1024]{1,0:T(8,128)S(1)}, bf16[136,1024]{1,0:T(8,128)(2,1)S(1)}) custom-call(bf16[1024,512]{1,0:T(8,128)(2,1)S(1)} %get-tuple-element.128.refs_0_.keep_ref, bf16[1024,256]{1,0:T(8,128)(2,1)S(1)} %collective-permute-done.27.other_ref, bf16[512,1024]{1,0:T(8,128)(2,1)S(1)} %copy-done.1, ...), custom_call_target="tpu_custom_call" | custom-call | flops 1 | bytes 1 | tf_op jit(solution)/shard_map/row_part/pallas_call | solution.py:24
  78.5 1.3 %row_part.3 = (f32[136,1024]{1,0:T(8,128)S(1)}, bf16[136,1024]{1,0:T(8,128)(2,1)S(1)}) custom-call(bf16[1024,512]{1,0:T(8,128)(2,1)S(1)} %get-tuple-element.128.refs_0_.keep_ref, bf16[1024,256]{1,0:T(8,128)(2,1)S(1)} %collective-permute-done.26.other_ref, bf16[512,1024]{1,0:T(8,128)(2,1)S(1)} %copy-done.1, ...), custom_call_target="tpu_custom_call" | custom-call | flops 1 | bytes 1 | tf_op jit(solution)/shard_map/row_part/pallas_call | solution.py:24
  81.0 4.6 %collective-permute-done.31.other_ref = bf16[136,1024]{1,0:T(8,128)(2,1)S(1)} collective-permute-done((bf16[136,1024]{1,0:T(8,128)(2,1)S(1)}, bf16[136,1024]{1,0:T(8,128)(2,1)S(1)}, u32[]{:S(2)}, u32[]{:S(2)}) %collective-permute-start.31) | collective-permute-done | bytes 278560 | tf_op jit(solution)/shard_map/ppermute | solution.py:47
  85.7 2.0 %collective-permute-start.32 = (bf16[136,1024]{1,0:T(8,128)(2,1)S(1)}, bf16[136,1024]{1,0:T(8,128)(2,1)S(1)}, u32[]{:S(2)}, u32[]{:S(2)}) collective-permute-start(bf16[136,1024]{1,0:T(8,128)(2,1)S(1)} %line.1), channel_id=1, source_target_pairs={{0,8},{1,9},{2,10},{3,11},{4,12},{5,13},{6,14},{7,15},{8,0},{9,1},... | collective-permute-start | bytes 835592 | tf_op jit(solution)/shard_map/ppermute | solution.py:47
  89.8 4.4 %collective-permute-done.29.refs_1_ = bf16[392,1024]{1,0:T(8,128)(2,1)S(1)} collective-permute-done((bf16[392,1024]{1,0:T(8,128)(2,1)S(1)}, bf16[392,1024]{1,0:T(8,128)(2,1)S(1)}, u32[]{:S(2)}, u32[]{:S(2)}) %collective-permute-start.29) | collective-permute-done | bytes 802848 | tf_op jit(solution)/shard_map/ppermute | solution.py:47
  94.2 1.3 %target.1.refs_4_ = f32[512,1024]{1,0:T(8,128)} custom-call(f32[512,1024]{1,0:T(8,128)S(1)} %col_keep.1.refs_0_, bf16[392,1024]{1,0:T(8,128)(2,1)S(1)} %collective-permute-done.29.refs_1_, f32[1,1024]{1,0:T(1,128)S(1)} %get-tuple-element.114.refs_5_.refs_2_, bf16[512,1024]{1,0:T(8,128)(2,1)S(1)} %copy-done.1), custom_call_target="tpu_custom_call" | custom-call | flops 1 | bytes 2097152 | tf_op jit(solution)/shard_map/target/pallas_call | solution.py:24
  95.6 3.7 %collective-permute-done.28.refs_1_ = bf16[136,1024]{1,0:T(8,128)(2,1)S(1)} collective-permute-done((bf16[136,1024]{1,0:T(8,128)(2,1)S(1)}, bf16[136,1024]{1,0:T(8,128)(2,1)S(1)}, u32[]{:S(2)}, u32[]{:S(2)}) %collective-permute-start.28) | collective-permute-done | bytes 278560 | tf_op jit(solution)/shard_map/ppermute | solution.py:47
  (83 shorter events, 37.6 us)
Async XLA Ops:
  0.6 27.5 %collective-permute-start.8 = (bf16[512,1024]{1,0:T(8,128)(2,1)}, bf16[512,1024]{1,0:T(8,128)(2,1)S(1)}, u32[]{:S(2)}, u32[]{:S(2)}) collective-permute-start(bf16[512,1024]{1,0:T(8,128)(2,1)} %refs_3_.3), channel_id=1, source_target_pairs={{0,2},{1,3},{2,0},{3,1},{4,6},{5,7},{6,4},{7,5},{8,10},{9,11},{10,... | collective-permute-start | bytes 3145736 | tf_op jit(solution)/shard_map/ppermute | solution.py:47
  3.7 5.0 %collective-permute-start.1 = (bf16[128,1024]{1,0:T(8,128)(2,1)}, bf16[128,1024]{1,0:T(8,128)(2,1)S(1)}, u32[]{:S(2)}, u32[]{:S(2)}) collective-permute-start(bf16[128,1024]{1,0:T(8,128)(2,1)} %refs_0_.1), channel_id=1, source_target_pairs={{0,1},{1,0},{2,3},{3,2},{4,5},{5,4},{6,7},{7,6},{8,9},{9,8},{10,11... | collective-permute-start | bytes 786440 | tf_op jit(solution)/shard_map/ppermute | solution.py:47
  3.7 15.6 %collective-permute-start = (bf16[128,1024]{1,0:T(8,128)(2,1)}, bf16[128,1024]{1,0:T(8,128)(2,1)S(1)}, u32[]{:S(2)}, u32[]{:S(2)}) collective-permute-start(bf16[128,1024]{1,0:T(8,128)(2,1)} %refs_0_.1), channel_id=1, source_target_pairs={{0,8},{1,9},{2,10},{3,11},{4,12},{5,13},{6,14},{7,15},{8,0},{9,1},... | collective-permute-start | bytes 786440 | tf_op jit(solution)/shard_map/ppermute | solution.py:47
  6.3 13.2 %collective-permute-start.4 = (bf16[128,1024]{1,0:T(8,128)(2,1)}, bf16[128,1024]{1,0:T(8,128)(2,1)S(1)}, u32[]{:S(2)}, u32[]{:S(2)}) collective-permute-start(bf16[128,1024]{1,0:T(8,128)(2,1)} %refs_0_.1), channel_id=1, source_target_pairs={{0,4},{1,5},{2,6},{3,7},{4,0},{5,1},{6,2},{7,3},{8,12},{9,13},{10,... | collective-permute-start | bytes 786440 | tf_op jit(solution)/shard_map/ppermute | solution.py:47
  19.7 8.4 %collective-permute-start.2 = (bf16[128,1024]{1,0:T(8,128)(2,1)S(1)}, bf16[128,1024]{1,0:T(8,128)(2,1)S(1)}, u32[]{:S(2)}, u32[]{:S(2)}) collective-permute-start(bf16[128,1024]{1,0:T(8,128)(2,1)S(1)} %collective-permute-done.refs_0_), channel_id=1, source_target_pairs={{0,4},{1,5},{2,6},{3,7},{4,0},{5,1},{6,2},{7,3},{8,12},{9,13},{10,... | collective-permute-start | bytes 786440 | tf_op jit(solution)/shard_map/ppermute | solution.py:47
  20.8 6.2 %collective-permute-start.3 = (f32[1,512]{1,0:T(1,128)S(1)}, f32[1,512]{1,0:T(1,128)S(1)}, u32[]{:S(2)}, u32[]{:S(2)}) collective-permute-start(f32[1,512]{1,0:T(1,128)S(1)} %bitcast.8), channel_id=1, source_target_pairs={{0,2},{1,3},{2,0},{3,1},{4,6},{5,7},{6,4},{7,5},{8,10},{9,11},{10,... | collective-permute-start | bytes 6152 | tf_op jit(solution)/shard_map/ppermute | solution.py:47
  31.8 14.2 %collective-permute-start.14 = (bf16[512,1024]{1,0:T(8,128)(2,1)S(1)}, bf16[512,1024]{1,0:T(8,128)(2,1)S(1)}, u32[]{:S(2)}, u32[]{:S(2)}) collective-permute-start(bf16[512,1024]{1,0:T(8,128)(2,1)S(1)} %copy-done.1), channel_id=1, source_target_pairs={{0,1},{1,0},{2,3},{3,2},{4,5},{5,4},{6,7},{7,6},{8,9},{9,8},{10,11... | collective-permute-start | bytes 3145736 | tf_op jit(solution)/shard_map/ppermute | solution.py:47
  32.7 13.4 %collective-permute-start.15 = (bf16[512,1024]{1,0:T(8,128)(2,1)S(1)}, bf16[512,1024]{1,0:T(8,128)(2,1)S(1)}, u32[]{:S(2)}, u32[]{:S(2)}) collective-permute-start(bf16[512,1024]{1,0:T(8,128)(2,1)S(1)} %collective-permute-done.8.refs_2_.refs_3_.refs_1_), channel_id=1, source_target_pairs={{0,1},{1,0},{2,3},{3,2},{4,5},{5,4},{6,7},{7,6},{8,9},{9,8},{10,11... | collective-permute-start | bytes 3145736 | tf_op jit(solution)/shard_map/ppermute | solution.py:47
  33.1 5.6 %collective-permute-start.10 = (f32[3,1024]{1,0:T(4,128)S(1)}, f32[3,1024]{1,0:T(4,128)S(1)}, u32[]{:S(2)}, u32[]{:S(2)}) collective-permute-start(f32[3,1024]{1,0:T(4,128)S(1)} %merge.1.refs_0_), channel_id=1, source_target_pairs={{0,12},{1,13},{2,14},{3,15},{4,8},{5,9},{6,10},{7,11},{8,4},{9,5},... | collective-permute-start | bytes 36872 | tf_op jit(solution)/shard_map/ppermute | solution.py:47
  36.4 4.6 %collective-permute-start.11 = (f32[3,1024]{1,0:T(4,128)S(1)}, f32[3,1024]{1,0:T(4,128)S(1)}, u32[]{:S(2)}, u32[]{:S(2)}) collective-permute-start(f32[3,1024]{1,0:T(4,128)S(1)} %merge.1.refs_0_), channel_id=1, source_target_pairs={{0,8},{1,9},{2,10},{3,11},{4,12},{5,13},{6,14},{7,15},{8,0},{9,1},... | collective-permute-start | bytes 36872 | tf_op jit(solution)/shard_map/ppermute | solution.py:47
  36.4 4.6 %collective-permute-start.12 = (f32[3,1024]{1,0:T(4,128)S(1)}, f32[3,1024]{1,0:T(4,128)S(1)}, u32[]{:S(2)}, u32[]{:S(2)}) collective-permute-start(f32[3,1024]{1,0:T(4,128)S(1)} %merge.1.refs_0_), channel_id=1, source_target_pairs={{0,4},{1,5},{2,6},{3,7},{4,0},{5,1},{6,2},{7,3},{8,12},{9,13},{10,... | collective-permute-start | bytes 36872 | tf_op jit(solution)/shard_map/ppermute | solution.py:47
  42.4 3.7 %collective-permute-start.13 = (f32[2,1024]{1,0:T(2,128)S(1)}, f32[2,1024]{1,0:T(2,128)S(1)}, u32[]{:S(2)}, u32[]{:S(2)}) collective-permute-start(f32[2,1024]{1,0:T(2,128)S(1)} %get-tuple-element.97.own_ref), channel_id=1, source_target_pairs={{0,2},{1,3},{2,0},{3,1},{4,6},{5,7},{6,4},{7,5},{8,10},{9,11},{10,... | collective-permute-start | bytes 24584 | tf_op jit(solution)/shard_map/ppermute | solution.py:47
  47.8 5.5 %collective-permute-start.17 = (f32[1,1024]{1,0:T(1,128)S(1)}, f32[1,1024]{1,0:T(1,128)S(1)}, u32[]{:S(2)}, u32[]{:S(2)}) collective-permute-start(f32[1,1024]{1,0:T(1,128)S(1)} %maximum_add_fusion.refs_0_), channel_id=1, source_target_pairs={{0,12},{1,13},{2,14},{3,15},{4,8},{5,9},{6,10},{7,11},{8,4},{9,5},... | collective-permute-start | bytes 12296 | tf_op jit(solution)/shard_map/ppermute | solution.py:47
  49.3 4.5 %collective-permute-start.18 = (f32[1,1024]{1,0:T(1,128)S(1)}, f32[1,1024]{1,0:T(1,128)S(1)}, u32[]{:S(2)}, u32[]{:S(2)}) collective-permute-start(f32[1,1024]{1,0:T(1,128)S(1)} %maximum_add_fusion.refs_0_), channel_id=1, source_target_pairs={{0,8},{1,9},{2,10},{3,11},{4,12},{5,13},{6,14},{7,15},{8,0},{9,1},... | collective-permute-start | bytes 12296 | tf_op jit(solution)/shard_map/ppermute | solution.py:47
  50.0 3.9 %collective-permute-start.19 = (f32[1,1024]{1,0:T(1,128)S(1)}, f32[1,1024]{1,0:T(1,128)S(1)}, u32[]{:S(2)}, u32[]{:S(2)}) collective-permute-start(f32[1,1024]{1,0:T(1,128)S(1)} %maximum_add_fusion.refs_0_), channel_id=1, source_target_pairs={{0,4},{1,5},{2,6},{3,7},{4,0},{5,1},{6,2},{7,3},{8,12},{9,13},{10,... | collective-permute-start | bytes 12296 | tf_op jit(solution)/shard_map/ppermute | solution.py:47
  59.6 5.5 %collective-permute-start.22 = (f32[1,1024]{1,0:T(1,128)S(1)}, f32[1,1024]{1,0:T(1,128)S(1)}, u32[]{:S(2)}, u32[]{:S(2)}) collective-permute-start(f32[1,1024]{1,0:T(1,128)S(1)} %maximum_add_fusion.1.refs_0_), channel_id=1, source_target_pairs={{0,12},{1,13},{2,14},{3,15},{4,8},{5,9},{6,10},{7,11},{8,4},{9,5},... | collective-permute-start | bytes 12296 | tf_op jit(solution)/shard_map/ppermute | solution.py:47
  62.2 4.5 %collective-permute-start.23 = (f32[1,1024]{1,0:T(1,128)S(1)}, f32[1,1024]{1,0:T(1,128)S(1)}, u32[]{:S(2)}, u32[]{:S(2)}) collective-permute-start(f32[1,1024]{1,0:T(1,128)S(1)} %maximum_add_fusion.1.refs_0_), channel_id=1, source_target_pairs={{0,8},{1,9},{2,10},{3,11},{4,12},{5,13},{6,14},{7,15},{8,0},{9,1},... | collective-permute-start | bytes 12296 | tf_op jit(solution)/shard_map/ppermute | solution.py:47
  67.2 3.7 %collective-permute-start.25 = (f32[2,1024]{1,0:T(2,128)S(1)}, f32[2,1024]{1,0:T(2,128)S(1)}, u32[]{:S(2)}, u32[]{:S(2)}) collective-permute-start(f32[2,1024]{1,0:T(2,128)S(1)} %get-tuple-element.108.refs_3_.own_ref), channel_id=1, source_target_pairs={{0,2},{1,3},{2,0},{3,1},{4,6},{5,7},{6,4},{7,5},{8,10},{9,11},{10,... | collective-permute-start | bytes 24584 | tf_op jit(solution)/shard_map/ppermute | solution.py:47
  71.9 6.6 %collective-permute-start.26 = (bf16[1024,256]{1,0:T(8,128)(2,1)S(1)}, bf16[1024,256]{1,0:T(8,128)(2,1)S(1)}, u32[]{:S(2)}, u32[]{:S(2)}) collective-permute-start(bf16[1024,256]{1,0:T(8,128)(2,1)S(1)} %get-tuple-element.112.refs_1_), channel_id=1, source_target_pairs={{0,1},{1,0},{2,3},{3,2},{4,5},{5,4},{6,7},{7,6},{8,9},{9,8},{10,11... | collective-permute-start | bytes 1572872 | tf_op jit(solution)/shard_map/ppermute | solution.py:47
  73.4 20.8 %collective-permute-start.29 = (bf16[392,1024]{1,0:T(8,128)(2,1)S(1)}, bf16[392,1024]{1,0:T(8,128)(2,1)S(1)}, u32[]{:S(2)}, u32[]{:S(2)}) collective-permute-start(bf16[392,1024]{1,0:T(8,128)(2,1)S(1)} %col_send.2), channel_id=1, source_target_pairs={{0,2},{1,3},{2,0},{3,1},{4,6},{5,7},{6,4},{7,5},{8,10},{9,11},{10,... | collective-permute-start | bytes 2408456 | tf_op jit(solution)/shard_map/ppermute | solution.py:47
  76.0 9.6 %collective-permute-start.31 = (bf16[136,1024]{1,0:T(8,128)(2,1)S(1)}, bf16[136,1024]{1,0:T(8,128)(2,1)S(1)}, u32[]{:S(2)}, u32[]{:S(2)}) collective-permute-start(bf16[136,1024]{1,0:T(8,128)(2,1)S(1)} %get-tuple-element.121), channel_id=1, source_target_pairs={{0,4},{1,5},{2,6},{3,7},{4,0},{5,1},{6,2},{7,3},{8,12},{9,13},{10,... | collective-permute-start | bytes 835592 | tf_op jit(solution)/shard_map/ppermute | solution.py:47
  77.4 21.9 %collective-permute-start.28 = (bf16[136,1024]{1,0:T(8,128)(2,1)S(1)}, bf16[136,1024]{1,0:T(8,128)(2,1)S(1)}, u32[]{:S(2)}, u32[]{:S(2)}) collective-permute-start(bf16[136,1024]{1,0:T(8,128)(2,1)S(1)} %col_send.3), channel_id=1, source_target_pairs={{0,2},{1,3},{2,0},{3,1},{4,6},{5,7},{6,4},{7,5},{8,10},{9,11},{10,... | collective-permute-start | bytes 835592 | tf_op jit(solution)/shard_map/ppermute | solution.py:47
  79.8 15.8 %collective-permute-start.30 = (bf16[136,1024]{1,0:T(8,128)(2,1)S(1)}, bf16[136,1024]{1,0:T(8,128)(2,1)S(1)}, u32[]{:S(2)}, u32[]{:S(2)}) collective-permute-start(bf16[136,1024]{1,0:T(8,128)(2,1)S(1)} %get-tuple-element.125), channel_id=1, source_target_pairs={{0,4},{1,5},{2,6},{3,7},{4,0},{5,1},{6,2},{7,3},{8,12},{9,13},{10,... | collective-permute-start | bytes 835592 | tf_op jit(solution)/shard_map/ppermute | solution.py:47
  85.7 13.7 %collective-permute-start.32 = (bf16[136,1024]{1,0:T(8,128)(2,1)S(1)}, bf16[136,1024]{1,0:T(8,128)(2,1)S(1)}, u32[]{:S(2)}, u32[]{:S(2)}) collective-permute-start(bf16[136,1024]{1,0:T(8,128)(2,1)S(1)} %line.1), channel_id=1, source_target_pairs={{0,8},{1,9},{2,10},{3,11},{4,12},{5,13},{6,14},{7,15},{8,0},{9,1},... | collective-permute-start | bytes 835592 | tf_op jit(solution)/shard_map/ppermute | solution.py:47
  (15 other events, 33.9 us)

commit v7 on v6

--- a/solution.py
+++ b/solution.py
@@ -257,15 +257,17 @@
     keep_ref, near_ref, far_ref, mass_ref, logb_ref = refs[7:]
     c = own_ref[0:1, :] + turn(other_ref[0:1, :])
     logb_ref[...] = -jnp.log(c)
-    share = jnp.exp(logit_ref[...]) * phi_ref[...] * (source_count / h_ref[1:2, :1]) / c
+    mass = jnp.exp(logit_ref[...]) * (source_count / h_ref[1:2, :1])
+    mass_ref[...] = mass
+    share = mass * phi_ref[...] / c
     half = keep_ref.shape[1]
+    split = half + near_ref.shape[1]
     a = a_ref[...]
     for t in tiles(e_ref.shape[0]):
         plan = ((e_ref[t, :] * a) * to_column(share[:, t])).astype(BF16)
         keep_ref[t, :] = plan[:, :half]
-        near_ref[t, :] = plan[:, half : half + half // 2]
-        far_ref[t, :] = plan[:, half + half // 2 :]
-        mass_ref[:, t] = to_row(jnp.sum(plan.astype(F32), axis=1, keepdims=True))
+        near_ref[t, :] = plan[:, half:split]
+        far_ref[t, :] = plan[:, split:]
 
 
 def split_mass(mass, width):
@@ -282,8 +284,8 @@
     return jnp.sum(ref[ref.shape[0] - TAIL :, :width].astype(F32), axis=0, keepdims=True)
 
 
-def row_part_kernel(lanes, keep_ref, other_ref, *refs):
-    y_refs, (own_ref, out_ref) = refs[:-2], refs[-2:]
+def row_part_kernel(lanes, count, keep_ref, other_ref, *refs):
+    y_refs, out_refs = refs[:-count], refs[-count:]
     group = len(y_refs) // 2
     part = mass = 0.0
     for plan_ref, part_lanes, ys in (
@@ -298,15 +300,15 @@
                 block, y[...], (((0,), (0,)), ((), ())), preferred_element_type=F32
             )
             mass = mass + jnp.sum(block.astype(F32), axis=0, keepdims=True)
-    rows = own_ref.shape[0] - TAIL
-    width = own_ref.shape[1]
-    own_ref[:rows, :] = part[:rows, :]
-    own_ref[rows:, :] = jnp.concatenate(
-        [jnp.broadcast_to(mass[:, :rows], (TAIL, rows)), jnp.zeros((TAIL, width - rows), F32)],
-        axis=1,
-    )
-    out_ref[:rows, :] = part[rows:, :].astype(BF16)
-    out_ref[rows:, :] = split_mass(mass[:, rows:], width)
+    rows, width = out_refs[0].shape[0] - TAIL, out_refs[0].shape[1]
+    for n, ref in enumerate(out_refs):
+        here = slice(n * rows, (n + 1) * rows)
+        ref[:rows, :] = part[here, :].astype(ref.dtype)
+        if ref.dtype == BF16:
+            ref[rows:, :] = split_mass(mass[:, here], width)
+        else:
+            ref[rows:, :rows] = jnp.broadcast_to(mass[:, here], (TAIL, rows))
+            ref[rows:, rows:] = jnp.zeros((TAIL, width - rows), F32)
 
 
 def line_kernel(own_ref, other_ref, out_ref):
@@ -325,17 +327,15 @@
 
 
 def col_part(keep_ref, near_ref, far_ref, x0_ref, x1_ref, cols):
-    half = near_ref.shape[1]
+    near = near_ref.shape[1]
     part = jnp.dot(keep_ref[cols, :], x0_ref[...], preferred_element_type=F32)
-    part = part + jnp.dot(near_ref[cols, :], x1_ref[:half, :], preferred_element_type=F32)
-    return part + jnp.dot(far_ref[cols, :], x1_ref[half:, :], preferred_element_type=F32)
+    part = part + jnp.dot(near_ref[cols, :], x1_ref[:near, :], preferred_element_type=F32)
+    return part + jnp.dot(far_ref[cols, :], x1_ref[near:, :], preferred_element_type=F32)
 
 
 def col_send_kernel(cols, *refs):
-    *refs, mass_ref, out_ref = refs
-    part = col_part(*refs, cols)
-    out_ref[: part.shape[0], :] = part.astype(BF16)
-    out_ref[part.shape[0] :, :] = split_mass(mass_ref[:, cols], part.shape[1])
+    *refs, out_ref = refs
+    out_ref[...] = col_part(*refs, cols).astype(BF16)
 
 
 def col_keep_kernel(*refs):
@@ -345,7 +345,7 @@
 
 def target_rows(factor, cols, own_ref, other_ref, mass_ref, y_ref, out_ref, held_ref, sem_ref):
     count = cols.stop - cols.start
-    mass = mass_ref[:, cols] + joined_mass(other_ref, count)
+    mass = mass_ref[:, cols]
     copies = []
     for n, t in enumerate(slice(i, i + 128) for i in range(0, count, 128)):
         here = slice(cols.start + t.start, cols.start + t.stop)
@@ -536,7 +536,7 @@
         "plan",
         [e, a, h, col, col_other, logits, phi],
         [shape((2 * cols, half), BF16)]
-        + [shape((2 * cols, half // 2), BF16)] * 2
+        + [shape((2 * cols, size), BF16) for size in (half * 3 // 4, half // 4)]
         + [lane_shape, lane_shape],
     )
 
@@ -545,8 +545,8 @@
         (out,) = call(
             functools.partial(col_send_kernel, piece),
             "col_send",
-            [keep, *sends, x0, x1, mass],
-            [shape((parts[p].stop - parts[p].start + TAIL, width), BF16)],
+            [keep, *sends, x0, x1],
+            [shape((parts[p].stop - parts[p].start, width), BF16)],
         )
         return out
 
@@ -557,27 +557,28 @@
         others[0] = swap(sends[0], 1)
         block, block_out = shape((rows + TAIL, width)), shape((rows + TAIL, width), BF16)
 
-        def row_parts(pair, gate):
-            plan, other, _ = lax.optimization_barrier((keep, others[pair], gate))
-            lanes = slice(2 * pair * rows, 2 * (pair + 1) * rows)
+        def row_parts(far, gate):
+            plan, other, _ = lax.optimization_barrier((keep, others[far], gate))
+            outs = [block_out] if far else [block, block_out, block]
+            lanes = slice(3 * rows, half) if far else slice(0, 3 * rows)
             return call(
-                functools.partial(row_part_kernel, lanes),
+                functools.partial(row_part_kernel, lanes, len(outs)),
                 "row_part",
                 [plan, other, *ys],
-                [block, block_out],
+                outs,
             )
 
-        own2, out3 = row_parts(1, out)
+        (out3,) = row_parts(True, out)
         near3 = swap(out3, 4)
         keep_gated, _ = lax.optimization_barrier((keep, out3))
         out = col_send(1, keep_gated)
         back.append(swap(out, 2))
-        own0, out1 = row_parts(0, out)
+        own0, out1, own2 = row_parts(False, out)
         near1 = swap(out1, 4)
         (out2,) = call(line_kernel, "line", [own2, near3], [block_out])
         far2 = swap(out2, 8)
         ends = [own0, near1, far2, x0]
-        gate = out1
+        gate = near1
     else:
         out = col_send(1, keep)
         back.append(swap(out, 2))

time: 101 us -> 100 us (0.990)
  transfers between devices with their start and end apart: 33 -> 33, of which waited for: 19 -> 20; matrix products, arithmetic and copies ran while one was open for 0% -> 1% of each run, Pallas kernels for 13% -> 14%
where the time goes in v7:
time: 100 us; the launch traced here: 99.9 us
  waiting for transfers between devices  41.6 us (42%)
  starting transfers between devices  33.7 us (34%)
  Pallas kernels  18.8 us (19%)
  local copies, waits for them, and re-layouts  4.27 us (4%)
    ppermute x33, waiting for transfers between devices, swap(): return lax.ppermute(value, AXIS, [(i, i ^ mask) for i in range(count)])  41.6 us
    ppermute x33, starting transfers between devices, swap(): return lax.ppermute(value, AXIS, [(i, i ^ mask) for i in range(count)])  33.7 us
    pallas_call x22, Pallas kernels, call(): pl.pallas_call(body, name=name, out_shape=outs, in_specs=specs, out_specs...  18.8 us
    unnamed x12, local copies, waits for them, and re-layouts  4.27 us
  transfers between devices with their start and end apart: 33, of which 20 were waited for; matrix products, arithmetic and copies ran while one was open for 1% of the time, Pallas kernels for 14%

profile of v7, /device:TPU:0, one launch (start us, length us, event | category | flops | bytes accessed | tf_op | source)
XLA Modules:
  0.0 99.9 jit_solution(8069368328806004035)
XLA Ops:
  0.6 3.0 %collective-permute-start.8 = (bf16[512,1024]{1,0:T(8,128)(2,1)}, bf16[512,1024]{1,0:T(8,128)(2,1)S(1)}, u32[]{:S(2)}, u32[]{:S(2)}) collective-permute-start(bf16[512,1024]{1,0:T(8,128)(2,1)} %refs_3_.3), channel_id=1, source_target_pairs={{0,2},{1,3},{2,0},{3,1},{4,6},{5,7},{6,4},{7,5},{8,10},{9,11},{10,... | collective-permute-start | bytes 3145736 | tf_op jit(solution)/shard_map/ppermute | solution.py:47
  3.7 2.6 %collective-permute-start = (bf16[128,1024]{1,0:T(8,128)(2,1)}, bf16[128,1024]{1,0:T(8,128)(2,1)S(1)}, u32[]{:S(2)}, u32[]{:S(2)}) collective-permute-start(bf16[128,1024]{1,0:T(8,128)(2,1)} %refs_0_.1), channel_id=1, source_target_pairs={{0,8},{1,9},{2,10},{3,11},{4,12},{5,13},{6,14},{7,15},{8,0},{9,1},... | collective-permute-start | bytes 786440 | tf_op jit(solution)/shard_map/ppermute | solution.py:47
  6.3 1.6 %collective-permute-start.4 = (bf16[128,1024]{1,0:T(8,128)(2,1)}, bf16[128,1024]{1,0:T(8,128)(2,1)S(1)}, u32[]{:S(2)}, u32[]{:S(2)}) collective-permute-start(bf16[128,1024]{1,0:T(8,128)(2,1)} %refs_0_.1), channel_id=1, source_target_pairs={{0,4},{1,5},{2,6},{3,7},{4,0},{5,1},{6,2},{7,3},{8,12},{9,13},{10,... | collective-permute-start | bytes 786440 | tf_op jit(solution)/shard_map/ppermute | solution.py:47
  13.2 6.1 %collective-permute-done.refs_0_ = bf16[128,1024]{1,0:T(8,128)(2,1)S(1)} collective-permute-done((bf16[128,1024]{1,0:T(8,128)(2,1)}, bf16[128,1024]{1,0:T(8,128)(2,1)S(1)}, u32[]{:S(2)}, u32[]{:S(2)}) %collective-permute-start) | collective-permute-done | bytes 262176 | tf_op jit(solution)/shard_map/ppermute | solution.py:47
  23.0 4.0 %collective-permute-done.3.refs_3_ = f32[1,512]{1,0:T(1,128)S(1)} collective-permute-done((f32[1,512]{1,0:T(1,128)S(1)}, f32[1,512]{1,0:T(1,128)S(1)}, u32[]{:S(2)}, u32[]{:S(2)}) %collective-permute-start.3) | collective-permute-done | bytes 2080 | tf_op jit(solution)/shard_map/ppermute | solution.py:47
  28.1 1.7 %cost.8 = (f32[1024,512]{1,0:T(8,128)S(1)}, f32[1024,512]{1,0:T(8,128)S(1)}, f32[3,1024]{1,0:T(4,128)S(1)}, f32[512,1]{1,0:T(8,128)S(1)}) custom-call(bf16[512,1024]{1,0:T(8,128)(2,1)S(1)} %get-tuple-element.83.refs_0_.refs_9_, bf16[512,1024]{1,0:T(8,128)(2,1)S(1)} %get-tuple-element.84.refs_1_.refs_10_, ...), custom_call_target="tpu_custom_call", output_to_operand_aliasing={{0}: (5, {}), {1}: (6, {})} | custom-call | flops 1 | bytes 1 | tf_op jit(solution)/shard_map/cost/pallas_call | solution.py:24
  29.8 1.4 %cost.9 = (f32[1024,512]{1,0:T(8,128)S(1)}, f32[1024,512]{1,0:T(8,128)S(1)}, bf16[512,1024]{1,0:T(8,128)(2,1)S(1)}, bf16[512,1024]{1,0:T(8,128)(2,1)S(1)}, f32[3,1024]{1,0:T(4,128)S(1)}) custom-call(bf16[128,1024]{1,0:T(8,128)(2,1)S(1)} %collective-permute-done.2.refs_0_, ...), custom_call_target="tpu_custom_call", output_to_operand_aliasing={{0}: (7, {}), {1}: (8, {}), {2}: (9, {}), {3}: (10, {})} | custom-call | flops 1 | bytes 1 | tf_op jit(solution)/shard_map/cost/pallas_call | solution.py:24
  33.1 3.3 %collective-permute-start.10 = (f32[3,1024]{1,0:T(4,128)S(1)}, f32[3,1024]{1,0:T(4,128)S(1)}, u32[]{:S(2)}, u32[]{:S(2)}) collective-permute-start(f32[3,1024]{1,0:T(4,128)S(1)} %merge.1.refs_0_), channel_id=1, source_target_pairs={{0,12},{1,13},{2,14},{3,15},{4,8},{5,9},{6,10},{7,11},{8,4},{9,5},... | collective-permute-start | bytes 36872 | tf_op jit(solution)/shard_map/ppermute | solution.py:47
  37.5 1.2 %collective-permute-done.10.refs_1_ = f32[3,1024]{1,0:T(4,128)S(1)} collective-permute-done((f32[3,1024]{1,0:T(4,128)S(1)}, f32[3,1024]{1,0:T(4,128)S(1)}, u32[]{:S(2)}, u32[]{:S(2)}) %collective-permute-start.10) | collective-permute-done | bytes 12320 | tf_op jit(solution)/shard_map/ppermute | solution.py:47
  38.7 2.3 %collective-permute-done.11.refs_2_ = f32[3,1024]{1,0:T(4,128)S(1)} collective-permute-done((f32[3,1024]{1,0:T(4,128)S(1)}, f32[3,1024]{1,0:T(4,128)S(1)}, u32[]{:S(2)}, u32[]{:S(2)}) %collective-permute-start.11) | collective-permute-done | bytes 12320 | tf_op jit(solution)/shard_map/ppermute | solution.py:47
  41.0 1.3 %first.1 = (f32[1024,1024]{1,0:T(8,128)S(1)}, f32[2,1024]{1,0:T(2,128)S(1)}, f32[1,1024]{1,0:T(1,128)S(1)}, f32[2,1024]{1,0:T(2,128)S(1)}) custom-call(f32[3,1024]{1,0:T(4,128)S(1)} %merge.1.refs_0_, f32[3,1024]{1,0:T(4,128)S(1)} %collective-permute-done.10.refs_1_, f32[3,1024]{1,0:T(4,128)S(1)} %collective-permute-done.11.refs_2_, ...), custom_call_target="tpu_custom_call" | custom-call | flops 1 | bytes 1 | tf_op jit(solution)/shard_map/first/pallas_call | solution.py:24
  43.5 2.6 %collective-permute-done.13.other_ref = f32[2,1024]{1,0:T(2,128)S(1)} collective-permute-done((f32[2,1024]{1,0:T(2,128)S(1)}, f32[2,1024]{1,0:T(2,128)S(1)}, u32[]{:S(2)}, u32[]{:S(2)}) %collective-permute-start.13) | collective-permute-done | bytes 8224 | tf_op jit(solution)/shard_map/ppermute | solution.py:47
  47.8 1.5 %collective-permute-start.17 = (f32[1,1024]{1,0:T(1,128)S(1)}, f32[1,1024]{1,0:T(1,128)S(1)}, u32[]{:S(2)}, u32[]{:S(2)}) collective-permute-start(f32[1,1024]{1,0:T(1,128)S(1)} %maximum_add_fusion.refs_0_), channel_id=1, source_target_pairs={{0,12},{1,13},{2,14},{3,15},{4,8},{5,9},{6,10},{7,11},{8,4},{9,5},... | collective-permute-start | bytes 12296 | tf_op jit(solution)/shard_map/ppermute | solution.py:47
  50.0 2.3 %collective-permute-start.19 = (f32[1,1024]{1,0:T(1,128)S(1)}, f32[1,1024]{1,0:T(1,128)S(1)}, u32[]{:S(2)}, u32[]{:S(2)}) collective-permute-start(f32[1,1024]{1,0:T(1,128)S(1)} %maximum_add_fusion.refs_0_), channel_id=1, source_target_pairs={{0,4},{1,5},{2,6},{3,7},{4,0},{5,1},{6,2},{7,3},{8,12},{9,13},{10,... | collective-permute-start | bytes 12296 | tf_op jit(solution)/shard_map/ppermute | solution.py:47
  55.4 2.6 %collective-permute-done.20.other_ref = f32[1,1024]{1,0:T(1,128)S(1)} collective-permute-done((f32[1,1024]{1,0:T(1,128)S(1)}, f32[1,1024]{1,0:T(1,128)S(1)}, u32[]{:S(2)}, u32[]{:S(2)}) %collective-permute-start.20) | collective-permute-done | bytes 4128 | tf_op jit(solution)/shard_map/ppermute | solution.py:47
  59.6 2.6 %collective-permute-start.22 = (f32[1,1024]{1,0:T(1,128)S(1)}, f32[1,1024]{1,0:T(1,128)S(1)}, u32[]{:S(2)}, u32[]{:S(2)}) collective-permute-start(f32[1,1024]{1,0:T(1,128)S(1)} %maximum_add_fusion.1.refs_0_), channel_id=1, source_target_pairs={{0,12},{1,13},{2,14},{3,15},{4,8},{5,9},{6,10},{7,11},{8,4},{9,5},... | collective-permute-start | bytes 12296 | tf_op jit(solution)/shard_map/ppermute | solution.py:47
  65.1 1.6 %collective-permute-done.23.refs_2_ = f32[1,1024]{1,0:T(1,128)S(1)} collective-permute-done((f32[1,1024]{1,0:T(1,128)S(1)}, f32[1,1024]{1,0:T(1,128)S(1)}, u32[]{:S(2)}, u32[]{:S(2)}) %collective-permute-start.23) | collective-permute-done | bytes 4128 | tf_op jit(solution)/shard_map/ppermute | solution.py:47
  68.3 2.6 %collective-permute-done.25.refs_4_.other_ref = f32[2,1024]{1,0:T(2,128)S(1)} collective-permute-done((f32[2,1024]{1,0:T(2,128)S(1)}, f32[2,1024]{1,0:T(2,128)S(1)}, u32[]{:S(2)}, u32[]{:S(2)}) %collective-permute-start.25) | collective-permute-done | bytes 8224 | tf_op jit(solution)/shard_map/ppermute | solution.py:47
  76.7 1.9 %row_part.3 = (f32[136,1024]{1,0:T(8,128)S(1)}, bf16[136,1024]{1,0:T(8,128)(2,1)S(1)}, f32[136,1024]{1,0:T(8,128)S(1)}) custom-call(bf16[1024,512]{1,0:T(8,128)(2,1)S(1)} %get-tuple-element.125.refs_0_.keep_ref, bf16[1024,384]{1,0:T(8,128)(2,1)S(1)} %collective-permute-done.26.other_ref, bf16[512,1024]{1,0:T(8,128)(2,1)S(1)} %copy-done.1, ...), custom_call_target="tpu_custom_call" | custom-call | flops 1 | bytes 1 | tf_op jit(solution)/shard_map/row_part/pallas_call | solution.py:24
  79.8 5.1 %collective-permute-done.31.other_ref = bf16[136,1024]{1,0:T(8,128)(2,1)S(1)} collective-permute-done((bf16[136,1024]{1,0:T(8,128)(2,1)S(1)}, bf16[136,1024]{1,0:T(8,128)(2,1)S(1)}, u32[]{:S(2)}, u32[]{:S(2)}) %collective-permute-start.31) | collective-permute-done | bytes 278560 | tf_op jit(solution)/shard_map/ppermute | solution.py:47
  84.9 2.0 %collective-permute-start.32 = (bf16[136,1024]{1,0:T(8,128)(2,1)S(1)}, bf16[136,1024]{1,0:T(8,128)(2,1)S(1)}, u32[]{:S(2)}, u32[]{:S(2)}) collective-permute-start(bf16[136,1024]{1,0:T(8,128)(2,1)S(1)} %line.1), channel_id=1, source_target_pairs={{0,8},{1,9},{2,10},{3,11},{4,12},{5,13},{6,14},{7,15},{8,0},{9,1},... | collective-permute-start | bytes 835592 | tf_op jit(solution)/shard_map/ppermute | solution.py:47
  87.9 6.6 %collective-permute-done.28.refs_6_ = bf16[136,1024]{1,0:T(8,128)(2,1)S(1)} collective-permute-done((bf16[136,1024]{1,0:T(8,128)(2,1)S(1)}, bf16[136,1024]{1,0:T(8,128)(2,1)S(1)}, u32[]{:S(2)}, u32[]{:S(2)}) %collective-permute-start.28) | collective-permute-done | bytes 278560 | tf_op jit(solution)/shard_map/ppermute | solution.py:47
  95.4 1.5 %col_keep.1.refs_0_ = f32[512,1024]{1,0:T(8,128)S(1)} custom-call(bf16[1024,512]{1,0:T(8,128)(2,1)S(1)} %get-tuple-element.125.refs_0_.keep_ref, bf16[1024,384]{1,0:T(8,128)(2,1)S(1)} %get-tuple-element.111.refs_1_, bf16[1024,128]{1,0:T(8,128)(2,1)S(1)} %get-tuple-element.112.refs_2_, bf16[512,1024]{1,0:T(8,128)(2,1)S(1)} %get-tuple-element.104.refs_3_.refs_8_, ...), custom_call_target="tpu_custom_call" | custom-call | flops 1 | bytes 1 | tf_op jit(solution)/shard_map/col_keep/pallas_call | solution.py:24
  96.9 1.3 %target.1.refs_4_ = f32[512,1024]{1,0:T(8,128)} custom-call(f32[512,1024]{1,0:T(8,128)S(1)} %col_keep.1.refs_0_, bf16[384,1024]{1,0:T(8,128)(2,1)S(1)} %collective-permute-done.30.refs_1_, f32[1,1024]{1,0:T(1,128)S(1)} %get-tuple-element.126.refs_2_, bf16[512,1024]{1,0:T(8,128)(2,1)S(1)} %copy-done.1), custom_call_target="tpu_custom_call" | custom-call | flops 1 | bytes 2097152 | tf_op jit(solution)/shard_map/target/pallas_call | solution.py:24
  (83 shorter events, 36.2 us)
Async XLA Ops:
  0.6 27.5 %collective-permute-start.8 = (bf16[512,1024]{1,0:T(8,128)(2,1)}, bf16[512,1024]{1,0:T(8,128)(2,1)S(1)}, u32[]{:S(2)}, u32[]{:S(2)}) collective-permute-start(bf16[512,1024]{1,0:T(8,128)(2,1)} %refs_3_.3), channel_id=1, source_target_pairs={{0,2},{1,3},{2,0},{3,1},{4,6},{5,7},{6,4},{7,5},{8,10},{9,11},{10,... | collective-permute-start | bytes 3145736 | tf_op jit(solution)/shard_map/ppermute | solution.py:47
  3.7 5.0 %collective-permute-start.1 = (bf16[128,1024]{1,0:T(8,128)(2,1)}, bf16[128,1024]{1,0:T(8,128)(2,1)S(1)}, u32[]{:S(2)}, u32[]{:S(2)}) collective-permute-start(bf16[128,1024]{1,0:T(8,128)(2,1)} %refs_0_.1), channel_id=1, source_target_pairs={{0,1},{1,0},{2,3},{3,2},{4,5},{5,4},{6,7},{7,6},{8,9},{9,8},{10,11... | collective-permute-start | bytes 786440 | tf_op jit(solution)/shard_map/ppermute | solution.py:47
  3.7 15.6 %collective-permute-start = (bf16[128,1024]{1,0:T(8,128)(2,1)}, bf16[128,1024]{1,0:T(8,128)(2,1)S(1)}, u32[]{:S(2)}, u32[]{:S(2)}) collective-permute-start(bf16[128,1024]{1,0:T(8,128)(2,1)} %refs_0_.1), channel_id=1, source_target_pairs={{0,8},{1,9},{2,10},{3,11},{4,12},{5,13},{6,14},{7,15},{8,0},{9,1},... | collective-permute-start | bytes 786440 | tf_op jit(solution)/shard_map/ppermute | solution.py:47
  6.3 13.2 %collective-permute-start.4 = (bf16[128,1024]{1,0:T(8,128)(2,1)}, bf16[128,1024]{1,0:T(8,128)(2,1)S(1)}, u32[]{:S(2)}, u32[]{:S(2)}) collective-permute-start(bf16[128,1024]{1,0:T(8,128)(2,1)} %refs_0_.1), channel_id=1, source_target_pairs={{0,4},{1,5},{2,6},{3,7},{4,0},{5,1},{6,2},{7,3},{8,12},{9,13},{10,... | collective-permute-start | bytes 786440 | tf_op jit(solution)/shard_map/ppermute | solution.py:47
  19.7 8.4 %collective-permute-start.2 = (bf16[128,1024]{1,0:T(8,128)(2,1)S(1)}, bf16[128,1024]{1,0:T(8,128)(2,1)S(1)}, u32[]{:S(2)}, u32[]{:S(2)}) collective-permute-start(bf16[128,1024]{1,0:T(8,128)(2,1)S(1)} %collective-permute-done.refs_0_), channel_id=1, source_target_pairs={{0,4},{1,5},{2,6},{3,7},{4,0},{5,1},{6,2},{7,3},{8,12},{9,13},{10,... | collective-permute-start | bytes 786440 | tf_op jit(solution)/shard_map/ppermute | solution.py:47
  20.8 6.2 %collective-permute-start.3 = (f32[1,512]{1,0:T(1,128)S(1)}, f32[1,512]{1,0:T(1,128)S(1)}, u32[]{:S(2)}, u32[]{:S(2)}) collective-permute-start(f32[1,512]{1,0:T(1,128)S(1)} %bitcast.8), channel_id=1, source_target_pairs={{0,2},{1,3},{2,0},{3,1},{4,6},{5,7},{6,4},{7,5},{8,10},{9,11},{10,... | collective-permute-start | bytes 6152 | tf_op jit(solution)/shard_map/ppermute | solution.py:47
  31.8 14.2 %collective-permute-start.14 = (bf16[512,1024]{1,0:T(8,128)(2,1)S(1)}, bf16[512,1024]{1,0:T(8,128)(2,1)S(1)}, u32[]{:S(2)}, u32[]{:S(2)}) collective-permute-start(bf16[512,1024]{1,0:T(8,128)(2,1)S(1)} %copy-done.1), channel_id=1, source_target_pairs={{0,1},{1,0},{2,3},{3,2},{4,5},{5,4},{6,7},{7,6},{8,9},{9,8},{10,11... | collective-permute-start | bytes 3145736 | tf_op jit(solution)/shard_map/ppermute | solution.py:47
  32.7 13.4 %collective-permute-start.15 = (bf16[512,1024]{1,0:T(8,128)(2,1)S(1)}, bf16[512,1024]{1,0:T(8,128)(2,1)S(1)}, u32[]{:S(2)}, u32[]{:S(2)}) collective-permute-start(bf16[512,1024]{1,0:T(8,128)(2,1)S(1)} %collective-permute-done.8.refs_2_.refs_3_.refs_1_), channel_id=1, source_target_pairs={{0,1},{1,0},{2,3},{3,2},{4,5},{5,4},{6,7},{7,6},{8,9},{9,8},{10,11... | collective-permute-start | bytes 3145736 | tf_op jit(solution)/shard_map/ppermute | solution.py:47
  33.1 5.6 %collective-permute-start.10 = (f32[3,1024]{1,0:T(4,128)S(1)}, f32[3,1024]{1,0:T(4,128)S(1)}, u32[]{:S(2)}, u32[]{:S(2)}) collective-permute-start(f32[3,1024]{1,0:T(4,128)S(1)} %merge.1.refs_0_), channel_id=1, source_target_pairs={{0,12},{1,13},{2,14},{3,15},{4,8},{5,9},{6,10},{7,11},{8,4},{9,5},... | collective-permute-start | bytes 36872 | tf_op jit(solution)/shard_map/ppermute | solution.py:47
  36.4 4.6 %collective-permute-start.11 = (f32[3,1024]{1,0:T(4,128)S(1)}, f32[3,1024]{1,0:T(4,128)S(1)}, u32[]{:S(2)}, u32[]{:S(2)}) collective-permute-start(f32[3,1024]{1,0:T(4,128)S(1)} %merge.1.refs_0_), channel_id=1, source_target_pairs={{0,8},{1,9},{2,10},{3,11},{4,12},{5,13},{6,14},{7,15},{8,0},{9,1},... | collective-permute-start | bytes 36872 | tf_op jit(solution)/shard_map/ppermute | solution.py:47
  36.4 4.6 %collective-permute-start.12 = (f32[3,1024]{1,0:T(4,128)S(1)}, f32[3,1024]{1,0:T(4,128)S(1)}, u32[]{:S(2)}, u32[]{:S(2)}) collective-permute-start(f32[3,1024]{1,0:T(4,128)S(1)} %merge.1.refs_0_), channel_id=1, source_target_pairs={{0,4},{1,5},{2,6},{3,7},{4,0},{5,1},{6,2},{7,3},{8,12},{9,13},{10,... | collective-permute-start | bytes 36872 | tf_op jit(solution)/shard_map/ppermute | solution.py:47
  42.4 3.7 %collective-permute-start.13 = (f32[2,1024]{1,0:T(2,128)S(1)}, f32[2,1024]{1,0:T(2,128)S(1)}, u32[]{:S(2)}, u32[]{:S(2)}) collective-permute-start(f32[2,1024]{1,0:T(2,128)S(1)} %get-tuple-element.96.own_ref), channel_id=1, source_target_pairs={{0,2},{1,3},{2,0},{3,1},{4,6},{5,7},{6,4},{7,5},{8,10},{9,11},{10,... | collective-permute-start | bytes 24584 | tf_op jit(solution)/shard_map/ppermute | solution.py:47
  47.8 5.5 %collective-permute-start.17 = (f32[1,1024]{1,0:T(1,128)S(1)}, f32[1,1024]{1,0:T(1,128)S(1)}, u32[]{:S(2)}, u32[]{:S(2)}) collective-permute-start(f32[1,1024]{1,0:T(1,128)S(1)} %maximum_add_fusion.refs_0_), channel_id=1, source_target_pairs={{0,12},{1,13},{2,14},{3,15},{4,8},{5,9},{6,10},{7,11},{8,4},{9,5},... | collective-permute-start | bytes 12296 | tf_op jit(solution)/shard_map/ppermute | solution.py:47
  49.3 4.5 %collective-permute-start.18 = (f32[1,1024]{1,0:T(1,128)S(1)}, f32[1,1024]{1,0:T(1,128)S(1)}, u32[]{:S(2)}, u32[]{:S(2)}) collective-permute-start(f32[1,1024]{1,0:T(1,128)S(1)} %maximum_add_fusion.refs_0_), channel_id=1, source_target_pairs={{0,8},{1,9},{2,10},{3,11},{4,12},{5,13},{6,14},{7,15},{8,0},{9,1},... | collective-permute-start | bytes 12296 | tf_op jit(solution)/shard_map/ppermute | solution.py:47
  50.0 3.9 %collective-permute-start.19 = (f32[1,1024]{1,0:T(1,128)S(1)}, f32[1,1024]{1,0:T(1,128)S(1)}, u32[]{:S(2)}, u32[]{:S(2)}) collective-permute-start(f32[1,1024]{1,0:T(1,128)S(1)} %maximum_add_fusion.refs_0_), channel_id=1, source_target_pairs={{0,4},{1,5},{2,6},{3,7},{4,0},{5,1},{6,2},{7,3},{8,12},{9,13},{10,... | collective-permute-start | bytes 12296 | tf_op jit(solution)/shard_map/ppermute | solution.py:47
  59.6 5.5 %collective-permute-start.22 = (f32[1,1024]{1,0:T(1,128)S(1)}, f32[1,1024]{1,0:T(1,128)S(1)}, u32[]{:S(2)}, u32[]{:S(2)}) collective-permute-start(f32[1,1024]{1,0:T(1,128)S(1)} %maximum_add_fusion.1.refs_0_), channel_id=1, source_target_pairs={{0,12},{1,13},{2,14},{3,15},{4,8},{5,9},{6,10},{7,11},{8,4},{9,5},... | collective-permute-start | bytes 12296 | tf_op jit(solution)/shard_map/ppermute | solution.py:47
  62.2 4.5 %collective-permute-start.23 = (f32[1,1024]{1,0:T(1,128)S(1)}, f32[1,1024]{1,0:T(1,128)S(1)}, u32[]{:S(2)}, u32[]{:S(2)}) collective-permute-start(f32[1,1024]{1,0:T(1,128)S(1)} %maximum_add_fusion.1.refs_0_), channel_id=1, source_target_pairs={{0,8},{1,9},{2,10},{3,11},{4,12},{5,13},{6,14},{7,15},{8,0},{9,1},... | collective-permute-start | bytes 12296 | tf_op jit(solution)/shard_map/ppermute | solution.py:47
  67.2 3.7 %collective-permute-start.25 = (f32[2,1024]{1,0:T(2,128)S(1)}, f32[2,1024]{1,0:T(2,128)S(1)}, u32[]{:S(2)}, u32[]{:S(2)}) collective-permute-start(f32[2,1024]{1,0:T(2,128)S(1)} %get-tuple-element.107.refs_3_.own_ref), channel_id=1, source_target_pairs={{0,2},{1,3},{2,0},{3,1},{4,6},{5,7},{6,4},{7,5},{8,10},{9,11},{10,... | collective-permute-start | bytes 24584 | tf_op jit(solution)/shard_map/ppermute | solution.py:47
  71.4 5.3 %collective-permute-start.26 = (bf16[1024,384]{1,0:T(8,128)(2,1)S(1)}, bf16[1024,384]{1,0:T(8,128)(2,1)S(1)}, u32[]{:S(2)}, u32[]{:S(2)}) collective-permute-start(bf16[1024,384]{1,0:T(8,128)(2,1)S(1)} %get-tuple-element.111.refs_1_), channel_id=1, source_target_pairs={{0,1},{1,0},{2,3},{3,2},{4,5},{5,4},{6,7},{7,6},{8,9},{9,8},{10,11... | collective-permute-start | bytes 2359304 | tf_op jit(solution)/shard_map/ppermute | solution.py:47
  73.2 23.7 %collective-permute-start.30 = (bf16[384,1024]{1,0:T(8,128)(2,1)S(1)}, bf16[384,1024]{1,0:T(8,128)(2,1)S(1)}, u32[]{:S(2)}, u32[]{:S(2)}) collective-permute-start(bf16[384,1024]{1,0:T(8,128)(2,1)S(1)} %col_send.2), channel_id=1, source_target_pairs={{0,2},{1,3},{2,0},{3,1},{4,6},{5,7},{6,4},{7,5},{8,10},{9,11},{10,... | collective-permute-start | bytes 2359304 | tf_op jit(solution)/shard_map/ppermute | solution.py:47
  75.2 9.6 %collective-permute-start.31 = (bf16[136,1024]{1,0:T(8,128)(2,1)S(1)}, bf16[136,1024]{1,0:T(8,128)(2,1)S(1)}, u32[]{:S(2)}, u32[]{:S(2)}) collective-permute-start(bf16[136,1024]{1,0:T(8,128)(2,1)S(1)} %row_part.2), channel_id=1, source_target_pairs={{0,4},{1,5},{2,6},{3,7},{4,0},{5,1},{6,2},{7,3},{8,12},{9,13},{10,... | collective-permute-start | bytes 835592 | tf_op jit(solution)/shard_map/ppermute | solution.py:47
  78.6 15.9 %collective-permute-start.28 = (bf16[136,1024]{1,0:T(8,128)(2,1)S(1)}, bf16[136,1024]{1,0:T(8,128)(2,1)S(1)}, u32[]{:S(2)}, u32[]{:S(2)}) collective-permute-start(bf16[136,1024]{1,0:T(8,128)(2,1)S(1)} %get-tuple-element.122), channel_id=1, source_target_pairs={{0,4},{1,5},{2,6},{3,7},{4,0},{5,1},{6,2},{7,3},{8,12},{9,13},{10,... | collective-permute-start | bytes 835592 | tf_op jit(solution)/shard_map/ppermute | solution.py:47
  84.9 13.7 %collective-permute-start.32 = (bf16[136,1024]{1,0:T(8,128)(2,1)S(1)}, bf16[136,1024]{1,0:T(8,128)(2,1)S(1)}, u32[]{:S(2)}, u32[]{:S(2)}) collective-permute-start(bf16[136,1024]{1,0:T(8,128)(2,1)S(1)} %line.1), channel_id=1, source_target_pairs={{0,8},{1,9},{2,10},{3,11},{4,12},{5,13},{6,14},{7,15},{8,0},{9,1},... | collective-permute-start | bytes 835592 | tf_op jit(solution)/shard_map/ppermute | solution.py:47
  86.9 11.5 %collective-permute-start.29 = (bf16[128,1024]{1,0:T(8,128)(2,1)S(1)}, bf16[128,1024]{1,0:T(8,128)(2,1)S(1)}, u32[]{:S(2)}, u32[]{:S(2)}) collective-permute-start(bf16[128,1024]{1,0:T(8,128)(2,1)S(1)} %col_send.3), channel_id=1, source_target_pairs={{0,2},{1,3},{2,0},{3,1},{4,6},{5,7},{6,4},{7,5},{8,10},{9,11},{10,... | collective-permute-start | bytes 786440 | tf_op jit(solution)/shard_map/ppermute | solution.py:47
  (15 other events, 34.0 us)

commit v8 on v7

--- a/solution.py
+++ b/solution.py
@@ -495,15 +495,17 @@
     )
     col_other = swap(col, 2)
     if direct:
-        crossed, _ = lax.optimization_barrier((crossed, pack))
+        crossed, _ = lax.optimization_barrier((crossed, h))
         ys = [ys[0], crossed[0], ys[1], swap(crossed[0], 1)]
-        col_other, *ys = lax.optimization_barrier((col_other, *ys))
     row, phi, g = call(
         first_row_kernel,
         "first_row",
         [e, col, col_other, logits],
         [flat_shape, lane_shape, lane_shape],
     )
+
+    if direct:
+        row, *ys = lax.optimization_barrier((row, *ys))
 
     def columns(row, *base):
         for level in levels:

time: 100 us -> 100 us (level)
  no operation moved by 1% of the time
where the time goes in v8:
time: 100 us; the launch traced here: 99.7 us
  waiting for transfers between devices  41.7 us (42%)
  starting transfers between devices  33.4 us (33%)
  Pallas kernels  18.8 us (19%)
  local copies, waits for them, and re-layouts  4.27 us (4%)
  between operations  1 us (1%)
    ppermute x33, waiting for transfers between devices, swap(): return lax.ppermute(value, AXIS, [(i, i ^ mask) for i in range(count)])  41.7 us
    ppermute x33, starting transfers between devices, swap(): return lax.ppermute(value, AXIS, [(i, i ^ mask) for i in range(count)])  33.4 us
    pallas_call x22, Pallas kernels, call(): pl.pallas_call(body, name=name, out_shape=outs, in_specs=specs, out_specs...  18.8 us
    unnamed x12, local copies, waits for them, and re-layouts  4.27 us
  transfers between devices with their start and end apart: 33, of which 20 were waited for; matrix products, arithmetic and copies ran while one was open for 1% of the time, Pallas kernels for 14%

profile of v8, /device:TPU:0, one launch (start us, length us, event | category | flops | bytes accessed | tf_op | source)
XLA Modules:
  0.0 99.7 jit_solution(18313095873570503294)
XLA Ops:
  0.6 3.0 %collective-permute-start.8 = (bf16[512,1024]{1,0:T(8,128)(2,1)}, bf16[512,1024]{1,0:T(8,128)(2,1)S(1)}, u32[]{:S(2)}, u32[]{:S(2)}) collective-permute-start(bf16[512,1024]{1,0:T(8,128)(2,1)} %refs_3_.3), channel_id=1, source_target_pairs={{0,2},{1,3},{2,0},{3,1},{4,6},{5,7},{6,4},{7,5},{8,10},{9,11},{10,... | collective-permute-start | bytes 3145736 | tf_op jit(solution)/shard_map/ppermute | solution.py:47
  3.7 2.6 %collective-permute-start = (bf16[128,1024]{1,0:T(8,128)(2,1)}, bf16[128,1024]{1,0:T(8,128)(2,1)S(1)}, u32[]{:S(2)}, u32[]{:S(2)}) collective-permute-start(bf16[128,1024]{1,0:T(8,128)(2,1)} %refs_0_.1), channel_id=1, source_target_pairs={{0,8},{1,9},{2,10},{3,11},{4,12},{5,13},{6,14},{7,15},{8,0},{9,1},... | collective-permute-start | bytes 786440 | tf_op jit(solution)/shard_map/ppermute | solution.py:47
  6.3 1.6 %collective-permute-start.4 = (bf16[128,1024]{1,0:T(8,128)(2,1)}, bf16[128,1024]{1,0:T(8,128)(2,1)S(1)}, u32[]{:S(2)}, u32[]{:S(2)}) collective-permute-start(bf16[128,1024]{1,0:T(8,128)(2,1)} %refs_0_.1), channel_id=1, source_target_pairs={{0,4},{1,5},{2,6},{3,7},{4,0},{5,1},{6,2},{7,3},{8,12},{9,13},{10,... | collective-permute-start | bytes 786440 | tf_op jit(solution)/shard_map/ppermute | solution.py:47
  8.7 1.2 %copy-done = bf16[512,1024]{1,0:T(8,128)(2,1)S(1)} copy-done((bf16[512,1024]{1,0:T(8,128)(2,1)S(1)}, bf16[512,1024]{1,0:T(8,128)(2,1)}, u32[]{:S(2)}) %copy-start) | copy-done | bytes 1048600
  13.2 6.1 %collective-permute-done.refs_0_ = bf16[128,1024]{1,0:T(8,128)(2,1)S(1)} collective-permute-done((bf16[128,1024]{1,0:T(8,128)(2,1)}, bf16[128,1024]{1,0:T(8,128)(2,1)S(1)}, u32[]{:S(2)}, u32[]{:S(2)}) %collective-permute-start) | collective-permute-done | bytes 262176 | tf_op jit(solution)/shard_map/ppermute | solution.py:47
  23.0 4.0 %collective-permute-done.3.refs_3_ = f32[1,512]{1,0:T(1,128)S(1)} collective-permute-done((f32[1,512]{1,0:T(1,128)S(1)}, f32[1,512]{1,0:T(1,128)S(1)}, u32[]{:S(2)}, u32[]{:S(2)}) %collective-permute-start.3) | collective-permute-done | bytes 2080 | tf_op jit(solution)/shard_map/ppermute | solution.py:47
  28.1 1.7 %cost.8 = (f32[1024,512]{1,0:T(8,128)S(1)}, f32[1024,512]{1,0:T(8,128)S(1)}, f32[3,1024]{1,0:T(4,128)S(1)}, f32[512,1]{1,0:T(8,128)S(1)}) custom-call(bf16[512,1024]{1,0:T(8,128)(2,1)S(1)} %get-tuple-element.83.refs_0_.refs_9_, bf16[512,1024]{1,0:T(8,128)(2,1)S(1)} %get-tuple-element.84.refs_1_.refs_10_, ...), custom_call_target="tpu_custom_call", output_to_operand_aliasing={{0}: (5, {}), {1}: (6, {})} | custom-call | flops 1 | bytes 1 | tf_op jit(solution)/shard_map/cost/pallas_call | solution.py:24
  29.8 1.4 %cost.9 = (f32[1024,512]{1,0:T(8,128)S(1)}, f32[1024,512]{1,0:T(8,128)S(1)}, bf16[512,1024]{1,0:T(8,128)(2,1)S(1)}, bf16[512,1024]{1,0:T(8,128)(2,1)S(1)}, f32[3,1024]{1,0:T(4,128)S(1)}) custom-call(bf16[128,1024]{1,0:T(8,128)(2,1)S(1)} %collective-permute-done.2.refs_0_, ...), custom_call_target="tpu_custom_call", output_to_operand_aliasing={{0}: (7, {}), {1}: (8, {}), {2}: (9, {}), {3}: (10, {})} | custom-call | flops 1 | bytes 1 | tf_op jit(solution)/shard_map/cost/pallas_call | solution.py:24
  32.7 3.3 %collective-permute-start.10 = (f32[3,1024]{1,0:T(4,128)S(1)}, f32[3,1024]{1,0:T(4,128)S(1)}, u32[]{:S(2)}, u32[]{:S(2)}) collective-permute-start(f32[3,1024]{1,0:T(4,128)S(1)} %merge.1.refs_0_), channel_id=1, source_target_pairs={{0,12},{1,13},{2,14},{3,15},{4,8},{5,9},{6,10},{7,11},{8,4},{9,5},... | collective-permute-start | bytes 36872 | tf_op jit(solution)/shard_map/ppermute | solution.py:47
  38.3 2.4 %collective-permute-done.11.refs_2_ = f32[3,1024]{1,0:T(4,128)S(1)} collective-permute-done((f32[3,1024]{1,0:T(4,128)S(1)}, f32[3,1024]{1,0:T(4,128)S(1)}, u32[]{:S(2)}, u32[]{:S(2)}) %collective-permute-start.11) | collective-permute-done | bytes 12320 | tf_op jit(solution)/shard_map/ppermute | solution.py:47
  40.7 1.3 %first.1 = (f32[1024,1024]{1,0:T(8,128)S(1)}, f32[2,1024]{1,0:T(2,128)S(1)}, f32[1,1024]{1,0:T(1,128)S(1)}, f32[2,1024]{1,0:T(2,128)S(1)}) custom-call(f32[3,1024]{1,0:T(4,128)S(1)} %merge.1.refs_0_, f32[3,1024]{1,0:T(4,128)S(1)} %collective-permute-done.10.refs_1_, f32[3,1024]{1,0:T(4,128)S(1)} %collective-permute-done.11.refs_2_, ...), custom_call_target="tpu_custom_call" | custom-call | flops 1 | bytes 1 | tf_op jit(solution)/shard_map/first/pallas_call | solution.py:24
  43.2 2.6 %collective-permute-done.13.other_ref = f32[2,1024]{1,0:T(2,128)S(1)} collective-permute-done((f32[2,1024]{1,0:T(2,128)S(1)}, f32[2,1024]{1,0:T(2,128)S(1)}, u32[]{:S(2)}, u32[]{:S(2)}) %collective-permute-start.13) | collective-permute-done | bytes 8224 | tf_op jit(solution)/shard_map/ppermute | solution.py:47
  47.5 1.5 %collective-permute-start.17 = (f32[1,1024]{1,0:T(1,128)S(1)}, f32[1,1024]{1,0:T(1,128)S(1)}, u32[]{:S(2)}, u32[]{:S(2)}) collective-permute-start(f32[1,1024]{1,0:T(1,128)S(1)} %maximum_add_fusion.refs_0_), channel_id=1, source_target_pairs={{0,12},{1,13},{2,14},{3,15},{4,8},{5,9},{6,10},{7,11},{8,4},{9,5},... | collective-permute-start | bytes 12296 | tf_op jit(solution)/shard_map/ppermute | solution.py:47
  49.7 2.3 %collective-permute-start.19 = (f32[1,1024]{1,0:T(1,128)S(1)}, f32[1,1024]{1,0:T(1,128)S(1)}, u32[]{:S(2)}, u32[]{:S(2)}) collective-permute-start(f32[1,1024]{1,0:T(1,128)S(1)} %maximum_add_fusion.refs_0_), channel_id=1, source_target_pairs={{0,4},{1,5},{2,6},{3,7},{4,0},{5,1},{6,2},{7,3},{8,12},{9,13},{10,... | collective-permute-start | bytes 12296 | tf_op jit(solution)/shard_map/ppermute | solution.py:47
  55.1 2.6 %collective-permute-done.20.other_ref = f32[1,1024]{1,0:T(1,128)S(1)} collective-permute-done((f32[1,1024]{1,0:T(1,128)S(1)}, f32[1,1024]{1,0:T(1,128)S(1)}, u32[]{:S(2)}, u32[]{:S(2)}) %collective-permute-start.20) | collective-permute-done | bytes 4128 | tf_op jit(solution)/shard_map/ppermute | solution.py:47
  59.4 2.6 %collective-permute-start.22 = (f32[1,1024]{1,0:T(1,128)S(1)}, f32[1,1024]{1,0:T(1,128)S(1)}, u32[]{:S(2)}, u32[]{:S(2)}) collective-permute-start(f32[1,1024]{1,0:T(1,128)S(1)} %maximum_add_fusion.1.refs_0_), channel_id=1, source_target_pairs={{0,12},{1,13},{2,14},{3,15},{4,8},{5,9},{6,10},{7,11},{8,4},{9,5},... | collective-permute-start | bytes 12296 | tf_op jit(solution)/shard_map/ppermute | solution.py:47
  64.9 1.6 %collective-permute-done.23.refs_2_ = f32[1,1024]{1,0:T(1,128)S(1)} collective-permute-done((f32[1,1024]{1,0:T(1,128)S(1)}, f32[1,1024]{1,0:T(1,128)S(1)}, u32[]{:S(2)}, u32[]{:S(2)}) %collective-permute-start.23) | collective-permute-done | bytes 4128 | tf_op jit(solution)/shard_map/ppermute | solution.py:47
  68.0 2.6 %collective-permute-done.25.refs_4_.other_ref = f32[2,1024]{1,0:T(2,128)S(1)} collective-permute-done((f32[2,1024]{1,0:T(2,128)S(1)}, f32[2,1024]{1,0:T(2,128)S(1)}, u32[]{:S(2)}, u32[]{:S(2)}) %collective-permute-start.25) | collective-permute-done | bytes 8224 | tf_op jit(solution)/shard_map/ppermute | solution.py:47
  76.5 1.8 %row_part.3 = (f32[136,1024]{1,0:T(8,128)S(1)}, bf16[136,1024]{1,0:T(8,128)(2,1)S(1)}, f32[136,1024]{1,0:T(8,128)S(1)}) custom-call(bf16[1024,512]{1,0:T(8,128)(2,1)S(1)} %get-tuple-element.125.refs_0_.keep_ref, bf16[1024,384]{1,0:T(8,128)(2,1)S(1)} %collective-permute-done.26.other_ref, bf16[512,1024]{1,0:T(8,128)(2,1)S(1)} %copy-done.1, ...), custom_call_target="tpu_custom_call" | custom-call | flops 1 | bytes 1 | tf_op jit(solution)/shard_map/row_part/pallas_call | solution.py:24
  79.5 5.1 %collective-permute-done.31.other_ref = bf16[136,1024]{1,0:T(8,128)(2,1)S(1)} collective-permute-done((bf16[136,1024]{1,0:T(8,128)(2,1)S(1)}, bf16[136,1024]{1,0:T(8,128)(2,1)S(1)}, u32[]{:S(2)}, u32[]{:S(2)}) %collective-permute-start.31) | collective-permute-done | bytes 278560 | tf_op jit(solution)/shard_map/ppermute | solution.py:47
  84.6 2.0 %collective-permute-start.32 = (bf16[136,1024]{1,0:T(8,128)(2,1)S(1)}, bf16[136,1024]{1,0:T(8,128)(2,1)S(1)}, u32[]{:S(2)}, u32[]{:S(2)}) collective-permute-start(bf16[136,1024]{1,0:T(8,128)(2,1)S(1)} %line.1), channel_id=1, source_target_pairs={{0,8},{1,9},{2,10},{3,11},{4,12},{5,13},{6,14},{7,15},{8,0},{9,1},... | collective-permute-start | bytes 835592 | tf_op jit(solution)/shard_map/ppermute | solution.py:47
  87.7 6.6 %collective-permute-done.28.refs_6_ = bf16[136,1024]{1,0:T(8,128)(2,1)S(1)} collective-permute-done((bf16[136,1024]{1,0:T(8,128)(2,1)S(1)}, bf16[136,1024]{1,0:T(8,128)(2,1)S(1)}, u32[]{:S(2)}, u32[]{:S(2)}) %collective-permute-start.28) | collective-permute-done | bytes 278560 | tf_op jit(solution)/shard_map/ppermute | solution.py:47
  95.1 1.5 %col_keep.1.refs_0_ = f32[512,1024]{1,0:T(8,128)S(1)} custom-call(bf16[1024,512]{1,0:T(8,128)(2,1)S(1)} %get-tuple-element.125.refs_0_.keep_ref, bf16[1024,384]{1,0:T(8,128)(2,1)S(1)} %get-tuple-element.111.refs_1_, bf16[1024,128]{1,0:T(8,128)(2,1)S(1)} %get-tuple-element.112.refs_2_, bf16[512,1024]{1,0:T(8,128)(2,1)S(1)} %get-tuple-element.104.refs_3_.refs_8_, ...), custom_call_target="tpu_custom_call" | custom-call | flops 1 | bytes 1 | tf_op jit(solution)/shard_map/col_keep/pallas_call | solution.py:24
  96.6 1.3 %target.1.refs_4_ = f32[512,1024]{1,0:T(8,128)} custom-call(f32[512,1024]{1,0:T(8,128)S(1)} %col_keep.1.refs_0_, bf16[384,1024]{1,0:T(8,128)(2,1)S(1)} %collective-permute-done.30.refs_1_, f32[1,1024]{1,0:T(1,128)S(1)} %get-tuple-element.126.refs_2_, bf16[512,1024]{1,0:T(8,128)(2,1)S(1)} %copy-done.1), custom_call_target="tpu_custom_call" | custom-call | flops 1 | bytes 2097152 | tf_op jit(solution)/shard_map/target/pallas_call | solution.py:24
  (83 shorter events, 35.8 us)
Async XLA Ops:
  0.6 27.5 %collective-permute-start.8 = (bf16[512,1024]{1,0:T(8,128)(2,1)}, bf16[512,1024]{1,0:T(8,128)(2,1)S(1)}, u32[]{:S(2)}, u32[]{:S(2)}) collective-permute-start(bf16[512,1024]{1,0:T(8,128)(2,1)} %refs_3_.3), channel_id=1, source_target_pairs={{0,2},{1,3},{2,0},{3,1},{4,6},{5,7},{6,4},{7,5},{8,10},{9,11},{10,... | collective-permute-start | bytes 3145736 | tf_op jit(solution)/shard_map/ppermute | solution.py:47
  3.7 5.0 %collective-permute-start.1 = (bf16[128,1024]{1,0:T(8,128)(2,1)}, bf16[128,1024]{1,0:T(8,128)(2,1)S(1)}, u32[]{:S(2)}, u32[]{:S(2)}) collective-permute-start(bf16[128,1024]{1,0:T(8,128)(2,1)} %refs_0_.1), channel_id=1, source_target_pairs={{0,1},{1,0},{2,3},{3,2},{4,5},{5,4},{6,7},{7,6},{8,9},{9,8},{10,11... | collective-permute-start | bytes 786440 | tf_op jit(solution)/shard_map/ppermute | solution.py:47
  3.7 15.6 %collective-permute-start = (bf16[128,1024]{1,0:T(8,128)(2,1)}, bf16[128,1024]{1,0:T(8,128)(2,1)S(1)}, u32[]{:S(2)}, u32[]{:S(2)}) collective-permute-start(bf16[128,1024]{1,0:T(8,128)(2,1)} %refs_0_.1), channel_id=1, source_target_pairs={{0,8},{1,9},{2,10},{3,11},{4,12},{5,13},{6,14},{7,15},{8,0},{9,1},... | collective-permute-start | bytes 786440 | tf_op jit(solution)/shard_map/ppermute | solution.py:47
  6.3 13.2 %collective-permute-start.4 = (bf16[128,1024]{1,0:T(8,128)(2,1)}, bf16[128,1024]{1,0:T(8,128)(2,1)S(1)}, u32[]{:S(2)}, u32[]{:S(2)}) collective-permute-start(bf16[128,1024]{1,0:T(8,128)(2,1)} %refs_0_.1), channel_id=1, source_target_pairs={{0,4},{1,5},{2,6},{3,7},{4,0},{5,1},{6,2},{7,3},{8,12},{9,13},{10,... | collective-permute-start | bytes 786440 | tf_op jit(solution)/shard_map/ppermute | solution.py:47
  19.7 8.4 %collective-permute-start.2 = (bf16[128,1024]{1,0:T(8,128)(2,1)S(1)}, bf16[128,1024]{1,0:T(8,128)(2,1)S(1)}, u32[]{:S(2)}, u32[]{:S(2)}) collective-permute-start(bf16[128,1024]{1,0:T(8,128)(2,1)S(1)} %collective-permute-done.refs_0_), channel_id=1, source_target_pairs={{0,4},{1,5},{2,6},{3,7},{4,0},{5,1},{6,2},{7,3},{8,12},{9,13},{10,... | collective-permute-start | bytes 786440 | tf_op jit(solution)/shard_map/ppermute | solution.py:47
  20.8 6.2 %collective-permute-start.3 = (f32[1,512]{1,0:T(1,128)S(1)}, f32[1,512]{1,0:T(1,128)S(1)}, u32[]{:S(2)}, u32[]{:S(2)}) collective-permute-start(f32[1,512]{1,0:T(1,128)S(1)} %bitcast.8), channel_id=1, source_target_pairs={{0,2},{1,3},{2,0},{3,1},{4,6},{5,7},{6,4},{7,5},{8,10},{9,11},{10,... | collective-permute-start | bytes 6152 | tf_op jit(solution)/shard_map/ppermute | solution.py:47
  32.7 5.6 %collective-permute-start.10 = (f32[3,1024]{1,0:T(4,128)S(1)}, f32[3,1024]{1,0:T(4,128)S(1)}, u32[]{:S(2)}, u32[]{:S(2)}) collective-permute-start(f32[3,1024]{1,0:T(4,128)S(1)} %merge.1.refs_0_), channel_id=1, source_target_pairs={{0,12},{1,13},{2,14},{3,15},{4,8},{5,9},{6,10},{7,11},{8,4},{9,5},... | collective-permute-start | bytes 36872 | tf_op jit(solution)/shard_map/ppermute | solution.py:47
  36.0 4.6 %collective-permute-start.11 = (f32[3,1024]{1,0:T(4,128)S(1)}, f32[3,1024]{1,0:T(4,128)S(1)}, u32[]{:S(2)}, u32[]{:S(2)}) collective-permute-start(f32[3,1024]{1,0:T(4,128)S(1)} %merge.1.refs_0_), channel_id=1, source_target_pairs={{0,8},{1,9},{2,10},{3,11},{4,12},{5,13},{6,14},{7,15},{8,0},{9,1},... | collective-permute-start | bytes 36872 | tf_op jit(solution)/shard_map/ppermute | solution.py:47
  36.0 4.6 %collective-permute-start.12 = (f32[3,1024]{1,0:T(4,128)S(1)}, f32[3,1024]{1,0:T(4,128)S(1)}, u32[]{:S(2)}, u32[]{:S(2)}) collective-permute-start(f32[3,1024]{1,0:T(4,128)S(1)} %merge.1.refs_0_), channel_id=1, source_target_pairs={{0,4},{1,5},{2,6},{3,7},{4,0},{5,1},{6,2},{7,3},{8,12},{9,13},{10,... | collective-permute-start | bytes 36872 | tf_op jit(solution)/shard_map/ppermute | solution.py:47
  37.2 9.1 %collective-permute-start.14 = (bf16[512,1024]{1,0:T(8,128)(2,1)S(1)}, bf16[512,1024]{1,0:T(8,128)(2,1)S(1)}, u32[]{:S(2)}, u32[]{:S(2)}) collective-permute-start(bf16[512,1024]{1,0:T(8,128)(2,1)S(1)} %copy-done.1), channel_id=1, source_target_pairs={{0,1},{1,0},{2,3},{3,2},{4,5},{5,4},{6,7},{7,6},{8,9},{9,8},{10,11... | collective-permute-start | bytes 3145736 | tf_op jit(solution)/shard_map/ppermute | solution.py:47
  42.0 4.3 %collective-permute-start.15 = (bf16[512,1024]{1,0:T(8,128)(2,1)S(1)}, bf16[512,1024]{1,0:T(8,128)(2,1)S(1)}, u32[]{:S(2)}, u32[]{:S(2)}) collective-permute-start(bf16[512,1024]{1,0:T(8,128)(2,1)S(1)} %collective-permute-done.8.refs_2_.refs_3_.refs_1_), channel_id=1, source_target_pairs={{0,1},{1,0},{2,3},{3,2},{4,5},{5,4},{6,7},{7,6},{8,9},{9,8},{10,11... | collective-permute-start | bytes 3145736 | tf_op jit(solution)/shard_map/ppermute | solution.py:47
  42.1 3.7 %collective-permute-start.13 = (f32[2,1024]{1,0:T(2,128)S(1)}, f32[2,1024]{1,0:T(2,128)S(1)}, u32[]{:S(2)}, u32[]{:S(2)}) collective-permute-start(f32[2,1024]{1,0:T(2,128)S(1)} %get-tuple-element.96.own_ref), channel_id=1, source_target_pairs={{0,2},{1,3},{2,0},{3,1},{4,6},{5,7},{6,4},{7,5},{8,10},{9,11},{10,... | collective-permute-start | bytes 24584 | tf_op jit(solution)/shard_map/ppermute | solution.py:47
  47.5 5.5 %collective-permute-start.17 = (f32[1,1024]{1,0:T(1,128)S(1)}, f32[1,1024]{1,0:T(1,128)S(1)}, u32[]{:S(2)}, u32[]{:S(2)}) collective-permute-start(f32[1,1024]{1,0:T(1,128)S(1)} %maximum_add_fusion.refs_0_), channel_id=1, source_target_pairs={{0,12},{1,13},{2,14},{3,15},{4,8},{5,9},{6,10},{7,11},{8,4},{9,5},... | collective-permute-start | bytes 12296 | tf_op jit(solution)/shard_map/ppermute | solution.py:47
  49.1 4.5 %collective-permute-start.18 = (f32[1,1024]{1,0:T(1,128)S(1)}, f32[1,1024]{1,0:T(1,128)S(1)}, u32[]{:S(2)}, u32[]{:S(2)}) collective-permute-start(f32[1,1024]{1,0:T(1,128)S(1)} %maximum_add_fusion.refs_0_), channel_id=1, source_target_pairs={{0,8},{1,9},{2,10},{3,11},{4,12},{5,13},{6,14},{7,15},{8,0},{9,1},... | collective-permute-start | bytes 12296 | tf_op jit(solution)/shard_map/ppermute | solution.py:47
  49.7 3.9 %collective-permute-start.19 = (f32[1,1024]{1,0:T(1,128)S(1)}, f32[1,1024]{1,0:T(1,128)S(1)}, u32[]{:S(2)}, u32[]{:S(2)}) collective-permute-start(f32[1,1024]{1,0:T(1,128)S(1)} %maximum_add_fusion.refs_0_), channel_id=1, source_target_pairs={{0,4},{1,5},{2,6},{3,7},{4,0},{5,1},{6,2},{7,3},{8,12},{9,13},{10,... | collective-permute-start | bytes 12296 | tf_op jit(solution)/shard_map/ppermute | solution.py:47
  59.4 5.5 %collective-permute-start.22 = (f32[1,1024]{1,0:T(1,128)S(1)}, f32[1,1024]{1,0:T(1,128)S(1)}, u32[]{:S(2)}, u32[]{:S(2)}) collective-permute-start(f32[1,1024]{1,0:T(1,128)S(1)} %maximum_add_fusion.1.refs_0_), channel_id=1, source_target_pairs={{0,12},{1,13},{2,14},{3,15},{4,8},{5,9},{6,10},{7,11},{8,4},{9,5},... | collective-permute-start | bytes 12296 | tf_op jit(solution)/shard_map/ppermute | solution.py:47
  62.0 4.5 %collective-permute-start.23 = (f32[1,1024]{1,0:T(1,128)S(1)}, f32[1,1024]{1,0:T(1,128)S(1)}, u32[]{:S(2)}, u32[]{:S(2)}) collective-permute-start(f32[1,1024]{1,0:T(1,128)S(1)} %maximum_add_fusion.1.refs_0_), channel_id=1, source_target_pairs={{0,8},{1,9},{2,10},{3,11},{4,12},{5,13},{6,14},{7,15},{8,0},{9,1},... | collective-permute-start | bytes 12296 | tf_op jit(solution)/shard_map/ppermute | solution.py:47
  66.9 3.7 %collective-permute-start.25 = (f32[2,1024]{1,0:T(2,128)S(1)}, f32[2,1024]{1,0:T(2,128)S(1)}, u32[]{:S(2)}, u32[]{:S(2)}) collective-permute-start(f32[2,1024]{1,0:T(2,128)S(1)} %get-tuple-element.107.refs_3_.own_ref), channel_id=1, source_target_pairs={{0,2},{1,3},{2,0},{3,1},{4,6},{5,7},{6,4},{7,5},{8,10},{9,11},{10,... | collective-permute-start | bytes 24584 | tf_op jit(solution)/shard_map/ppermute | solution.py:47
  71.2 5.3 %collective-permute-start.26 = (bf16[1024,384]{1,0:T(8,128)(2,1)S(1)}, bf16[1024,384]{1,0:T(8,128)(2,1)S(1)}, u32[]{:S(2)}, u32[]{:S(2)}) collective-permute-start(bf16[1024,384]{1,0:T(8,128)(2,1)S(1)} %get-tuple-element.111.refs_1_), channel_id=1, source_target_pairs={{0,1},{1,0},{2,3},{3,2},{4,5},{5,4},{6,7},{7,6},{8,9},{9,8},{10,11... | collective-permute-start | bytes 2359304 | tf_op jit(solution)/shard_map/ppermute | solution.py:47
  72.9 23.7 %collective-permute-start.30 = (bf16[384,1024]{1,0:T(8,128)(2,1)S(1)}, bf16[384,1024]{1,0:T(8,128)(2,1)S(1)}, u32[]{:S(2)}, u32[]{:S(2)}) collective-permute-start(bf16[384,1024]{1,0:T(8,128)(2,1)S(1)} %col_send.2), channel_id=1, source_target_pairs={{0,2},{1,3},{2,0},{3,1},{4,6},{5,7},{6,4},{7,5},{8,10},{9,11},{10,... | collective-permute-start | bytes 2359304 | tf_op jit(solution)/shard_map/ppermute | solution.py:47
  75.0 9.6 %collective-permute-start.31 = (bf16[136,1024]{1,0:T(8,128)(2,1)S(1)}, bf16[136,1024]{1,0:T(8,128)(2,1)S(1)}, u32[]{:S(2)}, u32[]{:S(2)}) collective-permute-start(bf16[136,1024]{1,0:T(8,128)(2,1)S(1)} %row_part.2), channel_id=1, source_target_pairs={{0,4},{1,5},{2,6},{3,7},{4,0},{5,1},{6,2},{7,3},{8,12},{9,13},{10,... | collective-permute-start | bytes 835592 | tf_op jit(solution)/shard_map/ppermute | solution.py:47
  78.3 15.9 %collective-permute-start.28 = (bf16[136,1024]{1,0:T(8,128)(2,1)S(1)}, bf16[136,1024]{1,0:T(8,128)(2,1)S(1)}, u32[]{:S(2)}, u32[]{:S(2)}) collective-permute-start(bf16[136,1024]{1,0:T(8,128)(2,1)S(1)} %get-tuple-element.122), channel_id=1, source_target_pairs={{0,4},{1,5},{2,6},{3,7},{4,0},{5,1},{6,2},{7,3},{8,12},{9,13},{10,... | collective-permute-start | bytes 835592 | tf_op jit(solution)/shard_map/ppermute | solution.py:47
  84.6 13.8 %collective-permute-start.32 = (bf16[136,1024]{1,0:T(8,128)(2,1)S(1)}, bf16[136,1024]{1,0:T(8,128)(2,1)S(1)}, u32[]{:S(2)}, u32[]{:S(2)}) collective-permute-start(bf16[136,1024]{1,0:T(8,128)(2,1)S(1)} %line.1), channel_id=1, source_target_pairs={{0,8},{1,9},{2,10},{3,11},{4,12},{5,13},{6,14},{7,15},{8,0},{9,1},... | collective-permute-start | bytes 835592 | tf_op jit(solution)/shard_map/ppermute | solution.py:47
  86.7 11.5 %collective-permute-start.29 = (bf16[128,1024]{1,0:T(8,128)(2,1)S(1)}, bf16[128,1024]{1,0:T(8,128)(2,1)S(1)}, u32[]{:S(2)}, u32[]{:S(2)}) collective-permute-start(bf16[128,1024]{1,0:T(8,128)(2,1)S(1)} %col_send.3), channel_id=1, source_target_pairs={{0,2},{1,3},{2,0},{3,1},{4,6},{5,7},{6,4},{7,5},{8,10},{9,11},{10,... | collective-permute-start | bytes 786440 | tf_op jit(solution)/shard_map/ppermute | solution.py:47
  (15 other events, 34.0 us)

commit v9 on v8

--- a/solution.py
+++ b/solution.py
@@ -91,7 +91,7 @@
 
 
 def potential_kernel(
-    count, scale, me_ref, own_ref, other_ref, g_ref, logb_ref, y_ref, source_ref, target_ref
+    count, scale, me_ref, own_ref, other_ref, g_ref, last_ref, y_ref, source_ref, target_ref
 ):
     rows = source_ref.shape[1] // count
     lines = count // 4
@@ -104,7 +104,7 @@
     cols = target_ref.shape[1]
     wide = y_ref[...].astype(F32)
     square = to_row(jnp.sum(wide * wide, axis=1, keepdims=True))
-    target_ref[...] = g_ref[:, :cols] + logb_ref[:, :cols] + scale * square
+    target_ref[...] = g_ref[:, :cols] + jnp.log(last_ref[:, :cols]) + scale * square
 
 
 def diagonal():
@@ -252,22 +252,27 @@
         col_ref[1:2, :] = rest[0][...] + jnp.log(a)
 
 
-def plan_kernel(source_count, *refs):
-    e_ref, a_ref, h_ref, own_ref, other_ref, logit_ref, phi_ref = refs[:7]
-    keep_ref, near_ref, far_ref, mass_ref, logb_ref = refs[7:]
-    c = own_ref[0:1, :] + turn(other_ref[0:1, :])
-    logb_ref[...] = -jnp.log(c)
+def store_plan(e_ref, a, share, outs):
+    for t in tiles(e_ref.shape[0]):
+        plan = ((e_ref[t, :] * a) * to_column(share[:, t])).astype(BF16)
+        start = 0
+        for ref in outs:
+            ref[t, :] = plan[:, start : start + ref.shape[1]]
+            start += ref.shape[1]
+
+
+def early_plan_kernel(source_count, e_ref, a_ref, h_ref, logit_ref, phi_ref, *outs):
+    *outs, mass_ref = outs
     mass = jnp.exp(logit_ref[...]) * (source_count / h_ref[1:2, :1])
     mass_ref[...] = mass
-    share = mass * phi_ref[...] / c
-    half = keep_ref.shape[1]
-    split = half + near_ref.shape[1]
-    a = a_ref[...]
-    for t in tiles(e_ref.shape[0]):
-        plan = ((e_ref[t, :] * a) * to_column(share[:, t])).astype(BF16)
-        keep_ref[t, :] = plan[:, :half]
-        near_ref[t, :] = plan[:, half:split]
-        far_ref[t, :] = plan[:, split:]
+    store_plan(e_ref, a_ref[...], mass * phi_ref[...], outs)
+
+
+def plan_kernel(e_ref, a_ref, mass_ref, own_ref, other_ref, phi_ref, *outs):
+    *outs, last_ref = outs
+    last = 1.0 / (own_ref[0:1, :] + turn(other_ref[0:1, :]))
+    last_ref[...] = last
+    store_plan(e_ref, a_ref[...], mass_ref[...] * phi_ref[...] * last, outs)
 
 
 def split_mass(mass, width):
@@ -343,13 +348,16 @@
     out_ref[...] = col_part(*refs, slice(0, out_ref.shape[0]))
 
 
-def target_rows(factor, cols, own_ref, other_ref, mass_ref, y_ref, out_ref, held_ref, sem_ref):
+def target_rows(
+    factor, cols, own_ref, other_ref, mass_ref, last_ref, y_ref, out_ref, held_ref, sem_ref
+):
     count = cols.stop - cols.start
-    mass = mass_ref[:, cols]
+    mass, last = mass_ref[:, cols], last_ref[:, cols]
     copies = []
     for n, t in enumerate(slice(i, i + 128) for i in range(0, count, 128)):
         here = slice(cols.start + t.start, cols.start + t.stop)
         part = own_ref[here, :] + other_ref[t, :].astype(F32)
+        part = to_column(last[:, t]) * part
         held_ref[t, :] = factor * (to_column(mass[:, t]) * y_ref[here, :].astype(F32) - part)
         copies.append(pltpu.make_async_copy(held_ref.at[t], out_ref.at[here], sem_ref.at[n]))
         copies[-1].start()
@@ -362,7 +370,7 @@
 
 
 def last_kernel(factor, cols, *refs):
-    target_ins, (_, own_ref, near_ref, far_ref, x_ref), refs = refs[:4], refs[4:9], refs[9:]
+    target_ins, (_, own_ref, near_ref, far_ref, x_ref), refs = refs[:5], refs[5:10], refs[10:]
     target_out, source_out, held_target, sem_target, held_source, sem_source = refs
     source_kernel(own_ref, near_ref, far_ref, x_ref, held_source)
     first = pltpu.make_async_copy(held_source, source_out, sem_source)
@@ -533,27 +541,33 @@
     base = q - source_log + source_sq.reshape(1, mine)
     col, a = columns(row, base)
     col_other = swap(col, 2)
-    keep, *sends, mass, logb = call(
-        functools.partial(plan_kernel, source_count),
-        "plan",
-        [e, a, h, col, col_other, logits, phi],
-        [shape((2 * cols, half), BF16)]
-        + [shape((2 * cols, size), BF16) for size in (half * 3 // 4, half // 4)]
-        + [lane_shape, lane_shape],
-    )
-
-    def col_send(p, keep):
+    plan_shapes = [shape((2 * cols, n), BF16) for n in (half, half * 3 // 4, half // 4)]
+    *early, mass = call(
+        functools.partial(early_plan_kernel, source_count),
+        "early_plan",
+        [e, a, h, logits, phi],
+        plan_shapes + [lane_shape],
+    )
+
+    def col_send(p, first):
         piece = slice(cols + parts[p].start, cols + parts[p].stop)
         (out,) = call(
             functools.partial(col_send_kernel, piece),
             "col_send",
-            [keep, *sends, x0, x1],
+            [first, *early[1:], x0, x1],
             [shape((parts[p].stop - parts[p].start, width), BF16)],
         )
         return out
 
-    out = col_send(0, keep)
+    out = col_send(0, early[0])
     back = [swap(out, 2)]
+    col_last, _ = lax.optimization_barrier((col_other, out))
+    keep, *sends, final = call(
+        plan_kernel,
+        "plan",
+        [e, a, mass, col, col_last, phi],
+        plan_shapes + [lane_shape],
+    )
     if direct:
         others = [None, swap(sends[1], 1)]
         others[0] = swap(sends[0], 1)
@@ -570,10 +584,10 @@
                 outs,
             )
 
-        (out3,) = row_parts(True, out)
+        (out3,) = row_parts(True, keep)
         near3 = swap(out3, 4)
-        keep_gated, _ = lax.optimization_barrier((keep, out3))
-        out = col_send(1, keep_gated)
+        first, _ = lax.optimization_barrier((early[0], out3))
+        out = col_send(1, first)
         back.append(swap(out, 2))
         own0, out1, own2 = row_parts(False, out)
         near1 = swap(out1, 4)
@@ -582,7 +596,7 @@
         ends = [own0, near1, far2, x0]
         gate = near1
     else:
-        out = col_send(1, keep)
+        out = col_send(1, early[0])
         back.append(swap(out, 2))
         gate = out
         plan = jnp.concatenate([keep, *sends], axis=1)
@@ -597,19 +611,19 @@
             source_feats.astype(F32)
         ) - lax.psum_scatter(full, AXIS, scatter_dimension=0)
 
-    logb, _ = lax.optimization_barrier((logb, gate))
+    final, _ = lax.optimization_barrier((final, gate))
     potential_src, potential_tgt = call(
         functools.partial(potential_kernel, count, scale),
         "potential",
-        [here, col, col_other, g, logb, target_feats],
+        [here, col, col_other, g, final, target_feats],
         [shape((1, source_count)), shape((1, cols))],
         scalar=True,
     )
-    keep_later, _ = lax.optimization_barrier((keep, potential_tgt))
+    first, _ = lax.optimization_barrier((early[0], potential_tgt))
     (own_col,) = call(
         col_keep_kernel,
         "col_keep",
-        [keep_later, *sends, x0, x1],
+        [first, *early[1:], x0, x1],
         [shape((cols, width))],
     )
     factor = target_count / source_count
@@ -618,7 +632,7 @@
         size = parts[p].stop - parts[p].start
         return [pltpu.VMEM((size, width), F32), pltpu.SemaphoreType.DMA((size // 128,))]
 
-    ins = [own_col, back[0], mass, target_feats]
+    ins = [own_col, back[0], mass, final, target_feats]
     (grad_target,) = call(
         functools.partial(target_kernel, factor, parts[0]),
         "target",
@@ -628,8 +642,8 @@
         out_hbm=True,
         scratch_shapes=held(0),
     )
-    ins = [own_col, back[1], mass, target_feats, grad_target]
-    kw = dict(size=cols * width, in_hbm=(4,), out_hbm=True, input_output_aliases={4: 0})
+    ins = [own_col, back[1], mass, final, target_feats, grad_target]
+    kw = dict(size=cols * width, in_hbm=(5,), out_hbm=True, input_output_aliases={5: 0})
     if direct:
         grad_target, grad_source = call(
             functools.partial(last_kernel, factor, parts[1]),
@@ -641,7 +655,7 @@
         )
     else:
         (grad_target,) = call(
-            lambda *refs: target_kernel(factor, parts[1], *refs[:4], *refs[5:]),
+            lambda *refs: target_kernel(factor, parts[1], *refs[:5], *refs[6:]),
             "target",
             ins,
             [shape((cols, width))],

time: 100 us -> 100 us (level)
    pallas_call x22 -> x23, Pallas kernels: 18.8 us -> 19.3 us  [call(): pl.pallas_call(body, name=name, out_shape=outs, in_specs=specs, out_specs...]
  transfers between devices with their start and end apart: 33 -> 33, of which waited for: 20 -> 20; matrix products, arithmetic and copies ran while one was open for 1% -> 1% of each run, Pallas kernels for 14% -> 15%
where the time goes in v9:
time: 100 us; the launch traced here: 99.8 us
  waiting for transfers between devices  41.3 us (41%)
  starting transfers between devices  33.4 us (33%)
  Pallas kernels  19.3 us (19%)
  local copies, waits for them, and re-layouts  4.27 us (4%)
  between operations  1.02 us (1%)
    ppermute x33, waiting for transfers between devices, swap(): return lax.ppermute(value, AXIS, [(i, i ^ mask) for i in range(count)])  41.3 us
    ppermute x33, starting transfers between devices, swap(): return lax.ppermute(value, AXIS, [(i, i ^ mask) for i in range(count)])  33.4 us
    pallas_call x23, Pallas kernels, call(): pl.pallas_call(body, name=name, out_shape=outs, in_specs=specs, out_specs...  19.3 us
    unnamed x12, local copies, waits for them, and re-layouts  4.27 us
  transfers between devices with their start and end apart: 33, of which 20 were waited for; matrix products, arithmetic and copies ran while one was open for 1% of the time, Pallas kernels for 15%

profile of v9, /device:TPU:0, one launch (start us, length us, event | category | flops | bytes accessed | tf_op | source)
XLA Modules:
  0.0 99.8 jit_solution(5553520284288587322)
XLA Ops:
  0.6 3.0 %collective-permute-start.8 = (bf16[512,1024]{1,0:T(8,128)(2,1)}, bf16[512,1024]{1,0:T(8,128)(2,1)S(1)}, u32[]{:S(2)}, u32[]{:S(2)}) collective-permute-start(bf16[512,1024]{1,0:T(8,128)(2,1)} %refs_4_.3), channel_id=1, source_target_pairs={{0,2},{1,3},{2,0},{3,1},{4,6},{5,7},{6,4},{7,5},{8,10},{9,11},{10,... | collective-permute-start | bytes 3145736 | tf_op jit(solution)/shard_map/ppermute | solution.py:47
  3.7 2.6 %collective-permute-start = (bf16[128,1024]{1,0:T(8,128)(2,1)}, bf16[128,1024]{1,0:T(8,128)(2,1)S(1)}, u32[]{:S(2)}, u32[]{:S(2)}) collective-permute-start(bf16[128,1024]{1,0:T(8,128)(2,1)} %refs_0_.1), channel_id=1, source_target_pairs={{0,8},{1,9},{2,10},{3,11},{4,12},{5,13},{6,14},{7,15},{8,0},{9,1},... | collective-permute-start | bytes 786440 | tf_op jit(solution)/shard_map/ppermute | solution.py:47
  6.3 1.6 %collective-permute-start.4 = (bf16[128,1024]{1,0:T(8,128)(2,1)}, bf16[128,1024]{1,0:T(8,128)(2,1)S(1)}, u32[]{:S(2)}, u32[]{:S(2)}) collective-permute-start(bf16[128,1024]{1,0:T(8,128)(2,1)} %refs_0_.1), channel_id=1, source_target_pairs={{0,4},{1,5},{2,6},{3,7},{4,0},{5,1},{6,2},{7,3},{8,12},{9,13},{10,... | collective-permute-start | bytes 786440 | tf_op jit(solution)/shard_map/ppermute | solution.py:47
  8.7 1.2 %copy-done = bf16[512,1024]{1,0:T(8,128)(2,1)S(1)} copy-done((bf16[512,1024]{1,0:T(8,128)(2,1)S(1)}, bf16[512,1024]{1,0:T(8,128)(2,1)}, u32[]{:S(2)}) %copy-start) | copy-done | bytes 1048600
  13.2 6.1 %collective-permute-done.refs_0_ = bf16[128,1024]{1,0:T(8,128)(2,1)S(1)} collective-permute-done((bf16[128,1024]{1,0:T(8,128)(2,1)}, bf16[128,1024]{1,0:T(8,128)(2,1)S(1)}, u32[]{:S(2)}, u32[]{:S(2)}) %collective-permute-start) | collective-permute-done | bytes 262176 | tf_op jit(solution)/shard_map/ppermute | solution.py:47
  23.0 4.0 %collective-permute-done.3.refs_3_ = f32[1,512]{1,0:T(1,128)S(1)} collective-permute-done((f32[1,512]{1,0:T(1,128)S(1)}, f32[1,512]{1,0:T(1,128)S(1)}, u32[]{:S(2)}, u32[]{:S(2)}) %collective-permute-start.3) | collective-permute-done | bytes 2080 | tf_op jit(solution)/shard_map/ppermute | solution.py:47
  28.1 1.7 %cost.8 = (f32[1024,512]{1,0:T(8,128)S(1)}, f32[1024,512]{1,0:T(8,128)S(1)}, f32[3,1024]{1,0:T(4,128)S(1)}, f32[512,1]{1,0:T(8,128)S(1)}) custom-call(bf16[512,1024]{1,0:T(8,128)(2,1)S(1)} %get-tuple-element.87.refs_0_.refs_9_, bf16[512,1024]{1,0:T(8,128)(2,1)S(1)} %get-tuple-element.88.refs_1_.refs_10_, ...), custom_call_target="tpu_custom_call", output_to_operand_aliasing={{0}: (5, {}), {1}: (6, {})} | custom-call | flops 1 | bytes 1 | tf_op jit(solution)/shard_map/cost/pallas_call | solution.py:24
  29.8 1.4 %cost.9 = (f32[1024,512]{1,0:T(8,128)S(1)}, f32[1024,512]{1,0:T(8,128)S(1)}, bf16[512,1024]{1,0:T(8,128)(2,1)S(1)}, bf16[512,1024]{1,0:T(8,128)(2,1)S(1)}, f32[3,1024]{1,0:T(4,128)S(1)}) custom-call(bf16[128,1024]{1,0:T(8,128)(2,1)S(1)} %collective-permute-done.2.refs_0_, ...), custom_call_target="tpu_custom_call", output_to_operand_aliasing={{0}: (7, {}), {1}: (8, {}), {2}: (9, {}), {3}: (10, {})} | custom-call | flops 1 | bytes 1 | tf_op jit(solution)/shard_map/cost/pallas_call | solution.py:24
  32.7 3.3 %collective-permute-start.10 = (f32[3,1024]{1,0:T(4,128)S(1)}, f32[3,1024]{1,0:T(4,128)S(1)}, u32[]{:S(2)}, u32[]{:S(2)}) collective-permute-start(f32[3,1024]{1,0:T(4,128)S(1)} %merge.1.refs_0_), channel_id=1, source_target_pairs={{0,12},{1,13},{2,14},{3,15},{4,8},{5,9},{6,10},{7,11},{8,4},{9,5},... | collective-permute-start | bytes 36872 | tf_op jit(solution)/shard_map/ppermute | solution.py:47
  38.3 2.4 %collective-permute-done.11.refs_2_ = f32[3,1024]{1,0:T(4,128)S(1)} collective-permute-done((f32[3,1024]{1,0:T(4,128)S(1)}, f32[3,1024]{1,0:T(4,128)S(1)}, u32[]{:S(2)}, u32[]{:S(2)}) %collective-permute-start.11) | collective-permute-done | bytes 12320 | tf_op jit(solution)/shard_map/ppermute | solution.py:47
  40.7 1.3 %first.1 = (f32[1024,1024]{1,0:T(8,128)S(1)}, f32[2,1024]{1,0:T(2,128)S(1)}, f32[1,1024]{1,0:T(1,128)S(1)}, f32[2,1024]{1,0:T(2,128)S(1)}) custom-call(f32[3,1024]{1,0:T(4,128)S(1)} %merge.1.refs_0_, f32[3,1024]{1,0:T(4,128)S(1)} %collective-permute-done.10.refs_1_, f32[3,1024]{1,0:T(4,128)S(1)} %collective-permute-done.11.refs_2_, ...), custom_call_target="tpu_custom_call" | custom-call | flops 1 | bytes 1 | tf_op jit(solution)/shard_map/first/pallas_call | solution.py:24
  43.2 2.6 %collective-permute-done.13.other_ref = f32[2,1024]{1,0:T(2,128)S(1)} collective-permute-done((f32[2,1024]{1,0:T(2,128)S(1)}, f32[2,1024]{1,0:T(2,128)S(1)}, u32[]{:S(2)}, u32[]{:S(2)}) %collective-permute-start.13) | collective-permute-done | bytes 8224 | tf_op jit(solution)/shard_map/ppermute | solution.py:47
  47.5 1.5 %collective-permute-start.17 = (f32[1,1024]{1,0:T(1,128)S(1)}, f32[1,1024]{1,0:T(1,128)S(1)}, u32[]{:S(2)}, u32[]{:S(2)}) collective-permute-start(f32[1,1024]{1,0:T(1,128)S(1)} %maximum_add_fusion.refs_0_), channel_id=1, source_target_pairs={{0,12},{1,13},{2,14},{3,15},{4,8},{5,9},{6,10},{7,11},{8,4},{9,5},... | collective-permute-start | bytes 12296 | tf_op jit(solution)/shard_map/ppermute | solution.py:47
  49.7 2.3 %collective-permute-start.19 = (f32[1,1024]{1,0:T(1,128)S(1)}, f32[1,1024]{1,0:T(1,128)S(1)}, u32[]{:S(2)}, u32[]{:S(2)}) collective-permute-start(f32[1,1024]{1,0:T(1,128)S(1)} %maximum_add_fusion.refs_0_), channel_id=1, source_target_pairs={{0,4},{1,5},{2,6},{3,7},{4,0},{5,1},{6,2},{7,3},{8,12},{9,13},{10,... | collective-permute-start | bytes 12296 | tf_op jit(solution)/shard_map/ppermute | solution.py:47
  55.1 2.6 %collective-permute-done.20.other_ref = f32[1,1024]{1,0:T(1,128)S(1)} collective-permute-done((f32[1,1024]{1,0:T(1,128)S(1)}, f32[1,1024]{1,0:T(1,128)S(1)}, u32[]{:S(2)}, u32[]{:S(2)}) %collective-permute-start.20) | collective-permute-done | bytes 4128 | tf_op jit(solution)/shard_map/ppermute | solution.py:47
  59.4 2.6 %collective-permute-start.22 = (f32[1,1024]{1,0:T(1,128)S(1)}, f32[1,1024]{1,0:T(1,128)S(1)}, u32[]{:S(2)}, u32[]{:S(2)}) collective-permute-start(f32[1,1024]{1,0:T(1,128)S(1)} %maximum_add_fusion.1.refs_0_), channel_id=1, source_target_pairs={{0,12},{1,13},{2,14},{3,15},{4,8},{5,9},{6,10},{7,11},{8,4},{9,5},... | collective-permute-start | bytes 12296 | tf_op jit(solution)/shard_map/ppermute | solution.py:47
  64.9 1.6 %collective-permute-done.23.refs_2_ = f32[1,1024]{1,0:T(1,128)S(1)} collective-permute-done((f32[1,1024]{1,0:T(1,128)S(1)}, f32[1,1024]{1,0:T(1,128)S(1)}, u32[]{:S(2)}, u32[]{:S(2)}) %collective-permute-start.23) | collective-permute-done | bytes 4128 | tf_op jit(solution)/shard_map/ppermute | solution.py:47
  76.2 1.8 %row_part.3 = (f32[136,1024]{1,0:T(8,128)S(1)}, bf16[136,1024]{1,0:T(8,128)(2,1)S(1)}, f32[136,1024]{1,0:T(8,128)S(1)}) custom-call(bf16[1024,512]{1,0:T(8,128)(2,1)S(1)} %get-tuple-element.129.keep_ref, bf16[1024,384]{1,0:T(8,128)(2,1)S(1)} %collective-permute-done.26.other_ref, bf16[512,1024]{1,0:T(8,128)(2,1)S(1)} %copy-done.1, ...), custom_call_target="tpu_custom_call" | custom-call | flops 1 | bytes 1 | tf_op jit(solution)/shard_map/row_part/pallas_call | solution.py:24
  79.3 5.0 %collective-permute-done.31.other_ref = bf16[136,1024]{1,0:T(8,128)(2,1)S(1)} collective-permute-done((bf16[136,1024]{1,0:T(8,128)(2,1)S(1)}, bf16[136,1024]{1,0:T(8,128)(2,1)S(1)}, u32[]{:S(2)}, u32[]{:S(2)}) %collective-permute-start.31) | collective-permute-done | bytes 278560 | tf_op jit(solution)/shard_map/ppermute | solution.py:47
  84.4 2.1 %collective-permute-start.32 = (bf16[136,1024]{1,0:T(8,128)(2,1)S(1)}, bf16[136,1024]{1,0:T(8,128)(2,1)S(1)}, u32[]{:S(2)}, u32[]{:S(2)}) collective-permute-start(bf16[136,1024]{1,0:T(8,128)(2,1)S(1)} %line.1), channel_id=1, source_target_pairs={{0,8},{1,9},{2,10},{3,11},{4,12},{5,13},{6,14},{7,15},{8,0},{9,1},... | collective-permute-start | bytes 835592 | tf_op jit(solution)/shard_map/ppermute | solution.py:47
  87.5 6.5 %collective-permute-done.28.refs_7_ = bf16[136,1024]{1,0:T(8,128)(2,1)S(1)} collective-permute-done((bf16[136,1024]{1,0:T(8,128)(2,1)S(1)}, bf16[136,1024]{1,0:T(8,128)(2,1)S(1)}, u32[]{:S(2)}, u32[]{:S(2)}) %collective-permute-start.28) | collective-permute-done | bytes 278560 | tf_op jit(solution)/shard_map/ppermute | solution.py:47
  94.9 1.5 %col_keep.1.refs_0_ = f32[512,1024]{1,0:T(8,128)S(1)} custom-call(bf16[1024,512]{1,0:T(8,128)(2,1)S(1)} %get-tuple-element.134.refs_0_, bf16[1024,384]{1,0:T(8,128)(2,1)S(1)} %get-tuple-element.115.refs_1_, bf16[1024,128]{1,0:T(8,128)(2,1)S(1)} %get-tuple-element.116.refs_2_, bf16[512,1024]{1,0:T(8,128)(2,1)S(1)} %get-tuple-element.108.refs_3_.refs_9_, ...), custom_call_target="tpu_custom_call" | custom-call | flops 1 | bytes 1 | tf_op jit(solution)/shard_map/col_keep/pallas_call | solution.py:24
  96.4 1.4 %target.1.refs_5_ = f32[512,1024]{1,0:T(8,128)} custom-call(f32[512,1024]{1,0:T(8,128)S(1)} %col_keep.1.refs_0_, bf16[384,1024]{1,0:T(8,128)(2,1)S(1)} %collective-permute-done.30.refs_1_, f32[1,1024]{1,0:T(1,128)S(1)} %get-tuple-element.114.mass_ref.refs_2_, f32[1,1024]{1,0:T(1,128)S(1)} %get-tuple-element.132.last_ref.refs_3_, bf16[512,1024]{1,0:T(8,128)(2,1)S(1)} %copy-done.1), custom_call_target="tpu_custom_call" | custom-call | flops 1 | bytes 2097152 | tf_op jit(solution)/shard_map/target/pallas_call | solution.py:24
  98.4 1.2 %last.1 = (f32[512,1024]{1,0:T(8,128)}, f32[128,1024]{1,0:T(8,128)}) custom-call(f32[512,1024]{1,0:T(8,128)S(1)} %col_keep.1.refs_0_, bf16[128,1024]{1,0:T(8,128)(2,1)S(1)} %collective-permute-done.29.refs_1_, f32[1,1024]{1,0:T(1,128)S(1)} %get-tuple-element.114.mass_ref.refs_2_, ...), custom_call_target="tpu_custom_call", output_to_operand_aliasing={{0}: (5, {})} | custom-call | flops 1 | bytes 524288 | tf_op jit(solution)/shard_map/last/pallas_call | solution.py:24
  (84 shorter events, 37.3 us)
Async XLA Ops:
  0.6 27.5 %collective-permute-start.8 = (bf16[512,1024]{1,0:T(8,128)(2,1)}, bf16[512,1024]{1,0:T(8,128)(2,1)S(1)}, u32[]{:S(2)}, u32[]{:S(2)}) collective-permute-start(bf16[512,1024]{1,0:T(8,128)(2,1)} %refs_4_.3), channel_id=1, source_target_pairs={{0,2},{1,3},{2,0},{3,1},{4,6},{5,7},{6,4},{7,5},{8,10},{9,11},{10,... | collective-permute-start | bytes 3145736 | tf_op jit(solution)/shard_map/ppermute | solution.py:47
  3.7 5.0 %collective-permute-start.1 = (bf16[128,1024]{1,0:T(8,128)(2,1)}, bf16[128,1024]{1,0:T(8,128)(2,1)S(1)}, u32[]{:S(2)}, u32[]{:S(2)}) collective-permute-start(bf16[128,1024]{1,0:T(8,128)(2,1)} %refs_0_.1), channel_id=1, source_target_pairs={{0,1},{1,0},{2,3},{3,2},{4,5},{5,4},{6,7},{7,6},{8,9},{9,8},{10,11... | collective-permute-start | bytes 786440 | tf_op jit(solution)/shard_map/ppermute | solution.py:47
  3.7 15.6 %collective-permute-start = (bf16[128,1024]{1,0:T(8,128)(2,1)}, bf16[128,1024]{1,0:T(8,128)(2,1)S(1)}, u32[]{:S(2)}, u32[]{:S(2)}) collective-permute-start(bf16[128,1024]{1,0:T(8,128)(2,1)} %refs_0_.1), channel_id=1, source_target_pairs={{0,8},{1,9},{2,10},{3,11},{4,12},{5,13},{6,14},{7,15},{8,0},{9,1},... | collective-permute-start | bytes 786440 | tf_op jit(solution)/shard_map/ppermute | solution.py:47
  6.3 13.2 %collective-permute-start.4 = (bf16[128,1024]{1,0:T(8,128)(2,1)}, bf16[128,1024]{1,0:T(8,128)(2,1)S(1)}, u32[]{:S(2)}, u32[]{:S(2)}) collective-permute-start(bf16[128,1024]{1,0:T(8,128)(2,1)} %refs_0_.1), channel_id=1, source_target_pairs={{0,4},{1,5},{2,6},{3,7},{4,0},{5,1},{6,2},{7,3},{8,12},{9,13},{10,... | collective-permute-start | bytes 786440 | tf_op jit(solution)/shard_map/ppermute | solution.py:47
  19.7 8.4 %collective-permute-start.2 = (bf16[128,1024]{1,0:T(8,128)(2,1)S(1)}, bf16[128,1024]{1,0:T(8,128)(2,1)S(1)}, u32[]{:S(2)}, u32[]{:S(2)}) collective-permute-start(bf16[128,1024]{1,0:T(8,128)(2,1)S(1)} %collective-permute-done.refs_0_), channel_id=1, source_target_pairs={{0,4},{1,5},{2,6},{3,7},{4,0},{5,1},{6,2},{7,3},{8,12},{9,13},{10,... | collective-permute-start | bytes 786440 | tf_op jit(solution)/shard_map/ppermute | solution.py:47
  20.8 6.2 %collective-permute-start.3 = (f32[1,512]{1,0:T(1,128)S(1)}, f32[1,512]{1,0:T(1,128)S(1)}, u32[]{:S(2)}, u32[]{:S(2)}) collective-permute-start(f32[1,512]{1,0:T(1,128)S(1)} %bitcast.8), channel_id=1, source_target_pairs={{0,2},{1,3},{2,0},{3,1},{4,6},{5,7},{6,4},{7,5},{8,10},{9,11},{10,... | collective-permute-start | bytes 6152 | tf_op jit(solution)/shard_map/ppermute | solution.py:47
  32.7 5.6 %collective-permute-start.10 = (f32[3,1024]{1,0:T(4,128)S(1)}, f32[3,1024]{1,0:T(4,128)S(1)}, u32[]{:S(2)}, u32[]{:S(2)}) collective-permute-start(f32[3,1024]{1,0:T(4,128)S(1)} %merge.1.refs_0_), channel_id=1, source_target_pairs={{0,12},{1,13},{2,14},{3,15},{4,8},{5,9},{6,10},{7,11},{8,4},{9,5},... | collective-permute-start | bytes 36872 | tf_op jit(solution)/shard_map/ppermute | solution.py:47
  36.0 4.6 %collective-permute-start.11 = (f32[3,1024]{1,0:T(4,128)S(1)}, f32[3,1024]{1,0:T(4,128)S(1)}, u32[]{:S(2)}, u32[]{:S(2)}) collective-permute-start(f32[3,1024]{1,0:T(4,128)S(1)} %merge.1.refs_0_), channel_id=1, source_target_pairs={{0,8},{1,9},{2,10},{3,11},{4,12},{5,13},{6,14},{7,15},{8,0},{9,1},... | collective-permute-start | bytes 36872 | tf_op jit(solution)/shard_map/ppermute | solution.py:47
  36.0 4.6 %collective-permute-start.12 = (f32[3,1024]{1,0:T(4,128)S(1)}, f32[3,1024]{1,0:T(4,128)S(1)}, u32[]{:S(2)}, u32[]{:S(2)}) collective-permute-start(f32[3,1024]{1,0:T(4,128)S(1)} %merge.1.refs_0_), channel_id=1, source_target_pairs={{0,4},{1,5},{2,6},{3,7},{4,0},{5,1},{6,2},{7,3},{8,12},{9,13},{10,... | collective-permute-start | bytes 36872 | tf_op jit(solution)/shard_map/ppermute | solution.py:47
  37.2 9.1 %collective-permute-start.14 = (bf16[512,1024]{1,0:T(8,128)(2,1)S(1)}, bf16[512,1024]{1,0:T(8,128)(2,1)S(1)}, u32[]{:S(2)}, u32[]{:S(2)}) collective-permute-start(bf16[512,1024]{1,0:T(8,128)(2,1)S(1)} %copy-done.1), channel_id=1, source_target_pairs={{0,1},{1,0},{2,3},{3,2},{4,5},{5,4},{6,7},{7,6},{8,9},{9,8},{10,11... | collective-permute-start | bytes 3145736 | tf_op jit(solution)/shard_map/ppermute | solution.py:47
  42.0 4.3 %collective-permute-start.15 = (bf16[512,1024]{1,0:T(8,128)(2,1)S(1)}, bf16[512,1024]{1,0:T(8,128)(2,1)S(1)}, u32[]{:S(2)}, u32[]{:S(2)}) collective-permute-start(bf16[512,1024]{1,0:T(8,128)(2,1)S(1)} %collective-permute-done.8.refs_2_.refs_3_.refs_1_), channel_id=1, source_target_pairs={{0,1},{1,0},{2,3},{3,2},{4,5},{5,4},{6,7},{7,6},{8,9},{9,8},{10,11... | collective-permute-start | bytes 3145736 | tf_op jit(solution)/shard_map/ppermute | solution.py:47
  42.1 3.7 %collective-permute-start.13 = (f32[2,1024]{1,0:T(2,128)S(1)}, f32[2,1024]{1,0:T(2,128)S(1)}, u32[]{:S(2)}, u32[]{:S(2)}) collective-permute-start(f32[2,1024]{1,0:T(2,128)S(1)} %get-tuple-element.100.own_ref), channel_id=1, source_target_pairs={{0,2},{1,3},{2,0},{3,1},{4,6},{5,7},{6,4},{7,5},{8,10},{9,11},{10,... | collective-permute-start | bytes 24584 | tf_op jit(solution)/shard_map/ppermute | solution.py:47
  47.5 5.5 %collective-permute-start.17 = (f32[1,1024]{1,0:T(1,128)S(1)}, f32[1,1024]{1,0:T(1,128)S(1)}, u32[]{:S(2)}, u32[]{:S(2)}) collective-permute-start(f32[1,1024]{1,0:T(1,128)S(1)} %maximum_add_fusion.refs_0_), channel_id=1, source_target_pairs={{0,12},{1,13},{2,14},{3,15},{4,8},{5,9},{6,10},{7,11},{8,4},{9,5},... | collective-permute-start | bytes 12296 | tf_op jit(solution)/shard_map/ppermute | solution.py:47
  49.1 4.5 %collective-permute-start.18 = (f32[1,1024]{1,0:T(1,128)S(1)}, f32[1,1024]{1,0:T(1,128)S(1)}, u32[]{:S(2)}, u32[]{:S(2)}) collective-permute-start(f32[1,1024]{1,0:T(1,128)S(1)} %maximum_add_fusion.refs_0_), channel_id=1, source_target_pairs={{0,8},{1,9},{2,10},{3,11},{4,12},{5,13},{6,14},{7,15},{8,0},{9,1},... | collective-permute-start | bytes 12296 | tf_op jit(solution)/shard_map/ppermute | solution.py:47
  49.7 3.9 %collective-permute-start.19 = (f32[1,1024]{1,0:T(1,128)S(1)}, f32[1,1024]{1,0:T(1,128)S(1)}, u32[]{:S(2)}, u32[]{:S(2)}) collective-permute-start(f32[1,1024]{1,0:T(1,128)S(1)} %maximum_add_fusion.refs_0_), channel_id=1, source_target_pairs={{0,4},{1,5},{2,6},{3,7},{4,0},{5,1},{6,2},{7,3},{8,12},{9,13},{10,... | collective-permute-start | bytes 12296 | tf_op jit(solution)/shard_map/ppermute | solution.py:47
  59.4 5.5 %collective-permute-start.22 = (f32[1,1024]{1,0:T(1,128)S(1)}, f32[1,1024]{1,0:T(1,128)S(1)}, u32[]{:S(2)}, u32[]{:S(2)}) collective-permute-start(f32[1,1024]{1,0:T(1,128)S(1)} %maximum_add_fusion.1.refs_0_), channel_id=1, source_target_pairs={{0,12},{1,13},{2,14},{3,15},{4,8},{5,9},{6,10},{7,11},{8,4},{9,5},... | collective-permute-start | bytes 12296 | tf_op jit(solution)/shard_map/ppermute | solution.py:47
  62.0 4.5 %collective-permute-start.23 = (f32[1,1024]{1,0:T(1,128)S(1)}, f32[1,1024]{1,0:T(1,128)S(1)}, u32[]{:S(2)}, u32[]{:S(2)}) collective-permute-start(f32[1,1024]{1,0:T(1,128)S(1)} %maximum_add_fusion.1.refs_0_), channel_id=1, source_target_pairs={{0,8},{1,9},{2,10},{3,11},{4,12},{5,13},{6,14},{7,15},{8,0},{9,1},... | collective-permute-start | bytes 12296 | tf_op jit(solution)/shard_map/ppermute | solution.py:47
  66.9 3.7 %collective-permute-start.25 = (f32[2,1024]{1,0:T(2,128)S(1)}, f32[2,1024]{1,0:T(2,128)S(1)}, u32[]{:S(2)}, u32[]{:S(2)}) collective-permute-start(f32[2,1024]{1,0:T(2,128)S(1)} %get-tuple-element.112.own_ref), channel_id=1, source_target_pairs={{0,2},{1,3},{2,0},{3,1},{4,6},{5,7},{6,4},{7,5},{8,10},{9,11},{10,... | collective-permute-start | bytes 24584 | tf_op jit(solution)/shard_map/ppermute | solution.py:47
  71.1 5.1 %collective-permute-start.26 = (bf16[1024,384]{1,0:T(8,128)(2,1)S(1)}, bf16[1024,384]{1,0:T(8,128)(2,1)S(1)}, u32[]{:S(2)}, u32[]{:S(2)}) collective-permute-start(bf16[1024,384]{1,0:T(8,128)(2,1)S(1)} %get-tuple-element.120), channel_id=1, source_target_pairs={{0,1},{1,0},{2,3},{3,2},{4,5},{5,4},{6,7},{7,6},{8,9},{9,8},{10,11... | collective-permute-start | bytes 2359304 | tf_op jit(solution)/shard_map/ppermute | solution.py:47
  71.7 24.7 %collective-permute-start.30 = (bf16[384,1024]{1,0:T(8,128)(2,1)S(1)}, bf16[384,1024]{1,0:T(8,128)(2,1)S(1)}, u32[]{:S(2)}, u32[]{:S(2)}) collective-permute-start(bf16[384,1024]{1,0:T(8,128)(2,1)S(1)} %col_send.2), channel_id=1, source_target_pairs={{0,2},{1,3},{2,0},{3,1},{4,6},{5,7},{6,4},{7,5},{8,10},{9,11},{10,... | collective-permute-start | bytes 2359304 | tf_op jit(solution)/shard_map/ppermute | solution.py:47
  74.8 9.6 %collective-permute-start.31 = (bf16[136,1024]{1,0:T(8,128)(2,1)S(1)}, bf16[136,1024]{1,0:T(8,128)(2,1)S(1)}, u32[]{:S(2)}, u32[]{:S(2)}) collective-permute-start(bf16[136,1024]{1,0:T(8,128)(2,1)S(1)} %row_part.2), channel_id=1, source_target_pairs={{0,4},{1,5},{2,6},{3,7},{4,0},{5,1},{6,2},{7,3},{8,12},{9,13},{10,... | collective-permute-start | bytes 835592 | tf_op jit(solution)/shard_map/ppermute | solution.py:47
  78.1 15.9 %collective-permute-start.28 = (bf16[136,1024]{1,0:T(8,128)(2,1)S(1)}, bf16[136,1024]{1,0:T(8,128)(2,1)S(1)}, u32[]{:S(2)}, u32[]{:S(2)}) collective-permute-start(bf16[136,1024]{1,0:T(8,128)(2,1)S(1)} %get-tuple-element.131), channel_id=1, source_target_pairs={{0,4},{1,5},{2,6},{3,7},{4,0},{5,1},{6,2},{7,3},{8,12},{9,13},{10,... | collective-permute-start | bytes 835592 | tf_op jit(solution)/shard_map/ppermute | solution.py:47
  84.4 14.0 %collective-permute-start.32 = (bf16[136,1024]{1,0:T(8,128)(2,1)S(1)}, bf16[136,1024]{1,0:T(8,128)(2,1)S(1)}, u32[]{:S(2)}, u32[]{:S(2)}) collective-permute-start(bf16[136,1024]{1,0:T(8,128)(2,1)S(1)} %line.1), channel_id=1, source_target_pairs={{0,8},{1,9},{2,10},{3,11},{4,12},{5,13},{6,14},{7,15},{8,0},{9,1},... | collective-permute-start | bytes 835592 | tf_op jit(solution)/shard_map/ppermute | solution.py:47
  86.4 11.3 %collective-permute-start.29 = (bf16[128,1024]{1,0:T(8,128)(2,1)S(1)}, bf16[128,1024]{1,0:T(8,128)(2,1)S(1)}, u32[]{:S(2)}, u32[]{:S(2)}) collective-permute-start(bf16[128,1024]{1,0:T(8,128)(2,1)S(1)} %col_send.3), channel_id=1, source_target_pairs={{0,2},{1,3},{2,0},{3,1},{4,6},{5,7},{6,4},{7,5},{8,10},{9,11},{10,... | collective-permute-start | bytes 786440 | tf_op jit(solution)/shard_map/ppermute | solution.py:47
  (15 other events, 33.9 us)

commit v10 on v9

--- a/solution.py
+++ b/solution.py
@@ -314,6 +314,36 @@
         else:
             ref[rows:, :rows] = jnp.broadcast_to(mass[:, here], (TAIL, rows))
             ref[rows:, rows:] = jnp.zeros((TAIL, width - rows), F32)
+
+
+def contract(plan_ref, lanes, y_refs):
+    part = mass = 0.0
+    start = 0
+    for y in y_refs:
+        block = plan_ref[start : start + y.shape[0], lanes]
+        start += y.shape[0]
+        part = part + lax.dot_general(
+            block, y[...], (((0,), (0,)), ((), ())), preferred_element_type=F32
+        )
+        mass = mass + jnp.sum(block.astype(F32), axis=0, keepdims=True)
+    return part, mass
+
+
+def far_own_kernel(lanes, plan_ref, *refs):
+    *y_refs, out_ref = refs
+    part, mass = contract(plan_ref, lanes, y_refs)
+    rows, width = part.shape
+    out_ref[:rows, :] = part
+    out_ref[rows:, :rows] = jnp.broadcast_to(mass, (TAIL, rows))
+    out_ref[rows:, rows:] = jnp.zeros((TAIL, width - rows), F32)
+
+
+def far_send_kernel(own_ref, plan_ref, *refs):
+    *y_refs, out_ref = refs
+    part, mass = contract(plan_ref, slice(None), y_refs)
+    rows, width = part.shape
+    out_ref[:rows, :] = (own_ref[:rows, :] + part).astype(BF16)
+    out_ref[rows:, :] = split_mass(own_ref[rows : rows + 1, :rows] + mass, width)
 
 
 def line_kernel(own_ref, other_ref, out_ref):
@@ -573,23 +603,22 @@
         others[0] = swap(sends[0], 1)
         block, block_out = shape((rows + TAIL, width)), shape((rows + TAIL, width), BF16)
 
-        def row_parts(far, gate):
-            plan, other, _ = lax.optimization_barrier((keep, others[far], gate))
-            outs = [block_out] if far else [block, block_out, block]
-            lanes = slice(3 * rows, half) if far else slice(0, 3 * rows)
-            return call(
-                functools.partial(row_part_kernel, lanes, len(outs)),
-                "row_part",
-                [plan, other, *ys],
-                outs,
-            )
-
-        (out3,) = row_parts(True, keep)
+        far = slice(3 * rows, half)
+        (own3,) = call(
+            functools.partial(far_own_kernel, far), "far_own", [keep, *ys[:2]], [block]
+        )
+        (out3,) = call(far_send_kernel, "far_send", [own3, others[1], *ys[2:]], [block_out])
         near3 = swap(out3, 4)
         first, _ = lax.optimization_barrier((early[0], out3))
         out = col_send(1, first)
         back.append(swap(out, 2))
-        own0, out1, own2 = row_parts(False, out)
+        rest, _ = lax.optimization_barrier((keep, out))
+        own0, out1, own2 = call(
+            functools.partial(row_part_kernel, slice(0, 3 * rows), 3),
+            "row_part",
+            [rest, others[0], *ys],
+            [block, block_out, block],
+        )
         near1 = swap(out1, 4)
         (out2,) = call(line_kernel, "line", [own2, near3], [block_out])
         far2 = swap(out2, 8)

time: 100 us -> 99.7 us (level)
    pallas_call x23 -> x24, Pallas kernels: 19.3 us -> 19.5 us  [call(): pl.pallas_call(body, name=name, out_shape=outs, in_specs=specs, out_specs...]
where the time goes in v10:
time: 99.7 us; the launch traced here: 99.4 us
  waiting for transfers between devices  40.7 us (41%)
  starting transfers between devices  33.4 us (34%)
  Pallas kernels  19.5 us (20%)
  local copies, waits for them, and re-layouts  4.27 us (4%)
  between operations  1.02 us (1%)
    ppermute x33, waiting for transfers between devices, swap(): return lax.ppermute(value, AXIS, [(i, i ^ mask) for i in range(count)])  40.7 us
    ppermute x33, starting transfers between devices, swap(): return lax.ppermute(value, AXIS, [(i, i ^ mask) for i in range(count)])  33.4 us
    pallas_call x24, Pallas kernels, call(): pl.pallas_call(body, name=name, out_shape=outs, in_specs=specs, out_specs...  19.5 us
    unnamed x12, local copies, waits for them, and re-layouts  4.27 us
  transfers between devices with their start and end apart: 33, of which 20 were waited for; matrix products, arithmetic and copies ran while one was open for 1% of the time, Pallas kernels for 15%

profile of v10, /device:TPU:0, one launch (start us, length us, event | category | flops | bytes accessed | tf_op | source)
XLA Modules:
  0.0 99.4 jit_solution(7556078700532576850)
XLA Ops:
  0.6 3.0 %collective-permute-start.8 = (bf16[512,1024]{1,0:T(8,128)(2,1)}, bf16[512,1024]{1,0:T(8,128)(2,1)S(1)}, u32[]{:S(2)}, u32[]{:S(2)}) collective-permute-start(bf16[512,1024]{1,0:T(8,128)(2,1)} %refs_4_.3), channel_id=1, source_target_pairs={{0,2},{1,3},{2,0},{3,1},{4,6},{5,7},{6,4},{7,5},{8,10},{9,11},{10,... | collective-permute-start | bytes 3145736 | tf_op jit(solution)/shard_map/ppermute | solution.py:47
  3.7 2.6 %collective-permute-start = (bf16[128,1024]{1,0:T(8,128)(2,1)}, bf16[128,1024]{1,0:T(8,128)(2,1)S(1)}, u32[]{:S(2)}, u32[]{:S(2)}) collective-permute-start(bf16[128,1024]{1,0:T(8,128)(2,1)} %refs_0_.1), channel_id=1, source_target_pairs={{0,8},{1,9},{2,10},{3,11},{4,12},{5,13},{6,14},{7,15},{8,0},{9,1},... | collective-permute-start | bytes 786440 | tf_op jit(solution)/shard_map/ppermute | solution.py:47
  6.3 1.6 %collective-permute-start.4 = (bf16[128,1024]{1,0:T(8,128)(2,1)}, bf16[128,1024]{1,0:T(8,128)(2,1)S(1)}, u32[]{:S(2)}, u32[]{:S(2)}) collective-permute-start(bf16[128,1024]{1,0:T(8,128)(2,1)} %refs_0_.1), channel_id=1, source_target_pairs={{0,4},{1,5},{2,6},{3,7},{4,0},{5,1},{6,2},{7,3},{8,12},{9,13},{10,... | collective-permute-start | bytes 786440 | tf_op jit(solution)/shard_map/ppermute | solution.py:47
  8.7 1.2 %copy-done = bf16[512,1024]{1,0:T(8,128)(2,1)S(1)} copy-done((bf16[512,1024]{1,0:T(8,128)(2,1)S(1)}, bf16[512,1024]{1,0:T(8,128)(2,1)}, u32[]{:S(2)}) %copy-start) | copy-done | bytes 1048600
  13.2 6.1 %collective-permute-done.refs_0_ = bf16[128,1024]{1,0:T(8,128)(2,1)S(1)} collective-permute-done((bf16[128,1024]{1,0:T(8,128)(2,1)}, bf16[128,1024]{1,0:T(8,128)(2,1)S(1)}, u32[]{:S(2)}, u32[]{:S(2)}) %collective-permute-start) | collective-permute-done | bytes 262176 | tf_op jit(solution)/shard_map/ppermute | solution.py:47
  23.0 4.0 %collective-permute-done.3.refs_3_ = f32[1,512]{1,0:T(1,128)S(1)} collective-permute-done((f32[1,512]{1,0:T(1,128)S(1)}, f32[1,512]{1,0:T(1,128)S(1)}, u32[]{:S(2)}, u32[]{:S(2)}) %collective-permute-start.3) | collective-permute-done | bytes 2080 | tf_op jit(solution)/shard_map/ppermute | solution.py:47
  28.1 1.7 %cost.8 = (f32[1024,512]{1,0:T(8,128)S(1)}, f32[1024,512]{1,0:T(8,128)S(1)}, f32[3,1024]{1,0:T(4,128)S(1)}, f32[512,1]{1,0:T(8,128)S(1)}) custom-call(bf16[512,1024]{1,0:T(8,128)(2,1)S(1)} %get-tuple-element.84.refs_0_.refs_9_, bf16[512,1024]{1,0:T(8,128)(2,1)S(1)} %get-tuple-element.85.refs_1_.refs_10_, ...), custom_call_target="tpu_custom_call", output_to_operand_aliasing={{0}: (5, {}), {1}: (6, {})} | custom-call | flops 1 | bytes 1 | tf_op jit(solution)/shard_map/cost/pallas_call | solution.py:24
  29.8 1.4 %cost.9 = (f32[1024,512]{1,0:T(8,128)S(1)}, f32[1024,512]{1,0:T(8,128)S(1)}, bf16[512,1024]{1,0:T(8,128)(2,1)S(1)}, bf16[512,1024]{1,0:T(8,128)(2,1)S(1)}, f32[3,1024]{1,0:T(4,128)S(1)}) custom-call(bf16[128,1024]{1,0:T(8,128)(2,1)S(1)} %collective-permute-done.2.refs_0_, ...), custom_call_target="tpu_custom_call", output_to_operand_aliasing={{0}: (7, {}), {1}: (8, {}), {2}: (9, {}), {3}: (10, {})} | custom-call | flops 1 | bytes 1 | tf_op jit(solution)/shard_map/cost/pallas_call | solution.py:24
  32.7 3.3 %collective-permute-start.10 = (f32[3,1024]{1,0:T(4,128)S(1)}, f32[3,1024]{1,0:T(4,128)S(1)}, u32[]{:S(2)}, u32[]{:S(2)}) collective-permute-start(f32[3,1024]{1,0:T(4,128)S(1)} %merge.1.refs_0_), channel_id=1, source_target_pairs={{0,12},{1,13},{2,14},{3,15},{4,8},{5,9},{6,10},{7,11},{8,4},{9,5},... | collective-permute-start | bytes 36872 | tf_op jit(solution)/shard_map/ppermute | solution.py:47
  38.3 2.4 %collective-permute-done.11.refs_2_ = f32[3,1024]{1,0:T(4,128)S(1)} collective-permute-done((f32[3,1024]{1,0:T(4,128)S(1)}, f32[3,1024]{1,0:T(4,128)S(1)}, u32[]{:S(2)}, u32[]{:S(2)}) %collective-permute-start.11) | collective-permute-done | bytes 12320 | tf_op jit(solution)/shard_map/ppermute | solution.py:47
  40.7 1.3 %first.1 = (f32[1024,1024]{1,0:T(8,128)S(1)}, f32[2,1024]{1,0:T(2,128)S(1)}, f32[1,1024]{1,0:T(1,128)S(1)}, f32[2,1024]{1,0:T(2,128)S(1)}) custom-call(f32[3,1024]{1,0:T(4,128)S(1)} %merge.1.refs_0_, f32[3,1024]{1,0:T(4,128)S(1)} %collective-permute-done.10.refs_1_, f32[3,1024]{1,0:T(4,128)S(1)} %collective-permute-done.11.refs_2_, ...), custom_call_target="tpu_custom_call" | custom-call | flops 1 | bytes 1 | tf_op jit(solution)/shard_map/first/pallas_call | solution.py:24
  43.2 2.6 %collective-permute-done.13.other_ref = f32[2,1024]{1,0:T(2,128)S(1)} collective-permute-done((f32[2,1024]{1,0:T(2,128)S(1)}, f32[2,1024]{1,0:T(2,128)S(1)}, u32[]{:S(2)}, u32[]{:S(2)}) %collective-permute-start.13) | collective-permute-done | bytes 8224 | tf_op jit(solution)/shard_map/ppermute | solution.py:47
  47.5 1.5 %collective-permute-start.17 = (f32[1,1024]{1,0:T(1,128)S(1)}, f32[1,1024]{1,0:T(1,128)S(1)}, u32[]{:S(2)}, u32[]{:S(2)}) collective-permute-start(f32[1,1024]{1,0:T(1,128)S(1)} %maximum_add_fusion.refs_0_), channel_id=1, source_target_pairs={{0,12},{1,13},{2,14},{3,15},{4,8},{5,9},{6,10},{7,11},{8,4},{9,5},... | collective-permute-start | bytes 12296 | tf_op jit(solution)/shard_map/ppermute | solution.py:47
  49.7 2.3 %collective-permute-start.19 = (f32[1,1024]{1,0:T(1,128)S(1)}, f32[1,1024]{1,0:T(1,128)S(1)}, u32[]{:S(2)}, u32[]{:S(2)}) collective-permute-start(f32[1,1024]{1,0:T(1,128)S(1)} %maximum_add_fusion.refs_0_), channel_id=1, source_target_pairs={{0,4},{1,5},{2,6},{3,7},{4,0},{5,1},{6,2},{7,3},{8,12},{9,13},{10,... | collective-permute-start | bytes 12296 | tf_op jit(solution)/shard_map/ppermute | solution.py:47
  55.1 2.6 %collective-permute-done.20.other_ref = f32[1,1024]{1,0:T(1,128)S(1)} collective-permute-done((f32[1,1024]{1,0:T(1,128)S(1)}, f32[1,1024]{1,0:T(1,128)S(1)}, u32[]{:S(2)}, u32[]{:S(2)}) %collective-permute-start.20) | collective-permute-done | bytes 4128 | tf_op jit(solution)/shard_map/ppermute | solution.py:47
  59.4 2.6 %collective-permute-start.22 = (f32[1,1024]{1,0:T(1,128)S(1)}, f32[1,1024]{1,0:T(1,128)S(1)}, u32[]{:S(2)}, u32[]{:S(2)}) collective-permute-start(f32[1,1024]{1,0:T(1,128)S(1)} %maximum_add_fusion.1.refs_0_), channel_id=1, source_target_pairs={{0,12},{1,13},{2,14},{3,15},{4,8},{5,9},{6,10},{7,11},{8,4},{9,5},... | collective-permute-start | bytes 12296 | tf_op jit(solution)/shard_map/ppermute | solution.py:47
  64.9 1.6 %collective-permute-done.23.refs_2_ = f32[1,1024]{1,0:T(1,128)S(1)} collective-permute-done((f32[1,1024]{1,0:T(1,128)S(1)}, f32[1,1024]{1,0:T(1,128)S(1)}, u32[]{:S(2)}, u32[]{:S(2)}) %collective-permute-start.23) | collective-permute-done | bytes 4128 | tf_op jit(solution)/shard_map/ppermute | solution.py:47
  75.8 1.8 %row_part.1 = (f32[136,1024]{1,0:T(8,128)S(1)}, bf16[136,1024]{1,0:T(8,128)(2,1)S(1)}, f32[136,1024]{1,0:T(8,128)S(1)}) custom-call(bf16[1024,512]{1,0:T(8,128)(2,1)S(1)} %get-tuple-element.123.plan_ref.keep_ref, bf16[1024,384]{1,0:T(8,128)(2,1)S(1)} %collective-permute-done.27.other_ref, bf16[512,1024]{1,0:T(8,128)(2,1)S(1)} %copy-done.1, ...), custom_call_target="tpu_custom_call" | custom-call | flops 1 | bytes 1 | tf_op jit(solution)/shard_map/row_part/pallas_call | solution.py:24
  78.8 5.1 %collective-permute-done.31.other_ref = bf16[136,1024]{1,0:T(8,128)(2,1)S(1)} collective-permute-done((bf16[136,1024]{1,0:T(8,128)(2,1)S(1)}, bf16[136,1024]{1,0:T(8,128)(2,1)S(1)}, u32[]{:S(2)}, u32[]{:S(2)}) %collective-permute-start.31) | collective-permute-done | bytes 278560 | tf_op jit(solution)/shard_map/ppermute | solution.py:47
  83.9 2.0 %collective-permute-start.32 = (bf16[136,1024]{1,0:T(8,128)(2,1)S(1)}, bf16[136,1024]{1,0:T(8,128)(2,1)S(1)}, u32[]{:S(2)}, u32[]{:S(2)}) collective-permute-start(bf16[136,1024]{1,0:T(8,128)(2,1)S(1)} %line.1), channel_id=1, source_target_pairs={{0,8},{1,9},{2,10},{3,11},{4,12},{5,13},{6,14},{7,15},{8,0},{9,1},... | collective-permute-start | bytes 835592 | tf_op jit(solution)/shard_map/ppermute | solution.py:47
  87.0 6.5 %collective-permute-done.28.refs_7_ = bf16[136,1024]{1,0:T(8,128)(2,1)S(1)} collective-permute-done((bf16[136,1024]{1,0:T(8,128)(2,1)S(1)}, bf16[136,1024]{1,0:T(8,128)(2,1)S(1)}, u32[]{:S(2)}, u32[]{:S(2)}) %collective-permute-start.28) | collective-permute-done | bytes 278560 | tf_op jit(solution)/shard_map/ppermute | solution.py:47
  94.4 1.5 %col_keep.1.refs_0_ = f32[512,1024]{1,0:T(8,128)S(1)} custom-call(bf16[1024,512]{1,0:T(8,128)(2,1)S(1)} %get-tuple-element.128.refs_0_, bf16[1024,384]{1,0:T(8,128)(2,1)S(1)} %get-tuple-element.112.refs_1_, bf16[1024,128]{1,0:T(8,128)(2,1)S(1)} %get-tuple-element.113.refs_2_, bf16[512,1024]{1,0:T(8,128)(2,1)S(1)} %get-tuple-element.105.refs_3_.refs_9_, ...), custom_call_target="tpu_custom_call" | custom-call | flops 1 | bytes 1 | tf_op jit(solution)/shard_map/col_keep/pallas_call | solution.py:24
  96.0 1.3 %target.1.refs_5_ = f32[512,1024]{1,0:T(8,128)} custom-call(f32[512,1024]{1,0:T(8,128)S(1)} %col_keep.1.refs_0_, bf16[384,1024]{1,0:T(8,128)(2,1)S(1)} %collective-permute-done.30.refs_1_, f32[1,1024]{1,0:T(1,128)S(1)} %get-tuple-element.111.mass_ref.refs_2_, f32[1,1024]{1,0:T(1,128)S(1)} %get-tuple-element.126.last_ref.refs_3_, bf16[512,1024]{1,0:T(8,128)(2,1)S(1)} %copy-done.1), custom_call_target="tpu_custom_call" | custom-call | flops 1 | bytes 2097152 | tf_op jit(solution)/shard_map/target/pallas_call | solution.py:24
  98.0 1.2 %last.1 = (f32[512,1024]{1,0:T(8,128)}, f32[128,1024]{1,0:T(8,128)}) custom-call(f32[512,1024]{1,0:T(8,128)S(1)} %col_keep.1.refs_0_, bf16[128,1024]{1,0:T(8,128)(2,1)S(1)} %collective-permute-done.29.refs_1_, f32[1,1024]{1,0:T(1,128)S(1)} %get-tuple-element.111.mass_ref.refs_2_, ...), custom_call_target="tpu_custom_call", output_to_operand_aliasing={{0}: (5, {})} | custom-call | flops 1 | bytes 524288 | tf_op jit(solution)/shard_map/last/pallas_call | solution.py:24
  (85 shorter events, 36.9 us)
Async XLA Ops:
  0.6 27.5 %collective-permute-start.8 = (bf16[512,1024]{1,0:T(8,128)(2,1)}, bf16[512,1024]{1,0:T(8,128)(2,1)S(1)}, u32[]{:S(2)}, u32[]{:S(2)}) collective-permute-start(bf16[512,1024]{1,0:T(8,128)(2,1)} %refs_4_.3), channel_id=1, source_target_pairs={{0,2},{1,3},{2,0},{3,1},{4,6},{5,7},{6,4},{7,5},{8,10},{9,11},{10,... | collective-permute-start | bytes 3145736 | tf_op jit(solution)/shard_map/ppermute | solution.py:47
  3.7 5.0 %collective-permute-start.1 = (bf16[128,1024]{1,0:T(8,128)(2,1)}, bf16[128,1024]{1,0:T(8,128)(2,1)S(1)}, u32[]{:S(2)}, u32[]{:S(2)}) collective-permute-start(bf16[128,1024]{1,0:T(8,128)(2,1)} %refs_0_.1), channel_id=1, source_target_pairs={{0,1},{1,0},{2,3},{3,2},{4,5},{5,4},{6,7},{7,6},{8,9},{9,8},{10,11... | collective-permute-start | bytes 786440 | tf_op jit(solution)/shard_map/ppermute | solution.py:47
  3.7 15.6 %collective-permute-start = (bf16[128,1024]{1,0:T(8,128)(2,1)}, bf16[128,1024]{1,0:T(8,128)(2,1)S(1)}, u32[]{:S(2)}, u32[]{:S(2)}) collective-permute-start(bf16[128,1024]{1,0:T(8,128)(2,1)} %refs_0_.1), channel_id=1, source_target_pairs={{0,8},{1,9},{2,10},{3,11},{4,12},{5,13},{6,14},{7,15},{8,0},{9,1},... | collective-permute-start | bytes 786440 | tf_op jit(solution)/shard_map/ppermute | solution.py:47
  6.3 13.2 %collective-permute-start.4 = (bf16[128,1024]{1,0:T(8,128)(2,1)}, bf16[128,1024]{1,0:T(8,128)(2,1)S(1)}, u32[]{:S(2)}, u32[]{:S(2)}) collective-permute-start(bf16[128,1024]{1,0:T(8,128)(2,1)} %refs_0_.1), channel_id=1, source_target_pairs={{0,4},{1,5},{2,6},{3,7},{4,0},{5,1},{6,2},{7,3},{8,12},{9,13},{10,... | collective-permute-start | bytes 786440 | tf_op jit(solution)/shard_map/ppermute | solution.py:47
  19.7 8.4 %collective-permute-start.2 = (bf16[128,1024]{1,0:T(8,128)(2,1)S(1)}, bf16[128,1024]{1,0:T(8,128)(2,1)S(1)}, u32[]{:S(2)}, u32[]{:S(2)}) collective-permute-start(bf16[128,1024]{1,0:T(8,128)(2,1)S(1)} %collective-permute-done.refs_0_), channel_id=1, source_target_pairs={{0,4},{1,5},{2,6},{3,7},{4,0},{5,1},{6,2},{7,3},{8,12},{9,13},{10,... | collective-permute-start | bytes 786440 | tf_op jit(solution)/shard_map/ppermute | solution.py:47
  20.8 6.2 %collective-permute-start.3 = (f32[1,512]{1,0:T(1,128)S(1)}, f32[1,512]{1,0:T(1,128)S(1)}, u32[]{:S(2)}, u32[]{:S(2)}) collective-permute-start(f32[1,512]{1,0:T(1,128)S(1)} %bitcast.8), channel_id=1, source_target_pairs={{0,2},{1,3},{2,0},{3,1},{4,6},{5,7},{6,4},{7,5},{8,10},{9,11},{10,... | collective-permute-start | bytes 6152 | tf_op jit(solution)/shard_map/ppermute | solution.py:47
  32.7 5.6 %collective-permute-start.10 = (f32[3,1024]{1,0:T(4,128)S(1)}, f32[3,1024]{1,0:T(4,128)S(1)}, u32[]{:S(2)}, u32[]{:S(2)}) collective-permute-start(f32[3,1024]{1,0:T(4,128)S(1)} %merge.1.refs_0_), channel_id=1, source_target_pairs={{0,12},{1,13},{2,14},{3,15},{4,8},{5,9},{6,10},{7,11},{8,4},{9,5},... | collective-permute-start | bytes 36872 | tf_op jit(solution)/shard_map/ppermute | solution.py:47
  36.0 4.6 %collective-permute-start.11 = (f32[3,1024]{1,0:T(4,128)S(1)}, f32[3,1024]{1,0:T(4,128)S(1)}, u32[]{:S(2)}, u32[]{:S(2)}) collective-permute-start(f32[3,1024]{1,0:T(4,128)S(1)} %merge.1.refs_0_), channel_id=1, source_target_pairs={{0,8},{1,9},{2,10},{3,11},{4,12},{5,13},{6,14},{7,15},{8,0},{9,1},... | collective-permute-start | bytes 36872 | tf_op jit(solution)/shard_map/ppermute | solution.py:47
  36.0 4.6 %collective-permute-start.12 = (f32[3,1024]{1,0:T(4,128)S(1)}, f32[3,1024]{1,0:T(4,128)S(1)}, u32[]{:S(2)}, u32[]{:S(2)}) collective-permute-start(f32[3,1024]{1,0:T(4,128)S(1)} %merge.1.refs_0_), channel_id=1, source_target_pairs={{0,4},{1,5},{2,6},{3,7},{4,0},{5,1},{6,2},{7,3},{8,12},{9,13},{10,... | collective-permute-start | bytes 36872 | tf_op jit(solution)/shard_map/ppermute | solution.py:47
  37.2 9.1 %collective-permute-start.14 = (bf16[512,1024]{1,0:T(8,128)(2,1)S(1)}, bf16[512,1024]{1,0:T(8,128)(2,1)S(1)}, u32[]{:S(2)}, u32[]{:S(2)}) collective-permute-start(bf16[512,1024]{1,0:T(8,128)(2,1)S(1)} %copy-done.1), channel_id=1, source_target_pairs={{0,1},{1,0},{2,3},{3,2},{4,5},{5,4},{6,7},{7,6},{8,9},{9,8},{10,11... | collective-permute-start | bytes 3145736 | tf_op jit(solution)/shard_map/ppermute | solution.py:47
  42.0 4.3 %collective-permute-start.15 = (bf16[512,1024]{1,0:T(8,128)(2,1)S(1)}, bf16[512,1024]{1,0:T(8,128)(2,1)S(1)}, u32[]{:S(2)}, u32[]{:S(2)}) collective-permute-start(bf16[512,1024]{1,0:T(8,128)(2,1)S(1)} %collective-permute-done.8.refs_2_.refs_3_.refs_1_), channel_id=1, source_target_pairs={{0,1},{1,0},{2,3},{3,2},{4,5},{5,4},{6,7},{7,6},{8,9},{9,8},{10,11... | collective-permute-start | bytes 3145736 | tf_op jit(solution)/shard_map/ppermute | solution.py:47
  42.1 3.7 %collective-permute-start.13 = (f32[2,1024]{1,0:T(2,128)S(1)}, f32[2,1024]{1,0:T(2,128)S(1)}, u32[]{:S(2)}, u32[]{:S(2)}) collective-permute-start(f32[2,1024]{1,0:T(2,128)S(1)} %get-tuple-element.97.own_ref), channel_id=1, source_target_pairs={{0,2},{1,3},{2,0},{3,1},{4,6},{5,7},{6,4},{7,5},{8,10},{9,11},{10,... | collective-permute-start | bytes 24584 | tf_op jit(solution)/shard_map/ppermute | solution.py:47
  47.5 5.5 %collective-permute-start.17 = (f32[1,1024]{1,0:T(1,128)S(1)}, f32[1,1024]{1,0:T(1,128)S(1)}, u32[]{:S(2)}, u32[]{:S(2)}) collective-permute-start(f32[1,1024]{1,0:T(1,128)S(1)} %maximum_add_fusion.refs_0_), channel_id=1, source_target_pairs={{0,12},{1,13},{2,14},{3,15},{4,8},{5,9},{6,10},{7,11},{8,4},{9,5},... | collective-permute-start | bytes 12296 | tf_op jit(solution)/shard_map/ppermute | solution.py:47
  49.1 4.5 %collective-permute-start.18 = (f32[1,1024]{1,0:T(1,128)S(1)}, f32[1,1024]{1,0:T(1,128)S(1)}, u32[]{:S(2)}, u32[]{:S(2)}) collective-permute-start(f32[1,1024]{1,0:T(1,128)S(1)} %maximum_add_fusion.refs_0_), channel_id=1, source_target_pairs={{0,8},{1,9},{2,10},{3,11},{4,12},{5,13},{6,14},{7,15},{8,0},{9,1},... | collective-permute-start | bytes 12296 | tf_op jit(solution)/shard_map/ppermute | solution.py:47
  49.7 3.9 %collective-permute-start.19 = (f32[1,1024]{1,0:T(1,128)S(1)}, f32[1,1024]{1,0:T(1,128)S(1)}, u32[]{:S(2)}, u32[]{:S(2)}) collective-permute-start(f32[1,1024]{1,0:T(1,128)S(1)} %maximum_add_fusion.refs_0_), channel_id=1, source_target_pairs={{0,4},{1,5},{2,6},{3,7},{4,0},{5,1},{6,2},{7,3},{8,12},{9,13},{10,... | collective-permute-start | bytes 12296 | tf_op jit(solution)/shard_map/ppermute | solution.py:47
  59.4 5.5 %collective-permute-start.22 = (f32[1,1024]{1,0:T(1,128)S(1)}, f32[1,1024]{1,0:T(1,128)S(1)}, u32[]{:S(2)}, u32[]{:S(2)}) collective-permute-start(f32[1,1024]{1,0:T(1,128)S(1)} %maximum_add_fusion.1.refs_0_), channel_id=1, source_target_pairs={{0,12},{1,13},{2,14},{3,15},{4,8},{5,9},{6,10},{7,11},{8,4},{9,5},... | collective-permute-start | bytes 12296 | tf_op jit(solution)/shard_map/ppermute | solution.py:47
  62.0 4.5 %collective-permute-start.23 = (f32[1,1024]{1,0:T(1,128)S(1)}, f32[1,1024]{1,0:T(1,128)S(1)}, u32[]{:S(2)}, u32[]{:S(2)}) collective-permute-start(f32[1,1024]{1,0:T(1,128)S(1)} %maximum_add_fusion.1.refs_0_), channel_id=1, source_target_pairs={{0,8},{1,9},{2,10},{3,11},{4,12},{5,13},{6,14},{7,15},{8,0},{9,1},... | collective-permute-start | bytes 12296 | tf_op jit(solution)/shard_map/ppermute | solution.py:47
  66.9 3.7 %collective-permute-start.25 = (f32[2,1024]{1,0:T(2,128)S(1)}, f32[2,1024]{1,0:T(2,128)S(1)}, u32[]{:S(2)}, u32[]{:S(2)}) collective-permute-start(f32[2,1024]{1,0:T(2,128)S(1)} %get-tuple-element.109.own_ref), channel_id=1, source_target_pairs={{0,2},{1,3},{2,0},{3,1},{4,6},{5,7},{6,4},{7,5},{8,10},{9,11},{10,... | collective-permute-start | bytes 24584 | tf_op jit(solution)/shard_map/ppermute | solution.py:47
  71.1 4.7 %collective-permute-start.27 = (bf16[1024,384]{1,0:T(8,128)(2,1)S(1)}, bf16[1024,384]{1,0:T(8,128)(2,1)S(1)}, u32[]{:S(2)}, u32[]{:S(2)}) collective-permute-start(bf16[1024,384]{1,0:T(8,128)(2,1)S(1)} %get-tuple-element.124), channel_id=1, source_target_pairs={{0,1},{1,0},{2,3},{3,2},{4,5},{5,4},{6,7},{7,6},{8,9},{9,8},{10,11... | collective-permute-start | bytes 2359304 | tf_op jit(solution)/shard_map/ppermute | solution.py:47
  71.7 24.3 %collective-permute-start.30 = (bf16[384,1024]{1,0:T(8,128)(2,1)S(1)}, bf16[384,1024]{1,0:T(8,128)(2,1)S(1)}, u32[]{:S(2)}, u32[]{:S(2)}) collective-permute-start(bf16[384,1024]{1,0:T(8,128)(2,1)S(1)} %col_send.2), channel_id=1, source_target_pairs={{0,2},{1,3},{2,0},{3,1},{4,6},{5,7},{6,4},{7,5},{8,10},{9,11},{10,... | collective-permute-start | bytes 2359304 | tf_op jit(solution)/shard_map/ppermute | solution.py:47
  74.3 9.6 %collective-permute-start.31 = (bf16[136,1024]{1,0:T(8,128)(2,1)S(1)}, bf16[136,1024]{1,0:T(8,128)(2,1)S(1)}, u32[]{:S(2)}, u32[]{:S(2)}) collective-permute-start(bf16[136,1024]{1,0:T(8,128)(2,1)S(1)} %far_send.1), channel_id=1, source_target_pairs={{0,4},{1,5},{2,6},{3,7},{4,0},{5,1},{6,2},{7,3},{8,12},{9,13},{10,... | collective-permute-start | bytes 835592 | tf_op jit(solution)/shard_map/ppermute | solution.py:47
  77.6 15.9 %collective-permute-start.28 = (bf16[136,1024]{1,0:T(8,128)(2,1)S(1)}, bf16[136,1024]{1,0:T(8,128)(2,1)S(1)}, u32[]{:S(2)}, u32[]{:S(2)}) collective-permute-start(bf16[136,1024]{1,0:T(8,128)(2,1)S(1)} %get-tuple-element.125), channel_id=1, source_target_pairs={{0,4},{1,5},{2,6},{3,7},{4,0},{5,1},{6,2},{7,3},{8,12},{9,13},{10,... | collective-permute-start | bytes 835592 | tf_op jit(solution)/shard_map/ppermute | solution.py:47
  83.9 14.0 %collective-permute-start.32 = (bf16[136,1024]{1,0:T(8,128)(2,1)S(1)}, bf16[136,1024]{1,0:T(8,128)(2,1)S(1)}, u32[]{:S(2)}, u32[]{:S(2)}) collective-permute-start(bf16[136,1024]{1,0:T(8,128)(2,1)S(1)} %line.1), channel_id=1, source_target_pairs={{0,8},{1,9},{2,10},{3,11},{4,12},{5,13},{6,14},{7,15},{8,0},{9,1},... | collective-permute-start | bytes 835592 | tf_op jit(solution)/shard_map/ppermute | solution.py:47
  86.0 11.3 %collective-permute-start.29 = (bf16[128,1024]{1,0:T(8,128)(2,1)S(1)}, bf16[128,1024]{1,0:T(8,128)(2,1)S(1)}, u32[]{:S(2)}, u32[]{:S(2)}) collective-permute-start(bf16[128,1024]{1,0:T(8,128)(2,1)S(1)} %col_send.3), channel_id=1, source_target_pairs={{0,2},{1,3},{2,0},{3,1},{4,6},{5,7},{6,4},{7,5},{8,10},{9,11},{10,... | collective-permute-start | bytes 786440 | tf_op jit(solution)/shard_map/ppermute | solution.py:47
  (15 other events, 33.9 us)
